TPU v7x, 32 devices: a whole 2x2x4 slice. The times are simulated.
32 devices in a mesh: dp: 4 (over x, core), ctx: 2 (over y), tensor: 4 (over z).
Axes of the slice: x: 2, y: 2, z: 4, core: 2. Of those that a mesh axis runs over, the one named last changes fastest.
Arguments:
- tokens: bfloat16 [4096, 2048], P(('dp', 'ctx')), may hold values from -6 to 6
- cotangent: bfloat16 [4096, 2048], P(('dp', 'ctx')), may hold values from -6 to 6
- first_gain: bfloat16 [2048], P('dp'), may hold values from 0.5 to 1.5
- query_weight: bfloat16 [2048, 2048], P('dp', 'tensor'), may hold values from -0.5 to 0.5
- key_weight: bfloat16 [2048, 512], P('dp', 'tensor'), may hold values from -0.5 to 0.5
- value_weight: bfloat16 [2048, 512], P('dp', 'tensor'), may hold values from -0.125 to 0.125
- output_weight: bfloat16 [2048, 2048], P('tensor', 'dp'), may hold values from -4 to 4
- second_gain: bfloat16 [2048], P('dp'), may hold values from 0.5 to 1.5
- gate_weight: bfloat16 [2048, 8192], P('dp', 'tensor'), may hold values from -0.125 to 0.125
- up_weight: bfloat16 [2048, 8192], P('dp', 'tensor'), may hold values from -0.125 to 0.125
- down_weight: bfloat16 [8192, 2048], P('tensor', 'dp'), may hold values from -0.5 to 0.5
- block_order: int32 [4, 4], P('dp'), may hold values from 0 to 3, each once within a row
- prefix_seen: int32 [4, 1], P('dp'), may hold values from 1 to 512, as said below
Outputs:
- layer_out: bfloat16 [4096, 2048], P(('dp', 'ctx'))
- tokens_grad: bfloat16 [4096, 2048], P(('dp', 'ctx'))
- first_gain_grad: float32 [2048], P('dp')
- query_grad: float32 [2048, 2048], P('dp', 'tensor')
- key_grad: float32 [2048, 512], P('dp', 'tensor')
- value_grad: float32 [2048, 512], P('dp', 'tensor')
- output_grad: float32 [2048, 2048], P('tensor', 'dp')
- second_gain_grad: float32 [2048], P('dp')
- gate_grad: float32 [2048, 8192], P('dp', 'tensor')
- up_grad: float32 [2048, 8192], P('dp', 'tensor')
- down_grad: float32 [8192, 2048], P('tensor', 'dp')
Inputs may be any that keep to these rules, and one draw needn't show every extreme that they name: Each row is a permutation. A group's sequences are its prompt of 512 tokens followed by 1 continuations of 512 tokens; block_order[g, b] names which block of 256 tokens of them rows b * 256 to (b + 1) * 256 - 1 of group g hold. Continuation c of group g follows the first prefix_seen[g, c] tokens of the group's prompt. The largest value over all groups is exactly 512.
All inputs are finite; a program needn't handle non-finite values.
Results may differ from a plain program's by a relative error of at most 0.023.
Values may be sent and summed in bfloat16 or wider, within the bound.
No kernel may reach another device: no remote copies, remote signals or barrier semaphores. Data moves between devices by JAX's collectives and lax.ppermute only.
A program may use at most 192 MiB of HBM per device.

v0:
```python
import jax
import jax.numpy as jnp
from jax import lax
from jax.sharding import PartitionSpec as P

H = 32
KVH = 8
HD = 64
CLEN = 512


EPSILON = 1e-05
ROPE_BASE = 10000000.0
ATTN_SCALE = 0.015625
RESIDUAL = 0.22
NEGATIVE = -1e30


def matmul(left, right):
    return jnp.dot(left, right, preferred_element_type=jnp.float32)


def inner_rows(left, right):
    return lax.dot_general(
        left, right, (((0,), (0,)), ((), ())), preferred_element_type=jnp.float32
    )


def inner_cols(left, right):
    return lax.dot_general(
        left, right, (((1,), (1,)), ((), ())), preferred_element_type=jnp.float32
    )


def normalize(values, gain):
    return values * lax.rsqrt(jnp.mean(values * values, axis=-1, keepdims=True) + EPSILON) * gain


def rotate(values, places, sign):
    head_count = values.shape[1] // HD
    half_size = HD // 2
    freq = ROPE_BASE ** (-(jnp.arange(half_size, dtype=jnp.float32) * 2.0) / HD)
    angle = places.astype(jnp.float32)[:, None] * freq[None, :]
    cosine = jnp.cos(angle)[:, None]
    sine = (jnp.sin(angle) * sign)[:, None]
    shaped = values.reshape(values.shape[0], head_count, 2, half_size)
    first = shaped[:, :, 0]
    second = shaped[:, :, 1]
    out_first = first * cosine - second * sine
    out_second = second * cosine + first * sine
    return jnp.stack([out_first, out_second], axis=2).reshape(values.shape)


def token_places(row_ids, order_row, seen_row, prompt_len, block_rows, cont_len):
    block_total = order_row.shape[0]
    block_pick = (row_ids // block_rows)[:, None] == jnp.arange(block_total, dtype=jnp.int32)[
        None, :
    ]
    chosen = jnp.sum(jnp.where(block_pick, order_row[None, :], 0), axis=1)
    global_ids = chosen * block_rows + row_ids % block_rows
    in_prompt = global_ids < prompt_len
    segment = jnp.where(in_prompt, 0, 1 + (global_ids - prompt_len) // cont_len)
    cont_count = seen_row.shape[0]
    which_cont = (segment - 1)[:, None] == jnp.arange(cont_count, dtype=jnp.int32)[None, :]
    limit = jnp.sum(jnp.where(which_cont, seen_row[None, :], 0), axis=1)
    places = jnp.where(in_prompt, global_ids, limit + (global_ids - prompt_len) % cont_len)
    return (segment, places, limit)


def visible(query_seg, query_pos, query_lim, key_seg, key_pos):
    same_seq = (query_seg[:, None] == key_seg[None, :]) & (key_pos[None, :] <= query_pos[:, None])
    shared = (key_seg[None, :] == 0) & (key_pos[None, :] < query_lim[:, None])
    return same_seq | shared


def head_scores(query_heads, key_block, mask):
    key_heads = key_block.reshape(key_block.shape[0], -1, HD)
    scores = (
        jnp.einsum("qgrd,tgd->grqt", query_heads, key_heads, preferred_element_type=jnp.float32)
        * ATTN_SCALE
    )
    return jnp.where(mask[None, None], scores, NEGATIVE)


def probabilities(query_heads, key_block, mask, log_total):
    scores = head_scores(query_heads, key_block, mask)
    return jnp.where(mask[None, None], jnp.exp(scores - log_total[..., None]), 0.0)


def attend_forward(query_heads, key_blocks, value_blocks, seg_blocks, pos_blocks, query_info):
    local_rows, heads_kv, repeat = (
        query_heads.shape[0],
        query_heads.shape[1],
        query_heads.shape[2],
    )
    start_top = jnp.full((heads_kv, repeat, local_rows), NEGATIVE, jnp.float32)
    start_total = jnp.zeros((heads_kv, repeat, local_rows), jnp.float32)

    def stats_step(carry, inputs):
        running_top, running_total = carry
        key_block, seg_block, pos_block = inputs
        mask = visible(query_info[0], query_info[1], query_info[2], seg_block, pos_block)
        scores = head_scores(query_heads, key_block, mask)
        new_top = jnp.maximum(running_top, jnp.max(scores, axis=-1))
        weights = jnp.where(mask[None, None], jnp.exp(scores - new_top[..., None]), 0.0)
        new_total = running_total * jnp.exp(running_top - new_top) + jnp.sum(weights, axis=-1)
        return ((new_top, new_total), None)

    stats, unused = lax.scan(
        stats_step, (start_top, start_total), (key_blocks, seg_blocks, pos_blocks)
    )
    log_total = stats[0] + jnp.log(stats[1])

    def output_step(carry, inputs):
        key_block, value_block, seg_block, pos_block = inputs
        mask = visible(query_info[0], query_info[1], query_info[2], seg_block, pos_block)
        probs = probabilities(query_heads, key_block, mask, log_total).astype(jnp.bfloat16)
        value_heads = value_block.reshape(value_block.shape[0], heads_kv, HD)
        return (
            carry
            + jnp.einsum("grqt,tgd->qgrd", probs, value_heads, preferred_element_type=jnp.float32),
            None,
        )

    start_out = jnp.zeros((local_rows, heads_kv, repeat, HD), jnp.float32)
    mixed, unused = lax.scan(
        output_step, start_out, (key_blocks, value_blocks, seg_blocks, pos_blocks)
    )
    return (mixed, log_total)


def attend_backward(
    query_heads, grad_heads, key_blocks, value_blocks, seg_blocks, pos_blocks, query_info, log_total
):
    local_rows, heads_kv, repeat = (
        query_heads.shape[0],
        query_heads.shape[1],
        query_heads.shape[2],
    )

    def delta_step(carry, inputs):
        key_block, value_block, seg_block, pos_block = inputs
        mask = visible(query_info[0], query_info[1], query_info[2], seg_block, pos_block)
        probs = probabilities(query_heads, key_block, mask, log_total)
        value_heads = value_block.reshape(value_block.shape[0], heads_kv, HD)
        grad_probs = jnp.einsum(
            "qgrd,tgd->grqt", grad_heads, value_heads, preferred_element_type=jnp.float32
        )
        return (carry + jnp.sum(probs * grad_probs, axis=-1), None)

    start_delta = jnp.zeros((heads_kv, repeat, local_rows), jnp.float32)
    delta, unused = lax.scan(
        delta_step, start_delta, (key_blocks, value_blocks, seg_blocks, pos_blocks)
    )

    def grad_step(carry, inputs):
        key_block, value_block, seg_block, pos_block = inputs
        mask = visible(query_info[0], query_info[1], query_info[2], seg_block, pos_block)
        probs = probabilities(query_heads, key_block, mask, log_total)
        key_heads = key_block.reshape(key_block.shape[0], heads_kv, HD)
        value_heads = value_block.reshape(value_block.shape[0], heads_kv, HD)
        grad_probs = jnp.einsum(
            "qgrd,tgd->grqt", grad_heads, value_heads, preferred_element_type=jnp.float32
        )
        scores_grad = (probs * (grad_probs - delta[..., None])).astype(jnp.bfloat16)
        new_carry = carry + jnp.einsum(
            "grqt,tgd->qgrd", scores_grad, key_heads, preferred_element_type=jnp.float32
        )
        key_part = jnp.einsum(
            "grqt,qgrd->tgd", scores_grad, query_heads, preferred_element_type=jnp.float32
        )
        value_part = jnp.einsum(
            "grqt,qgrd->tgd",
            probs.astype(jnp.bfloat16),
            grad_heads,
            preferred_element_type=jnp.float32,
        )
        return (new_carry, (key_part, value_part))

    start_query = jnp.zeros((local_rows, heads_kv, repeat, HD), jnp.float32)
    query_part, key_value = lax.scan(
        grad_step, start_query, (key_blocks, value_blocks, seg_blocks, pos_blocks)
    )
    return (query_part, key_value[0], key_value[1])


def shards(
    tokens,
    cotangent,
    first_gain,
    query_weight,
    key_weight,
    value_weight,
    output_weight,
    second_gain,
    gate_weight,
    up_weight,
    down_weight,
    block_order,
    prefix_seen,
):
    ctx_size = lax.axis_size("ctx")
    local_rows = tokens.shape[0]
    group_rows = local_rows * ctx_size
    offset = lax.axis_index("ctx") * local_rows
    all_ids = jnp.arange(group_rows, dtype=jnp.int32)
    key_seg, key_pos, key_lim = token_places(
        all_ids, block_order[0], prefix_seen[0], group_rows // 2, local_rows // 2, CLEN
    )
    query_seg = lax.dynamic_slice_in_dim(key_seg, offset, local_rows)
    query_pos = lax.dynamic_slice_in_dim(key_pos, offset, local_rows)
    query_lim = lax.dynamic_slice_in_dim(key_lim, offset, local_rows)
    query_info = (query_seg, query_pos, query_lim)
    key_len = min(512, group_rows)
    block_count = group_rows // key_len
    seg_blocks = key_seg.reshape(block_count, key_len)
    pos_blocks = key_pos.reshape(block_count, key_len)
    gain_one, query_full, key_full, value_full, output_full = (
        lax.all_gather(first_gain, "dp", axis=0, tiled=True),
        lax.all_gather(query_weight, "dp", axis=0, tiled=True),
        lax.all_gather(key_weight, "dp", axis=0, tiled=True),
        lax.all_gather(value_weight, "dp", axis=0, tiled=True),
        lax.all_gather(output_weight, "dp", axis=1, tiled=True),
    )
    inputs = tokens.astype(jnp.float32)
    normed_one, norm_pull_one = jax.vjp(normalize, inputs, gain_one.astype(jnp.float32))
    normed = normed_one.astype(jnp.bfloat16)
    queries = rotate(matmul(normed, query_full), query_pos, 1.0).astype(jnp.bfloat16)
    keys_rot = rotate(matmul(normed, key_full), query_pos, 1.0).astype(jnp.bfloat16)
    values_low = matmul(normed, value_full).astype(jnp.bfloat16)
    key_all, value_all = (
        lax.all_gather(keys_rot, "ctx", axis=0, tiled=True),
        lax.all_gather(values_low, "ctx", axis=0, tiled=True),
    )
    width_kv = keys_rot.shape[1]
    heads_kv = width_kv // HD
    repeat = H // KVH
    query_heads = queries.reshape(local_rows, heads_kv, repeat, HD)
    key_blocks = key_all.reshape(block_count, key_len, width_kv)
    value_blocks = value_all.reshape(block_count, key_len, width_kv)
    mixed, log_total = attend_forward(
        query_heads, key_blocks, value_blocks, seg_blocks, pos_blocks, query_info
    )
    attended = mixed.reshape(local_rows, -1).astype(jnp.bfloat16)
    branch = lax.psum(matmul(attended, output_full), "tensor")
    middle = inputs + RESIDUAL * branch
    gain_two, gate_full, up_full, down_full = (
        lax.all_gather(second_gain, "dp", axis=0, tiled=True),
        lax.all_gather(gate_weight, "dp", axis=0, tiled=True),
        lax.all_gather(up_weight, "dp", axis=0, tiled=True),
        lax.all_gather(down_weight, "dp", axis=1, tiled=True),
    )
    normed_mid, norm_pull_two = jax.vjp(normalize, middle, gain_two.astype(jnp.float32))
    normed_two = normed_mid.astype(jnp.bfloat16)
    gate = matmul(normed_two, gate_full)
    upper = matmul(normed_two, up_full)
    sigma = jax.nn.sigmoid(gate)
    active = gate * sigma
    hidden = (active * upper).astype(jnp.bfloat16)
    mlp_sum = lax.psum(matmul(hidden, down_full).astype(jnp.bfloat16), "tensor").astype(jnp.float32)
    layer_out = (middle + RESIDUAL * mlp_sum).astype(jnp.bfloat16)
    grad_out = cotangent.astype(jnp.float32)
    grad_mlp = (RESIDUAL * grad_out).astype(jnp.bfloat16)
    down_part = inner_rows(hidden, grad_mlp)
    grad_hidden = inner_cols(grad_mlp, down_full)
    grad_gate = (grad_hidden * upper * sigma * (1.0 + gate * (1.0 - sigma))).astype(jnp.bfloat16)
    grad_up = (grad_hidden * active).astype(jnp.bfloat16)
    gate_part = inner_rows(normed_two, grad_gate)
    up_part = inner_rows(normed_two, grad_up)
    grad_two = lax.psum(inner_cols(grad_gate, gate_full) + inner_cols(grad_up, up_full), "tensor")
    grad_mid_norm, gain_two_part = norm_pull_two(grad_two)
    grad_middle = grad_out + grad_mid_norm
    grad_branch = (RESIDUAL * grad_middle).astype(jnp.bfloat16)
    output_part = inner_rows(attended, grad_branch)
    grad_attended = inner_cols(grad_branch, output_full).astype(jnp.bfloat16)
    grad_heads = grad_attended.reshape(local_rows, heads_kv, repeat, HD)
    query_acc, key_parts, value_parts = attend_backward(
        query_heads,
        grad_heads,
        key_blocks,
        value_blocks,
        seg_blocks,
        pos_blocks,
        query_info,
        log_total,
    )
    key_sums, value_sums = (
        lax.psum_scatter(
            key_parts.reshape(group_rows, width_kv).astype(jnp.bfloat16),
            "ctx",
            scatter_dimension=0,
            tiled=True,
        ).astype(jnp.float32),
        lax.psum_scatter(
            value_parts.reshape(group_rows, width_kv).astype(jnp.bfloat16),
            "ctx",
            scatter_dimension=0,
            tiled=True,
        ).astype(jnp.float32),
    )
    query_low = rotate(query_acc.reshape(local_rows, -1) * ATTN_SCALE, query_pos, -1.0).astype(
        jnp.bfloat16
    )
    key_low = rotate(key_sums * ATTN_SCALE, query_pos, -1.0).astype(jnp.bfloat16)
    value_low = value_sums.astype(jnp.bfloat16)
    query_part = inner_rows(normed, query_low)
    key_part = inner_rows(normed, key_low)
    value_part = inner_rows(normed, value_low)
    grad_one = lax.psum(
        (
            inner_cols(query_low, query_full)
            + inner_cols(key_low, key_full)
            + inner_cols(value_low, value_full)
        ).astype(jnp.bfloat16),
        "tensor",
    ).astype(jnp.float32)
    grad_in_norm, gain_one_part = norm_pull_one(grad_one)
    tokens_grad = (grad_middle + grad_in_norm).astype(jnp.bfloat16)
    shares = (
        lax.psum_scatter(
            gain_one_part.astype(jnp.bfloat16), ("dp", "ctx"), scatter_dimension=0, tiled=True
        ).astype(jnp.float32),
        lax.psum_scatter(
            query_part.astype(jnp.bfloat16), ("dp", "ctx"), scatter_dimension=0, tiled=True
        ).astype(jnp.float32),
        lax.psum_scatter(
            key_part.astype(jnp.bfloat16), ("dp", "ctx"), scatter_dimension=0, tiled=True
        ).astype(jnp.float32),
        lax.psum_scatter(
            value_part.astype(jnp.bfloat16), ("dp", "ctx"), scatter_dimension=0, tiled=True
        ).astype(jnp.float32),
        lax.psum_scatter(
            output_part.astype(jnp.bfloat16), ("dp", "ctx"), scatter_dimension=1, tiled=True
        ).astype(jnp.float32),
        lax.psum_scatter(
            gain_two_part.astype(jnp.bfloat16), ("dp", "ctx"), scatter_dimension=0, tiled=True
        ).astype(jnp.float32),
        lax.psum_scatter(
            gate_part.astype(jnp.bfloat16), ("dp", "ctx"), scatter_dimension=0, tiled=True
        ).astype(jnp.float32),
        lax.psum_scatter(
            up_part.astype(jnp.bfloat16), ("dp", "ctx"), scatter_dimension=0, tiled=True
        ).astype(jnp.float32),
        lax.psum_scatter(
            down_part.astype(jnp.bfloat16), ("dp", "ctx"), scatter_dimension=1, tiled=True
        ).astype(jnp.float32),
    )
    totals = (
        lax.all_gather(shares[0].astype(jnp.bfloat16), "ctx", axis=0, tiled=True).astype(
            jnp.float32
        ),
        lax.all_gather(shares[1].astype(jnp.bfloat16), "ctx", axis=0, tiled=True).astype(
            jnp.float32
        ),
        lax.all_gather(shares[2].astype(jnp.bfloat16), "ctx", axis=0, tiled=True).astype(
            jnp.float32
        ),
        lax.all_gather(shares[3].astype(jnp.bfloat16), "ctx", axis=0, tiled=True).astype(
            jnp.float32
        ),
        lax.all_gather(shares[4].astype(jnp.bfloat16), "ctx", axis=1, tiled=True).astype(
            jnp.float32
        ),
        lax.all_gather(shares[5].astype(jnp.bfloat16), "ctx", axis=0, tiled=True).astype(
            jnp.float32
        ),
        lax.all_gather(shares[6].astype(jnp.bfloat16), "ctx", axis=0, tiled=True).astype(
            jnp.float32
        ),
        lax.all_gather(shares[7].astype(jnp.bfloat16), "ctx", axis=0, tiled=True).astype(
            jnp.float32
        ),
        lax.all_gather(shares[8].astype(jnp.bfloat16), "ctx", axis=1, tiled=True).astype(
            jnp.float32
        ),
    )
    return (
        layer_out,
        tokens_grad,
        totals[0],
        totals[1],
        totals[2],
        totals[3],
        totals[4],
        totals[5],
        totals[6],
        totals[7],
        totals[8],
    )


def solution(mesh):
    return jax.shard_map(
        shards,
        mesh=mesh,
        in_specs=(
            P(("dp", "ctx"), None),
            P(("dp", "ctx"), None),
            P("dp"),
            P("dp", "tensor"),
            P("dp", "tensor"),
            P("dp", "tensor"),
            P("tensor", "dp"),
            P("dp"),
            P("dp", "tensor"),
            P("dp", "tensor"),
            P("tensor", "dp"),
            P("dp", None),
            P("dp", None),
        ),
        out_specs=(
            P(("dp", "ctx"), None),
            P(("dp", "ctx"), None),
            P("dp"),
            P("dp", "tensor"),
            P("dp", "tensor"),
            P("dp", "tensor"),
            P("tensor", "dp"),
            P("dp"),
            P("dp", "tensor"),
            P("dp", "tensor"),
            P("tensor", "dp"),
        ),
        check_vma=False,
    )
```

profile of v0, /device:TPU:0, one launch (start us, length us, event | category | flops | bytes accessed | tf_op | source)
XLA Modules:
  0.0 1376.6 jit_solution(15361748024739871354)
XLA Ops:
  18.5 10.6 all_gather.63
  40.4 7.9 all_gather.61
  61.2 20.9 %while.50 = (s32[]{:T(128)}, f32[2,4,512]{2,1,0:T(4,128)S(1)}, f32[2,4,512]{2,1,0:T(4,128)S(1)}, s32[512]{0:T(512)S(1)}, s32[2,512]{1,0:T(2,128)}, /*index=5*/s3...) while((s32[]{:T(128)}, f32[2,4,512]{2,1,0:T(4,128)S(1)}, ...), condition=%wide.region_5.6_spmd.clone, body=%wide.region_2.5_spmd.clone.sunk | while | flops 286806528 | bytes 18713740 | solution.py:109
  82.7 13.6 while.51
  110.5 148.8 %all-reduce.8.cloned.1.call-done = f32[512,2048]{1,0:T(8,128)} async-done(((f32[512,2048]{1,0:T(8,128)}), f32[512,2048]{1,0:T(8,128)}) %all-reduce.8.cloned.1.call-update) | async-done | bytes 4194320 | tf_op jit(solution)/shard_map/psum | solution.py:245
  264.6 53.4 %all-gather.17.cloned.1.call-done = bf16[2048,2048]{1,0:T(8,128)(2,1)} async-done(((bf16[512,2048]{1,0:T(8,128)(2,1)}), bf16[2048,2048]{1,0:T(8,128)(2,1)}) %all-gather.17.cloned.1.call-update) | async-done | bytes 8388624 | tf_op jit(solution)/shard_map/all_gather | solution.py:249
  318.1 9.5 fusion.94
  327.6 50.3 %all-gather.19.cloned.1.call-done = bf16[2048,2048]{1,0:T(8,128)(2,1)} async-done(((bf16[512,2048]{1,0:T(8,128)(2,1)}), bf16[2048,2048]{1,0:T(8,128)(2,1)}) %all-gather.19.cloned.1.call-update) | async-done | bytes 8388624 | tf_op jit(solution)/shard_map/all_gather | solution.py:250
  377.9 9.4 fusion.95
  387.3 50.4 %all-gather.21.cloned.1.call-done = bf16[2048,2048]{1,0:T(8,128)(2,1)} async-done(((bf16[2048,512]{1,0:T(8,128)(2,1)}), bf16[2048,2048]{1,0:T(8,128)(2,1)}) %all-gather.21.cloned.1.call-update) | async-done | bytes 8388624 | tf_op jit(solution)/shard_map/all_gather | solution.py:251
  437.7 13.6 multiply_convert_fusion.1
  451.3 8.5 fusion.96
  466.3 155.0 %all-reduce.10.cloned.1.call-done = f32[512,2048]{1,0:T(8,128)} async-done(((f32[512,2048]{1,0:T(8,128)}), f32[512,2048]{1,0:T(8,128)}) %all-reduce.10.cloned.1.call-update) | async-done | bytes 4194320 | tf_op jit(solution)/shard_map/psum | solution.py:270
  633.4 11.8 while.52
  645.2 42.7 %while.53 = (s32[]{:T(128)}, f32[512,2,4,64]{0,3,2,1:T(8,128)S(1)}, bf16[2,512,2,64]{1,3,2,0:T(8,128)(2,1)S(1)}, bf16[2,512,2,64]{1,3,2,0:T(8,128)(2,1)}, bf16[2...) while((s32[]{:T(128)}, f32[512,2,4,64]{0,3,2,1:T(8,128)S(1)}, ...), condition=%wide.region_17.18_spmd.clone, body=%wide.region_16.17_spmd.clone.sunk | while | flops 1369440768 | bytes 94572264 | solution.py:181
  691.4 10.0 convolution_convert_fusion.2
  701.6 10.1 convolution_convert_fusion.1
  711.9 10.1 convolution_convert_fusion
  741.3 10.7 convolution_convert_fusion.5
  756.5 32.5 %reduce-scatter.22.cloned.1.call-done = bf16[256,2048]{1,0:T(8,128)(2,1)} async-done(((bf16[2048,2048]{1,0:T(8,128)(2,1)}), bf16[256,2048]{1,0:T(8,128)(2,1)}) %reduce-scatter.22.cloned.1.call-update) | async-done | bytes 1048592 | tf_op jit(solution)/shard_map/reduce_scatter | solution.py:338
  789.1 75.0 %reduce-scatter.24.cloned.1.call-done = bf16[256,2048]{1,0:T(8,128)(2,1)} async-done(((bf16[2048,2048]{1,0:T(8,128)(2,1)}), bf16[256,2048]{1,0:T(8,128)(2,1)}) %reduce-scatter.24.cloned.1.call-update) | async-done | bytes 1048592 | tf_op jit(solution)/shard_map/reduce_scatter | solution.py:341
  864.2 74.6 %reduce-scatter.26.cloned.1.call-done = bf16[2048,256]{1,0:T(8,128)(2,1)} async-done(((bf16[2048,2048]{1,0:T(8,128)(2,1)}), bf16[2048,256]{1,0:T(8,128)(2,1)}) %reduce-scatter.26.cloned.1.call-update) | async-done | bytes 1048592 | tf_op jit(solution)/shard_map/reduce_scatter | solution.py:344
  940.0 36.8 %reduce-scatter.16.cloned.1.call-done = bf16[256,128]{1,0:T(8,128)(2,1)} async-done(((bf16[2048,128]{1,0:T(8,128)(2,1)}), bf16[256,128]{1,0:T(8,128)(2,1)}) %reduce-scatter.16.cloned.1.call-update) | async-done | bytes 65552 | tf_op jit(solution)/shard_map/reduce_scatter | solution.py:326
  982.7 31.2 %reduce-scatter.18.cloned.1.call-done = bf16[256,128]{1,0:T(8,128)(2,1)} async-done(((bf16[2048,128]{1,0:T(8,128)(2,1)}), bf16[256,128]{1,0:T(8,128)(2,1)}) %reduce-scatter.18.cloned.1.call-update) | async-done | bytes 65552 | tf_op jit(solution)/shard_map/reduce_scatter | solution.py:329
  1019.8 38.9 %reduce-scatter.20.cloned.1.call-done = bf16[512,256]{1,0:T(8,128)(2,1)} async-done(((bf16[512,2048]{1,0:T(8,128)(2,1)}), bf16[512,256]{1,0:T(8,128)(2,1)}) %reduce-scatter.20.cloned.1.call-update) | async-done | bytes 262160 | tf_op jit(solution)/shard_map/reduce_scatter | solution.py:332
  1058.7 8.9 all_gather.75
  1068.7 34.9 %reduce-scatter.14.cloned.1.call-done = bf16[256,512]{1,0:T(8,128)(2,1)} async-done(((bf16[2048,512]{1,0:T(8,128)(2,1)}), bf16[256,512]{1,0:T(8,128)(2,1)}) %reduce-scatter.14.cloned.1.call-update) | async-done | bytes 262160 | tf_op jit(solution)/shard_map/reduce_scatter | solution.py:323
  1103.6 8.9 all_gather.72
  1113.6 148.3 %all-reduce.12.cloned.1.call-done = (bf16[512,2048]{1,0:T(8,128)(2,1)}, bf16[512,2048]{1,0:T(8,128)(2,1)}) async-done(((bf16[512,2048]{1,0:T(8,128)(2,1)}, bf16[512,2048]{1,0:T(8,128)(2,1)}), (bf16[512,2048]{1,0:T(8,128)(2,1)}, bf16[512,2048]{1,0:T(8,128)(2,1)})) %all-reduce.12.cloned.1.call-update) | async-done | bytes 4194320 | tf_op jit(solution)/shard_map/psum | solution.py:260
  1265.3 14.2 %all-reduce.2 = (bf16[2048]{0:T(1024)(128)(2,1)S(1)}, bf16[2048]{0:T(1024)(128)(2,1)S(1)}) all-reduce(bf16[2048]{0:T(1024)(128)(2,1)S(1)} %get-tuple-element.657, bf16[2048]{0:T(1024)(128)(2,1)S(1)} %copy-done.26), channel_id=4, replica_groups=mesh['dp'=4,'ctx'=2,'tensor'=4] {'dp','ctx'}, use_global_device_ids=true, to_apply=%region_23.24.clone | all-reduce | flops 4096 | bytes 16384
  1300.6 30.2 %all-gather.25.cloned.1.call-done = bf16[512,2048]{1,0:T(8,128)(2,1)} async-done(((bf16[256,2048]{1,0:T(8,128)(2,1)}), bf16[512,2048]{1,0:T(8,128)(2,1)}) %all-gather.25.cloned.1.call-update) | async-done | bytes 2097168 | tf_op jit(solution)/shard_map/all_gather | solution.py:370
  1334.9 30.4 %all-gather.27.cloned.1.call-done = bf16[2048,512]{1,0:T(8,128)(2,1)} async-done(((bf16[2048,256]{1,0:T(8,128)(2,1)}), bf16[2048,512]{1,0:T(8,128)(2,1)}) %all-gather.27.cloned.1.call-update) | async-done | bytes 2097168 | tf_op jit(solution)/shard_map/all_gather | solution.py:373
  (263 shorter events, 236.4 us)
Async XLA Ops:
  7.2 50.7 %all-gather.13.cloned.1.call-start = ((), (), s32[]{:S(2)}) async-start(), calls=%async_computation.9 | async-start | bytes 2621440 | tf_op jit(solution)/shard_map/all_gather | solution.py:220
  7.9 90.5 %all-gather.15.cloned.1.call-start = ((), (), s32[]{:S(2)}) async-start(), calls=%async_computation.10 | async-start | bytes 2621440 | tf_op jit(solution)/shard_map/all_gather | solution.py:223
  8.7 250.6 %all-reduce.8.cloned.1.call-start = ((), (), s32[]{:S(2)}) async-start(), calls=%async_computation.11 | async-start | bytes 8388608 | tf_op jit(solution)/shard_map/psum | solution.py:245
  11.5 36.8 %copy-start.4 = (bf16[512,2048]{1,0:T(8,128)(2,1)S(1)}, bf16[512,2048]{1,0:T(8,128)(2,1)}, u32[]{:S(2)}) copy-start(bf16[512,2048]{1,0:T(8,128)(2,1)} %param.21) | copy-start | bytes 6291460
  11.5 46.4 %copy-start.22 = (f32[512]{0:T(512)}, f32[512]{0:T(512)S(1)}, u32[]{:S(2)}) copy-start(f32[512]{0:T(512)S(1)} %fusion.75) | copy-start | bytes 6148
  18.5 39.5 %copy-start.20 = (f32[4,1,512]{2,1,0:T(1,128)}, f32[4,1,512]{2,1,0:T(1,128)S(1)}, u32[]{:S(2)}) copy-start(f32[4,1,512]{2,1,0:T(1,128)S(1)} %convert_element_type.233) | copy-start | bytes 24580
  29.1 20.0 %copy-start.9 = (bf16[2048,128]{1,0:T(8,128)(2,1)}, bf16[2048,128]{1,0:T(8,128)(2,1)S(1)}, u32[]{:S(2)}) copy-start(bf16[2048,128]{1,0:T(8,128)(2,1)S(1)} %all_gather.63) | copy-start | bytes 1572868
  30.9 30.1 %copy-start.16 = (f32[512,32]{0,1:T(8,128)}, f32[512,32]{0,1:T(8,128)S(1)}, u32[]{:S(2)}) copy-start(f32[512,32]{0,1:T(8,128)S(1)} %get-tuple-element.801) | copy-start | bytes 196612
  103.5 214.6 %all-gather.17.cloned.1.call-start = ((), (), s32[]{:S(2)}) async-start(), calls=%async_computation.12 | async-start | bytes 10485760 | tf_op jit(solution)/shard_map/all_gather | solution.py:249
  104.0 273.8 %all-gather.19.cloned.1.call-start = ((), (), s32[]{:S(2)}) async-start(), calls=%async_computation.13 | async-start | bytes 10485760 | tf_op jit(solution)/shard_map/all_gather | solution.py:250
  104.6 333.1 %all-gather.21.cloned.1.call-start = ((), (), s32[]{:S(2)}) async-start(), calls=%async_computation.14 | async-start | bytes 10485760 | tf_op jit(solution)/shard_map/all_gather | solution.py:251
  105.2 516.1 %all-reduce.10.cloned.1.call-start = ((), (), s32[]{:S(2)}) async-start(), calls=%async_computation.15 | async-start | bytes 8388608 | tf_op jit(solution)/shard_map/psum | solution.py:270
  264.6 113.3 %copy-start.8 = (bf16[512,2048]{1,0:T(8,128)(2,1)}, bf16[512,2048]{1,0:T(8,128)(2,1)S(1)}, u32[]{:S(2)}) copy-start(bf16[512,2048]{1,0:T(8,128)(2,1)S(1)} %multiply_convert_fusion.4) | copy-start | bytes 6291460
  451.3 8.5 copy-start.29
  466.2 255.9 %reduce-scatter.10.cloned.1.call-start = ((), (), s32[]{:S(2)}) async-start(), calls=%async_computation.16 | async-start | bytes 393216 | tf_op jit(solution)/shard_map/reduce_scatter | solution.py:288
  689.0 37.8 %reduce-scatter.12.cloned.1.call-start = ((), (), s32[]{:S(2)}) async-start(), calls=%async_computation.17 | async-start | bytes 393216 | tf_op jit(solution)/shard_map/reduce_scatter | solution.py:294
  691.0 98.0 %reduce-scatter.22.cloned.1.call-start = ((), (), s32[]{:S(2)}) async-start(), calls=%async_computation.22 | async-start | bytes 9437184 | tf_op jit(solution)/shard_map/reduce_scatter | solution.py:338
  701.5 162.6 %reduce-scatter.24.cloned.1.call-start = ((), (), s32[]{:S(2)}) async-start(), calls=%async_computation.24 | async-start | bytes 9437184 | tf_op jit(solution)/shard_map/reduce_scatter | solution.py:341
  711.7 227.1 %reduce-scatter.26.cloned.1.call-start = ((), (), s32[]{:S(2)}) async-start(), calls=%async_computation.26 | async-start | bytes 9437184 | tf_op jit(solution)/shard_map/reduce_scatter | solution.py:344
  722.0 254.8 %reduce-scatter.16.cloned.1.call-start = ((), (), s32[]{:S(2)}) async-start(), calls=%async_computation.19 | async-start | bytes 589824 | tf_op jit(solution)/shard_map/reduce_scatter | solution.py:326
  726.7 287.2 %reduce-scatter.18.cloned.1.call-start = ((), (), s32[]{:S(2)}) async-start(), calls=%async_computation.20 | async-start | bytes 589824 | tf_op jit(solution)/shard_map/reduce_scatter | solution.py:329
  730.6 328.1 %reduce-scatter.20.cloned.1.call-start = ((), (), s32[]{:S(2)}) async-start(), calls=%async_computation.21 | async-start | bytes 2359296 | tf_op jit(solution)/shard_map/reduce_scatter | solution.py:332
  736.2 367.4 %reduce-scatter.14.cloned.1.call-start = ((), (), s32[]{:S(2)}) async-start(), calls=%async_computation.18 | async-start | bytes 2359296 | tf_op jit(solution)/shard_map/reduce_scatter | solution.py:323
  741.0 10.9 copy-start.14
  741.0 520.9 %all-reduce.12.cloned.1.call-start = ((), (), s32[]{:S(2)}) async-start(), calls=%async_computation.28 | async-start | bytes 8388608 | tf_op jit(solution)/shard_map/psum | solution.py:260
  756.4 182.4 %copy-start.30 = (u32[32]{0:T(128)S(1)}, u32[32]{0:T(128)}, u32[]{:S(2)}) copy-start(u32[32]{0:T(128)} %constant.184) | copy-start | bytes 388
  756.4 540.0 %all-gather.23.cloned.1.call-start = ((), (), s32[]{:S(2)}) async-start(), calls=%async_computation.23 | async-start | bytes 3145728 | tf_op jit(solution)/shard_map/all_gather | solution.py:367
  789.0 472.9 %copy-start.5 = (bf16[512,2048]{1,0:T(8,128)(2,1)S(1)}, bf16[512,2048]{1,0:T(8,128)(2,1)}, u32[]{:S(2)}) copy-start(bf16[512,2048]{1,0:T(8,128)(2,1)} %param.21) | copy-start | bytes 6291460
  789.0 541.8 %all-gather.25.cloned.1.call-start = ((), (), s32[]{:S(2)}) async-start(), calls=%async_computation.25 | async-start | bytes 3145728 | tf_op jit(solution)/shard_map/all_gather | solution.py:370
  864.2 501.1 %all-gather.27.cloned.1.call-start = ((), (), s32[]{:S(2)}) async-start(), calls=%async_computation.27 | async-start | bytes 3145728 | tf_op jit(solution)/shard_map/all_gather | solution.py:373
  1067.6 197.7 %copy-start.26 = (bf16[2048]{0:T(1024)(128)(2,1)S(1)}, bf16[2048]{0:T(1024)(128)(2,1)}, u32[]{:S(2)}) copy-start(bf16[2048]{0:T(1024)(128)(2,1)} %get-tuple-element.655) | copy-start | bytes 12292
  1067.6 221.8 %copy-start.25 = (f32[512]{0:T(512)S(1)}, f32[512]{0:T(512)}, u32[]{:S(2)}) copy-start(f32[512]{0:T(512)} %copy-done.24) | copy-start | bytes 6148
  (23 other events, 77.7 us)
Sparse Core Ops, SparseCore 0:
  9.6 28.0 all-gather.12
  39.3 22.5 all-gather.14
  103.6 155.6 all-reduce.7
  260.8 57.2 all-gather.16
  319.6 58.2 all-gather.18
  379.4 58.2 all-gather.20
  466.3 154.9 all-reduce.9
  689.1 10.6 reduce-scatter.9
  702.7 11.6 reduce-scatter.11
  717.7 71.2 reduce-scatter.21
  792.9 71.2 reduce-scatter.23
  867.4 71.2 reduce-scatter.25
  942.7 34.0 reduce-scatter.15
  979.8 34.1 reduce-scatter.17
  1017.4 41.2 reduce-scatter.19
  1062.4 41.1 reduce-scatter.13
  1106.6 155.3 all-reduce.11
  1263.4 33.0 all-gather.22
  1298.0 32.7 all-gather.24
  1332.2 33.0 all-gather.26
where the time goes:
time: 1380 us
  waiting for transfers between devices  994 us (72%)
  matrix products  184 us (13%)
  blocking collectives  94.1 us (7%)
  other arithmetic  65.9 us (5%)
  local copies, waits for them, and re-layouts  19.6 us (1%)
  between operations  16.5 us (1%)
    psum x1, waiting for transfers between devices, shards(): lax.psum(inner_cols(grad_gate, gate_full) + inner_cols(grad_up, up_full),...  155 us
    psum x1, waiting for transfers between devices, shards(): branch = lax.psum(matmul(attended, output_full), 'tensor')  149 us
    psum x1, waiting for transfers between devices, shards(): lax.psum(matmul(hidden, down_full).astype(jnp.bfloat16), 'tensor')  148 us
    reduce_scatter x1, waiting for transfers between devices, shards(): lax.psum_scatter(up_part.astype(jnp.bfloat16), ('dp', 'ctx'), scatter_dim...  75 us
    reduce_scatter x1, waiting for transfers between devices, shards(): lax.psum_scatter(down_part.astype(jnp.bfloat16), ('dp', 'ctx'), scatter_d...  74.6 us
    all_gather x1, waiting for transfers between devices, shards(): lax.all_gather(gate_weight, 'dp', axis=0, tiled=True)  53.4 us
    all_gather x1, waiting for transfers between devices, shards(): lax.all_gather(down_weight, 'dp', axis=1, tiled=True)  50.4 us
    all_gather x1, waiting for transfers between devices, shards(): lax.all_gather(up_weight, 'dp', axis=0, tiled=True)  50.3 us
  transfers between devices with their start and end apart: 20, of which 15 were waited for; matrix products, arithmetic and copies ran while one was open for 12% of the time, Pallas kernels for 0%

commit v1 on v0

v1 whole, which is shorter than its diff:
```python
import jax
import jax.numpy as jnp
from jax import lax
from jax.sharding import PartitionSpec as P

H = 32
KVH = 8
HD = 64
CLEN = 512

EPSILON = 1e-05
ROPE_BASE = 10000000.0
ATTN_SCALE = 0.015625
RESIDUAL = 0.22
NEGATIVE = -1e30
BF = jnp.bfloat16
F32 = jnp.float32


def matmul(left, right):
    return jnp.dot(left, right, preferred_element_type=F32)


def inner_rows(left, right):
    return lax.dot_general(left, right, (((0,), (0,)), ((), ())), preferred_element_type=F32)


def inner_cols(left, right):
    return lax.dot_general(left, right, (((1,), (1,)), ((), ())), preferred_element_type=F32)


def swap_core(value):
    return lax.ppermute(value, "dp", [(i, i ^ 1) for i in range(4)])


def swap_x(value):
    return lax.ppermute(value, "dp", [(i, i ^ 2) for i in range(4)])


def swap_ctx(value):
    return lax.ppermute(value, "ctx", [(0, 1), (1, 0)])


def gather_plain(shard):
    far = swap_x(shard)
    return [shard, swap_core(shard), far, swap_core(far)]


def gather_split(shard):
    if lax.axis_size("ctx") != 2:
        return gather_plain(shard)
    half = shard.shape[0] // 2
    mine = lax.axis_index("ctx")
    got = swap_x(lax.dynamic_slice_in_dim(shard, mine * half, half))
    other = swap_ctx(got)
    first = mine == 0
    far = jnp.concatenate([jnp.where(first, got, other), jnp.where(first, other, got)], axis=0)
    return [shard, swap_core(shard), far, swap_core(far)]


def reduce_blocks(blocks):
    near = swap_core(blocks[1].astype(BF))
    far = swap_core(blocks[3].astype(BF))
    sent = swap_x((blocks[2] + far.astype(F32)).astype(BF))
    total = blocks[0] + near.astype(F32) + sent.astype(F32)
    if lax.axis_size("ctx") == 2:
        low = total.astype(BF)
        return low.astype(F32) + swap_ctx(low).astype(F32)
    return lax.psum(total.astype(BF), "ctx").astype(F32)


def relative(value, axis):
    size = value.shape[axis] // 4
    mine = lax.axis_index("dp")
    return jnp.concatenate(
        [lax.dynamic_slice_in_dim(value, (mine ^ r) * size, size, axis) for r in range(4)], axis
    )


def split4(value, axis):
    size = value.shape[axis] // 4
    return [lax.slice_in_dim(value, r * size, (r + 1) * size, axis=axis) for r in range(4)]


def rotation(places):
    half_size = HD // 2
    freq = ROPE_BASE ** (-(jnp.arange(half_size, dtype=F32) * 2.0) / HD)
    angle = places.astype(F32)[:, None] * freq[None, :]
    return jnp.cos(angle), jnp.sin(angle)


def rotate(values, cosine, sine):
    head_count = values.shape[1] // HD
    shaped = values.reshape(values.shape[0], head_count, 2, HD // 2)
    first = shaped[:, :, 0]
    second = shaped[:, :, 1]
    cosine = cosine[:, None]
    sine = sine[:, None]
    out_first = first * cosine - second * sine
    out_second = second * cosine + first * sine
    return jnp.stack([out_first, out_second], axis=2).reshape(values.shape)


def token_places(row_ids, order_row, seen_row, prompt_len, block_rows, cont_len):
    block_total = order_row.shape[0]
    block_pick = (row_ids // block_rows)[:, None] == jnp.arange(block_total, dtype=jnp.int32)[
        None, :
    ]
    chosen = jnp.sum(jnp.where(block_pick, order_row[None, :], 0), axis=1)
    global_ids = chosen * block_rows + row_ids % block_rows
    in_prompt = global_ids < prompt_len
    segment = jnp.where(in_prompt, 0, 1 + (global_ids - prompt_len) // cont_len)
    cont_count = seen_row.shape[0]
    which_cont = (segment - 1)[:, None] == jnp.arange(cont_count, dtype=jnp.int32)[None, :]
    limit = jnp.sum(jnp.where(which_cont, seen_row[None, :], 0), axis=1)
    places = jnp.where(in_prompt, global_ids, limit + (global_ids - prompt_len) % cont_len)
    return (segment, places, limit)


def visible(query_seg, query_pos, query_lim, key_seg, key_pos):
    same_seq = (query_seg[:, None] == key_seg[None, :]) & (key_pos[None, :] <= query_pos[:, None])
    shared = (key_seg[None, :] == 0) & (key_pos[None, :] < query_lim[:, None])
    return same_seq | shared


def head_scores(query_heads, key_block, mask):
    key_heads = key_block.reshape(key_block.shape[0], -1, HD)
    scores = (
        jnp.einsum("qgrd,tgd->grqt", query_heads, key_heads, preferred_element_type=jnp.float32)
        * ATTN_SCALE
    )
    return jnp.where(mask[None, None], scores, NEGATIVE)


def probabilities(query_heads, key_block, mask, log_total):
    scores = head_scores(query_heads, key_block, mask)
    return jnp.where(mask[None, None], jnp.exp(scores - log_total[..., None]), 0.0)


def attend_forward(query_heads, key_blocks, value_blocks, seg_blocks, pos_blocks, query_info):
    local_rows, heads_kv, repeat = (
        query_heads.shape[0],
        query_heads.shape[1],
        query_heads.shape[2],
    )
    start_top = jnp.full((heads_kv, repeat, local_rows), NEGATIVE, jnp.float32)
    start_total = jnp.zeros((heads_kv, repeat, local_rows), jnp.float32)

    def stats_step(carry, inputs):
        running_top, running_total = carry
        key_block, seg_block, pos_block = inputs
        mask = visible(query_info[0], query_info[1], query_info[2], seg_block, pos_block)
        scores = head_scores(query_heads, key_block, mask)
        new_top = jnp.maximum(running_top, jnp.max(scores, axis=-1))
        weights = jnp.where(mask[None, None], jnp.exp(scores - new_top[..., None]), 0.0)
        new_total = running_total * jnp.exp(running_top - new_top) + jnp.sum(weights, axis=-1)
        return ((new_top, new_total), None)

    stats, unused = lax.scan(
        stats_step, (start_top, start_total), (key_blocks, seg_blocks, pos_blocks)
    )
    log_total = stats[0] + jnp.log(stats[1])

    def output_step(carry, inputs):
        key_block, value_block, seg_block, pos_block = inputs
        mask = visible(query_info[0], query_info[1], query_info[2], seg_block, pos_block)
        probs = probabilities(query_heads, key_block, mask, log_total).astype(jnp.bfloat16)
        value_heads = value_block.reshape(value_block.shape[0], heads_kv, HD)
        return (
            carry
            + jnp.einsum("grqt,tgd->qgrd", probs, value_heads, preferred_element_type=jnp.float32),
            None,
        )

    start_out = jnp.zeros((local_rows, heads_kv, repeat, HD), jnp.float32)
    mixed, unused = lax.scan(
        output_step, start_out, (key_blocks, value_blocks, seg_blocks, pos_blocks)
    )
    return (mixed, log_total)


def attend_backward(
    query_heads, grad_heads, key_blocks, value_blocks, seg_blocks, pos_blocks, query_info, log_total
):
    local_rows, heads_kv, repeat = (
        query_heads.shape[0],
        query_heads.shape[1],
        query_heads.shape[2],
    )

    def delta_step(carry, inputs):
        key_block, value_block, seg_block, pos_block = inputs
        mask = visible(query_info[0], query_info[1], query_info[2], seg_block, pos_block)
        probs = probabilities(query_heads, key_block, mask, log_total)
        value_heads = value_block.reshape(value_block.shape[0], heads_kv, HD)
        grad_probs = jnp.einsum(
            "qgrd,tgd->grqt", grad_heads, value_heads, preferred_element_type=jnp.float32
        )
        return (carry + jnp.sum(probs * grad_probs, axis=-1), None)

    start_delta = jnp.zeros((heads_kv, repeat, local_rows), jnp.float32)
    delta, unused = lax.scan(
        delta_step, start_delta, (key_blocks, value_blocks, seg_blocks, pos_blocks)
    )

    def grad_step(carry, inputs):
        key_block, value_block, seg_block, pos_block = inputs
        mask = visible(query_info[0], query_info[1], query_info[2], seg_block, pos_block)
        probs = probabilities(query_heads, key_block, mask, log_total)
        key_heads = key_block.reshape(key_block.shape[0], heads_kv, HD)
        value_heads = value_block.reshape(value_block.shape[0], heads_kv, HD)
        grad_probs = jnp.einsum(
            "qgrd,tgd->grqt", grad_heads, value_heads, preferred_element_type=jnp.float32
        )
        scores_grad = (probs * (grad_probs - delta[..., None])).astype(jnp.bfloat16)
        new_carry = carry + jnp.einsum(
            "grqt,tgd->qgrd", scores_grad, key_heads, preferred_element_type=jnp.float32
        )
        key_part = jnp.einsum(
            "grqt,qgrd->tgd", scores_grad, query_heads, preferred_element_type=jnp.float32
        )
        value_part = jnp.einsum(
            "grqt,qgrd->tgd",
            probs.astype(jnp.bfloat16),
            grad_heads,
            preferred_element_type=jnp.float32,
        )
        return (new_carry, (key_part, value_part))

    start_query = jnp.zeros((local_rows, heads_kv, repeat, HD), jnp.float32)
    query_part, key_value = lax.scan(
        grad_step, start_query, (key_blocks, value_blocks, seg_blocks, pos_blocks)
    )
    return (query_part, key_value[0], key_value[1])


def norm_scale(values):
    return lax.rsqrt(jnp.mean(values * values, axis=-1, keepdims=True) + EPSILON)


def norm_back(values, scale, gain, grad):
    weighted = gain * grad
    inner = jnp.mean(weighted * values, axis=-1, keepdims=True)
    return scale * weighted - values * (scale * scale * scale) * inner


def psum_tensor(value):
    return lax.psum(value.astype(BF), "tensor").astype(F32)


def shards(
    tokens,
    cotangent,
    first_gain,
    query_weight,
    key_weight,
    value_weight,
    output_weight,
    second_gain,
    gate_weight,
    up_weight,
    down_weight,
    block_order,
    prefix_seen,
):
    ctx_size = lax.axis_size("ctx")
    local_rows = tokens.shape[0]
    group_rows = local_rows * ctx_size
    offset = lax.axis_index("ctx") * local_rows
    width_q = query_weight.shape[1]
    width_kv = key_weight.shape[1]
    block_d = query_weight.shape[0]

    gains = jnp.pad(jnp.stack([first_gain, second_gain]), ((0, 30), (0, width_q + 2 * width_kv - block_d)))
    qkv_shard = jnp.concatenate(
        [jnp.concatenate([query_weight, key_weight, value_weight], axis=1), gains], axis=0
    )
    qkv_pieces = gather_plain(qkv_shard)
    out_pieces = gather_plain(output_weight)
    qkv_full = jnp.concatenate([p[:block_d] for p in qkv_pieces], axis=0)
    gain_one = jnp.concatenate([p[block_d, :block_d] for p in qkv_pieces]).astype(F32)
    gain_two = jnp.concatenate([p[block_d + 1, :block_d] for p in qkv_pieces]).astype(F32)
    output_full = jnp.concatenate(out_pieces, axis=1)
    gate_full = jnp.concatenate(gather_split(gate_weight), axis=0)
    up_full = jnp.concatenate(gather_split(up_weight), axis=0)
    down_full = jnp.concatenate(gather_split(down_weight), axis=1)

    all_ids = jnp.arange(group_rows, dtype=jnp.int32)
    key_seg, key_pos, key_lim = token_places(
        all_ids, block_order[0], prefix_seen[0], group_rows // 2, local_rows // 2, CLEN
    )
    query_seg = lax.dynamic_slice_in_dim(key_seg, offset, local_rows)
    query_pos = lax.dynamic_slice_in_dim(key_pos, offset, local_rows)
    query_lim = lax.dynamic_slice_in_dim(key_lim, offset, local_rows)
    query_info = (query_seg, query_pos, query_lim)
    key_len = min(512, group_rows)
    block_count = group_rows // key_len
    seg_blocks = key_seg.reshape(block_count, key_len)
    pos_blocks = key_pos.reshape(block_count, key_len)
    cosine, sine = rotation(query_pos)

    inputs = relative(tokens, 1).astype(F32)
    grad_out = relative(cotangent, 1).astype(F32)
    scale_one = norm_scale(inputs)
    normed = (inputs * scale_one * gain_one).astype(BF)
    proj = matmul(normed, qkv_full)
    rotated = rotate(proj[:, : width_q + width_kv], cosine, sine).astype(BF)
    queries = rotated[:, :width_q]
    key_value = jnp.concatenate(
        [rotated[:, width_q:], proj[:, width_q + width_kv :].astype(BF)], axis=1
    )
    key_value_all = lax.all_gather(key_value, "ctx", axis=0, tiled=True)
    heads_kv = width_kv // HD
    repeat = H // KVH
    query_heads = queries.reshape(local_rows, heads_kv, repeat, HD)
    key_blocks = key_value_all[:, :width_kv].reshape(block_count, key_len, width_kv)
    value_blocks = key_value_all[:, width_kv:].reshape(block_count, key_len, width_kv)
    mixed, log_total = attend_forward(
        query_heads, key_blocks, value_blocks, seg_blocks, pos_blocks, query_info
    )
    attended = mixed.reshape(local_rows, -1).astype(BF)
    middle = inputs + RESIDUAL * psum_tensor(matmul(attended, output_full))

    scale_two = norm_scale(middle)
    normed_two = (middle * scale_two * gain_two).astype(BF)
    gate = matmul(normed_two, gate_full)
    upper = matmul(normed_two, up_full)
    sigma = jax.nn.sigmoid(gate)
    active = gate * sigma
    hidden = (active * upper).astype(BF)
    grad_mlp = (RESIDUAL * grad_out).astype(BF)
    grad_hidden = inner_cols(grad_mlp, down_full)
    grad_gate = (grad_hidden * upper * sigma * (1.0 + gate * (1.0 - sigma))).astype(BF)
    grad_up = (grad_hidden * active).astype(BF)
    grad_two = psum_tensor(inner_cols(grad_gate, gate_full) + inner_cols(grad_up, up_full))
    mlp_sum = psum_tensor(matmul(hidden, down_full))
    layer_out = relative((middle + RESIDUAL * mlp_sum).astype(BF), 1)

    down_grad = reduce_blocks([inner_rows(hidden, g) for g in split4(grad_mlp, 1)])
    gate_grad = reduce_blocks([inner_rows(h, grad_gate) for h in split4(normed_two, 1)])
    up_grad = reduce_blocks([inner_rows(h, grad_up) for h in split4(normed_two, 1)])

    gain_two_part = jnp.sum(grad_two * middle * scale_two, axis=0)
    grad_middle = grad_out + norm_back(middle, scale_two, gain_two, grad_two)
    grad_branch = (RESIDUAL * grad_middle).astype(BF)
    output_grad = reduce_blocks([inner_rows(attended, g) for g in split4(grad_branch, 1)])
    grad_attended = inner_cols(grad_branch, output_full).astype(BF)
    grad_heads = grad_attended.reshape(local_rows, heads_kv, repeat, HD)
    query_acc, key_parts, value_parts = attend_backward(
        query_heads,
        grad_heads,
        key_blocks,
        value_blocks,
        seg_blocks,
        pos_blocks,
        query_info,
        log_total,
    )
    key_value_parts = jnp.concatenate(
        [key_parts.reshape(group_rows, width_kv), value_parts.reshape(group_rows, width_kv)], axis=1
    )
    if ctx_size == 2:
        kept = lax.dynamic_slice_in_dim(key_value_parts, offset, local_rows)
        sent = lax.dynamic_slice_in_dim(key_value_parts, local_rows - offset, local_rows)
        key_value_sums = kept + swap_ctx(sent.astype(BF)).astype(F32)
    else:
        key_value_sums = lax.psum_scatter(
            key_value_parts.astype(BF), "ctx", scatter_dimension=0, tiled=True
        ).astype(F32)
    query_key = jnp.concatenate(
        [query_acc.reshape(local_rows, -1), key_value_sums[:, :width_kv]], axis=1
    )
    query_key_low = rotate(query_key * ATTN_SCALE, cosine, -sine).astype(BF)
    qkv_low = jnp.concatenate([query_key_low, key_value_sums[:, width_kv:].astype(BF)], axis=1)
    grad_one = psum_tensor(inner_cols(qkv_low, qkv_full))
    qkv_grad = reduce_blocks([inner_rows(h, qkv_low) for h in split4(normed, 1)])
    gain_one_part = jnp.sum(grad_one * inputs * scale_one, axis=0)
    tokens_grad = relative(
        (grad_middle + norm_back(inputs, scale_one, gain_one, grad_one)).astype(BF), 1
    )
    gain_blocks = split4(jnp.stack([gain_one_part, gain_two_part]), 1)
    gain_grad = reduce_blocks(gain_blocks)
    return (
        layer_out,
        tokens_grad,
        gain_grad[0],
        qkv_grad[:, :width_q],
        qkv_grad[:, width_q : width_q + width_kv],
        qkv_grad[:, width_q + width_kv :],
        output_grad,
        gain_grad[1],
        gate_grad,
        up_grad,
        down_grad,
    )


def solution(mesh):
    return jax.shard_map(
        shards,
        mesh=mesh,
        in_specs=(
            P(("dp", "ctx"), None),
            P(("dp", "ctx"), None),
            P("dp"),
            P("dp", "tensor"),
            P("dp", "tensor"),
            P("dp", "tensor"),
            P("tensor", "dp"),
            P("dp"),
            P("dp", "tensor"),
            P("dp", "tensor"),
            P("tensor", "dp"),
            P("dp", None),
            P("dp", None),
        ),
        out_specs=(
            P(("dp", "ctx"), None),
            P(("dp", "ctx"), None),
            P("dp"),
            P("dp", "tensor"),
            P("dp", "tensor"),
            P("dp", "tensor"),
            P("tensor", "dp"),
            P("dp"),
            P("dp", "tensor"),
            P("dp", "tensor"),
            P("tensor", "dp"),
        ),
        check_vma=False,
    )
```

time: 1380 us -> 732 us (0.53)
  waiting for transfers between devices: 994 us -> 320 us
  blocking collectives: 94.1 us -> 19.6 us
  local copies, waits for them, and re-layouts: 19.6 us -> 81.1 us
  starting transfers between devices: 1.59 us -> 31.8 us
    psum x3, waiting for transfers between devices: 452 us -> 95.9 us  [psum_tensor(): return lax.psum(value.astype(BF), 'tensor').astype(F32)]
    reduce_scatter x9 -> x0, waiting for transfers between devices: 324 us -> none  [the longest x1 75 us: shards(): lax.psum_scatter(up_part.astype(jnp.bfloat16), ('dp', 'ctx'), scatter_dim...]
    ppermute x0 -> x43, waiting for transfers between devices: none -> 224 us  [the longest x10 154 us: swap_ctx(): return lax.ppermute(value, 'ctx', [(0, 1), (1, 0)])]
    all_gather x8 -> x0, waiting for transfers between devices: 215 us -> none  [the longest x1 53.4 us: shards(): lax.all_gather(gate_weight, 'dp', axis=0, tiled=True)]
    all_gather x12 -> x1, blocking collectives: 79.9 us -> 19.6 us  [shards(): key_value_all = lax.all_gather(key_value, 'ctx', axis=0, tiled=True)]
    ppermute x0 -> x43, starting transfers between devices: none -> 31.3 us  [the longest x11 13.4 us: swap_x(): return lax.ppermute(value, 'dp', [(i, i ^ 2) for i in range(4)])]
    dynamic_update_slice x0 -> x8, local copies, waits for them, and re-layouts: none -> 24.1 us  [attend_backward(): lax.scan(grad_step, start_query, (key_blocks, value_blocks, seg_blocks, p...]
    unnamed x73 -> x175, local copies, waits for them, and re-layouts: 9.43 us -> 23.8 us
  transfers between devices with their start and end apart: 20 -> 46, of which waited for: 15 -> 14; matrix products, arithmetic and copies ran while one was open for 12% -> 38% of each run, Pallas kernels for 0% -> 0%
where the time goes in v1:
time: 732 us; the launch traced here: 724 us
  waiting for transfers between devices  320 us (44%)
  matrix products  185 us (25%)
  local copies, waits for them, and re-layouts  81.1 us (11%)
  other arithmetic  68.7 us (9%)
  starting transfers between devices  31.8 us (4%)
  blocking collectives  19.6 us (3%)
  between operations  16.2 us (2%)
    ppermute x10, waiting for transfers between devices, swap_ctx(): return lax.ppermute(value, 'ctx', [(0, 1), (1, 0)])  154 us
    psum x3, waiting for transfers between devices, psum_tensor(): return lax.psum(value.astype(BF), 'tensor').astype(F32)  95.9 us
    ppermute x11, waiting for transfers between devices, swap_x(): return lax.ppermute(value, 'dp', [(i, i ^ 2) for i in range(4)])  70 us
    dot_general x20, matrix products, inner_rows(): lax.dot_general(left, right, (((0,), (0,)), ((), ())), preferred_element_...  53.4 us
    dot_general x5, matrix products, inner_cols(): lax.dot_general(left, right, (((1,), (1,)), ((), ())), preferred_element_...  47.8 us
    dot_general x5, matrix products, matmul(): return jnp.dot(left, right, preferred_element_type=F32)  39.8 us
    dynamic_update_slice x8, local copies, waits for them, and re-layouts, attend_backward(): lax.scan(grad_step, start_query, (key_blocks, value_blocks, seg_blocks, p...  24.1 us
    unnamed x175, local copies, waits for them, and re-layouts  23.8 us
  transfers between devices with their start and end apart: 46, of which 14 were waited for; matrix products, arithmetic and copies ran while one was open for 38% of the time, Pallas kernels for 0%

profile of v1, /device:TPU:0, one launch (start us, length us, event | category | flops | bytes accessed | tf_op | source)
XLA Modules:
  0.0 724.1 jit_solution(14723705781850883129)
XLA Ops:
  36.2 5.2 collective-permute-done.1
  56.1 7.7 %collective-permute-done.7 = bf16[256,2048]{1,0:T(8,128)(2,1)} collective-permute-done((bf16[256,2048]{1,0:T(8,128)(2,1)}, bf16[256,2048]{1,0:T(8,128)(2,1)}, u32[]{:S(2)}, u32[]{:S(2)}) %collective-permute-start.7) | collective-permute-done | bytes 1048608 | tf_op jit(solution)/shard_map/ppermute | solution.py:37
  75.9 19.6 %all_gather.3 = bf16[1024,256]{1,0:T(8,128)(2,1)S(1)} all-gather(bf16[512,256]{1,0:T(8,128)(2,1)S(1)} %pad_maximum_fusion.15), channel_id=1, replica_groups=mesh['dp'=4,'ctx'=2,'tensor'=4] {'ctx'}, dimensions={0}, use_global_device_ids=true | all-gather | bytes 786432 | tf_op jit(solution)/shard_map/all_gather | solution.py:312
  95.9 8.1 %while.50 = (s32[]{:T(128)}, f32[2,4,512]{2,1,0:T(4,128)S(1)}, f32[2,4,512]{2,1,0:T(4,128)S(1)}, s32[512]{0:T(512)S(1)}, s32[2,512]{1,0:T(2,128)S(1)}, /*index=5...) while((s32[]{:T(128)}, f32[2,4,512]{2,1,0:T(4,128)S(1)}, ...), condition=%wide.region_5.6_spmd.clone, body=%wide.region_2.5_spmd.clone.sunk | while | flops 286806528 | bytes 18713748 | solution.py:159
  104.1 7.2 while.51
  131.7 10.8 %collective-permute-done.12 = bf16[256,2048]{1,0:T(8,128)(2,1)S(1)} collective-permute-done((bf16[256,2048]{1,0:T(8,128)(2,1)}, bf16[256,2048]{1,0:T(8,128)(2,1)S(1)}, u32[]{:S(2)}, u32[]{:S(2)}) %collective-permute-start.12) | collective-permute-done | bytes 1048608 | tf_op jit(solution)/shard_map/ppermute | solution.py:41
  148.1 16.4 %collective-permute-done.16 = bf16[1024,512]{1,0:T(8,128)(2,1)S(1)} collective-permute-done((bf16[1024,512]{1,0:T(8,128)(2,1)}, bf16[1024,512]{1,0:T(8,128)(2,1)S(1)}, u32[]{:S(2)}, u32[]{:S(2)}) %collective-permute-start.16) | collective-permute-done | bytes 1048608 | tf_op jit(solution)/shard_map/ppermute | solution.py:41
  168.0 34.8 %all-reduce.6.cloned.1.call-done = bf16[512,2048]{1,0:T(8,128)(2,1)} async-done(((bf16[512,2048]{1,0:T(8,128)(2,1)}), bf16[512,2048]{1,0:T(8,128)(2,1)}) %all-reduce.6.cloned.1.call-update) | async-done | bytes 2097168 | tf_op jit(solution)/shard_map/psum | solution.py:248
  214.1 6.1 fusion.141
  220.3 26.2 %fusion.131 = f32[512,2048]{1,0:T(8,128)} fusion(bf16[2048,512]{1,0:T(8,128)(2,1)} %collective-permute-done.17, bf16[1024,512]{1,0:T(8,128)(2,1)S(1)} %copy-done.24, bf16[1024,512]{1,0:T(8,128)(2,1)S(1)} %copy-done.21, bf16[2048,512]{1,0:T(8,128)(2,1)} %collective-permute-done.14, bf16[2048,512]{1,0:T(8,128)(2,1)} %param.31, ...), kind=kOutput, calls=%fused_computation.333 | convolution fusion | flops 4347396096 | bytes 14680064 | tf_op jit(solution)/shard_map/dot_general | solution.py:29
  246.4 12.4 %multiply_convert_fusion.2 = (bf16[512,2048]{1,0:T(8,128)(2,1)S(1)}, bf16[512,2048]{1,0:T(8,128)(2,1)S(1)}, bf16[512,2048]{1,0:T(8,128)(2,1)}) fusion(f32[512,2048]{1,0:T(8,128)} %fusion.131, f32[512,2048]{1,0:T(8,128)} %fusion.141, bf16[512,2048]{1,0:T(8,128)(2,1)S(1)} %multiply_convert_fusion.4, bf16[2048,2048]{1,0:T(8,128)(2,1)} %constant_dynamic-update-slice_fusion.7), kind=kOutput, calls=%fused_computation.108 | convolution fusion | flops 4310695936 | bytes 25165824 | tf_op jit(solution)/shard_map/dot_general | solution.py:21
  258.8 4.5 fusion.142
  268.7 9.2 %add_convert_fusion.6 = bf16[512,2048]{1,0:T(8,128)(2,1)} fusion(f32[512,2048]{1,0:T(8,128)S(1)} %fusion.142, bf16[512,2048]{1,0:T(8,128)(2,1)S(1)} %get-tuple-element.713, bf16[2048,2048]{1,0:T(8,128)(2,1)} %constant_dynamic-update-slice_fusion.7), kind=kOutput, calls=%fused_computation.106 | convolution fusion | flops 4297064448 | bytes 16777216 | tf_op jit(solution)/shard_map/dot_general | solution.py:29
  287.2 15.1 %convolution_convert_fusion.7 = bf16[512,2048]{1,0:T(8,128)(2,1)} fusion(bf16[512,2048]{1,0:T(8,128)(2,1)S(1)} %copy-done.29, bf16[2048,512]{1,0:T(8,128)(2,1)} %collective-permute-done.17, bf16[1024,512]{1,0:T(8,128)(2,1)S(1)} %copy-done.25, bf16[1024,512]{1,0:T(8,128)(2,1)S(1)} %copy-done.22, bf16[2048,512]{1,0:T(8,128)(2,1)} %collective-permute-done.14, ...), kind=kOutput, calls=%fused_computation.123 | convolution fusion | flops 4337958912 | bytes 12582912 | tf_op jit(solution)/shard_map/dot_general | solution.py:21
  302.3 61.2 %all-reduce.8.cloned.1.call-done = bf16[512,2048]{1,0:T(8,128)(2,1)} async-done(((bf16[512,2048]{1,0:T(8,128)(2,1)}), bf16[512,2048]{1,0:T(8,128)(2,1)}) %all-reduce.8.cloned.1.call-update) | async-done | bytes 2097168 | tf_op jit(solution)/shard_map/psum | solution.py:248
  379.4 10.9 %while.52 = (s32[]{:T(128)}, f32[2,4,512]{2,1,0:T(4,128)S(1)}, s32[512]{0:T(512)S(1)}, s32[2,512]{1,0:T(2,128)S(1)}, s32[2,512]{1,0:T(2,128)S(1)}, /*index=5*/s3...) while((s32[]{:T(128)}, f32[2,4,512]{2,1,0:T(4,128)S(1)}, ...), condition=%wide.region_15.16_spmd.clone, body=%wide.region_13.15_spmd.clone.sunk | while | flops 551031296 | bytes 19238048 | solution.py:202
  390.3 51.2 %while.53 = (s32[]{:T(128)}, f32[512,2,4,64]{0,3,2,1:T(8,128)S(1)}, f32[2,512,2,64]{1,0,3,2:T(2,128)}, f32[2,512,2,64]{1,0,3,2:T(2,128)}, bf16[2,512,128]{1,2,0:...) while((s32[]{:T(128)}, f32[512,2,4,64]{0,3,2,1:T(8,128)S(1)}, ...), condition=%wide.region_17.18_spmd.clone, body=%wide.region_16.17_spmd.clone.sunk | while | flops 1369440768 | bytes 63114460 | solution.py:231
  394.5 4.6 fusion.246
  399.4 5.8 dynamic_update_slice.12
  410.0 5.8 dynamic_update_slice.11
  420.0 4.6 fusion.246
  424.9 5.8 dynamic_update_slice.12
  435.5 5.8 dynamic_update_slice.11
  470.6 6.6 convolution_convert_fusion.6
  479.0 5.2 collective-permute-done.29
  499.2 50.5 %collective-permute-done.25 = bf16[512,768]{1,0:T(8,128)(2,1)S(1)} collective-permute-done((bf16[512,768]{1,0:T(8,128)(2,1)S(1)}, bf16[512,768]{1,0:T(8,128)(2,1)S(1)}, u32[]{:S(2)}, u32[]{:S(2)}) %collective-permute-start.25) | collective-permute-done | bytes 786464 | tf_op jit(solution)/shard_map/ppermute | solution.py:37
  555.3 54.3 %collective-permute-done.30 = bf16[512,512]{1,0:T(8,128)(2,1)S(1)} collective-permute-done((bf16[512,512]{1,0:T(8,128)(2,1)S(1)}, bf16[512,512]{1,0:T(8,128)(2,1)S(1)}, u32[]{:S(2)}, u32[]{:S(2)}) %collective-permute-start.30) | collective-permute-done | bytes 524320 | tf_op jit(solution)/shard_map/ppermute | solution.py:41
  612.2 14.3 %collective-permute-done.26 = bf16[512,768]{1,0:T(8,128)(2,1)S(1)} collective-permute-done((bf16[512,768]{1,0:T(8,128)(2,1)S(1)}, bf16[512,768]{1,0:T(8,128)(2,1)S(1)}, u32[]{:S(2)}, u32[]{:S(2)}) %collective-permute-start.26) | collective-permute-done | bytes 786464 | tf_op jit(solution)/shard_map/ppermute | solution.py:41
  635.1 36.3 %collective-permute-done.34 = bf16[512,2048]{1,0:T(8,128)(2,1)S(1)} collective-permute-done((bf16[512,2048]{1,0:T(8,128)(2,1)S(1)}, bf16[512,2048]{1,0:T(8,128)(2,1)S(1)}, u32[]{:S(2)}, u32[]{:S(2)}) %collective-permute-start.34) | collective-permute-done | bytes 2097184 | tf_op jit(solution)/shard_map/ppermute | solution.py:41
  678.0 4.9 fusion.45
  690.3 21.5 %collective-permute-done.22 = bf16[2,512]{1,0:T(2,128)(2,1)S(1)} collective-permute-done((bf16[2,512]{1,0:T(2,128)(2,1)S(1)}, bf16[2,512]{1,0:T(2,128)(2,1)S(1)}, u32[]{:S(2)}, u32[]{:S(2)}) %collective-permute-start.22) | collective-permute-done | bytes 2080 | tf_op jit(solution)/shard_map/ppermute | solution.py:41
  712.5 4.9 convert_add_fusion.2
  (443 shorter events, 247.2 us)
Async XLA Ops:
  7.2 195.6 %all-reduce.6.cloned.1.call-start = ((), (), s32[]{:S(2)}) async-start(), calls=%async_computation | async-start | bytes 4194304 | tf_op jit(solution)/shard_map/psum | solution.py:248
  7.2 36.6 %collective-permute-start.3 = (bf16[512,512]{1,0:T(8,128)(2,1)}, bf16[512,512]{1,0:T(8,128)(2,1)}, u32[]{:S(2)}, u32[]{:S(2)}) collective-permute-start(bf16[512,512]{1,0:T(8,128)(2,1)} %param.27), channel_id=1, source_target_pairs={{0,8},{8,0},{16,24},{24,16},{1,9},{9,1},{17,25},{25,17},{2,10},{10... | collective-permute-start | bytes 1572872 | tf_op jit(solution)/shard_map/ppermute | solution.py:33
  7.8 35.4 %collective-permute-start.4 = (bf16[512,512]{1,0:T(8,128)(2,1)}, bf16[512,512]{1,0:T(8,128)(2,1)}, u32[]{:S(2)}, u32[]{:S(2)}) collective-permute-start(bf16[512,512]{1,0:T(8,128)(2,1)} %param.27), channel_id=1, source_target_pairs={{0,16},{8,24},{16,0},{24,8},{1,17},{9,25},{17,1},{25,9},{2,18},{10... | collective-permute-start | bytes 1572872 | tf_op jit(solution)/shard_map/ppermute | solution.py:37
  15.9 33.0 %collective-permute-start = (bf16[544,768]{1,0:T(8,128)(2,1)}, bf16[544,768]{1,0:T(8,128)(2,1)}, u32[]{:S(2)}, u32[]{:S(2)}) collective-permute-start(bf16[544,768]{1,0:T(8,128)(2,1)} %pad_maximum_fusion.9), channel_id=1, source_target_pairs={{0,8},{8,0},{16,24},{24,16},{1,9},{9,1},{17,25},{25,17},{2,10},{10... | collective-permute-start | bytes 2506760 | tf_op jit(solution)/shard_map/ppermute | solution.py:33
  18.2 45.6 %collective-permute-start.7 = (bf16[256,2048]{1,0:T(8,128)(2,1)}, bf16[256,2048]{1,0:T(8,128)(2,1)}, u32[]{:S(2)}, u32[]{:S(2)}) collective-permute-start(bf16[256,2048]{1,0:T(8,128)(2,1)} %constant_dynamic-slice_fusion.31), channel_id=1, source_target_pairs={{0,16},{8,24},{16,0},{24,8},{1,17},{9,25},{17,1},{25,9},{2,18},{10... | collective-permute-start | bytes 3145736 | tf_op jit(solution)/shard_map/ppermute | solution.py:37
  43.9 73.9 %collective-permute-start.6 = (bf16[512,2048]{1,0:T(8,128)(2,1)}, bf16[512,2048]{1,0:T(8,128)(2,1)}, u32[]{:S(2)}, u32[]{:S(2)}) collective-permute-start(bf16[512,2048]{1,0:T(8,128)(2,1)} %param.29), channel_id=1, source_target_pairs={{0,8},{8,0},{16,24},{24,16},{1,9},{9,1},{17,25},{25,17},{2,10},{10... | collective-permute-start | bytes 6291464 | tf_op jit(solution)/shard_map/ppermute | solution.py:33
  48.8 79.7 %collective-permute-start.10 = (bf16[512,2048]{1,0:T(8,128)(2,1)}, bf16[512,2048]{1,0:T(8,128)(2,1)}, u32[]{:S(2)}, u32[]{:S(2)}) collective-permute-start(bf16[512,2048]{1,0:T(8,128)(2,1)} %param.30), channel_id=1, source_target_pairs={{0,8},{8,0},{16,24},{24,16},{1,9},{9,1},{17,25},{25,17},{2,10},{10... | collective-permute-start | bytes 6291464 | tf_op jit(solution)/shard_map/ppermute | solution.py:33
  52.2 63.9 %collective-permute-start.11 = (bf16[256,2048]{1,0:T(8,128)(2,1)}, bf16[256,2048]{1,0:T(8,128)(2,1)}, u32[]{:S(2)}, u32[]{:S(2)}) collective-permute-start(bf16[256,2048]{1,0:T(8,128)(2,1)} %constant_dynamic-slice_fusion.30), channel_id=1, source_target_pairs={{0,16},{8,24},{16,0},{24,8},{1,17},{9,25},{17,1},{25,9},{2,18},{10... | collective-permute-start | bytes 3145736 | tf_op jit(solution)/shard_map/ppermute | solution.py:37
  63.8 52.4 %collective-permute-start.15 = (bf16[1024,512]{1,0:T(8,128)(2,1)}, bf16[1024,512]{1,0:T(8,128)(2,1)}, u32[]{:S(2)}, u32[]{:S(2)}) collective-permute-start(bf16[1024,512]{1,0:T(8,128)(2,1)} %constant_dynamic-slice_fusion.29), channel_id=1, source_target_pairs={{0,16},{8,24},{16,0},{24,8},{1,17},{9,25},{17,1},{25,9},{2,18},{10... | collective-permute-start | bytes 3145736 | tf_op jit(solution)/shard_map/ppermute | solution.py:37
  65.7 55.8 %collective-permute-start.8 = (bf16[256,2048]{1,0:T(8,128)(2,1)}, bf16[256,2048]{1,0:T(8,128)(2,1)}, u32[]{:S(2)}, u32[]{:S(2)}) collective-permute-start(bf16[256,2048]{1,0:T(8,128)(2,1)} %collective-permute-done.7), channel_id=1, source_target_pairs={{0,4},{4,0},{1,5},{5,1},{2,6},{6,2},{3,7},{7,3},{8,12},{12,8},{9,1... | collective-permute-start | bytes 3145736 | tf_op jit(solution)/shard_map/ppermute | solution.py:41
  115.8 247.7 %all-reduce.8.cloned.1.call-start = ((), (), s32[]{:S(2)}) async-start(), calls=%async_computation.1 | async-start | bytes 4194304 | tf_op jit(solution)/shard_map/psum | solution.py:248
  116.1 104.1 %collective-permute-start.14 = (bf16[2048,512]{1,0:T(8,128)(2,1)}, bf16[2048,512]{1,0:T(8,128)(2,1)}, u32[]{:S(2)}, u32[]{:S(2)}) collective-permute-start(bf16[2048,512]{1,0:T(8,128)(2,1)} %param.31), channel_id=1, source_target_pairs={{0,8},{8,0},{16,24},{24,16},{1,9},{9,1},{17,25},{25,17},{2,10},{10... | collective-permute-start | bytes 6291464 | tf_op jit(solution)/shard_map/ppermute | solution.py:33
  116.2 26.2 %collective-permute-start.12 = (bf16[256,2048]{1,0:T(8,128)(2,1)}, bf16[256,2048]{1,0:T(8,128)(2,1)S(1)}, u32[]{:S(2)}, u32[]{:S(2)}) collective-permute-start(bf16[256,2048]{1,0:T(8,128)(2,1)} %collective-permute-done.11), channel_id=1, source_target_pairs={{0,4},{4,0},{1,5},{5,1},{2,6},{6,2},{3,7},{7,3},{8,12},{12,8},{9,1... | collective-permute-start | bytes 3145736 | tf_op jit(solution)/shard_map/ppermute | solution.py:41
  117.8 46.7 %collective-permute-start.16 = (bf16[1024,512]{1,0:T(8,128)(2,1)}, bf16[1024,512]{1,0:T(8,128)(2,1)S(1)}, u32[]{:S(2)}, u32[]{:S(2)}) collective-permute-start(bf16[1024,512]{1,0:T(8,128)(2,1)} %collective-permute-done.15), channel_id=1, source_target_pairs={{0,4},{4,0},{1,5},{5,1},{2,6},{6,2},{3,7},{7,3},{8,12},{12,8},{9,1... | collective-permute-start | bytes 3145736 | tf_op jit(solution)/shard_map/ppermute | solution.py:41
  128.5 79.4 %collective-permute-start.9 = (bf16[512,2048]{1,0:T(8,128)(2,1)}, bf16[512,2048]{1,0:T(8,128)(2,1)}, u32[]{:S(2)}, u32[]{:S(2)}) collective-permute-start(bf16[512,2048]{1,0:T(8,128)(2,1)} %pad_maximum_fusion.3), channel_id=1, source_target_pairs={{0,8},{8,0},{16,24},{24,16},{1,9},{9,1},{17,25},{25,17},{2,10},{10... | collective-permute-start | bytes 6291464 | tf_op jit(solution)/shard_map/ppermute | solution.py:33
  148.1 64.2 %collective-permute-start.13 = (bf16[512,2048]{1,0:T(8,128)(2,1)}, bf16[512,2048]{1,0:T(8,128)(2,1)}, u32[]{:S(2)}, u32[]{:S(2)}) collective-permute-start(bf16[512,2048]{1,0:T(8,128)(2,1)} %pad_maximum_fusion.4), channel_id=1, source_target_pairs={{0,8},{8,0},{16,24},{24,16},{1,9},{9,1},{17,25},{25,17},{2,10},{10... | collective-permute-start | bytes 6291464 | tf_op jit(solution)/shard_map/ppermute | solution.py:33
  167.6 52.6 %collective-permute-start.17 = (bf16[2048,512]{1,0:T(8,128)(2,1)}, bf16[2048,512]{1,0:T(8,128)(2,1)}, u32[]{:S(2)}, u32[]{:S(2)}) collective-permute-start(bf16[2048,512]{1,0:T(8,128)(2,1)} %pad_maximum_fusion.5), channel_id=1, source_target_pairs={{0,8},{8,0},{16,24},{24,16},{1,9},{9,1},{17,25},{25,17},{2,10},{10... | collective-permute-start | bytes 6291464 | tf_op jit(solution)/shard_map/ppermute | solution.py:33
  277.9 396.3 %all-reduce.10.cloned.1.call-start = ((), (), s32[]{:S(2)}) async-start(), calls=%async_computation.2 | async-start | bytes 8388608 | tf_op jit(solution)/shard_map/psum | solution.py:248
  278.1 191.9 %collective-permute-start.35 = (bf16[512,2048]{1,0:T(8,128)(2,1)}, bf16[512,2048]{1,0:T(8,128)(2,1)}, u32[]{:S(2)}, u32[]{:S(2)}) collective-permute-start(bf16[512,2048]{1,0:T(8,128)(2,1)} %convolution_convert_fusion.3), channel_id=1, source_target_pairs={{0,8},{8,0},{16,24},{24,16},{1,9},{9,1},{17,25},{25,17},{2,10},{10... | collective-permute-start | bytes 6291464 | tf_op jit(solution)/shard_map/ppermute | solution.py:33
  278.2 89.4 %collective-permute-start.36 = (bf16[512,2048]{1,0:T(8,128)(2,1)}, bf16[512,2048]{1,0:T(8,128)(2,1)}, u32[]{:S(2)}, u32[]{:S(2)}) collective-permute-start(bf16[512,2048]{1,0:T(8,128)(2,1)} %convolution_convert_fusion.2), channel_id=1, source_target_pairs={{0,8},{8,0},{16,24},{24,16},{1,9},{9,1},{17,25},{25,17},{2,10},{10... | collective-permute-start | bytes 6291464 | tf_op jit(solution)/shard_map/ppermute | solution.py:33
  283.2 175.4 %collective-permute-start.32 = (bf16[512,2048]{1,0:T(8,128)(2,1)}, bf16[512,2048]{1,0:T(8,128)(2,1)}, u32[]{:S(2)}, u32[]{:S(2)}) collective-permute-start(bf16[512,2048]{1,0:T(8,128)(2,1)} %convolution_convert_fusion.4), channel_id=1, source_target_pairs={{0,8},{8,0},{16,24},{24,16},{1,9},{9,1},{17,25},{25,17},{2,10},{10... | collective-permute-start | bytes 6291464 | tf_op jit(solution)/shard_map/ppermute | solution.py:33
  372.1 123.2 %collective-permute-start.37 = (bf16[512,2048]{1,0:T(8,128)(2,1)}, bf16[512,2048]{1,0:T(8,128)(2,1)}, u32[]{:S(2)}, u32[]{:S(2)}) collective-permute-start(bf16[512,2048]{1,0:T(8,128)(2,1)} %add_convert_fusion.3), channel_id=1, source_target_pairs={{0,16},{8,24},{16,0},{24,8},{1,17},{9,25},{17,1},{25,9},{2,18},{10... | collective-permute-start | bytes 6291464 | tf_op jit(solution)/shard_map/ppermute | solution.py:37
  478.9 72.6 %collective-permute-start.31 = (bf16[512,2048]{1,0:T(8,128)(2,1)}, bf16[512,2048]{1,0:T(8,128)(2,1)S(1)}, u32[]{:S(2)}, u32[]{:S(2)}) collective-permute-start(bf16[512,2048]{1,0:T(8,128)(2,1)} %convolution_convert_fusion.5), channel_id=1, source_target_pairs={{0,8},{8,0},{16,24},{24,16},{1,9},{9,1},{17,25},{25,17},{2,10},{10... | collective-permute-start | bytes 6291464 | tf_op jit(solution)/shard_map/ppermute | solution.py:33
  484.1 68.0 %collective-permute-start.33 = (bf16[512,2048]{1,0:T(8,128)(2,1)}, bf16[512,2048]{1,0:T(8,128)(2,1)S(1)}, u32[]{:S(2)}, u32[]{:S(2)}) collective-permute-start(bf16[512,2048]{1,0:T(8,128)(2,1)} %add_convert_fusion.5), channel_id=1, source_target_pairs={{0,16},{8,24},{16,0},{24,8},{1,17},{9,25},{17,1},{25,9},{2,18},{10... | collective-permute-start | bytes 6291464 | tf_op jit(solution)/shard_map/ppermute | solution.py:37
  489.7 60.1 %collective-permute-start.25 = (bf16[512,768]{1,0:T(8,128)(2,1)S(1)}, bf16[512,768]{1,0:T(8,128)(2,1)S(1)}, u32[]{:S(2)}, u32[]{:S(2)}) collective-permute-start(bf16[512,768]{1,0:T(8,128)(2,1)S(1)} %add_convert_fusion.9), channel_id=1, source_target_pairs={{0,16},{8,24},{16,0},{24,8},{1,17},{9,25},{17,1},{25,9},{2,18},{10... | collective-permute-start | bytes 2359304 | tf_op jit(solution)/shard_map/ppermute | solution.py:37
  494.7 133.8 %collective-permute-start.39 = (bf16[2048,512]{1,0:T(8,128)(2,1)S(1)}, bf16[2048,512]{1,0:T(8,128)(2,1)S(1)}, u32[]{:S(2)}, u32[]{:S(2)}) collective-permute-start(bf16[2048,512]{1,0:T(8,128)(2,1)S(1)} %copy-done.73), channel_id=1, source_target_pairs={{0,8},{8,0},{16,24},{24,16},{1,9},{9,1},{17,25},{25,17},{2,10},{10... | collective-permute-start | bytes 6291464 | tf_op jit(solution)/shard_map/ppermute | solution.py:33
  495.3 133.3 %collective-permute-start.41 = (bf16[2048,512]{1,0:T(8,128)(2,1)S(1)}, bf16[2048,512]{1,0:T(8,128)(2,1)S(1)}, u32[]{:S(2)}, u32[]{:S(2)}) collective-permute-start(bf16[2048,512]{1,0:T(8,128)(2,1)S(1)} %add_convert_fusion.1), channel_id=1, source_target_pairs={{0,16},{8,24},{16,0},{24,8},{1,17},{9,25},{17,1},{25,9},{2,18},{10... | collective-permute-start | bytes 6291464 | tf_op jit(solution)/shard_map/ppermute | solution.py:37
  549.8 82.5 %collective-permute-start.38 = (bf16[512,2048]{1,0:T(8,128)(2,1)S(1)}, bf16[512,2048]{1,0:T(8,128)(2,1)S(1)}, u32[]{:S(2)}, u32[]{:S(2)}) collective-permute-start(bf16[512,2048]{1,0:T(8,128)(2,1)S(1)} %add_convert_fusion.2), channel_id=1, source_target_pairs={{0,4},{4,0},{1,5},{5,1},{2,6},{6,2},{3,7},{7,3},{8,12},{12,8},{9,1... | collective-permute-start | bytes 6291464 | tf_op jit(solution)/shard_map/ppermute | solution.py:41
  551.5 58.1 %collective-permute-start.30 = (bf16[512,512]{1,0:T(8,128)(2,1)S(1)}, bf16[512,512]{1,0:T(8,128)(2,1)S(1)}, u32[]{:S(2)}, u32[]{:S(2)}) collective-permute-start(bf16[512,512]{1,0:T(8,128)(2,1)S(1)} %add_convert_fusion.10), channel_id=1, source_target_pairs={{0,4},{4,0},{1,5},{5,1},{2,6},{6,2},{3,7},{7,3},{8,12},{12,8},{9,1... | collective-permute-start | bytes 1572872 | tf_op jit(solution)/shard_map/ppermute | solution.py:41
  552.2 74.3 %collective-permute-start.26 = (bf16[512,768]{1,0:T(8,128)(2,1)S(1)}, bf16[512,768]{1,0:T(8,128)(2,1)S(1)}, u32[]{:S(2)}, u32[]{:S(2)}) collective-permute-start(bf16[512,768]{1,0:T(8,128)(2,1)S(1)} %add_convert_fusion.8), channel_id=1, source_target_pairs={{0,4},{4,0},{1,5},{5,1},{2,6},{6,2},{3,7},{7,3},{8,12},{12,8},{9,1... | collective-permute-start | bytes 2359304 | tf_op jit(solution)/shard_map/ppermute | solution.py:41
  609.6 61.8 %collective-permute-start.34 = (bf16[512,2048]{1,0:T(8,128)(2,1)S(1)}, bf16[512,2048]{1,0:T(8,128)(2,1)S(1)}, u32[]{:S(2)}, u32[]{:S(2)}) collective-permute-start(bf16[512,2048]{1,0:T(8,128)(2,1)S(1)} %add_convert_fusion.4), channel_id=1, source_target_pairs={{0,4},{4,0},{1,5},{5,1},{2,6},{6,2},{3,7},{7,3},{8,12},{12,8},{9,1... | collective-permute-start | bytes 6291464 | tf_op jit(solution)/shard_map/ppermute | solution.py:41
  630.8 81.7 %collective-permute-start.42 = (bf16[2048,512]{1,0:T(8,128)(2,1)}, bf16[2048,512]{1,0:T(8,128)(2,1)}, u32[]{:S(2)}, u32[]{:S(2)}) collective-permute-start(bf16[2048,512]{1,0:T(8,128)(2,1)} %add_convert_fusion), channel_id=1, source_target_pairs={{0,4},{4,0},{1,5},{5,1},{2,6},{6,2},{3,7},{7,3},{8,12},{12,8},{9,1... | collective-permute-start | bytes 6291464 | tf_op jit(solution)/shard_map/ppermute | solution.py:41
  (96 other events, 1586.3 us)
Sparse Core Ops, SparseCore 0:
  115.9 86.8 all-reduce.5
  278.0 85.4 all-reduce.7
  477.3 154.5 all-reduce.9

commit v2 on v1

v2 whole, which is shorter than its diff:
```python
import functools

import jax
import jax.numpy as jnp
from jax import lax
from jax.experimental import pallas as pl
from jax.experimental.pallas import tpu as pltpu
from jax.sharding import PartitionSpec as P

HD = 64
CLEN = 512

EPSILON = 1e-05
ROPE_BASE = 10000000.0
ATTN_SCALE = 0.015625
RESIDUAL = 0.22
NEGATIVE = -1e30
SEGMENT_STEP = 1 << 16
BF = jnp.bfloat16
F32 = jnp.float32
LIGHT = pl.CostEstimate(flops=1, bytes_accessed=1, transcendentals=0)


def dot_nt(a, b):
    return lax.dot_general(a, b, (((1,), (1,)), ((), ())), preferred_element_type=F32)

def dot_nn(a, b):
    return lax.dot_general(a, b, (((1,), (0,)), ((), ())), preferred_element_type=F32)

def fill_bias(bias, key_code, query_codes):
    code = key_code[...]
    below = code < query_codes[0:1, :]
    own = (code >= query_codes[1:2, :]) & (code <= query_codes[2:3, :])
    bias[...] = jnp.where(below | own, 0.0, NEGATIVE)

def fill_padded(padded, source, lane0):
    block = source[:, lane0 : lane0 + 2 * HD]
    lane = lax.broadcasted_iota(jnp.int32, block.shape, 1)
    low = jnp.where(lane < HD, block, jnp.zeros_like(block))
    high = jnp.where(lane < HD, jnp.zeros_like(block), block)
    padded[0, 0] = low
    padded[0, 1] = pltpu.roll(low.astype(F32), HD, 1).astype(BF)
    padded[1, 0] = pltpu.roll(high.astype(F32), HD, 1).astype(BF)
    padded[1, 1] = high

def forward_kernel(chunk, q_ref, kv_ref, vt_ref, code_ref, codes_ref, o0, o1, o2, o3, out_ref, lse_ref, branch_ref, bias, keys):
    total = kv_ref.shape[0]
    rows = q_ref.shape[0]
    fill_bias(bias, code_ref, codes_ref)
    fill_padded(keys, kv_ref, 0)

    def pair_step(pair, unused):
        group = pair // 2
        lanes = pl.ds(pl.multiple_of(pair * 128, 128), 128)
        q_pair = q_ref[:, lanes]
        mixed = []
        for side in range(2):
            def chunk_step(part, carry):
                top, norm, acc = carry
                at = pl.ds(pl.multiple_of(part * chunk, chunk), chunk)
                scores = dot_nt(keys[group, side, at, :], q_pair) + bias[at, :]
                new_top = jnp.maximum(top, jnp.max(scores, axis=0, keepdims=True))
                weights = jnp.exp(scores - new_top)
                shrink = jnp.exp(top - new_top)
                norm = norm * shrink + jnp.sum(weights, axis=0, keepdims=True)
                values = vt_ref[pl.ds(pl.multiple_of(group * HD, HD), HD), at]
                acc = acc * shrink + dot_nn(values, weights.astype(BF))
                return new_top, norm, acc

            carry = (jnp.full((1, rows), NEGATIVE, F32), jnp.zeros((1, rows), F32), jnp.zeros((HD, rows), F32))
            if total == chunk:
                carry = chunk_step(0, carry)
            else:
                carry = lax.fori_loop(0, total // chunk, chunk_step, carry)
            top, norm, acc = carry
            mixed.append(acc / norm)
            lse_ref[pl.ds(pair * 2 + side, 1), :] = top + jnp.log(norm)
        out_ref[:, lanes] = jnp.concatenate(mixed, axis=0).T.astype(BF)
        return unused

    lax.fori_loop(0, q_ref.shape[1] // 128, pair_step, 0)
    block = o0.shape[1]
    for r, piece in enumerate((o0, o1, o2, o3)):
        branch_ref[:, r * block : (r + 1) * block] = dot_nn(out_ref[...], piece[...]).astype(BF)


def attend_forward(queries, key_value, values_t, key_code, query_codes, out_pieces):
    rows, width = queries.shape
    total = key_value.shape[0]
    chunk = min(total, 1024)
    return pl.pallas_call(
        functools.partial(forward_kernel, chunk),
        out_shape=(
            jax.ShapeDtypeStruct((rows, width), BF),
            jax.ShapeDtypeStruct((width // HD, rows), F32),
            jax.ShapeDtypeStruct((rows, 4 * out_pieces[0].shape[1]), BF),
        ),
        scratch_shapes=[pltpu.VMEM((total, rows), F32), pltpu.VMEM((2, 2, total, 128), BF)],
        compiler_params=pltpu.CompilerParams(vmem_limit_bytes=(32 if total <= 1024 else 58) << 20),
        cost_estimate=LIGHT,
        name="attend_forward",
    )(queries, key_value, values_t, key_code, query_codes, *out_pieces)

def backward_kernel(chunk, q_ref, kv_ref, kt_ref, code_ref, codes_ref, att_ref, branch_ref, lse_ref, rot_ref,
                    o0, o1, o2, o3, dq_ref, dkv_ref, grad_ref, bias, keys, values, delta, dk_acc, dv_acc):
    total = kv_ref.shape[0]
    rows = q_ref.shape[0]
    width = q_ref.shape[1]
    heads = width // HD
    fill_bias(bias, code_ref, codes_ref)
    fill_padded(keys, kv_ref, 0)
    fill_padded(values, kv_ref, 128)
    block = o0.shape[1]
    grad = jnp.zeros((rows, width), F32)
    for r, piece in enumerate((o0, o1, o2, o3)):
        grad += dot_nt(branch_ref[:, r * block : (r + 1) * block], piece[...])
    grad_ref[...] = grad.astype(BF)
    owner = lax.broadcasted_iota(jnp.int32, (heads, width), 1) // HD
    member = jnp.where(owner == lax.broadcasted_iota(jnp.int32, (heads, width), 0), 1.0, 0.0)
    product = att_ref[...].astype(F32) * grad_ref[...].astype(F32)
    delta[...] = lax.dot_general(member, product, (((1,), (1,)), ((), ())), precision=lax.Precision.HIGHEST, preferred_element_type=F32)
    dk_acc[...] = jnp.zeros_like(dk_acc)
    dv_acc[...] = jnp.zeros_like(dv_acc)
    half = HD // 2

    def pair_step(pair, unused):
        group = pair // 2
        lanes = pl.ds(pl.multiple_of(pair * 128, 128), 128)
        q_pair = q_ref[:, lanes]
        g_pair = grad_ref[:, lanes]
        turned = []
        for side in range(2):
            head = pl.ds(pair * 2 + side, 1)
            lse = lse_ref[head, :]
            dlt = delta[head, :]
            def chunk_step(part, acc):
                at = pl.ds(pl.multiple_of(part * chunk, chunk), chunk)
                scores = dot_nt(keys[group, side, at, :], q_pair) + bias[at, :]
                probs = jnp.exp(scores - lse)
                dprobs = dot_nt(values[group, side, at, :], g_pair)
                dscores = (probs * (dprobs - dlt)).astype(BF)
                dv_acc[group, side, at, :] += dot_nn(probs.astype(BF), g_pair)
                dk_acc[group, side, at, :] += dot_nn(dscores, q_pair)
                kt = kt_ref[pl.ds(pl.multiple_of(group * HD, HD), HD), at]
                return acc + dot_nn(kt, dscores)
            acc = jnp.zeros((HD, rows), F32)
            if total == chunk:
                acc = chunk_step(0, acc)
            else:
                acc = lax.fori_loop(0, total // chunk, chunk_step, acc)
            acc = acc * (1.0 / HD)
            first, second = acc[:half], acc[half:]
            cosine, sine = rot_ref[:half, :], rot_ref[half:, :]
            turned.append(first * cosine + second * sine)
            turned.append(second * cosine - first * sine)
        dq_ref[:, lanes] = jnp.concatenate(turned, axis=0).T.astype(BF)
        return unused

    lax.fori_loop(0, width // 128, pair_step, 0)
    lane = lax.broadcasted_iota(jnp.int32, (total, 128), 1)
    for which, acc in ((0, dk_acc), (1, dv_acc)):
        zero = acc[0, 0] + pltpu.roll(acc[0, 1], HD, 1)
        one = pltpu.roll(acc[1, 0], HD, 1) + acc[1, 1]
        dkv_ref[:, which * 128 : (which + 1) * 128] = jnp.where(lane < HD, zero, one)

def attend_backward(queries, key_value, keys_t, key_code, query_codes, attended, grad_branch, lse, turn, out_pieces):
    rows, width = queries.shape
    total = key_value.shape[0]
    chunk = min(total, 1024)
    return pl.pallas_call(
        functools.partial(backward_kernel, chunk),
        out_shape=(jax.ShapeDtypeStruct((rows, width), BF), jax.ShapeDtypeStruct((total, 256), F32)),
        scratch_shapes=[
            pltpu.VMEM((rows, width), BF),
            pltpu.VMEM((total, rows), F32),
            pltpu.VMEM((2, 2, total, 128), BF),
            pltpu.VMEM((2, 2, total, 128), BF),
            pltpu.VMEM((width // HD, rows), F32),
            pltpu.VMEM((2, 2, total, 128), F32),
            pltpu.VMEM((2, 2, total, 128), F32),
        ],
        compiler_params=pltpu.CompilerParams(vmem_limit_bytes=(32 if total <= 1024 else 58) << 20),
        cost_estimate=LIGHT,
        name="attend_backward",
    )(queries, key_value, keys_t, key_code, query_codes, attended, grad_branch, lse, turn, *out_pieces)


def rows_at(index, size):
    return pl.ds(pl.multiple_of(index * size, size), size)


def half_turn(block):
    lane = lax.broadcasted_iota(jnp.int32, block.shape, 1)
    return jnp.where(lane % HD < HD // 2, pltpu.roll(block, 128 - HD // 2, 1), pltpu.roll(block, HD // 2, 1))


def project_kernel(width_q, x_ref, cos_ref, sin_ref, p0, p1, p2, p3, normed_ref, q_ref, kv_ref):
    block = x_ref.shape[1] // 4
    width = p0.shape[1]
    total = jnp.zeros((x_ref.shape[0], width), F32)
    for r, piece in enumerate((p0, p1, p2, p3)):
        lanes = slice(r * block, (r + 1) * block)
        gain = piece[block : block + 1, :block].astype(F32)
        low = (x_ref[:, lanes] * gain).astype(BF)
        normed_ref[:, lanes] = low
        total += dot_nn(low, piece[:block, :])
    cosine, sine = cos_ref[...], sin_ref[...]
    turned_width = width_q + (width - width_q) // 2
    for at in range(0, width, 128):
        part = total[:, at : at + 128]
        if at < turned_width:
            part = part * cosine + half_turn(part) * sine
        low = part.astype(BF)
        if at < width_q:
            q_ref[:, at : at + 128] = low * jnp.asarray(ATTN_SCALE, BF)
        else:
            kv_ref[:, at - width_q : at - width_q + 128] = low


def project(scaled, cos_table, sin_table, pieces, width_q):
    rows, model = scaled.shape
    width = pieces[0].shape[1]
    return pl.pallas_call(
        functools.partial(project_kernel, width_q),
        out_shape=(
            jax.ShapeDtypeStruct((rows, model), BF),
            jax.ShapeDtypeStruct((rows, width_q), BF),
            jax.ShapeDtypeStruct((rows, width - width_q), BF),
        ),
        compiler_params=pltpu.CompilerParams(vmem_limit_bytes=24 << 20),
        cost_estimate=LIGHT,
        name="project",
    )(scaled, cos_table, sin_table, *pieces)


def mlp_kernel(h_ref, g_ref, *refs):
    gates, ups, downs = refs[:4], refs[4:8], refs[8:12]
    hidden_ref, dgate_ref, dup_ref, dh_ref, acc = refs[12:]
    step = pl.program_id(0)
    block = h_ref.shape[1] // 4
    gate = up = dhid = None
    for r in range(4):
        lanes = slice(r * block, (r + 1) * block)
        h = h_ref[:, lanes]
        terms = (dot_nn(h, gates[r][...]), dot_nn(h, ups[r][...]), dot_nt(g_ref[:, lanes], downs[r][...]))
        gate, up, dhid = terms if r == 0 else (gate + terms[0], up + terms[1], dhid + terms[2])
    sigma = jax.nn.sigmoid(gate)
    active = gate * sigma
    hidden_ref[...] = (active * up).astype(BF)
    dgate = (dhid * up * sigma * (1.0 + gate * (1.0 - sigma))).astype(BF)
    dup = (dhid * active).astype(BF)
    dgate_ref[...] = dgate
    dup_ref[...] = dup
    for r in range(4):
        lanes = slice(r * block, (r + 1) * block)
        term = dot_nt(dgate, gates[r][...]) + dot_nt(dup, ups[r][...])

        @pl.when(step == 0)
        def _():
            acc[:, lanes] = term

        @pl.when(step != 0)
        def _():
            acc[:, lanes] += term

    @pl.when(step == pl.num_programs(0) - 1)
    def _():
        dh_ref[...] = acc[...].astype(BF)


def mlp(normed, grad, gates, ups, downs):
    rows, model = normed.shape
    block, hidden = gates[0].shape
    tile = 512
    whole = pl.BlockSpec((rows, model), lambda j: (0, 0))
    wide = pl.BlockSpec((block, tile), lambda j: (0, j))
    tall = pl.BlockSpec((tile, block), lambda j: (j, 0))
    out = pl.BlockSpec((rows, tile), lambda j: (0, j))
    return pl.pallas_call(
        mlp_kernel,
        grid=(hidden // tile,),
        in_specs=[whole] * 2 + [wide] * 8 + [tall] * 4,
        out_specs=[out] * 3 + [whole],
        out_shape=[jax.ShapeDtypeStruct((rows, hidden), BF)] * 3
        + [jax.ShapeDtypeStruct((rows, model), BF)],
        scratch_shapes=[pltpu.VMEM((rows, model), F32)],
        compiler_params=pltpu.CompilerParams(vmem_limit_bytes=40 << 20),
        cost_estimate=LIGHT,
        name="mlp",
    )(normed, grad, *gates, *ups, *downs)


def entry_kernel(dq_ref, own_ref, got_ref, cos_ref, sin_ref, p0, p1, p2, p3, low_ref, dh_ref):
    block = dh_ref.shape[1] // 4
    width_q = dq_ref.shape[1]
    low_ref[:, :width_q] = dq_ref[...]
    sums = own_ref[...] + got_ref[...].astype(F32)
    dk = sums[:, :128]
    low_ref[:, width_q : width_q + 128] = (dk * cos_ref[...] - half_turn(dk) * sin_ref[...]).astype(BF)
    low_ref[:, width_q + 128 :] = sums[:, 128:].astype(BF)
    low = low_ref[...]
    for r, piece in enumerate((p0, p1, p2, p3)):
        dh_ref[:, r * block : (r + 1) * block] = dot_nt(low, piece[:block, :]).astype(BF)


def entry_grad(dq_low, own, got, cos_table, sin_table, pieces):
    rows, width_q = dq_low.shape
    block = pieces[0].shape[0] - 32
    width = pieces[0].shape[1]
    return pl.pallas_call(
        entry_kernel,
        out_shape=(
            jax.ShapeDtypeStruct((rows, width), BF),
            jax.ShapeDtypeStruct((rows, 4 * block), BF),
        ),
        compiler_params=pltpu.CompilerParams(vmem_limit_bytes=24 << 20),
        cost_estimate=LIGHT,
        name="entry_grad",
    )(dq_low, own, got, cos_table, sin_table, *pieces)


def outer_kernel(n_adds, a_ref, b_ref, *refs):
    total = lax.dot_general(
        a_ref[...], b_ref[...], (((0,), (0,)), ((), ())), preferred_element_type=F32
    )
    for add in refs[:n_adds]:
        total += add[...].astype(F32)
    refs[n_adds][...] = total.astype(BF)


def outer(left, right, left_blocks, right_blocks, adds, name):
    rows = left.shape[0]
    size_m, size_n = left.shape[1] // 4, right.shape[1] // 4
    first_m, count_m = left_blocks
    first_n, count_n = right_blocks
    cut_rows = count_m < 4
    wide = size_n * count_n
    in_specs = [
        pl.BlockSpec((rows, size_m), lambda i: (0, first_m + i)),
        pl.BlockSpec((rows, wide), lambda i: (0, first_n // count_n)),
    ]
    for array, first in adds:
        if cut_rows:
            in_specs.append(pl.BlockSpec((size_m, wide), lambda i, first=first: (first + i, 0)))
        else:
            in_specs.append(pl.BlockSpec((size_m, wide), lambda i, first=first: (i, first)))
    return pl.pallas_call(
        functools.partial(outer_kernel, len(adds)),
        grid=(count_m,),
        in_specs=in_specs,
        out_specs=pl.BlockSpec((size_m, wide), lambda i: (i, 0)),
        out_shape=jax.ShapeDtypeStruct((size_m * count_m, wide), BF),
        compiler_params=pltpu.CompilerParams(vmem_limit_bytes=32 << 20),
        cost_estimate=LIGHT,
        name=name,
    )(left, right, *[array for array, unused in adds])


def lift_kernel(hidden_ref, d0, d1, d2, d3, out_ref, acc):
    step = pl.program_id(0)
    block = d0.shape[1]
    for r, piece in enumerate((d0, d1, d2, d3)):
        lanes = slice(r * block, (r + 1) * block)
        term = dot_nn(hidden_ref[...], piece[...])

        @pl.when(step == 0)
        def _():
            acc[:, lanes] = term

        @pl.when(step != 0)
        def _():
            acc[:, lanes] += term

    @pl.when(step == pl.num_programs(0) - 1)
    def _():
        out_ref[...] = acc[...].astype(BF)


def lift(hidden, downs):
    rows, width = hidden.shape
    block = downs[0].shape[1]
    tile = 512
    return pl.pallas_call(
        lift_kernel,
        grid=(width // tile,),
        in_specs=[pl.BlockSpec((rows, tile), lambda j: (0, j))]
        + [pl.BlockSpec((tile, block), lambda j: (j, 0))] * 4,
        out_specs=pl.BlockSpec((rows, 4 * block), lambda j: (0, 0)),
        out_shape=jax.ShapeDtypeStruct((rows, 4 * block), BF),
        scratch_shapes=[pltpu.VMEM((rows, 4 * block), F32)],
        compiler_params=pltpu.CompilerParams(vmem_limit_bytes=32 << 20),
        cost_estimate=LIGHT,
        name="lift",
    )(hidden, *downs)


def entry_outer_kernel(n_adds, attended_ref, branch_ref, normed_ref, low_ref, *refs):
    out_ref = refs[n_adds]
    width = attended_ref.shape[1]
    head = lax.dot_general(
        attended_ref[...], branch_ref[...], (((0,), (0,)), ((), ())), preferred_element_type=F32
    )
    tail = lax.dot_general(
        normed_ref[...], low_ref[...], (((0,), (0,)), ((), ())), preferred_element_type=F32
    )
    for add in refs[:n_adds]:
        head += add[:, : head.shape[1]].astype(F32)
        tail += add[:, head.shape[1] :].astype(F32)
    out_ref[:, : head.shape[1]] = head.astype(BF)
    out_ref[:, head.shape[1] :] = tail.astype(BF)


def entry_outer(attended, branch, normed, low, first, count, adds):
    rows, heads = attended.shape
    block = branch.shape[1] // 4
    width = block + low.shape[1]
    column = pl.BlockSpec((rows, block), lambda i: (0, first + i))
    in_specs = [
        pl.BlockSpec((rows, heads), lambda i: (0, 0)),
        column,
        column,
        pl.BlockSpec(low.shape, lambda i: (0, 0)),
    ]
    for array, at in adds:
        in_specs.append(pl.BlockSpec((block, width), lambda i, at=at: (at + i, 0)))
    return pl.pallas_call(
        functools.partial(entry_outer_kernel, len(adds)),
        grid=(count,),
        in_specs=in_specs,
        out_specs=pl.BlockSpec((block, width), lambda i: (i, 0)),
        out_shape=jax.ShapeDtypeStruct((block * count, width), BF),
        compiler_params=pltpu.CompilerParams(vmem_limit_bytes=24 << 20),
        cost_estimate=LIGHT,
        name="entry_outer",
    )(attended, branch, normed, low, *[array for array, unused in adds])


def after(value, *others):
    if not others:
        return value
    return lax.optimization_barrier((value, *others))[0]


def sealed(step, *values):
    skipped = lambda *v: jax.tree.map(lambda a: jnp.zeros(a.shape, a.dtype), jax.eval_shape(step, *v))
    return lax.cond(lax.optimization_barrier(jnp.asarray(True)), step, skipped, *values)


def swap_core(value):
    return lax.ppermute(value, "dp", [(i, i ^ 1) for i in range(4)])


def swap_x(value):
    return lax.ppermute(value, "dp", [(i, i ^ 2) for i in range(4)])


def swap_both(value):
    return lax.ppermute(value, "dp", [(i, i ^ 3) for i in range(4)])


def swap_ctx(value):
    return lax.ppermute(value, "ctx", [(0, 1), (1, 0)])


def two_ctx():
    return lax.axis_size("ctx") == 2


def sum_ctx(total):
    low = total.astype(BF)
    if two_ctx():
        return low.astype(F32) + swap_ctx(low).astype(F32)
    return lax.psum(low, "ctx").astype(F32)


def far_halves(one, two, wait):
    if not two_ctx():
        return swap_x(after(jnp.concatenate([one, two]), wait))
    half = one.shape[0] // 2
    at = lax.axis_index("ctx") * half
    mine = [lax.dynamic_slice_in_dim(v, at, half) for v in (one, two)]
    return swap_x(after(jnp.concatenate(mine), wait))


def far_wholes(got):
    if not two_ctx():
        return jnp.split(got, 2)
    other = swap_ctx(got)
    half = got.shape[0] // 2
    first = lax.axis_index("ctx") == 0
    return [
        jnp.concatenate([jnp.where(first, a, b), jnp.where(first, b, a)])
        for a, b in ((got[:half], other[:half]), (got[half:], other[half:]))
    ]


def psum_tensor(value):
    return lax.psum(value, "tensor")


def swap_bits(index):
    return ((index & 1) << 1) | (index >> 1)


def take_blocks(value, indices):
    size = value.shape[1] // 4
    return jnp.concatenate(
        [lax.dynamic_slice_in_dim(value, i * size, size, 1) for i in indices], axis=1
    )


def relative(value):
    mine = lax.axis_index("dp")
    return take_blocks(value, [mine ^ k for k in (0, 2, 1, 3)])


def absolute(value):
    mine = lax.axis_index("dp")
    return take_blocks(value, [swap_bits(mine ^ k) for k in range(4)])


def split4(value, axis):
    size = value.shape[axis] // 4
    return [lax.slice_in_dim(value, r * size, (r + 1) * size, axis=axis) for r in range(4)]


def token_places(row_ids, order_row, seen_row, prompt_len, block_rows, cont_len):
    block_total = order_row.shape[0]
    block_pick = (row_ids // block_rows)[:, None] == jnp.arange(block_total, dtype=jnp.int32)[
        None, :
    ]
    chosen = jnp.sum(jnp.where(block_pick, order_row[None, :], 0), axis=1)
    global_ids = chosen * block_rows + row_ids % block_rows
    in_prompt = global_ids < prompt_len
    segment = jnp.where(in_prompt, 0, 1 + (global_ids - prompt_len) // cont_len)
    cont_count = seen_row.shape[0]
    which_cont = (segment - 1)[:, None] == jnp.arange(cont_count, dtype=jnp.int32)[None, :]
    limit = jnp.sum(jnp.where(which_cont, seen_row[None, :], 0), axis=1)
    places = jnp.where(in_prompt, global_ids, limit + (global_ids - prompt_len) % cont_len)
    return (segment, places, limit)


def norm_scale(values):
    return lax.rsqrt(jnp.mean(values * values, axis=-1, keepdims=True) + EPSILON)


def norm_back(values, scale, gain, grad):
    weighted = gain * grad
    inner = jnp.mean(weighted * values, axis=-1, keepdims=True)
    return scale * weighted - values * (scale * scale * scale) * inner


def combine(low, peer):
    if two_ctx():
        return low.astype(F32) + peer.astype(F32)
    return peer.astype(F32)


class BlockSum:
    def __init__(self, term):
        self.term = term

    def begin(self):
        other = swap_core(self.term(2, 2, ()))
        return other, self.term(1, 1, ((other, 1),))

    def cross(self, begun, *wait):
        self.other, self.sent = begun
        self.got = swap_x(after(self.sent, *wait))
        return self

    def joined(self, other, got):
        self.other, self.got = other, got
        return self

    def fold(self, *wait):
        self.low = self.term(0, 1, ((self.other, 0), (after(self.got, *wait), 0)))
        return self

    def swap(self, *wait):
        low = after(self.low, *wait)
        self.peer = swap_ctx(low) if two_ctx() else lax.psum(low, "ctx")
        return self

    def result(self):
        return combine(self.low, self.peer)


def outer_sum(left, right, cut_left, name):
    def term(k, n, adds):
        cut, whole = (k, n), (0, 4)
        if cut_left:
            return outer(left, right, cut, whole, adds, name)
        return outer(left, right, whole, cut, adds, name)

    return BlockSum(term)


def shards(
    tokens,
    cotangent,
    first_gain,
    query_weight,
    key_weight,
    value_weight,
    output_weight,
    second_gain,
    gate_weight,
    up_weight,
    down_weight,
    block_order,
    prefix_seen,
):
    ctx_size = lax.axis_size("ctx")
    local_rows = tokens.shape[0]
    group_rows = local_rows * ctx_size
    offset = lax.axis_index("ctx") * local_rows
    width_q = query_weight.shape[1]
    width_kv = key_weight.shape[1]
    block_d = query_weight.shape[0]

    gains = jnp.pad(
        jnp.stack([first_gain, second_gain]), ((0, 30), (0, width_q + 2 * width_kv - block_d))
    )
    qkv_shard = jnp.concatenate(
        [jnp.concatenate([query_weight, key_weight, value_weight], axis=1), gains], axis=0
    )
    qkv_far = swap_x(qkv_shard)
    qkv_near = swap_core(qkv_shard)
    out_far = swap_x(after(output_weight, qkv_near))
    out_near = swap_core(after(output_weight, qkv_near))
    wide_got = far_halves(gate_weight, up_weight, out_near)

    tokens, cotangent, block_order = (
        after(v, qkv_near) for v in (tokens, cotangent, block_order)
    )
    all_ids = jnp.arange(group_rows, dtype=jnp.int32)
    if two_ctx():
        all_ids = jnp.where(all_ids < local_rows, all_ids + offset, all_ids - offset)
    key_seg, key_pos, key_lim = token_places(
        all_ids, block_order[0], prefix_seen[0], group_rows // 2, local_rows // 2, CLEN
    )
    if two_ctx():
        query_seg, query_pos, query_lim = key_seg[:local_rows], key_pos[:local_rows], key_lim[:local_rows]
    else:
        query_seg = lax.dynamic_slice_in_dim(key_seg, offset, local_rows)
        query_pos = lax.dynamic_slice_in_dim(key_pos, offset, local_rows)
        query_lim = lax.dynamic_slice_in_dim(key_lim, offset, local_rows)
    key_code = (key_seg * SEGMENT_STEP + key_pos)[:, None]
    in_prompt = query_seg == 0
    below = jnp.where(in_prompt, query_pos + 1, query_lim)
    low_code = jnp.where(in_prompt, 1, query_seg * SEGMENT_STEP)
    high_code = jnp.where(in_prompt, 0, query_seg * SEGMENT_STEP + query_pos)
    query_codes = jnp.stack([below, low_code, high_code] + [below] * 5)
    half_size = HD // 2
    freq = ROPE_BASE ** (-(jnp.arange(half_size, dtype=F32) * 2.0) / HD)
    angle_t = freq[:, None] * query_pos.astype(F32)[None, :]
    turn = jnp.concatenate([jnp.cos(angle_t), jnp.sin(angle_t)], axis=0)
    cosine, sine = turn[:half_size].T, turn[half_size:].T
    cos_table = jnp.concatenate([cosine] * 4, axis=1)
    sin_table = jnp.concatenate([-sine, sine] * 2, axis=1)

    inputs = relative(tokens).astype(F32)
    grad_out = relative(cotangent).astype(F32)
    grad_mlp = (RESIDUAL * grad_out).astype(BF)
    scale_one = norm_scale(inputs)
    scaled = inputs * scale_one
    qkv_pieces = [qkv_shard, qkv_far, qkv_near, swap_core(qkv_far)]
    gain_one = jnp.concatenate([p[block_d, :block_d] for p in qkv_pieces]).astype(F32)
    gain_two = jnp.concatenate([p[block_d + 1, :block_d] for p in qkv_pieces]).astype(F32)
    normed, queries, key_value = project(scaled, cos_table, sin_table, qkv_pieces, width_q)
    out_far = after(out_far, queries)
    out_pieces = [output_weight, out_far, out_near, swap_core(out_far)]
    if two_ctx():
        key_value_all = jnp.concatenate([key_value, swap_ctx(key_value)], axis=0)
    else:
        key_value_all = lax.all_gather(key_value, "ctx", axis=0, tiled=True)
    attended, log_total, branch = attend_forward(
        queries, key_value_all, key_value_all[:, width_kv:].T, key_code, query_codes, out_pieces
    )
    branch = psum_tensor(branch)

    def spread_wide(got, gate, up):
        return *far_wholes(got), swap_core(gate), swap_core(up)

    def spread_last(*values):
        return tuple(swap_core(v) for v in values)

    down_far = swap_x(after(down_weight, log_total))
    gate_far, up_far, gate_near, up_near = sealed(
        spread_wide, after(wide_got, log_total), gate_weight, up_weight
    )
    gate_last, up_last, down_near, down_last = sealed(
        spread_last, gate_far, up_far, down_weight, down_far
    )
    gates = [gate_weight, gate_far, gate_near, gate_last]
    ups = [up_weight, up_far, up_near, up_last]
    downs = [down_weight, down_far, down_near, down_last]
    wait = down_last
    branch = after(branch, wait)
    middle = inputs + RESIDUAL * branch.astype(F32)

    scale_two = norm_scale(middle)
    normed_two = (middle * scale_two * gain_two).astype(BF)
    hidden, grad_gate, grad_up, grad_two = mlp(normed_two, grad_mlp, gates, ups, downs)
    grad_two = psum_tensor(grad_two)

    def begin_down(hidden, grad_mlp):
        return outer_sum(hidden, grad_mlp, False, "down_outer").begin()

    def begin_rest(hidden, normed_two, grad_gate, grad_up, *downs):
        return (
            outer_sum(normed_two, grad_gate, True, "gate_outer").begin(),
            outer_sum(normed_two, grad_up, True, "up_outer").begin(),
            lift(hidden, downs),
        )

    begun = sealed(begin_down, hidden, grad_mlp)
    down_sum = outer_sum(hidden, grad_mlp, False, "down_outer").cross(begun)
    begun_gate, begun_up, mlp_part = sealed(
        begin_rest, after(hidden, begun[1]), normed_two, grad_gate, grad_up, *downs
    )
    gate_sum = outer_sum(normed_two, grad_gate, True, "gate_outer").cross(begun_gate)
    up_sum = outer_sum(normed_two, grad_up, True, "up_outer").cross(begun_up, down_sum.got)
    grad_two = after(grad_two, down_sum.sent, gate_sum.sent, up_sum.sent, mlp_part)
    down_sum.fold(grad_two).swap()
    mlp_sum = psum_tensor(after(mlp_part, grad_two))
    grad_two = grad_two.astype(F32)

    gain_two_part = jnp.sum(grad_two * middle * scale_two, axis=0)
    grad_middle = grad_out + norm_back(middle, scale_two, gain_two, grad_two)
    grad_branch = after((RESIDUAL * grad_middle).astype(BF), down_sum.low)
    query_low, key_value_parts = attend_backward(
        queries,
        key_value_all,
        key_value_all[:, :width_kv].T,
        key_code,
        query_codes,
        attended,
        grad_branch,
        log_total,
        turn,
        out_pieces,
    )
    if two_ctx():
        own_part = key_value_parts[:local_rows]
        got_part = swap_ctx(key_value_parts[local_rows:].astype(BF))
    else:
        own_part = lax.psum_scatter(
            key_value_parts.astype(BF), "ctx", scatter_dimension=0, tiled=True
        ).astype(F32)
        got_part = jnp.zeros(own_part.shape, BF)
    qkv_low, grad_one = entry_grad(
        query_low, own_part, got_part, cos_table, sin_table, qkv_pieces
    )
    gate_sum.fold(query_low)
    gate_sum.swap(got_part)

    def entry_term(attended, grad_branch, normed, qkv_low):
        return BlockSum(
            lambda k, n, adds: entry_outer(attended, grad_branch, normed, qkv_low, k, n, adds)
        )

    entry_inputs = (attended, grad_branch, normed, qkv_low)
    begun = sealed(lambda *v: entry_term(*v).begin(), *entry_inputs)
    entry_sum = entry_term(*entry_inputs).cross(begun, gate_sum.low)
    mlp_sum = after(mlp_sum, qkv_low, down_sum.peer, gate_sum.low, up_sum.fold(qkv_low).low, entry_sum.sent)
    grad_one = psum_tensor(after(grad_one, mlp_sum))


    def finish_wide(up_low, *pairs):
        peer = swap_ctx(up_low) if two_ctx() else lax.psum(up_low, "ctx")
        totals = [combine(low, other) for low, other in zip(pairs[::2], pairs[1::2], strict=True)]
        return combine(up_low, peer), *totals

    up_grad, gate_grad, down_grad = sealed(
        finish_wide,
        after(up_sum.low, mlp_sum),
        gate_sum.low,
        gate_sum.peer,
        down_sum.low,
        down_sum.peer,
    )
    entry_total = sealed(
        lambda *v: entry_term(*v[:4]).joined(v[4], v[5]).fold().swap().result(),
        after(attended, up_grad),
        *entry_inputs[1:],
        entry_sum.other,
        entry_sum.got,
    )
    layer_out = absolute((middle + RESIDUAL * mlp_sum.astype(F32)).astype(BF))
    grad_one = after(grad_one, entry_total, layer_out)
    output_grad, qkv_grad = entry_total[:, :block_d], entry_total[:, block_d:]
    grad_one = grad_one.astype(F32)
    gain_one_part = jnp.sum(grad_one * inputs * scale_one, axis=0)
    tokens_grad = absolute(
        (grad_middle + norm_back(inputs, scale_one, gain_one, grad_one)).astype(BF)
    )
    gain_blocks = split4(jnp.stack([gain_one_part, gain_two_part]), 1)
    gain_grad = sum_ctx(
        gain_blocks[0]
        + swap_x(gain_blocks[1])
        + swap_core(gain_blocks[2])
        + swap_both(gain_blocks[3])
    )
    return (
        layer_out,
        tokens_grad,
        gain_grad[0],
        qkv_grad[:, :width_q],
        qkv_grad[:, width_q : width_q + width_kv],
        qkv_grad[:, width_q + width_kv :],
        output_grad,
        gain_grad[1],
        gate_grad,
        up_grad,
        down_grad,
    )


def solution(mesh):
    return jax.shard_map(
        shards,
        mesh=mesh,
        in_specs=(
            P(("dp", "ctx"), None),
            P(("dp", "ctx"), None),
            P("dp"),
            P("dp", "tensor"),
            P("dp", "tensor"),
            P("dp", "tensor"),
            P("tensor", "dp"),
            P("dp"),
            P("dp", "tensor"),
            P("dp", "tensor"),
            P("tensor", "dp"),
            P("dp", None),
            P("dp", None),
        ),
        out_specs=(
            P(("dp", "ctx"), None),
            P(("dp", "ctx"), None),
            P("dp"),
            P("dp", "tensor"),
            P("dp", "tensor"),
            P("dp", "tensor"),
            P("tensor", "dp"),
            P("dp"),
            P("dp", "tensor"),
            P("dp", "tensor"),
            P("tensor", "dp"),
        ),
        check_vma=False,
    )
```

time: 732 us -> 514 us (0.70)
  matrix products: 185 us -> 0 us
  Pallas kernels: 0 us -> 130 us
  waiting for transfers between devices: 320 us -> 238 us
  local copies, waits for them, and re-layouts: 81.1 us -> 32.7 us
  blocking collectives: 19.6 us -> 0 us
    dot_general x48 -> x0, matrix products: 185 us -> none  [the longest x20 53.4 us: inner_rows(): lax.dot_general(left, right, (((0,), (0,)), ((), ())), preferred_element_...]
    pallas_call x0 -> x18, Pallas kernels: none -> 130 us  [the longest x9 42.7 us: outer(): pl.pallas_call(functools.partial(outer_kernel, len(adds)), grid=(count_m,...]
    psum x3 -> x4, waiting for transfers between devices: 95.9 us -> 50 us  [psum_tensor(): return lax.psum(value, 'tensor')]
    ppermute x11 -> x9, waiting for transfers between devices: 70 us -> 27.5 us  [swap_x(): return lax.ppermute(value, 'dp', [(i, i ^ 2) for i in range(4)])]
    ppermute x22 -> x15, waiting for transfers between devices: 0.06 us -> 24.7 us  [swap_core(): return lax.ppermute(value, 'dp', [(i, i ^ 1) for i in range(4)])]
    dynamic_update_slice x8 -> x0, local copies, waits for them, and re-layouts: 24.1 us -> none  [attend_backward(): lax.scan(grad_step, start_query, (key_blocks, value_blocks, seg_blocks, p...]
    all_gather x1 -> x0, blocking collectives: 19.6 us -> none  [shards(): key_value_all = lax.all_gather(key_value, 'ctx', axis=0, tiled=True)]
    ppermute x10 -> x8, waiting for transfers between devices: 154 us -> 136 us  [swap_ctx(): return lax.ppermute(value, 'ctx', [(0, 1), (1, 0)])]
  transfers between devices with their start and end apart: 46 -> 37, of which waited for: 14 -> 18; matrix products, arithmetic and copies ran while one was open for 38% -> 14% of each run, Pallas kernels for 0% -> 19%
where the time goes in v2:
time: 514 us; the launch traced here: 506 us
  waiting for transfers between devices  238 us (46%)
  Pallas kernels  130 us (25%)
  other arithmetic  61.5 us (12%)
  local copies, waits for them, and re-layouts  32.7 us (6%)
  starting transfers between devices  27.5 us (5%)
  between operations  15.8 us (3%)
    ppermute x8, waiting for transfers between devices, swap_ctx(): return lax.ppermute(value, 'ctx', [(0, 1), (1, 0)])  136 us
    psum x4, waiting for transfers between devices, psum_tensor(): return lax.psum(value, 'tensor')  50 us
    pallas_call x9, Pallas kernels, outer(): pl.pallas_call(functools.partial(outer_kernel, len(adds)), grid=(count_m,...  42.7 us
    pallas_call x1, Pallas kernels, mlp(): pl.pallas_call(mlp_kernel, grid=(hidden // tile,), in_specs=[whole] * 2 +...  32.1 us
    ppermute x9, waiting for transfers between devices, swap_x(): return lax.ppermute(value, 'dp', [(i, i ^ 2) for i in range(4)])  27.5 us
    ppermute x15, waiting for transfers between devices, swap_core(): return lax.ppermute(value, 'dp', [(i, i ^ 1) for i in range(4)])  24.7 us
    pallas_call x1, Pallas kernels, attend_backward(): pl.pallas_call(functools.partial(backward_kernel, chunk), out_shape=(jax....  17.4 us
    unnamed x154, local copies, waits for them, and re-layouts  12.7 us
  transfers between devices with their start and end apart: 37, of which 18 were waited for; matrix products, arithmetic and copies ran while one was open for 14% of the time, Pallas kernels for 19%

profile of v2, /device:TPU:0, one launch (start us, length us, event | category | flops | bytes accessed | tf_op | source)
XLA Modules:
  0.0 505.7 jit_solution(1529841960892291290)
XLA Ops:
  25.1 7.2 %collective-permute-done.14.p1 = bf16[544,768]{1,0:T(8,128)(2,1)S(1)} collective-permute-done((bf16[544,768]{1,0:T(8,128)(2,1)S(1)}, bf16[544,768]{1,0:T(8,128)(2,1)S(1)}, u32[]{:S(2)}, u32[]{:S(2)}) %collective-permute-start.14) | collective-permute-done | bytes 835616 | tf_op jit(solution)/shard_map/ppermute | solution.py:454
  61.0 11.3 %attend_forward.1 = (bf16[512,512]{1,0:T(8,128)(2,1)}, f32[8,512]{1,0:T(8,128)S(1)}, bf16[512,2048]{1,0:T(8,128)(2,1)S(1)}) custom-call(bf16[512,512]{1,0:T(8,128)(2,1)S(1)} %copy-done.7, bf16[1024,256]{1,0:T(8,128)(2,1)S(1)} %copy.42.kv_ref, bf16[128,1024]{1,0:T(8,128)(2,1)S(1)} %get-tuple-element.279.vt_ref, s32[1024,1]{1,0:T(8,128)S(1)} %get-tuple-element.281.code_ref, ...), custom_call_target="tpu_custom_call" | custom-call | flops 1 | bytes 1 | tf_op jit(solution)/shard_map/attend_forward/pallas_call | solution.py:91
  83.4 16.2 %collective-permute-done.20 = bf16[512,2048]{1,0:T(8,128)(2,1)} collective-permute-done((bf16[512,2048]{1,0:T(8,128)(2,1)}, bf16[512,2048]{1,0:T(8,128)(2,1)}, u32[]{:S(2)}, u32[]{:S(2)}) %collective-permute-start.20) | collective-permute-done | bytes 2097184 | tf_op jit(solution)/shard_map/ppermute | solution.py:454
  99.7 51.4 %conditional.7 = (bf16[512,2048]{1,0:T(8,128)(2,1)}, bf16[512,2048]{1,0:T(8,128)(2,1)}, bf16[512,2048]{1,0:T(8,128)(2,1)}, bf16[512,2048]{1,0:T(8,128)(2,1)}) conditional(s32[]{:T(128)} %convert_element_type.97, () %tuple.96, (bf16[512,2048]{1,0:T(8,128)(2,1)}, bf16[512,2048]{1,0:T(8,128)(2,1)}, bf16[512,2048]{1,0:T(8,128)(2,1)}) %tuple.99), branch_computations={%region_3.4_spmd, %region_4.5_spmd} | conditional | flops 10485764 | bytes 41943232 | solution.py:446
  100.5 45.8 %collective-permute-done.8 = bf16[512,2048]{1,0:T(8,128)(2,1)} collective-permute-done((bf16[512,2048]{1,0:T(8,128)(2,1)}, bf16[512,2048]{1,0:T(8,128)(2,1)}, u32[]{:S(2)}, u32[]{:S(2)}) %collective-permute-start.8) | collective-permute-done | bytes 2097184 | tf_op jit(solution)/shard_map/cond/branch_1_fun/ppermute | solution.py:462
  151.1 13.6 %conditional.8 = (bf16[512,2048]{1,0:T(8,128)(2,1)}, bf16[512,2048]{1,0:T(8,128)(2,1)}, bf16[2048,512]{1,0:T(8,128)(2,1)}, bf16[2048,512]{1,0:T(8,128)(2,1)}) conditional(s32[]{:T(128)} %convert_element_type.97, () %tuple.95, (bf16[512,2048]{1,0:T(8,128)(2,1)}, bf16[512,2048]{1,0:T(8,128)(2,1)}, bf16[2048,512]{1,0:T(8,128)(2,1)}, ...), branch_computations={%region_5.6_spmd, %region_6.7_spmd} | conditional | bytes 33554624 | solution.py:446
  170.0 32.1 %mlp.1 = (bf16[512,2048]{1,0:T(8,128)(2,1)}, bf16[512,2048]{1,0:T(8,128)(2,1)}, bf16[512,2048]{1,0:T(8,128)(2,1)}, bf16[512,2048]{1,0:T(8,128)(2,1)S(1)}) custom-call(bf16[512,2048]{1,0:T(8,128)(2,1)S(1)} %multiply_convert_fusion.1.h_ref.a_ref, bf16[512,2048]{1,0:T(8,128)(2,1)S(1)} %copy-done.20, bf16[512,2048]{1,0:T(8,128)(2,1)} %refs_0_.1, ...), custom_call_target="tpu_custom_call" | custom-call | flops 1 | bytes 1 | tf_op jit(solution)/shard_map/mlp/pallas_call | solution.py:279
  203.7 17.0 %conditional.9 = (bf16[2048,1024]{1,0:T(8,128)(2,1)}, bf16[2048,512]{1,0:T(8,128)(2,1)}) conditional(s32[]{:T(128)} %convert_element_type.97, () %tuple.105, (bf16[512,2048]{1,0:T(8,128)(2,1)}, bf16[512,2048]{1,0:T(8,128)(2,1)}) %tuple.106), branch_computations={%region_8.9_spmd, %region_9.10_spmd} | conditional | flops 2 | bytes 33554544 | solution.py:446
  203.7 4.9 down_outer.3
  208.8 7.1 %collective-permute-done.4.refs_0_ = bf16[2048,1024]{1,0:T(8,128)(2,1)} collective-permute-done((bf16[2048,1024]{1,0:T(8,128)(2,1)S(1)}, bf16[2048,1024]{1,0:T(8,128)(2,1)}, u32[]{:S(2)}, u32[]{:S(2)}) %collective-permute-start.4) | collective-permute-done | bytes 4194336 | tf_op jit(solution)/shard_map/cond/branch_1_fun/ppermute | solution.py:450
  216.0 4.8 down_outer.4
  222.2 28.0 %conditional.10 = (bf16[1024,2048]{1,0:T(8,128)(2,1)}, bf16[512,2048]{1,0:T(8,128)(2,1)}, bf16[1024,2048]{1,0:T(8,128)(2,1)}, bf16[512,2048]{1,0:T(8,128)(2,1)}, bf16[512,2048]{1,0:T(8,128)(2,1)}) conditional(s32[]{:T(128)} %convert_element_type.97, () %tuple.103, (bf16[512,2048]{1,0:T(8,128)(2,1)}, bf16[512,2048]{1,0:T(8,128)(2,1)}, ...), branch_computations={%region_10.11_spmd, %region_11.12_spmd} | conditional | flops 5 | bytes 75497728 | solution.py:446
  222.2 4.5 gate_outer.3
  230.1 11.6 %lift.1 = bf16[512,2048]{1,0:T(8,128)(2,1)} custom-call(bf16[512,2048]{1,0:T(8,128)(2,1)S(1)} %copy-done.42, bf16[2048,512]{1,0:T(8,128)(2,1)S(1)} %copy-done.49, bf16[2048,512]{1,0:T(8,128)(2,1)} %get-tuple-element.83.d1, bf16[2048,512]{1,0:T(8,128)(2,1)} %get-tuple-element.84.d2, bf16[2048,512]{1,0:T(8,128)(2,1)} %get-tuple-element.85.d3), custom_call_target="tpu_custom_call" | custom-call | flops 1 | bytes 1 | tf_op jit(solution)/shard_map/cond/branch_1_fun/lift/pallas_call | solution.py:383
  241.7 4.2 gate_outer.4
  246.0 4.2 up_outer.4
  250.8 39.6 %all-reduce.8.cloned.1.call-done = bf16[512,2048]{1,0:T(8,128)(2,1)} async-done(((bf16[512,2048]{1,0:T(8,128)(2,1)}), bf16[512,2048]{1,0:T(8,128)(2,1)}) %all-reduce.8.cloned.1.call-update) | async-done | bytes 2097168 | tf_op jit(solution)/shard_map/psum | solution.py:498
  291.9 6.0 %down_outer.5 = bf16[2048,512]{1,0:T(8,128)(2,1)} custom-call(bf16[512,2048]{1,0:T(8,128)(2,1)} %get-tuple-element.199.a_ref, bf16[512,2048]{1,0:T(8,128)(2,1)} %fusion.8.g_ref.b_ref, bf16[2048,1024]{1,0:T(8,128)(2,1)} %get-tuple-element.207.refs_0_, bf16[2048,512]{1,0:T(8,128)(2,1)} %collective-permute-done.22.refs_1_), custom_call_target="tpu_custom_call" | custom-call | flops 1 | bytes 1 | tf_op jit(solution)/shard_map/down_outer/pallas_call | solution.py:347
  300.9 5.2 %fusion.10 = (f32[2048]{0:T(1024)}, f32[512]{0:T(512)S(1)}) fusion(bf16[512,2048]{1,0:T(8,128)(2,1)} %all-reduce.8.cloned.1.call-done, f32[512]{0:T(512)} %copy-done.68, bf16[512,2048]{1,0:T(8,128)(2,1)} %all-reduce.6.cloned.1.call-done, bf16[512,512]{1,0:T(8,128)(2,1)} %copy-done.26, bf16[512,512]{1,0:T(8,128)(2,1)} %copy-done.30, ...), kind=kLoop, calls=%fused_computation.31 | loop fusion | flops 18871808 | bytes 6311936 | tf_op jit(solution)/shard_map/reduce_sum | solution.py:730
  306.2 5.8 %multiply_convert_fusion = (bf16[512,2048]{1,0:T(8,128)(2,1)S(1)}, f32[512,2048]{1,0:T(8,128)}) fusion(f32[512]{0:T(512)S(1)} %broadcast_multiply_fusion.2, f32[512]{0:T(512)S(1)} %copy-done.74, bf16[512,2048]{1,0:T(8,128)(2,1)S(1)} %copy-done.39, bf16[512,512]{1,0:T(8,128)(2,1)S(1)} %copy-done.28, bf16[512,512]{1,0:T(8,128)(2,1)S(1)} %copy-done.32, ...), kind=kLoop, calls=%fused_computation.38 | loop fusion | flops 29360128 | bytes 14694400 | tf_op jit(solution)/shard_map/convert_element_type | solution.py:732
  312.1 17.4 %attend_backward.1 = (bf16[512,512]{1,0:T(8,128)(2,1)S(1)}, f32[1024,256]{1,0:T(8,128)S(1)}) custom-call(bf16[512,512]{1,0:T(8,128)(2,1)S(1)} %copy-done.8, bf16[1024,256]{1,0:T(8,128)(2,1)S(1)} %copy.42.kv_ref, bf16[128,1024]{1,0:T(8,128)(2,1)S(1)} %copy-done.11, s32[1024,1]{1,0:T(8,128)S(1)} %get-tuple-element.281.code_ref, s32[8,512]{1,0:T(8,128)S(1)} %copy-done.14, ...), custom_call_target="tpu_custom_call" | custom-call | flops 1 | bytes 1 | tf_op jit(solution)/shard_map/attend_backward/pallas_call | solution.py:170
  330.1 5.1 %gate_outer.5 = bf16[512,2048]{1,0:T(8,128)(2,1)} custom-call(bf16[512,2048]{1,0:T(8,128)(2,1)S(1)} %copy-done.18, bf16[512,2048]{1,0:T(8,128)(2,1)S(1)} %copy-done.44, bf16[1024,2048]{1,0:T(8,128)(2,1)} %get-tuple-element.213.refs_0_, bf16[512,2048]{1,0:T(8,128)(2,1)} %collective-permute-done.25.refs_1_), custom_call_target="tpu_custom_call" | custom-call | flops 1 | bytes 1 | tf_op jit(solution)/shard_map/gate_outer/pallas_call | solution.py:347
  335.3 15.5 %collective-permute-done.23.got_ref = bf16[512,256]{1,0:T(8,128)(2,1)S(1)} collective-permute-done((bf16[512,256]{1,0:T(8,128)(2,1)S(1)}, bf16[512,256]{1,0:T(8,128)(2,1)S(1)}, u32[]{:S(2)}, u32[]{:S(2)}) %collective-permute-start.23) | collective-permute-done | bytes 262176 | tf_op jit(solution)/shard_map/ppermute | solution.py:462
  355.4 11.0 %conditional.11 = (bf16[1024,1280]{1,0:T(8,128)(2,1)}, bf16[512,1280]{1,0:T(8,128)(2,1)S(1)}) conditional(s32[]{:T(128)} %convert_element_type.97, () %tuple.116, (bf16[512,512]{1,0:T(8,128)(2,1)S(1)}, bf16[512,2048]{1,0:T(8,128)(2,1)S(1)}, bf16[512,2048]{1,0:T(8,128)(2,1)S(1)}, bf16[512,768]{1,0:T(8,128)(2,1)}) %tuple.197), branch_computations={%region_15.16_spmd, %region_16.17_spmd} | conditional | flops 2 | bytes 10485818 | solution.py:446
  358.8 5.0 collective-permute-done.7.refs_0_
  366.5 6.3 %up_outer.5 = bf16[512,2048]{1,0:T(8,128)(2,1)} custom-call(bf16[512,2048]{1,0:T(8,128)(2,1)} %copy-done.17, bf16[512,2048]{1,0:T(8,128)(2,1)} %get-tuple-element.196.b_ref, bf16[1024,2048]{1,0:T(8,128)(2,1)} %get-tuple-element.215.refs_0_, bf16[512,2048]{1,0:T(8,128)(2,1)} %collective-permute-done.26.refs_1_), custom_call_target="tpu_custom_call" | custom-call | flops 1 | bytes 1 | tf_op jit(solution)/shard_map/up_outer/pallas_call | solution.py:347
  372.8 10.4 %all-reduce.10.cloned.1.call-done = bf16[512,2048]{1,0:T(8,128)(2,1)} async-done(((bf16[512,2048]{1,0:T(8,128)(2,1)}), bf16[512,2048]{1,0:T(8,128)(2,1)}) %all-reduce.10.cloned.1.call-update) | async-done | bytes 2097168 | tf_op jit(solution)/shard_map/psum | solution.py:498
  389.7 7.7 %collective-permute-done.31 = bf16[512,2048]{1,0:T(8,128)(2,1)} collective-permute-done((bf16[512,2048]{1,0:T(8,128)(2,1)}, bf16[512,2048]{1,0:T(8,128)(2,1)}, u32[]{:S(2)}, u32[]{:S(2)}) %collective-permute-start.31) | collective-permute-done | bytes 2097184 | tf_op jit(solution)/shard_map/ppermute | solution.py:462
  397.4 46.2 %conditional.12 = (f32[512,2048]{1,0:T(8,128)S(1)}, f32[512,2048]{1,0:T(8,128)S(1)}, f32[2048,512]{1,0:T(8,128)S(1)}) conditional(s32[]{:T(128)} %convert_element_type.97, () %tuple.122, (bf16[512,2048]{1,0:T(8,128)(2,1)S(1)}, bf16[512,2048]{1,0:T(8,128)(2,1)}, bf16[512,2048]{1,0:T(8,128)(2,1)}, bf16[2048,512]{1,0:T(8,128)(2,1)}, ...), branch_computations={%region_21.22_spmd, %region_22.23_spmd} | conditional | flops 9437184 | bytes 33554496 | solution.py:446
  404.8 37.9 %collective-permute-done.11 = bf16[512,2048]{1,0:T(8,128)(2,1)S(1)} collective-permute-done((bf16[512,2048]{1,0:T(8,128)(2,1)S(1)}, bf16[512,2048]{1,0:T(8,128)(2,1)S(1)}, u32[]{:S(2)}, u32[]{:S(2)}) %collective-permute-start.11) | collective-permute-done | bytes 2097184 | tf_op jit(solution)/shard_map/cond/branch_1_fun/ppermute | solution.py:462
  448.2 38.0 %conditional.13 = (f32[512,1280]{1,0:T(8,128)}, f32[512,128]{1,0:T(8,128)}, f32[512,512]{1,0:T(8,128)}, f32[512,512]{1,0:T(8,128)}, f32[512,128]{1,0:T(8,128)}) conditional(s32[]{:T(128)} %convert_element_type.97, () %tuple.121, (bf16[512,512]{1,0:T(8,128)(2,1)}, bf16[512,2048]{1,0:T(8,128)(2,1)}, bf16[512,2048]{1,0:T(8,128)(2,1)}, ...), branch_computations={%region_23.24_spmd, %region_24.25_spmd} | conditional | flops 1966081 | bytes 15728721 | solution.py:446
  453.2 26.2 %collective-permute-done.12 = bf16[512,1280]{1,0:T(8,128)(2,1)S(1)} collective-permute-done((bf16[512,1280]{1,0:T(8,128)(2,1)S(1)}, bf16[512,1280]{1,0:T(8,128)(2,1)S(1)}, u32[]{:S(2)}, u32[]{:S(2)}) %collective-permute-start.12) | collective-permute-done | bytes 1310752 | tf_op jit(solution)/shard_map/cond/branch_1_fun/ppermute | solution.py:462
  (302 shorter events, 147.6 us)
Async XLA Ops:
  7.2 157.5 %all-reduce.6.cloned.1.call-start = ((), (), s32[]{:S(2)}) async-start(), calls=%async_computation | async-start | bytes 4194304 | tf_op jit(solution)/shard_map/psum | solution.py:498
  9.9 7.5 %collective-permute-start.13 = (bf16[544,768]{1,0:T(8,128)(2,1)S(1)}, bf16[544,768]{1,0:T(8,128)(2,1)S(1)}, u32[]{:S(2)}, u32[]{:S(2)}) collective-permute-start(bf16[544,768]{1,0:T(8,128)(2,1)S(1)} %pad_maximum_fusion.7.p0), channel_id=1, source_target_pairs={{0,8},{8,0},{16,24},{24,16},{1,9},{9,1},{17,25},{25,17},{2,10},{10... | collective-permute-start | bytes 2506760 | tf_op jit(solution)/shard_map/ppermute | solution.py:450
  10.4 22.0 %collective-permute-start.14 = (bf16[544,768]{1,0:T(8,128)(2,1)S(1)}, bf16[544,768]{1,0:T(8,128)(2,1)S(1)}, u32[]{:S(2)}, u32[]{:S(2)}) collective-permute-start(bf16[544,768]{1,0:T(8,128)(2,1)S(1)} %pad_maximum_fusion.7.p0), channel_id=1, source_target_pairs={{0,16},{8,24},{16,0},{24,8},{1,17},{9,25},{17,1},{25,9},{2,18},{10... | collective-permute-start | bytes 2506760 | tf_op jit(solution)/shard_map/ppermute | solution.py:454
  17.3 26.1 %collective-permute-start.17 = (bf16[512,512]{1,0:T(8,128)(2,1)}, bf16[512,512]{1,0:T(8,128)(2,1)}, u32[]{:S(2)}, u32[]{:S(2)}) collective-permute-start(bf16[512,512]{1,0:T(8,128)(2,1)} %o0.3), channel_id=1, source_target_pairs={{0,16},{8,24},{16,0},{24,8},{1,17},{9,25},{17,1},{25,9},{2,18},{10... | collective-permute-start | bytes 1572872 | tf_op jit(solution)/shard_map/ppermute | solution.py:454
  17.4 33.5 %collective-permute-start.18 = (bf16[512,512]{1,0:T(8,128)(2,1)}, bf16[512,512]{1,0:T(8,128)(2,1)}, u32[]{:S(2)}, u32[]{:S(2)}) collective-permute-start(bf16[512,512]{1,0:T(8,128)(2,1)} %o0.3), channel_id=1, source_target_pairs={{0,8},{8,0},{16,24},{24,16},{1,9},{9,1},{17,25},{25,17},{2,10},{10... | collective-permute-start | bytes 1572872 | tf_op jit(solution)/shard_map/ppermute | solution.py:450
  43.5 15.8 %collective-permute-start.19 = (bf16[512,512]{1,0:T(8,128)(2,1)}, bf16[512,512]{1,0:T(8,128)(2,1)}, u32[]{:S(2)}, u32[]{:S(2)}) collective-permute-start(bf16[512,512]{1,0:T(8,128)(2,1)} %collective-permute-done.17.o1), channel_id=1, source_target_pairs={{0,8},{8,0},{16,24},{24,16},{1,9},{9,1},{17,25},{25,17},{2,10},{10... | collective-permute-start | bytes 1572872 | tf_op jit(solution)/shard_map/ppermute | solution.py:450
  45.3 9.1 %collective-permute-start.16 = (bf16[512,256]{0,1:T(8,128)(2,1)}, bf16[512,256]{0,1:T(8,128)(2,1)}, u32[]{:S(2)}, u32[]{:S(2)}) collective-permute-start(bf16[512,256]{0,1:T(8,128)(2,1)} %copy.40), channel_id=1, source_target_pairs={{0,4},{4,0},{1,5},{5,1},{2,6},{6,2},{3,7},{7,3},{8,12},{12,8},{9,1... | collective-permute-start | bytes 786440 | tf_op jit(solution)/shard_map/ppermute | solution.py:462
  50.9 48.8 %collective-permute-start.20 = (bf16[512,2048]{1,0:T(8,128)(2,1)}, bf16[512,2048]{1,0:T(8,128)(2,1)}, u32[]{:S(2)}, u32[]{:S(2)}) collective-permute-start(bf16[512,2048]{1,0:T(8,128)(2,1)} %pad_maximum_fusion.3), channel_id=1, source_target_pairs={{0,16},{8,24},{16,0},{24,8},{1,17},{9,25},{17,1},{25,9},{2,18},{10... | collective-permute-start | bytes 6291464 | tf_op jit(solution)/shard_map/ppermute | solution.py:454
  74.3 76.8 %collective-permute-start.21 = (bf16[2048,512]{1,0:T(8,128)(2,1)}, bf16[2048,512]{1,0:T(8,128)(2,1)}, u32[]{:S(2)}, u32[]{:S(2)}) collective-permute-start(bf16[2048,512]{1,0:T(8,128)(2,1)} %refs_8_.1), channel_id=1, source_target_pairs={{0,16},{8,24},{16,0},{24,8},{1,17},{9,25},{17,1},{25,9},{2,18},{10... | collective-permute-start | bytes 6291464 | tf_op jit(solution)/shard_map/ppermute | solution.py:454
  76.0 214.4 %all-reduce.8.cloned.1.call-start = ((), (), s32[]{:S(2)}) async-start(), calls=%async_computation.1 | async-start | bytes 4194304 | tf_op jit(solution)/shard_map/psum | solution.py:498
  99.7 46.6 %collective-permute-start.8 = (bf16[512,2048]{1,0:T(8,128)(2,1)}, bf16[512,2048]{1,0:T(8,128)(2,1)}, u32[]{:S(2)}, u32[]{:S(2)}) collective-permute-start(bf16[512,2048]{1,0:T(8,128)(2,1)} %get-tuple-element.69), channel_id=1, source_target_pairs={{0,4},{4,0},{1,5},{5,1},{2,6},{6,2},{3,7},{7,3},{8,12},{12,8},{9,1... | collective-permute-start | bytes 6291464 | tf_op jit(solution)/shard_map/cond/branch_1_fun/ppermute | solution.py:462
  100.0 51.1 %collective-permute-start.10 = (bf16[512,2048]{1,0:T(8,128)(2,1)}, bf16[512,2048]{1,0:T(8,128)(2,1)}, u32[]{:S(2)}, u32[]{:S(2)}) collective-permute-start(bf16[512,2048]{1,0:T(8,128)(2,1)} %get-tuple-element.71), channel_id=1, source_target_pairs={{0,8},{8,0},{16,24},{24,16},{1,9},{9,1},{17,25},{25,17},{2,10},{10... | collective-permute-start | bytes 6291464 | tf_op jit(solution)/shard_map/cond/branch_1_fun/ppermute | solution.py:450
  100.0 51.1 %collective-permute-start.9 = (bf16[512,2048]{1,0:T(8,128)(2,1)}, bf16[512,2048]{1,0:T(8,128)(2,1)}, u32[]{:S(2)}, u32[]{:S(2)}) collective-permute-start(bf16[512,2048]{1,0:T(8,128)(2,1)} %get-tuple-element.70), channel_id=1, source_target_pairs={{0,8},{8,0},{16,24},{24,16},{1,9},{9,1},{17,25},{25,17},{2,10},{10... | collective-permute-start | bytes 6291464 | tf_op jit(solution)/shard_map/cond/branch_1_fun/ppermute | solution.py:450
  151.2 7.5 %collective-permute-start.1 = (bf16[512,2048]{1,0:T(8,128)(2,1)}, bf16[512,2048]{1,0:T(8,128)(2,1)}, u32[]{:S(2)}, u32[]{:S(2)}) collective-permute-start(bf16[512,2048]{1,0:T(8,128)(2,1)} %get-tuple-element.73), channel_id=1, source_target_pairs={{0,8},{8,0},{16,24},{24,16},{1,9},{9,1},{17,25},{25,17},{2,10},{10... | collective-permute-start | bytes 6291464 | tf_op jit(solution)/shard_map/cond/branch_1_fun/ppermute | solution.py:450
  151.7 10.0 %collective-permute-start.2 = (bf16[2048,512]{1,0:T(8,128)(2,1)}, bf16[2048,512]{1,0:T(8,128)(2,1)}, u32[]{:S(2)}, u32[]{:S(2)}) collective-permute-start(bf16[2048,512]{1,0:T(8,128)(2,1)} %get-tuple-element.74), channel_id=1, source_target_pairs={{0,8},{8,0},{16,24},{24,16},{1,9},{9,1},{17,25},{25,17},{2,10},{10... | collective-permute-start | bytes 6291464 | tf_op jit(solution)/shard_map/cond/branch_1_fun/ppermute | solution.py:450
  151.8 12.9 %collective-permute-start.3 = (bf16[2048,512]{1,0:T(8,128)(2,1)}, bf16[2048,512]{1,0:T(8,128)(2,1)}, u32[]{:S(2)}, u32[]{:S(2)}) collective-permute-start(bf16[2048,512]{1,0:T(8,128)(2,1)} %get-tuple-element.75), channel_id=1, source_target_pairs={{0,8},{8,0},{16,24},{24,16},{1,9},{9,1},{17,25},{25,17},{2,10},{10... | collective-permute-start | bytes 6291464 | tf_op jit(solution)/shard_map/cond/branch_1_fun/ppermute | solution.py:450
  203.5 179.7 %all-reduce.10.cloned.1.call-start = ((), (), s32[]{:S(2)}) async-start(), calls=%async_computation.2 | async-start | bytes 4194304 | tf_op jit(solution)/shard_map/psum | solution.py:498
  208.6 7.4 %collective-permute-start.4 = (bf16[2048,1024]{1,0:T(8,128)(2,1)S(1)}, bf16[2048,1024]{1,0:T(8,128)(2,1)}, u32[]{:S(2)}, u32[]{:S(2)}) collective-permute-start(bf16[2048,1024]{1,0:T(8,128)(2,1)S(1)} %down_outer.3), channel_id=1, source_target_pairs={{0,8},{8,0},{16,24},{24,16},{1,9},{9,1},{17,25},{25,17},{2,10},{10... | collective-permute-start | bytes 12582920 | tf_op jit(solution)/shard_map/cond/branch_1_fun/ppermute | solution.py:450
  220.7 69.7 %collective-permute-start.22 = (bf16[2048,512]{1,0:T(8,128)(2,1)}, bf16[2048,512]{1,0:T(8,128)(2,1)}, u32[]{:S(2)}, u32[]{:S(2)}) collective-permute-start(bf16[2048,512]{1,0:T(8,128)(2,1)} %get-tuple-element.198), channel_id=1, source_target_pairs={{0,16},{8,24},{16,0},{24,8},{1,17},{9,25},{17,1},{25,9},{2,18},{10... | collective-permute-start | bytes 6291464 | tf_op jit(solution)/shard_map/ppermute | solution.py:454
  226.8 15.0 %collective-permute-start.5 = (bf16[1024,2048]{1,0:T(8,128)(2,1)S(1)}, bf16[1024,2048]{1,0:T(8,128)(2,1)}, u32[]{:S(2)}, u32[]{:S(2)}) collective-permute-start(bf16[1024,2048]{1,0:T(8,128)(2,1)S(1)} %gate_outer.3), channel_id=1, source_target_pairs={{0,8},{8,0},{16,24},{24,16},{1,9},{9,1},{17,25},{25,17},{2,10},{10... | collective-permute-start | bytes 12582920 | tf_op jit(solution)/shard_map/cond/branch_1_fun/ppermute | solution.py:450
  229.6 16.4 %collective-permute-start.6 = (bf16[1024,2048]{1,0:T(8,128)(2,1)S(1)}, bf16[1024,2048]{1,0:T(8,128)(2,1)}, u32[]{:S(2)}, u32[]{:S(2)}) collective-permute-start(bf16[1024,2048]{1,0:T(8,128)(2,1)S(1)} %up_outer.3), channel_id=1, source_target_pairs={{0,8},{8,0},{16,24},{24,16},{1,9},{9,1},{17,25},{25,17},{2,10},{10... | collective-permute-start | bytes 12582920 | tf_op jit(solution)/shard_map/cond/branch_1_fun/ppermute | solution.py:450
  250.2 79.8 %collective-permute-start.25 = (bf16[512,2048]{1,0:T(8,128)(2,1)}, bf16[512,2048]{1,0:T(8,128)(2,1)}, u32[]{:S(2)}, u32[]{:S(2)}) collective-permute-start(bf16[512,2048]{1,0:T(8,128)(2,1)} %get-tuple-element.202), channel_id=1, source_target_pairs={{0,16},{8,24},{16,0},{24,8},{1,17},{9,25},{17,1},{25,9},{2,18},{10... | collective-permute-start | bytes 6291464 | tf_op jit(solution)/shard_map/ppermute | solution.py:454
  290.4 76.0 %collective-permute-start.26 = (bf16[512,2048]{1,0:T(8,128)(2,1)}, bf16[512,2048]{1,0:T(8,128)(2,1)}, u32[]{:S(2)}, u32[]{:S(2)}) collective-permute-start(bf16[512,2048]{1,0:T(8,128)(2,1)} %get-tuple-element.216), channel_id=1, source_target_pairs={{0,16},{8,24},{16,0},{24,8},{1,17},{9,25},{17,1},{25,9},{2,18},{10... | collective-permute-start | bytes 6291464 | tf_op jit(solution)/shard_map/ppermute | solution.py:454
  297.9 74.9 %collective-permute-start.24 = (bf16[2048,512]{1,0:T(8,128)(2,1)}, bf16[2048,512]{1,0:T(8,128)(2,1)}, u32[]{:S(2)}, u32[]{:S(2)}) collective-permute-start(bf16[2048,512]{1,0:T(8,128)(2,1)} %down_outer.5), channel_id=1, source_target_pairs={{0,4},{4,0},{1,5},{5,1},{2,6},{6,2},{3,7},{7,3},{8,12},{12,8},{9,1... | collective-permute-start | bytes 6291464 | tf_op jit(solution)/shard_map/ppermute | solution.py:462
  299.4 186.8 %all-reduce.12.cloned.1.call-start = ((), (), s32[]{:S(2)}) async-start(), calls=%async_computation.3 | async-start | bytes 4194304 | tf_op jit(solution)/shard_map/psum | solution.py:498
  329.5 21.3 %collective-permute-start.23 = (bf16[512,256]{1,0:T(8,128)(2,1)S(1)}, bf16[512,256]{1,0:T(8,128)(2,1)S(1)}, u32[]{:S(2)}, u32[]{:S(2)}) collective-permute-start(bf16[512,256]{1,0:T(8,128)(2,1)S(1)} %slice.215), channel_id=1, source_target_pairs={{0,4},{4,0},{1,5},{5,1},{2,6},{6,2},{3,7},{7,3},{8,12},{12,8},{9,1... | collective-permute-start | bytes 786440 | tf_op jit(solution)/shard_map/ppermute | solution.py:462
  350.8 46.6 %collective-permute-start.31 = (bf16[512,2048]{1,0:T(8,128)(2,1)}, bf16[512,2048]{1,0:T(8,128)(2,1)}, u32[]{:S(2)}, u32[]{:S(2)}) collective-permute-start(bf16[512,2048]{1,0:T(8,128)(2,1)} %gate_outer.5), channel_id=1, source_target_pairs={{0,4},{4,0},{1,5},{5,1},{2,6},{6,2},{3,7},{7,3},{8,12},{12,8},{9,1... | collective-permute-start | bytes 6291464 | tf_op jit(solution)/shard_map/ppermute | solution.py:462
  358.7 5.1 %collective-permute-start.7 = (bf16[1024,1280]{1,0:T(8,128)(2,1)S(1)}, bf16[1024,1280]{1,0:T(8,128)(2,1)}, u32[]{:S(2)}, u32[]{:S(2)}) collective-permute-start(bf16[1024,1280]{1,0:T(8,128)(2,1)S(1)} %entry_outer.3), channel_id=1, source_target_pairs={{0,8},{8,0},{16,24},{24,16},{1,9},{9,1},{17,25},{25,17},{2,10},{10... | collective-permute-start | bytes 7864328 | tf_op jit(solution)/shard_map/cond/branch_1_fun/ppermute | solution.py:450
  383.2 60.4 %collective-permute-start.32 = (bf16[512,1280]{1,0:T(8,128)(2,1)}, bf16[512,1280]{1,0:T(8,128)(2,1)}, u32[]{:S(2)}, u32[]{:S(2)}) collective-permute-start(bf16[512,1280]{1,0:T(8,128)(2,1)} %copy-done.62), channel_id=1, source_target_pairs={{0,16},{8,24},{16,0},{24,8},{1,17},{9,25},{17,1},{25,9},{2,18},{10... | collective-permute-start | bytes 3932168 | tf_op jit(solution)/shard_map/ppermute | solution.py:454
  397.4 45.4 %collective-permute-start.11 = (bf16[512,2048]{1,0:T(8,128)(2,1)S(1)}, bf16[512,2048]{1,0:T(8,128)(2,1)S(1)}, u32[]{:S(2)}, u32[]{:S(2)}) collective-permute-start(bf16[512,2048]{1,0:T(8,128)(2,1)S(1)} %get-tuple-element.90), channel_id=1, source_target_pairs={{0,4},{4,0},{1,5},{5,1},{2,6},{6,2},{3,7},{7,3},{8,12},{12,8},{9,1... | collective-permute-start | bytes 6291464 | tf_op jit(solution)/shard_map/cond/branch_1_fun/ppermute | solution.py:462
  451.6 27.8 %collective-permute-start.12 = (bf16[512,1280]{1,0:T(8,128)(2,1)S(1)}, bf16[512,1280]{1,0:T(8,128)(2,1)S(1)}, u32[]{:S(2)}, u32[]{:S(2)}) collective-permute-start(bf16[512,1280]{1,0:T(8,128)(2,1)S(1)} %entry_outer.5), channel_id=1, source_target_pairs={{0,4},{4,0},{1,5},{5,1},{2,6},{6,2},{3,7},{7,3},{8,12},{12,8},{9,1... | collective-permute-start | bytes 3932168 | tf_op jit(solution)/shard_map/cond/branch_1_fun/ppermute | solution.py:462
  489.3 5.2 %collective-permute-start.27 = (f32[2,512]{1,0:T(2,128)S(1)}, f32[2,512]{1,0:T(2,128)S(1)}, u32[]{:S(2)}, u32[]{:S(2)}) collective-permute-start(f32[2,512]{1,0:T(2,128)S(1)} %get-tuple-element.282), channel_id=1, source_target_pairs={{0,16},{8,24},{16,0},{24,8},{1,17},{9,25},{17,1},{25,9},{2,18},{10... | collective-permute-start | bytes 12296 | tf_op jit(solution)/shard_map/ppermute | solution.py:454
  (89 other events, 882.7 us)
Sparse Core Ops, SparseCore 0:
  76.1 86.8 all-reduce.5
  203.6 86.7 all-reduce.7
  299.5 83.6 all-reduce.9
  385.5 85.4 all-reduce.11

commit v3 on v2

--- a/solution.py
+++ b/solution.py
@@ -33,8 +33,8 @@
     own = (code >= query_codes[1:2, :]) & (code <= query_codes[2:3, :])
     bias[...] = jnp.where(below | own, 0.0, NEGATIVE)
 
-def fill_padded(padded, source, lane0):
-    block = source[:, lane0 : lane0 + 2 * HD]
+def fill_padded(padded, sources, lane0):
+    block = jnp.concatenate([v[:, lane0 : lane0 + 2 * HD] for v in sources], axis=0)
     lane = lax.broadcasted_iota(jnp.int32, block.shape, 1)
     low = jnp.where(lane < HD, block, jnp.zeros_like(block))
     high = jnp.where(lane < HD, jnp.zeros_like(block), block)
@@ -43,11 +43,21 @@
     padded[1, 0] = pltpu.roll(high.astype(F32), HD, 1).astype(BF)
     padded[1, 1] = high
 
-def forward_kernel(chunk, q_ref, kv_ref, vt_ref, code_ref, codes_ref, o0, o1, o2, o3, out_ref, lse_ref, branch_ref, bias, keys):
-    total = kv_ref.shape[0]
+def fill_turned(turned, sources, lane0):
+    at = 0
+    for v in sources:
+        turned[:, at : at + v.shape[0]] = v[:, lane0 : lane0 + 2 * HD].astype(F32).T.astype(BF)
+        at += v.shape[0]
+
+
+def forward_kernel(chunk, parts, q_ref, code_ref, codes_ref, *refs):
+    kv_refs = refs[:parts]
+    out_ref, lse_ref, bias, keys, vt_ref = refs[parts:]
+    total = code_ref.shape[0]
     rows = q_ref.shape[0]
+    fill_turned(vt_ref, kv_refs, 2 * HD)
     fill_bias(bias, code_ref, codes_ref)
-    fill_padded(keys, kv_ref, 0)
+    fill_padded(keys, kv_refs, 0)
 
     def pair_step(pair, unused):
         group = pair // 2
@@ -79,37 +89,41 @@
         return unused
 
     lax.fori_loop(0, q_ref.shape[1] // 128, pair_step, 0)
-    block = o0.shape[1]
-    for r, piece in enumerate((o0, o1, o2, o3)):
-        branch_ref[:, r * block : (r + 1) * block] = dot_nn(out_ref[...], piece[...]).astype(BF)
-
-
-def attend_forward(queries, key_value, values_t, key_code, query_codes, out_pieces):
+
+
+def attend_forward(queries, key_values, key_code, query_codes):
     rows, width = queries.shape
-    total = key_value.shape[0]
+    total = key_code.shape[0]
     chunk = min(total, 1024)
     return pl.pallas_call(
-        functools.partial(forward_kernel, chunk),
+        functools.partial(forward_kernel, chunk, len(key_values)),
         out_shape=(
             jax.ShapeDtypeStruct((rows, width), BF),
             jax.ShapeDtypeStruct((width // HD, rows), F32),
-            jax.ShapeDtypeStruct((rows, 4 * out_pieces[0].shape[1]), BF),
         ),
-        scratch_shapes=[pltpu.VMEM((total, rows), F32), pltpu.VMEM((2, 2, total, 128), BF)],
+        scratch_shapes=[
+            pltpu.VMEM((total, rows), F32),
+            pltpu.VMEM((2, 2, total, 128), BF),
+            pltpu.VMEM((128, total), BF),
+        ],
         compiler_params=pltpu.CompilerParams(vmem_limit_bytes=(32 if total <= 1024 else 58) << 20),
         cost_estimate=LIGHT,
         name="attend_forward",
-    )(queries, key_value, values_t, key_code, query_codes, *out_pieces)
-
-def backward_kernel(chunk, q_ref, kv_ref, kt_ref, code_ref, codes_ref, att_ref, branch_ref, lse_ref, rot_ref,
-                    o0, o1, o2, o3, dq_ref, dkv_ref, grad_ref, bias, keys, values, delta, dk_acc, dv_acc):
-    total = kv_ref.shape[0]
+    )(queries, key_code, query_codes, *key_values)
+
+def backward_kernel(
+    chunk, parts, q_ref, code_ref, codes_ref, att_ref, branch_ref, lse_ref, rot_ref, o0, o1, o2, o3, *refs
+):
+    kv_refs = refs[:parts]
+    dq_ref, dkv_ref, grad_ref, bias, keys, values, kt_ref, delta, dk_acc, dv_acc = refs[parts:]
+    total = code_ref.shape[0]
     rows = q_ref.shape[0]
     width = q_ref.shape[1]
     heads = width // HD
+    fill_turned(kt_ref, kv_refs, 0)
     fill_bias(bias, code_ref, codes_ref)
-    fill_padded(keys, kv_ref, 0)
-    fill_padded(values, kv_ref, 128)
+    fill_padded(keys, kv_refs, 0)
+    fill_padded(values, kv_refs, 128)
     block = o0.shape[1]
     grad = jnp.zeros((rows, width), F32)
     for r, piece in enumerate((o0, o1, o2, o3)):
@@ -163,18 +177,21 @@
         one = pltpu.roll(acc[1, 0], HD, 1) + acc[1, 1]
         dkv_ref[:, which * 128 : (which + 1) * 128] = jnp.where(lane < HD, zero, one)
 
-def attend_backward(queries, key_value, keys_t, key_code, query_codes, attended, grad_branch, lse, turn, out_pieces):
+def attend_backward(
+    queries, key_values, key_code, query_codes, attended, grad_branch, lse, turn, out_pieces
+):
     rows, width = queries.shape
-    total = key_value.shape[0]
+    total = key_code.shape[0]
     chunk = min(total, 1024)
     return pl.pallas_call(
-        functools.partial(backward_kernel, chunk),
+        functools.partial(backward_kernel, chunk, len(key_values)),
         out_shape=(jax.ShapeDtypeStruct((rows, width), BF), jax.ShapeDtypeStruct((total, 256), F32)),
         scratch_shapes=[
             pltpu.VMEM((rows, width), BF),
             pltpu.VMEM((total, rows), F32),
             pltpu.VMEM((2, 2, total, 128), BF),
             pltpu.VMEM((2, 2, total, 128), BF),
+            pltpu.VMEM((128, total), BF),
             pltpu.VMEM((width // HD, rows), F32),
             pltpu.VMEM((2, 2, total, 128), F32),
             pltpu.VMEM((2, 2, total, 128), F32),
@@ -182,7 +199,23 @@
         compiler_params=pltpu.CompilerParams(vmem_limit_bytes=(32 if total <= 1024 else 58) << 20),
         cost_estimate=LIGHT,
         name="attend_backward",
-    )(queries, key_value, keys_t, key_code, query_codes, attended, grad_branch, lse, turn, *out_pieces)
+    )(queries, key_code, query_codes, attended, grad_branch, lse, turn, *out_pieces, *key_values)
+
+
+def out_kernel(attended_ref, o0, o1, o2, o3, branch_ref):
+    block = o0.shape[1]
+    for r, piece in enumerate((o0, o1, o2, o3)):
+        branch_ref[:, r * block : (r + 1) * block] = dot_nn(attended_ref[...], piece[...]).astype(BF)
+
+
+def out_project(attended, out_pieces):
+    return pl.pallas_call(
+        out_kernel,
+        out_shape=jax.ShapeDtypeStruct((attended.shape[0], 4 * out_pieces[0].shape[1]), BF),
+        compiler_params=pltpu.CompilerParams(vmem_limit_bytes=16 << 20),
+        cost_estimate=LIGHT,
+        name="out_project",
+    )(attended, *out_pieces)
 
 
 def rows_at(index, size):
@@ -194,55 +227,83 @@
     return jnp.where(lane % HD < HD // 2, pltpu.roll(block, 128 - HD // 2, 1), pltpu.roll(block, HD // 2, 1))
 
 
-def project_kernel(width_q, x_ref, cos_ref, sin_ref, p0, p1, p2, p3, normed_ref, q_ref, kv_ref):
+def project_kv_kernel(x_ref, scale_ref, cos_ref, sin_ref, p0, p1, p2, p3, normed_ref, kv_ref):
     block = x_ref.shape[1] // 4
-    width = p0.shape[1]
-    total = jnp.zeros((x_ref.shape[0], width), F32)
+    total = jnp.zeros(kv_ref.shape, F32)
     for r, piece in enumerate((p0, p1, p2, p3)):
         lanes = slice(r * block, (r + 1) * block)
-        gain = piece[block : block + 1, :block].astype(F32)
-        low = (x_ref[:, lanes] * gain).astype(BF)
+        rows = block // piece.shape[1]
+        gain = jnp.concatenate([piece[block + i : block + i + 1, :] for i in range(rows)], axis=1)
+        low = (x_ref[:, lanes].astype(F32) * scale_ref[...] * gain.astype(F32)).astype(BF)
         normed_ref[:, lanes] = low
         total += dot_nn(low, piece[:block, :])
-    cosine, sine = cos_ref[...], sin_ref[...]
-    turned_width = width_q + (width - width_q) // 2
-    for at in range(0, width, 128):
-        part = total[:, at : at + 128]
-        if at < turned_width:
-            part = part * cosine + half_turn(part) * sine
-        low = part.astype(BF)
-        if at < width_q:
-            q_ref[:, at : at + 128] = low * jnp.asarray(ATTN_SCALE, BF)
-        else:
-            kv_ref[:, at - width_q : at - width_q + 128] = low
-
-
-def project(scaled, cos_table, sin_table, pieces, width_q):
-    rows, model = scaled.shape
-    width = pieces[0].shape[1]
+    keys = total[:, :128]
+    kv_ref[:, :128] = (keys * cos_ref[...] + half_turn(keys) * sin_ref[...]).astype(BF)
+    kv_ref[:, 128:] = total[:, 128:].astype(BF)
+
+
+def project_kv(tokens, scale, cos_table, sin_table, pieces):
+    rows, model = tokens.shape
     return pl.pallas_call(
-        functools.partial(project_kernel, width_q),
+        project_kv_kernel,
         out_shape=(
             jax.ShapeDtypeStruct((rows, model), BF),
-            jax.ShapeDtypeStruct((rows, width_q), BF),
-            jax.ShapeDtypeStruct((rows, width - width_q), BF),
+            jax.ShapeDtypeStruct((rows, pieces[0].shape[1]), BF),
         ),
         compiler_params=pltpu.CompilerParams(vmem_limit_bytes=24 << 20),
         cost_estimate=LIGHT,
-        name="project",
-    )(scaled, cos_table, sin_table, *pieces)
-
-
-def mlp_kernel(h_ref, g_ref, *refs):
-    gates, ups, downs = refs[:4], refs[4:8], refs[8:12]
-    hidden_ref, dgate_ref, dup_ref, dh_ref, acc = refs[12:]
+        name="project_kv",
+    )(tokens, scale, cos_table, sin_table, *pieces)
+
+
+def project_q_kernel(normed_ref, cos_ref, sin_ref, p0, p1, p2, p3, q_ref):
+    block = p0.shape[0]
+    total = jnp.zeros(q_ref.shape, F32)
+    for r, piece in enumerate((p0, p1, p2, p3)):
+        total += dot_nn(normed_ref[:, r * block : (r + 1) * block], piece[...])
+    for at in range(0, q_ref.shape[1], 128):
+        part = total[:, at : at + 128]
+        part = part * cos_ref[...] + half_turn(part) * sin_ref[...]
+        q_ref[:, at : at + 128] = part.astype(BF) * jnp.asarray(ATTN_SCALE, BF)
+
+
+def project_q(normed, cos_table, sin_table, pieces):
+    return pl.pallas_call(
+        project_q_kernel,
+        out_shape=jax.ShapeDtypeStruct((normed.shape[0], pieces[0].shape[1]), BF),
+        compiler_params=pltpu.CompilerParams(vmem_limit_bytes=24 << 20),
+        cost_estimate=LIGHT,
+        name="project_q",
+    )(normed, cos_table, sin_table, *pieces)
+
+
+def mlp_kernel(halves, index_ref, h_ref, g_ref, *refs):
+    count = 6 if halves else 4
+    given, downs = (refs[:count], refs[count : 2 * count]), refs[2 * count : 2 * count + 4]
+    hidden_ref, dgate_ref, dup_ref, dh_ref, acc, joined = refs[2 * count + 4 :]
     step = pl.program_id(0)
     block = h_ref.shape[1] // 4
+    sides = []
+    for which, pieces in enumerate(given):
+        if halves:
+            half = block // 2
+            first = pl.multiple_of(index_ref[0] * half, half)
+            second = pl.multiple_of((1 - index_ref[0]) * half, half)
+            for far in range(2):
+                joined[which, far, pl.ds(first, half), :] = pieces[3 * far + 1][...]
+                joined[which, far, pl.ds(second, half), :] = pieces[3 * far + 2][...]
+            pieces = (pieces[0], joined.at[which, 0], pieces[3], joined.at[which, 1])
+        sides.append(pieces)
+    gates, ups = sides
     gate = up = dhid = None
     for r in range(4):
         lanes = slice(r * block, (r + 1) * block)
         h = h_ref[:, lanes]
-        terms = (dot_nn(h, gates[r][...]), dot_nn(h, ups[r][...]), dot_nt(g_ref[:, lanes], downs[r][...]))
+        terms = (
+            dot_nn(h, gates[r][...]),
+            dot_nn(h, ups[r][...]),
+            dot_nt(g_ref[:, lanes], downs[r][...]),
+        )
         gate, up, dhid = terms if r == 0 else (gate + terms[0], up + terms[1], dhid + terms[2])
     sigma = jax.nn.sigmoid(gate)
     active = gate * sigma
@@ -268,29 +329,36 @@
         dh_ref[...] = acc[...].astype(BF)
 
 
-def mlp(normed, grad, gates, ups, downs):
+def mlp(normed, grad, index, gates, ups, downs):
     rows, model = normed.shape
-    block, hidden = gates[0].shape
+    hidden = downs[0].shape[0]
     tile = 512
-    whole = pl.BlockSpec((rows, model), lambda j: (0, 0))
-    wide = pl.BlockSpec((block, tile), lambda j: (0, j))
-    tall = pl.BlockSpec((tile, block), lambda j: (j, 0))
-    out = pl.BlockSpec((rows, tile), lambda j: (0, j))
+    whole = pl.BlockSpec((rows, model), lambda j, s: (0, 0))
+    wide = [pl.BlockSpec((size, tile), lambda j, s, at=at: (at, j)) for unused, size, at in gates + ups]
+    tall = pl.BlockSpec((tile, downs[0].shape[1]), lambda j, s: (j, 0))
+    out = pl.BlockSpec((rows, tile), lambda j, s: (0, j))
     return pl.pallas_call(
-        mlp_kernel,
-        grid=(hidden // tile,),
-        in_specs=[whole] * 2 + [wide] * 8 + [tall] * 4,
-        out_specs=[out] * 3 + [whole],
+        functools.partial(mlp_kernel, len(gates) > 4),
+        grid_spec=pltpu.PrefetchScalarGridSpec(
+            num_scalar_prefetch=1,
+            grid=(hidden // tile,),
+            in_specs=[whole] * 2 + wide + [tall] * 4,
+            out_specs=[out] * 3 + [whole],
+            scratch_shapes=[
+                pltpu.VMEM((rows, model), F32),
+                pltpu.VMEM((2, 2, model // 4, tile), BF),
+            ],
+        ),
         out_shape=[jax.ShapeDtypeStruct((rows, hidden), BF)] * 3
         + [jax.ShapeDtypeStruct((rows, model), BF)],
-        scratch_shapes=[pltpu.VMEM((rows, model), F32)],
-        compiler_params=pltpu.CompilerParams(vmem_limit_bytes=40 << 20),
+        compiler_params=pltpu.CompilerParams(vmem_limit_bytes=44 << 20),
         cost_estimate=LIGHT,
         name="mlp",
-    )(normed, grad, *gates, *ups, *downs)
-
-
-def entry_kernel(dq_ref, own_ref, got_ref, cos_ref, sin_ref, p0, p1, p2, p3, low_ref, dh_ref):
+    )(index, normed, grad, *[v[0] for v in gates + ups], *downs)
+
+
+def entry_kernel(dq_ref, own_ref, got_ref, cos_ref, sin_ref, *refs):
+    queries, keys, (low_ref, dh_ref) = refs[:4], refs[4:8], refs[8:]
     block = dh_ref.shape[1] // 4
     width_q = dq_ref.shape[1]
     low_ref[:, :width_q] = dq_ref[...]
@@ -298,25 +366,25 @@
     dk = sums[:, :128]
     low_ref[:, width_q : width_q + 128] = (dk * cos_ref[...] - half_turn(dk) * sin_ref[...]).astype(BF)
     low_ref[:, width_q + 128 :] = sums[:, 128:].astype(BF)
-    low = low_ref[...]
-    for r, piece in enumerate((p0, p1, p2, p3)):
-        dh_ref[:, r * block : (r + 1) * block] = dot_nt(low, piece[:block, :]).astype(BF)
-
-
-def entry_grad(dq_low, own, got, cos_table, sin_table, pieces):
+    low = low_ref[:, width_q:]
+    for r in range(4):
+        term = dot_nt(dq_ref[...], queries[r][...]) + dot_nt(low, keys[r][:block, :])
+        dh_ref[:, r * block : (r + 1) * block] = term.astype(BF)
+
+
+def entry_grad(dq_low, own, got, cos_table, sin_table, query_pieces, key_pieces):
     rows, width_q = dq_low.shape
-    block = pieces[0].shape[0] - 32
-    width = pieces[0].shape[1]
+    block = query_pieces[0].shape[0]
     return pl.pallas_call(
         entry_kernel,
         out_shape=(
-            jax.ShapeDtypeStruct((rows, width), BF),
+            jax.ShapeDtypeStruct((rows, width_q + key_pieces[0].shape[1]), BF),
             jax.ShapeDtypeStruct((rows, 4 * block), BF),
         ),
         compiler_params=pltpu.CompilerParams(vmem_limit_bytes=24 << 20),
         cost_estimate=LIGHT,
         name="entry_grad",
-    )(dq_low, own, got, cos_table, sin_table, *pieces)
+    )(dq_low, own, got, cos_table, sin_table, *query_pieces, *key_pieces)
 
 
 def outer_kernel(n_adds, a_ref, b_ref, *refs):
@@ -482,18 +550,6 @@
     return swap_x(after(jnp.concatenate(mine), wait))
 
 
-def far_wholes(got):
-    if not two_ctx():
-        return jnp.split(got, 2)
-    other = swap_ctx(got)
-    half = got.shape[0] // 2
-    first = lax.axis_index("ctx") == 0
-    return [
-        jnp.concatenate([jnp.where(first, a, b), jnp.where(first, b, a)])
-        for a, b in ((got[:half], other[:half]), (got[half:], other[half:]))
-    ]
-
-
 def psum_tensor(value):
     return lax.psum(value, "tensor")
 
@@ -619,21 +675,23 @@
     width_kv = key_weight.shape[1]
     block_d = query_weight.shape[0]
 
-    gains = jnp.pad(
-        jnp.stack([first_gain, second_gain]), ((0, 30), (0, width_q + 2 * width_kv - block_d))
-    )
-    qkv_shard = jnp.concatenate(
-        [jnp.concatenate([query_weight, key_weight, value_weight], axis=1), gains], axis=0
-    )
-    qkv_far = swap_x(qkv_shard)
-    qkv_near = swap_core(qkv_shard)
-    out_far = swap_x(after(output_weight, qkv_near))
-    out_near = swap_core(after(output_weight, qkv_near))
-    wide_got = far_halves(gate_weight, up_weight, out_near)
-
-    tokens, cotangent, block_order = (
-        after(v, qkv_near) for v in (tokens, cotangent, block_order)
-    )
+    query_far = swap_x(query_weight)
+    query_near = swap_core(query_weight)
+    gain_rows = jnp.stack([first_gain, second_gain]).reshape(-1, 2 * width_kv)
+    kv_shard = jnp.concatenate(
+        [
+            jnp.concatenate([after(key_weight, query_near), value_weight], axis=1),
+            jnp.pad(gain_rows, ((0, 32 - gain_rows.shape[0]), (0, 0))),
+        ],
+        axis=0,
+    )
+    kv_far = swap_x(kv_shard)
+    kv_near = swap_core(kv_shard)
+    out_far = swap_x(after(output_weight, kv_near))
+    out_near = swap_core(after(output_weight, kv_near))
+    wide_got = far_halves(gate_weight, up_weight, out_far)
+
+    tokens, block_order = (after(v, query_near) for v in (tokens, block_order))
     all_ids = jnp.arange(group_rows, dtype=jnp.int32)
     if two_ctx():
         all_ids = jnp.where(all_ids < local_rows, all_ids + offset, all_ids - offset)
@@ -660,80 +718,88 @@
     cos_table = jnp.concatenate([cosine] * 4, axis=1)
     sin_table = jnp.concatenate([-sine, sine] * 2, axis=1)
 
-    inputs = relative(tokens).astype(F32)
-    grad_out = relative(cotangent).astype(F32)
-    grad_mlp = (RESIDUAL * grad_out).astype(BF)
+    tokens = relative(tokens)
+    inputs = tokens.astype(F32)
     scale_one = norm_scale(inputs)
-    scaled = inputs * scale_one
-    qkv_pieces = [qkv_shard, qkv_far, qkv_near, swap_core(qkv_far)]
-    gain_one = jnp.concatenate([p[block_d, :block_d] for p in qkv_pieces]).astype(F32)
-    gain_two = jnp.concatenate([p[block_d + 1, :block_d] for p in qkv_pieces]).astype(F32)
-    normed, queries, key_value = project(scaled, cos_table, sin_table, qkv_pieces, width_q)
+    kv_pieces = [kv_shard, kv_far, kv_near, swap_core(kv_far)]
+    gain_at = block_d + block_d // (2 * width_kv)
+    gain_one, gain_two = (
+        jnp.concatenate([p[i : i + gain_at - block_d].reshape(-1) for p in kv_pieces]).astype(F32)
+        for i in (block_d, gain_at)
+    )
+    normed, key_value = project_kv(tokens, scale_one, cos_table, sin_table, kv_pieces)
+    if two_ctx():
+        key_values = (key_value, swap_ctx(key_value))
+    else:
+        key_values = (lax.all_gather(key_value, "ctx", axis=0, tiled=True),)
+    query_pieces = [query_weight, query_far, query_near, swap_core(query_far)]
+    queries = project_q(normed, cos_table, sin_table, query_pieces)
+    attended, log_total = attend_forward(queries, key_values, key_code, query_codes)
     out_far = after(out_far, queries)
     out_pieces = [output_weight, out_far, out_near, swap_core(out_far)]
-    if two_ctx():
-        key_value_all = jnp.concatenate([key_value, swap_ctx(key_value)], axis=0)
-    else:
-        key_value_all = lax.all_gather(key_value, "ctx", axis=0, tiled=True)
-    attended, log_total, branch = attend_forward(
-        queries, key_value_all, key_value_all[:, width_kv:].T, key_code, query_codes, out_pieces
-    )
+    branch = out_project(attended, out_pieces)
+    grad_out = relative(after(cotangent, log_total)).astype(F32)
+    grad_mlp = (RESIDUAL * grad_out).astype(BF)
     branch = psum_tensor(branch)
 
-    def spread_wide(got, gate, up):
-        return *far_wholes(got), swap_core(gate), swap_core(up)
+    def spread_wide(got, gate, up, down):
+        gate_near = swap_core(gate)
+        near = gate_near, swap_core(up), swap_core(after(got, gate_near)), swap_core(after(down, gate_near))
+        return swap_ctx(got) if two_ctx() else got, *near
 
     def spread_last(*values):
         return tuple(swap_core(v) for v in values)
 
     down_far = swap_x(after(down_weight, log_total))
-    gate_far, up_far, gate_near, up_near = sealed(
-        spread_wide, after(wide_got, log_total), gate_weight, up_weight
-    )
-    gate_last, up_last, down_near, down_last = sealed(
-        spread_last, gate_far, up_far, down_weight, down_far
-    )
-    gates = [gate_weight, gate_far, gate_near, gate_last]
-    ups = [up_weight, up_far, up_near, up_last]
+    wide_other, gate_near, up_near, last_got, down_near = sealed(
+        spread_wide, after(wide_got, log_total), gate_weight, up_weight, down_weight
+    )
+    last_other, down_last = sealed(spread_last, wide_other, down_far)
     downs = [down_weight, down_far, down_near, down_last]
+    half = block_d // 2 if two_ctx() else block_d
+    far = (wide_got, wide_other) if two_ctx() else (wide_got,)
+    last = (last_got, last_other) if two_ctx() else (last_got,)
+    gates, ups = (
+        [(own, block_d, 0), *[(v, half, at) for v in far], (near, block_d, 0), *[(v, half, at) for v in last]]
+        for own, near, at in ((gate_weight, gate_near, 0), (up_weight, up_near, 1))
+    )
     wait = down_last
     branch = after(branch, wait)
     middle = inputs + RESIDUAL * branch.astype(F32)
 
     scale_two = norm_scale(middle)
     normed_two = (middle * scale_two * gain_two).astype(BF)
-    hidden, grad_gate, grad_up, grad_two = mlp(normed_two, grad_mlp, gates, ups, downs)
+    hidden, grad_gate, grad_up, grad_two = mlp(
+        normed_two, grad_mlp, lax.axis_index("ctx")[None], gates, ups, downs
+    )
     grad_two = psum_tensor(grad_two)
 
-    def begin_down(hidden, grad_mlp):
-        return outer_sum(hidden, grad_mlp, False, "down_outer").begin()
-
-    def begin_rest(hidden, normed_two, grad_gate, grad_up, *downs):
-        return (
-            outer_sum(normed_two, grad_gate, True, "gate_outer").begin(),
-            outer_sum(normed_two, grad_up, True, "up_outer").begin(),
-            lift(hidden, downs),
-        )
-
-    begun = sealed(begin_down, hidden, grad_mlp)
-    down_sum = outer_sum(hidden, grad_mlp, False, "down_outer").cross(begun)
-    begun_gate, begun_up, mlp_part = sealed(
-        begin_rest, after(hidden, begun[1]), normed_two, grad_gate, grad_up, *downs
-    )
-    gate_sum = outer_sum(normed_two, grad_gate, True, "gate_outer").cross(begun_gate)
-    up_sum = outer_sum(normed_two, grad_up, True, "up_outer").cross(begun_up, down_sum.got)
-    grad_two = after(grad_two, down_sum.sent, gate_sum.sent, up_sum.sent, mlp_part)
-    down_sum.fold(grad_two).swap()
+    def begin(hidden, normed_two, grad_mlp, grad_gate, grad_up, *downs):
+        down_sum = outer_sum(hidden, grad_mlp, False, "down_outer")
+        down_sum.cross(down_sum.begin())
+        gate_begun = outer_sum(normed_two, grad_gate, True, "gate_outer").begin()
+        up_begun = outer_sum(normed_two, grad_up, True, "up_outer").begin()
+        part = lift(hidden, downs)
+        return down_sum.fold(gate_begun[1], up_begun[1], part).low, gate_begun, up_begun, part
+
+    down_sum = BlockSum(None)
+    down_sum.low, gate_begun, up_begun, mlp_part = sealed(
+        begin, hidden, normed_two, grad_mlp, grad_gate, grad_up, *downs
+    )
+    down_sum.swap()
+    gate_sum = outer_sum(normed_two, grad_gate, True, "gate_outer").cross(gate_begun)
+    up_sum = outer_sum(normed_two, grad_up, True, "up_outer")
+    grad_two = after(grad_two, down_sum.low)
     mlp_sum = psum_tensor(after(mlp_part, grad_two))
+    up_sum.cross(up_begun, grad_two)
     grad_two = grad_two.astype(F32)
 
     gain_two_part = jnp.sum(grad_two * middle * scale_two, axis=0)
     grad_middle = grad_out + norm_back(middle, scale_two, gain_two, grad_two)
-    grad_branch = after((RESIDUAL * grad_middle).astype(BF), down_sum.low)
+    grad_branch = (RESIDUAL * grad_middle).astype(BF)
     query_low, key_value_parts = attend_backward(
         queries,
-        key_value_all,
-        key_value_all[:, :width_kv].T,
+        key_values,
         key_code,
         query_codes,
         attended,
@@ -751,7 +817,7 @@
         ).astype(F32)
         got_part = jnp.zeros(own_part.shape, BF)
     qkv_low, grad_one = entry_grad(
-        query_low, own_part, got_part, cos_table, sin_table, qkv_pieces
+        query_low, own_part, got_part, cos_table, sin_table, query_pieces, kv_pieces
     )
     gate_sum.fold(query_low)
     gate_sum.swap(got_part)
@@ -768,28 +834,29 @@
     grad_one = psum_tensor(after(grad_one, mlp_sum))
 
 
-    def finish_wide(up_low, *pairs):
-        peer = swap_ctx(up_low) if two_ctx() else lax.psum(up_low, "ctx")
-        totals = [combine(low, other) for low, other in zip(pairs[::2], pairs[1::2], strict=True)]
-        return combine(up_low, peer), *totals
-
-    up_grad, gate_grad, down_grad = sealed(
-        finish_wide,
-        after(up_sum.low, mlp_sum),
+    up_sum.swap()
+
+    def finish(middle, mlp_sum, *values):
+        entry_sum = entry_term(*values[:4]).joined(*values[4:6]).fold().swap()
+        layer_out = absolute((middle + RESIDUAL * mlp_sum.astype(F32)).astype(BF))
+        totals = (combine(*values[i : i + 2]) for i in (6, 8, 10))
+        return layer_out, *totals, entry_sum.result()
+
+    layer_out, down_grad, gate_grad, up_grad, entry_total = sealed(
+        finish,
+        middle,
+        mlp_sum,
+        *entry_inputs,
+        entry_sum.other,
+        entry_sum.got,
+        down_sum.low,
+        down_sum.peer,
         gate_sum.low,
         gate_sum.peer,
-        down_sum.low,
-        down_sum.peer,
-    )
-    entry_total = sealed(
-        lambda *v: entry_term(*v[:4]).joined(v[4], v[5]).fold().swap().result(),
-        after(attended, up_grad),
-        *entry_inputs[1:],
-        entry_sum.other,
-        entry_sum.got,
-    )
-    layer_out = absolute((middle + RESIDUAL * mlp_sum.astype(F32)).astype(BF))
-    grad_one = after(grad_one, entry_total, layer_out)
+        up_sum.low,
+        up_sum.peer,
+    )
+    grad_one = after(grad_one, down_grad)
     output_grad, qkv_grad = entry_total[:, :block_d], entry_total[:, block_d:]
     grad_one = grad_one.astype(F32)
     gain_one_part = jnp.sum(grad_one * inputs * scale_one, axis=0)

time: 514 us -> 485 us (0.944)
  waiting for transfers between devices: 238 us -> 227 us
  local copies, waits for them, and re-layouts: 32.7 us -> 22 us
  other arithmetic: 61.5 us -> 52.4 us
    ppermute x9 -> x10, waiting for transfers between devices: 27.5 us -> 107 us  [swap_x(): return lax.ppermute(value, 'dp', [(i, i ^ 2) for i in range(4)])]
    ppermute x8, waiting for transfers between devices: 136 us -> 68.8 us  [swap_ctx(): return lax.ppermute(value, 'ctx', [(0, 1), (1, 0)])]
    psum x4, waiting for transfers between devices: 50 us -> 34 us  [psum_tensor(): return lax.psum(value, 'tensor')]
    add x4 -> x3, other arithmetic: 8.68 us -> 16.9 us  [combine(): return low.astype(F32) + peer.astype(F32)]
    ppermute x15 -> x17, waiting for transfers between devices: 24.7 us -> 16.9 us  [swap_core(): return lax.ppermute(value, 'dp', [(i, i ^ 1) for i in range(4)])]
    pallas_call x9, Pallas kernels: 42.7 us -> 35.5 us  [outer(): pl.pallas_call(functools.partial(outer_kernel, len(adds)), grid=(count_m,...]
    pallas_call x4 -> x6, Pallas kernels: 63.5 us -> 68 us  [the longest x1 32.7 us: mlp(): pl.pallas_call(functools.partial(mlp_kernel, len(gates) > 4), grid_spec=p...]
    ppermute x9 -> x10, starting transfers between devices: 11.5 us -> 15.4 us  [swap_x(): return lax.ppermute(value, 'dp', [(i, i ^ 2) for i in range(4)])]
  transfers between devices with their start and end apart: 37 -> 40, of which waited for: 18 -> 23; matrix products, arithmetic and copies ran while one was open for 14% -> 12% of each run, Pallas kernels for 19% -> 20%
where the time goes in v3:
time: 485 us; the launch traced here: 477 us
  waiting for transfers between devices  227 us (47%)
  Pallas kernels  128 us (26%)
  other arithmetic  52.4 us (11%)
  starting transfers between devices  31.3 us (6%)
  local copies, waits for them, and re-layouts  22 us (5%)
  between operations  15.7 us (3%)
    ppermute x10, waiting for transfers between devices, swap_x(): return lax.ppermute(value, 'dp', [(i, i ^ 2) for i in range(4)])  107 us
    ppermute x8, waiting for transfers between devices, swap_ctx(): return lax.ppermute(value, 'ctx', [(0, 1), (1, 0)])  68.8 us
    pallas_call x9, Pallas kernels, outer(): pl.pallas_call(functools.partial(outer_kernel, len(adds)), grid=(count_m,...  35.5 us
    psum x4, waiting for transfers between devices, psum_tensor(): return lax.psum(value, 'tensor')  34 us
    pallas_call x1, Pallas kernels, mlp(): pl.pallas_call(functools.partial(mlp_kernel, len(gates) > 4), grid_spec=p...  32.7 us
    pallas_call x1, Pallas kernels, attend_backward(): pl.pallas_call(functools.partial(backward_kernel, chunk, len(key_values))...  17.3 us
    ppermute x17, waiting for transfers between devices, swap_core(): return lax.ppermute(value, 'dp', [(i, i ^ 1) for i in range(4)])  16.9 us
    add x3, other arithmetic, combine(): return low.astype(F32) + peer.astype(F32)  16.9 us
  transfers between devices with their start and end apart: 40, of which 23 were waited for; matrix products, arithmetic and copies ran while one was open for 12% of the time, Pallas kernels for 20%

profile of v3, /device:TPU:0, one launch (start us, length us, event | category | flops | bytes accessed | tf_op | source)
XLA Modules:
  0.0 476.6 jit_solution(10399269257323587136)
XLA Ops:
  19.2 4.2 collective-permute-done.17.p1.refs_1_
  45.5 4.1 collective-permute-done.19.refs_1_
  49.6 9.6 %attend_forward.1 = (bf16[512,512]{1,0:T(8,128)(2,1)S(1)}, f32[8,512]{1,0:T(8,128)S(1)}) custom-call(bf16[512,512]{1,0:T(8,128)(2,1)S(1)} %project_q.1.q_ref, s32[1024,1]{1,0:T(8,128)S(1)} %get-tuple-element.264.code_ref, s32[8,512]{1,0:T(8,128)S(1)} %stack.41.codes_ref, bf16[512,256]{1,0:T(8,128)(2,1)} %get-tuple-element.176.refs_0_, ...), custom_call_target="tpu_custom_call" | custom-call | flops 1 | bytes 1 | tf_op jit(solution)/shard_map/attend_forward/pallas_call | solution.py:98
  72.6 20.2 %collective-permute-done.23.refs_1_.refs_7_ = bf16[512,2048]{1,0:T(8,128)(2,1)} collective-permute-done((bf16[512,2048]{1,0:T(8,128)(2,1)}, bf16[512,2048]{1,0:T(8,128)(2,1)}, u32[]{:S(2)}, u32[]{:S(2)}) %collective-permute-start.23) | collective-permute-done | bytes 2097184 | tf_op jit(solution)/shard_map/ppermute | solution.py:522
  92.9 48.5 %conditional.5 = (bf16[512,2048]{1,0:T(8,128)(2,1)}, bf16[512,2048]{1,0:T(8,128)(2,1)}, bf16[512,2048]{1,0:T(8,128)(2,1)}, bf16[512,2048]{1,0:T(8,128)(2,1)}, bf16[2048,512]{1,0:T(8,128)(2,1)}) conditional(s32[]{:T(128)} %convert_element_type.93, () %tuple.81, (bf16[512,2048]{1,0:T(8,128)(2,1)}, bf16[512,2048]{1,0:T(8,128)(2,1)S(1)}, ...), branch_computations={%region_3.4_spmd, %region_4.5_spmd} | conditional | bytes 41943280 | solution.py:514
  97.7 43.6 %collective-permute-done = bf16[512,2048]{1,0:T(8,128)(2,1)} collective-permute-done((bf16[512,2048]{1,0:T(8,128)(2,1)}, bf16[512,2048]{1,0:T(8,128)(2,1)}, u32[]{:S(2)}, u32[]{:S(2)}) %collective-permute-start) | collective-permute-done | bytes 2097184 | tf_op jit(solution)/shard_map/cond/branch_1_fun/ppermute | solution.py:530
  141.3 7.6 %conditional.6 = (bf16[512,2048]{1,0:T(8,128)(2,1)}, bf16[2048,512]{1,0:T(8,128)(2,1)}) conditional(s32[]{:T(128)} %convert_element_type.93, () %tuple.80, (bf16[512,2048]{1,0:T(8,128)(2,1)}, bf16[2048,512]{1,0:T(8,128)(2,1)}) %tuple.86), branch_computations={%region_5.6_spmd, %region_6.7_spmd} | conditional | bytes 16777312 | solution.py:514
  148.9 4.3 all-reduce.6.cloned.1.call-done
  153.2 4.6 convert_add_fusion.4
  161.4 32.7 %mlp.1 = (bf16[512,2048]{1,0:T(8,128)(2,1)}, bf16[512,2048]{1,0:T(8,128)(2,1)}, bf16[512,2048]{1,0:T(8,128)(2,1)}, bf16[512,2048]{1,0:T(8,128)(2,1)S(1)}) custom-call(s32[1]{0:T(128)} %bitcast.index_ref, bf16[512,2048]{1,0:T(8,128)(2,1)S(1)} %multiply_convert_fusion.1.h_ref.a_ref, bf16[512,2048]{1,0:T(8,128)(2,1)S(1)} %copy-done.24, ...), custom_call_target="tpu_custom_call" | custom-call | flops 1 | bytes 1 | tf_op jit(solution)/shard_map/mlp/pallas_call | solution.py:340
  195.7 65.7 %conditional.7 = (bf16[2048,512]{1,0:T(8,128)(2,1)}, bf16[1024,2048]{1,0:T(8,128)(2,1)}, bf16[512,2048]{1,0:T(8,128)(2,1)}, bf16[1024,2048]{1,0:T(8,128)(2,1)}, ...) conditional(s32[]{:T(128)} %convert_element_type.93, () %tuple.74, (bf16[512,2048]{1,0:T(8,128)(2,1)}, ...), branch_computations={%region_9.10_spmd, %region_10.11_spmd} | conditional | flops 8 | bytes 109052280 | solution.py:514
  195.7 4.9 %down_outer.3 = bf16[2048,1024]{1,0:T(8,128)(2,1)S(1)} custom-call(bf16[512,2048]{1,0:T(8,128)(2,1)} %get-tuple-element.78.a_ref.hidden_ref, bf16[512,2048]{1,0:T(8,128)(2,1)} %get-tuple-element.79.b_ref), custom_call_target="tpu_custom_call" | custom-call | flops 1 | bytes 1 | tf_op jit(solution)/shard_map/cond/branch_1_fun/down_outer/pallas_call | solution.py:415
  211.6 11.4 %lift.1 = bf16[512,2048]{1,0:T(8,128)(2,1)} custom-call(bf16[512,2048]{1,0:T(8,128)(2,1)S(1)} %copy-done.29, bf16[2048,512]{1,0:T(8,128)(2,1)S(1)} %copy-done.40, bf16[2048,512]{1,0:T(8,128)(2,1)} %get-tuple-element.84.d1, bf16[2048,512]{1,0:T(8,128)(2,1)} %get-tuple-element.85.d2, bf16[2048,512]{1,0:T(8,128)(2,1)} %get-tuple-element.86.d3), custom_call_target="tpu_custom_call" | custom-call | flops 1 | bytes 1 | tf_op jit(solution)/shard_map/cond/branch_1_fun/lift/pallas_call | solution.py:451
  223.0 4.2 gate_outer.4
  227.3 4.2 up_outer.4
  231.5 26.4 %collective-permute-done.8.refs_1_ = bf16[2048,512]{1,0:T(8,128)(2,1)S(1)} collective-permute-done((bf16[2048,512]{1,0:T(8,128)(2,1)S(1)}, bf16[2048,512]{1,0:T(8,128)(2,1)S(1)}, u32[]{:S(2)}, u32[]{:S(2)}) %collective-permute-start.8) | collective-permute-done | bytes 2097184 | tf_op jit(solution)/shard_map/cond/branch_1_fun/ppermute | solution.py:522
  264.2 16.7 %all-reduce.8.cloned.1.call-done = bf16[512,2048]{1,0:T(8,128)(2,1)} async-done(((bf16[512,2048]{1,0:T(8,128)(2,1)}), bf16[512,2048]{1,0:T(8,128)(2,1)}) %all-reduce.8.cloned.1.call-update) | async-done | bytes 2097168 | tf_op jit(solution)/shard_map/psum | solution.py:554
  282.9 4.0 fusion.10
  291.0 17.3 %attend_backward.1 = (bf16[512,512]{1,0:T(8,128)(2,1)S(1)}, f32[1024,256]{1,0:T(8,128)S(1)}) custom-call(bf16[512,512]{1,0:T(8,128)(2,1)S(1)} %project_q.1.q_ref, s32[1024,1]{1,0:T(8,128)S(1)} %get-tuple-element.264.code_ref, s32[8,512]{1,0:T(8,128)S(1)} %stack.41.codes_ref, bf16[512,512]{1,0:T(8,128)(2,1)S(1)} %copy-done.37, ...), custom_call_target="tpu_custom_call" | custom-call | flops 1 | bytes 1 | tf_op jit(solution)/shard_map/attend_backward/pallas_call | solution.py:186
  310.3 5.2 %gate_outer.5 = bf16[512,2048]{1,0:T(8,128)(2,1)} custom-call(bf16[512,2048]{1,0:T(8,128)(2,1)S(1)} %copy-done.22, bf16[512,2048]{1,0:T(8,128)(2,1)S(1)} %copy-done.33, bf16[1024,2048]{1,0:T(8,128)(2,1)} %get-tuple-element.204.refs_0_, bf16[512,2048]{1,0:T(8,128)(2,1)} %collective-permute-done.27.refs_1_), custom_call_target="tpu_custom_call" | custom-call | flops 1 | bytes 1 | tf_op jit(solution)/shard_map/gate_outer/pallas_call | solution.py:415
  321.6 11.0 %conditional.8 = (bf16[1024,1280]{1,0:T(8,128)(2,1)}, bf16[512,1280]{1,0:T(8,128)(2,1)S(1)}) conditional(s32[]{:T(128)} %convert_element_type.93, () %tuple.95, (bf16[512,512]{1,0:T(8,128)(2,1)S(1)}, bf16[512,2048]{1,0:T(8,128)(2,1)S(1)}, bf16[512,2048]{1,0:T(8,128)(2,1)S(1)}, bf16[512,768]{1,0:T(8,128)(2,1)}) %tuple.166), branch_computations={%region_12.13_spmd, %region_13.14_spmd} | conditional | flops 2 | bytes 10485818 | solution.py:514
  324.9 5.0 %collective-permute-done.11.refs_0_ = bf16[1024,1280]{1,0:T(8,128)(2,1)} collective-permute-done((bf16[1024,1280]{1,0:T(8,128)(2,1)S(1)}, bf16[1024,1280]{1,0:T(8,128)(2,1)}, u32[]{:S(2)}, u32[]{:S(2)}) %collective-permute-start.11) | collective-permute-done | bytes 2621472 | tf_op jit(solution)/shard_map/cond/branch_1_fun/ppermute | solution.py:518
  332.6 20.9 %collective-permute-done.28.refs_1_ = bf16[512,2048]{1,0:T(8,128)(2,1)} collective-permute-done((bf16[512,2048]{1,0:T(8,128)(2,1)}, bf16[512,2048]{1,0:T(8,128)(2,1)}, u32[]{:S(2)}, u32[]{:S(2)}) %collective-permute-start.28) | collective-permute-done | bytes 2097184 | tf_op jit(solution)/shard_map/ppermute | solution.py:522
  353.5 5.8 %up_outer.5 = bf16[512,2048]{1,0:T(8,128)(2,1)} custom-call(bf16[512,2048]{1,0:T(8,128)(2,1)} %copy-done.21, bf16[512,2048]{1,0:T(8,128)(2,1)} %get-tuple-element.195.b_ref, bf16[1024,2048]{1,0:T(8,128)(2,1)} %get-tuple-element.207.refs_0_, bf16[512,2048]{1,0:T(8,128)(2,1)} %collective-permute-done.28.refs_1_), custom_call_target="tpu_custom_call" | custom-call | flops 1 | bytes 1 | tf_op jit(solution)/shard_map/up_outer/pallas_call | solution.py:415
  360.8 8.1 %all-reduce.10.cloned.1.call-done = bf16[512,2048]{1,0:T(8,128)(2,1)} async-done(((bf16[512,2048]{1,0:T(8,128)(2,1)}), bf16[512,2048]{1,0:T(8,128)(2,1)}) %all-reduce.10.cloned.1.call-update) | async-done | bytes 2097168 | tf_op jit(solution)/shard_map/psum | solution.py:554
  370.4 29.1 %collective-permute-done.31 = bf16[512,1280]{1,0:T(8,128)(2,1)} collective-permute-done((bf16[512,1280]{1,0:T(8,128)(2,1)S(1)}, bf16[512,1280]{1,0:T(8,128)(2,1)}, u32[]{:S(2)}, u32[]{:S(2)}) %collective-permute-start.31) | collective-permute-done | bytes 1310752 | tf_op jit(solution)/shard_map/ppermute | solution.py:522
  399.6 12.1 %collective-permute-done.30 = bf16[512,2048]{1,0:T(8,128)(2,1)} collective-permute-done((bf16[512,2048]{1,0:T(8,128)(2,1)}, bf16[512,2048]{1,0:T(8,128)(2,1)}, u32[]{:S(2)}, u32[]{:S(2)}) %collective-permute-start.30) | collective-permute-done | bytes 2097184 | tf_op jit(solution)/shard_map/ppermute | solution.py:530
  411.7 40.2 %conditional.9 = (bf16[512,2048]{1,0:T(8,128)(2,1)}, f32[2048,512]{1,0:T(8,128)}, f32[512,2048]{1,0:T(8,128)}, f32[512,2048]{1,0:T(8,128)}, f32[512,1280]{1,0:T(...) conditional(s32[]{:T(128)} %convert_element_type.93, () %tuple.73, ...), branch_computations={%region_15.16_spmd, %region_16.17_spmd} | conditional | flops 23986216 | bytes 57672252 | solution.py:514
  420.4 5.0 %convert_add_fusion.2 = f32[2048,512]{1,0:T(8,128)} fusion(bf16[2048,512]{1,0:T(8,128)(2,1)} %get-tuple-element.95, bf16[2048,512]{1,0:T(8,128)(2,1)} %get-tuple-element.94), kind=kLoop, calls=%fused_computation.2 | loop fusion | flops 3145728 | bytes 8388608 | tf_op jit(solution)/shard_map/cond/branch_1_fun/add | solution.py:611
  427.2 8.8 %convert_add_fusion = (f32[512,2048]{1,0:T(8,128)}, f32[512,2048]{1,0:T(8,128)}) fusion(bf16[512,2048]{1,0:T(8,128)(2,1)} %get-tuple-element.99, bf16[512,2048]{1,0:T(8,128)(2,1)} %get-tuple-element.98, bf16[512,2048]{1,0:T(8,128)(2,1)} %get-tuple-element.97, bf16[512,2048]{1,0:T(8,128)(2,1)} %get-tuple-element.96), kind=kLoop, calls=%fused_computation | loop fusion | flops 6291456 | bytes 16777216 | tf_op jit(solution)/shard_map/cond/branch_1_fun/add | solution.py:611
  436.0 7.9 %collective-permute-done.12 = bf16[512,1280]{1,0:T(8,128)(2,1)} collective-permute-done((bf16[512,1280]{1,0:T(8,128)(2,1)S(1)}, bf16[512,1280]{1,0:T(8,128)(2,1)}, u32[]{:S(2)}, u32[]{:S(2)}) %collective-permute-start.12) | collective-permute-done | bytes 1310752 | tf_op jit(solution)/shard_map/cond/branch_1_fun/ppermute | solution.py:530
  451.9 4.8 %all-reduce.12.cloned.1.call-done = bf16[512,2048]{1,0:T(8,128)(2,1)} async-done(((bf16[512,2048]{1,0:T(8,128)(2,1)}), bf16[512,2048]{1,0:T(8,128)(2,1)}) %all-reduce.12.cloned.1.call-update) | async-done | bytes 2097168 | tf_op jit(solution)/shard_map/psum | solution.py:554
  (256 shorter events, 135.4 us)
Async XLA Ops:
  7.2 146.1 %all-reduce.6.cloned.1.call-start = ((), (), s32[]{:S(2)}) async-start(), calls=%async_computation | async-start | bytes 4194304 | tf_op jit(solution)/shard_map/psum | solution.py:554
  7.7 15.7 %collective-permute-start.17 = (bf16[512,512]{1,0:T(8,128)(2,1)}, bf16[512,512]{1,0:T(8,128)(2,1)}, u32[]{:S(2)}, u32[]{:S(2)}) collective-permute-start(bf16[512,512]{1,0:T(8,128)(2,1)} %refs_0_.3), channel_id=1, source_target_pairs={{0,16},{8,24},{16,0},{24,8},{1,17},{9,25},{17,1},{25,9},{2,18},{10... | collective-permute-start | bytes 1572872 | tf_op jit(solution)/shard_map/ppermute | solution.py:522
  13.6 15.6 %collective-permute-start.14 = (bf16[544,256]{1,0:T(8,128)(2,1)S(1)}, bf16[544,256]{1,0:T(8,128)(2,1)S(1)}, u32[]{:S(2)}, u32[]{:S(2)}) collective-permute-start(bf16[544,256]{1,0:T(8,128)(2,1)S(1)} %fusion.25.p0.refs_4_), channel_id=1, source_target_pairs={{0,16},{8,24},{16,0},{24,8},{1,17},{9,25},{17,1},{25,9},{2,18},{10... | collective-permute-start | bytes 835592 | tf_op jit(solution)/shard_map/ppermute | solution.py:522
  13.7 9.7 %collective-permute-start.15 = (bf16[544,256]{1,0:T(8,128)(2,1)S(1)}, bf16[544,256]{1,0:T(8,128)(2,1)}, u32[]{:S(2)}, u32[]{:S(2)}) collective-permute-start(bf16[544,256]{1,0:T(8,128)(2,1)S(1)} %fusion.25.p0.refs_4_), channel_id=1, source_target_pairs={{0,8},{8,0},{16,24},{24,16},{1,9},{9,1},{17,25},{25,17},{2,10},{10... | collective-permute-start | bytes 835592 | tf_op jit(solution)/shard_map/ppermute | solution.py:518
  23.4 11.5 %collective-permute-start.18 = (bf16[512,512]{1,0:T(8,128)(2,1)}, bf16[512,512]{1,0:T(8,128)(2,1)S(1)}, u32[]{:S(2)}, u32[]{:S(2)}) collective-permute-start(bf16[512,512]{1,0:T(8,128)(2,1)} %collective-permute-done.17.p1.refs_1_), channel_id=1, source_target_pairs={{0,8},{8,0},{16,24},{24,16},{1,9},{9,1},{17,25},{25,17},{2,10},{10... | collective-permute-start | bytes 1572872 | tf_op jit(solution)/shard_map/ppermute | solution.py:518
  23.4 16.9 %collective-permute-start.20 = (bf16[512,512]{1,0:T(8,128)(2,1)}, bf16[512,512]{1,0:T(8,128)(2,1)}, u32[]{:S(2)}, u32[]{:S(2)}) collective-permute-start(bf16[512,512]{1,0:T(8,128)(2,1)} %o0.3), channel_id=1, source_target_pairs={{0,16},{8,24},{16,0},{24,8},{1,17},{9,25},{17,1},{25,9},{2,18},{10... | collective-permute-start | bytes 1572872 | tf_op jit(solution)/shard_map/ppermute | solution.py:522
  30.8 30.3 %collective-permute-start.21 = (bf16[512,512]{1,0:T(8,128)(2,1)}, bf16[512,512]{1,0:T(8,128)(2,1)}, u32[]{:S(2)}, u32[]{:S(2)}) collective-permute-start(bf16[512,512]{1,0:T(8,128)(2,1)} %o0.3), channel_id=1, source_target_pairs={{0,8},{8,0},{16,24},{24,16},{1,9},{9,1},{17,25},{25,17},{2,10},{10... | collective-permute-start | bytes 1572872 | tf_op jit(solution)/shard_map/ppermute | solution.py:518
  40.3 20.7 %collective-permute-start.22 = (bf16[512,512]{1,0:T(8,128)(2,1)}, bf16[512,512]{1,0:T(8,128)(2,1)}, u32[]{:S(2)}, u32[]{:S(2)}) collective-permute-start(bf16[512,512]{1,0:T(8,128)(2,1)} %collective-permute-done.20.o1), channel_id=1, source_target_pairs={{0,8},{8,0},{16,24},{24,16},{1,9},{9,1},{17,25},{25,17},{2,10},{10... | collective-permute-start | bytes 1572872 | tf_op jit(solution)/shard_map/ppermute | solution.py:518
  40.5 9.1 %collective-permute-start.19 = (bf16[512,256]{1,0:T(8,128)(2,1)}, bf16[512,256]{1,0:T(8,128)(2,1)}, u32[]{:S(2)}, u32[]{:S(2)}) collective-permute-start(bf16[512,256]{1,0:T(8,128)(2,1)} %get-tuple-element.176.refs_0_), channel_id=1, source_target_pairs={{0,4},{4,0},{1,5},{5,1},{2,6},{6,2},{3,7},{7,3},{8,12},{12,8},{9,1... | collective-permute-start | bytes 786440 | tf_op jit(solution)/shard_map/ppermute | solution.py:530
  44.0 48.8 %collective-permute-start.23 = (bf16[512,2048]{1,0:T(8,128)(2,1)}, bf16[512,2048]{1,0:T(8,128)(2,1)}, u32[]{:S(2)}, u32[]{:S(2)}) collective-permute-start(bf16[512,2048]{1,0:T(8,128)(2,1)} %pad_maximum_fusion.2), channel_id=1, source_target_pairs={{0,16},{8,24},{16,0},{24,8},{1,17},{9,25},{17,1},{25,9},{2,18},{10... | collective-permute-start | bytes 6291464 | tf_op jit(solution)/shard_map/ppermute | solution.py:522
  59.3 82.0 %collective-permute-start.24 = (bf16[2048,512]{1,0:T(8,128)(2,1)}, bf16[2048,512]{1,0:T(8,128)(2,1)}, u32[]{:S(2)}, u32[]{:S(2)}) collective-permute-start(bf16[2048,512]{1,0:T(8,128)(2,1)} %refs_12_.1), channel_id=1, source_target_pairs={{0,16},{8,24},{16,0},{24,8},{1,17},{9,25},{17,1},{25,9},{2,18},{10... | collective-permute-start | bytes 6291464 | tf_op jit(solution)/shard_map/ppermute | solution.py:522
  66.1 214.9 %all-reduce.8.cloned.1.call-start = ((), (), s32[]{:S(2)}) async-start(), calls=%async_computation.1 | async-start | bytes 4194304 | tf_op jit(solution)/shard_map/psum | solution.py:554
  92.9 48.4 %collective-permute-start = (bf16[512,2048]{1,0:T(8,128)(2,1)}, bf16[512,2048]{1,0:T(8,128)(2,1)}, u32[]{:S(2)}, u32[]{:S(2)}) collective-permute-start(bf16[512,2048]{1,0:T(8,128)(2,1)} %get-tuple-element.73), channel_id=1, source_target_pairs={{0,4},{4,0},{1,5},{5,1},{2,6},{6,2},{3,7},{7,3},{8,12},{12,8},{9,1... | collective-permute-start | bytes 6291464 | tf_op jit(solution)/shard_map/cond/branch_1_fun/ppermute | solution.py:530
  93.3 48.1 %collective-permute-start.2 = (bf16[512,2048]{1,0:T(8,128)(2,1)S(1)}, bf16[512,2048]{1,0:T(8,128)(2,1)}, u32[]{:S(2)}, u32[]{:S(2)}) collective-permute-start(bf16[512,2048]{1,0:T(8,128)(2,1)S(1)} %get-tuple-element.72), channel_id=1, source_target_pairs={{0,8},{8,0},{16,24},{24,16},{1,9},{9,1},{17,25},{25,17},{2,10},{10... | collective-permute-start | bytes 6291464 | tf_op jit(solution)/shard_map/cond/branch_1_fun/ppermute | solution.py:518
  97.2 44.1 %collective-permute-start.3 = (bf16[512,2048]{1,0:T(8,128)(2,1)}, bf16[512,2048]{1,0:T(8,128)(2,1)}, u32[]{:S(2)}, u32[]{:S(2)}) collective-permute-start(bf16[512,2048]{1,0:T(8,128)(2,1)} %get-tuple-element.73), channel_id=1, source_target_pairs={{0,8},{8,0},{16,24},{24,16},{1,9},{9,1},{17,25},{25,17},{2,10},{10... | collective-permute-start | bytes 6291464 | tf_op jit(solution)/shard_map/cond/branch_1_fun/ppermute | solution.py:518
  97.4 44.0 %collective-permute-start.4 = (bf16[2048,512]{1,0:T(8,128)(2,1)S(1)}, bf16[2048,512]{1,0:T(8,128)(2,1)}, u32[]{:S(2)}, u32[]{:S(2)}) collective-permute-start(bf16[2048,512]{1,0:T(8,128)(2,1)S(1)} %get-tuple-element.75), channel_id=1, source_target_pairs={{0,8},{8,0},{16,24},{24,16},{1,9},{9,1},{17,25},{25,17},{2,10},{10... | collective-permute-start | bytes 6291464 | tf_op jit(solution)/shard_map/cond/branch_1_fun/ppermute | solution.py:518
  141.4 7.5 %collective-permute-start.6 = (bf16[2048,512]{1,0:T(8,128)(2,1)}, bf16[2048,512]{1,0:T(8,128)(2,1)}, u32[]{:S(2)}, u32[]{:S(2)}) collective-permute-start(bf16[2048,512]{1,0:T(8,128)(2,1)} %get-tuple-element.77), channel_id=1, source_target_pairs={{0,8},{8,0},{16,24},{24,16},{1,9},{9,1},{17,25},{25,17},{2,10},{10... | collective-permute-start | bytes 6291464 | tf_op jit(solution)/shard_map/cond/branch_1_fun/ppermute | solution.py:518
  195.4 173.4 %all-reduce.10.cloned.1.call-start = ((), (), s32[]{:S(2)}) async-start(), calls=%async_computation.2 | async-start | bytes 4194304 | tf_op jit(solution)/shard_map/psum | solution.py:554
  200.6 7.2 %collective-permute-start.7 = (bf16[2048,1024]{1,0:T(8,128)(2,1)S(1)}, bf16[2048,1024]{1,0:T(8,128)(2,1)S(1)}, u32[]{:S(2)}, u32[]{:S(2)}) collective-permute-start(bf16[2048,1024]{1,0:T(8,128)(2,1)S(1)} %down_outer.3), channel_id=1, source_target_pairs={{0,8},{8,0},{16,24},{24,16},{1,9},{9,1},{17,25},{25,17},{2,10},{10... | collective-permute-start | bytes 12582920 | tf_op jit(solution)/shard_map/cond/branch_1_fun/ppermute | solution.py:518
  203.4 19.6 %collective-permute-start.9 = (bf16[1024,2048]{1,0:T(8,128)(2,1)S(1)}, bf16[1024,2048]{1,0:T(8,128)(2,1)}, u32[]{:S(2)}, u32[]{:S(2)}) collective-permute-start(bf16[1024,2048]{1,0:T(8,128)(2,1)S(1)} %gate_outer.3), channel_id=1, source_target_pairs={{0,8},{8,0},{16,24},{24,16},{1,9},{9,1},{17,25},{25,17},{2,10},{10... | collective-permute-start | bytes 12582920 | tf_op jit(solution)/shard_map/cond/branch_1_fun/ppermute | solution.py:518
  206.7 20.6 %collective-permute-start.10 = (bf16[1024,2048]{1,0:T(8,128)(2,1)S(1)}, bf16[1024,2048]{1,0:T(8,128)(2,1)}, u32[]{:S(2)}, u32[]{:S(2)}) collective-permute-start(bf16[1024,2048]{1,0:T(8,128)(2,1)S(1)} %up_outer.3), channel_id=1, source_target_pairs={{0,8},{8,0},{16,24},{24,16},{1,9},{9,1},{17,25},{25,17},{2,10},{10... | collective-permute-start | bytes 12582920 | tf_op jit(solution)/shard_map/cond/branch_1_fun/ppermute | solution.py:518
  210.1 47.7 %collective-permute-start.8 = (bf16[2048,512]{1,0:T(8,128)(2,1)S(1)}, bf16[2048,512]{1,0:T(8,128)(2,1)S(1)}, u32[]{:S(2)}, u32[]{:S(2)}) collective-permute-start(bf16[2048,512]{1,0:T(8,128)(2,1)S(1)} %down_outer.4), channel_id=1, source_target_pairs={{0,16},{8,24},{16,0},{24,8},{1,17},{9,25},{17,1},{25,9},{2,18},{10... | collective-permute-start | bytes 6291464 | tf_op jit(solution)/shard_map/cond/branch_1_fun/ppermute | solution.py:522
  261.3 48.9 %collective-permute-start.27 = (bf16[512,2048]{1,0:T(8,128)(2,1)}, bf16[512,2048]{1,0:T(8,128)(2,1)}, u32[]{:S(2)}, u32[]{:S(2)}) collective-permute-start(bf16[512,2048]{1,0:T(8,128)(2,1)} %get-tuple-element.205), channel_id=1, source_target_pairs={{0,16},{8,24},{16,0},{24,8},{1,17},{9,25},{17,1},{25,9},{2,18},{10... | collective-permute-start | bytes 6291464 | tf_op jit(solution)/shard_map/ppermute | solution.py:522
  262.7 98.0 %collective-permute-start.26 = (bf16[2048,512]{1,0:T(8,128)(2,1)}, bf16[2048,512]{1,0:T(8,128)(2,1)}, u32[]{:S(2)}, u32[]{:S(2)}) collective-permute-start(bf16[2048,512]{1,0:T(8,128)(2,1)} %get-tuple-element.198), channel_id=1, source_target_pairs={{0,4},{4,0},{1,5},{5,1},{2,6},{6,2},{3,7},{7,3},{8,12},{12,8},{9,1... | collective-permute-start | bytes 6291464 | tf_op jit(solution)/shard_map/ppermute | solution.py:530
  281.0 72.5 %collective-permute-start.28 = (bf16[512,2048]{1,0:T(8,128)(2,1)}, bf16[512,2048]{1,0:T(8,128)(2,1)}, u32[]{:S(2)}, u32[]{:S(2)}) collective-permute-start(bf16[512,2048]{1,0:T(8,128)(2,1)} %get-tuple-element.209), channel_id=1, source_target_pairs={{0,16},{8,24},{16,0},{24,8},{1,17},{9,25},{17,1},{25,9},{2,18},{10... | collective-permute-start | bytes 6291464 | tf_op jit(solution)/shard_map/ppermute | solution.py:522
  282.5 174.2 %all-reduce.12.cloned.1.call-start = ((), (), s32[]{:S(2)}) async-start(), calls=%async_computation.3 | async-start | bytes 4194304 | tf_op jit(solution)/shard_map/psum | solution.py:554
  308.3 7.8 %collective-permute-start.25 = (bf16[512,256]{1,0:T(8,128)(2,1)S(1)}, bf16[512,256]{1,0:T(8,128)(2,1)S(1)}, u32[]{:S(2)}, u32[]{:S(2)}) collective-permute-start(bf16[512,256]{1,0:T(8,128)(2,1)S(1)} %slice.167), channel_id=1, source_target_pairs={{0,4},{4,0},{1,5},{5,1},{2,6},{6,2},{3,7},{7,3},{8,12},{12,8},{9,1... | collective-permute-start | bytes 786440 | tf_op jit(solution)/shard_map/ppermute | solution.py:530
  320.1 79.5 %collective-permute-start.29 = (bf16[512,2048]{1,0:T(8,128)(2,1)}, bf16[512,2048]{1,0:T(8,128)(2,1)}, u32[]{:S(2)}, u32[]{:S(2)}) collective-permute-start(bf16[512,2048]{1,0:T(8,128)(2,1)} %gate_outer.5), channel_id=1, source_target_pairs={{0,4},{4,0},{1,5},{5,1},{2,6},{6,2},{3,7},{7,3},{8,12},{12,8},{9,1... | collective-permute-start | bytes 6291464 | tf_op jit(solution)/shard_map/ppermute | solution.py:530
  359.3 52.4 %collective-permute-start.30 = (bf16[512,2048]{1,0:T(8,128)(2,1)}, bf16[512,2048]{1,0:T(8,128)(2,1)}, u32[]{:S(2)}, u32[]{:S(2)}) collective-permute-start(bf16[512,2048]{1,0:T(8,128)(2,1)} %up_outer.5), channel_id=1, source_target_pairs={{0,4},{4,0},{1,5},{5,1},{2,6},{6,2},{3,7},{7,3},{8,12},{12,8},{9,1... | collective-permute-start | bytes 6291464 | tf_op jit(solution)/shard_map/ppermute | solution.py:530
  368.9 30.7 %collective-permute-start.31 = (bf16[512,1280]{1,0:T(8,128)(2,1)S(1)}, bf16[512,1280]{1,0:T(8,128)(2,1)}, u32[]{:S(2)}, u32[]{:S(2)}) collective-permute-start(bf16[512,1280]{1,0:T(8,128)(2,1)S(1)} %get-tuple-element.215), channel_id=1, source_target_pairs={{0,16},{8,24},{16,0},{24,8},{1,17},{9,25},{17,1},{25,9},{2,18},{10... | collective-permute-start | bytes 3932168 | tf_op jit(solution)/shard_map/ppermute | solution.py:522
  415.2 28.8 %collective-permute-start.12 = (bf16[512,1280]{1,0:T(8,128)(2,1)S(1)}, bf16[512,1280]{1,0:T(8,128)(2,1)}, u32[]{:S(2)}, u32[]{:S(2)}) collective-permute-start(bf16[512,1280]{1,0:T(8,128)(2,1)S(1)} %entry_outer.5), channel_id=1, source_target_pairs={{0,4},{4,0},{1,5},{5,1},{2,6},{6,2},{3,7},{7,3},{8,12},{12,8},{9,1... | collective-permute-start | bytes 3932168 | tf_op jit(solution)/shard_map/cond/branch_1_fun/ppermute | solution.py:530
  460.0 5.3 %collective-permute-start.32 = (f32[2,512]{1,0:T(2,128)S(1)}, f32[2,512]{1,0:T(2,128)S(1)}, u32[]{:S(2)}, u32[]{:S(2)}) collective-permute-start(f32[2,512]{1,0:T(2,128)S(1)} %get-tuple-element.271), channel_id=1, source_target_pairs={{0,16},{8,24},{16,0},{24,8},{1,17},{9,25},{17,1},{25,9},{2,18},{10... | collective-permute-start | bytes 12296 | tf_op jit(solution)/shard_map/ppermute | solution.py:522
  (66 other events, 519.1 us)
Sparse Core Ops, SparseCore 0:
  66.2 86.9 all-reduce.5
  195.6 85.3 all-reduce.7
  283.3 85.4 all-reduce.9
  371.2 85.4 all-reduce.11

commit v4 on v3

--- a/solution.py
+++ b/solution.py
@@ -212,7 +212,7 @@
     return pl.pallas_call(
         out_kernel,
         out_shape=jax.ShapeDtypeStruct((attended.shape[0], 4 * out_pieces[0].shape[1]), BF),
-        compiler_params=pltpu.CompilerParams(vmem_limit_bytes=16 << 20),
+        compiler_params=pltpu.CompilerParams(vmem_limit_bytes=60 << 20),
         cost_estimate=LIGHT,
         name="out_project",
     )(attended, *out_pieces)
@@ -277,12 +277,26 @@
     )(normed, cos_table, sin_table, *pieces)
 
 
-def mlp_kernel(halves, index_ref, h_ref, g_ref, *refs):
+def mlp_kernel(halves, index_ref, x_ref, branch_ref, gain_ref, g_ref, *refs):
     count = 6 if halves else 4
     given, downs = (refs[:count], refs[count : 2 * count]), refs[2 * count : 2 * count + 4]
-    hidden_ref, dgate_ref, dup_ref, dh_ref, acc, joined = refs[2 * count + 4 :]
+    h_ref, hidden_ref, dgate_ref, dup_ref, dh_ref, acc, joined = refs[2 * count + 4 :]
     step = pl.program_id(0)
     block = h_ref.shape[1] // 4
+
+    @pl.when(step == 0)
+    def _():
+        height = 128
+
+        def norm(i, unused):
+            at = rows_at(i, height)
+            middle = x_ref[at, :].astype(F32) + RESIDUAL * branch_ref[at, :].astype(F32)
+            square = jnp.mean(middle * middle, axis=1, keepdims=True)
+            h_ref[at, :] = (middle * lax.rsqrt(square + EPSILON) * gain_ref[...]).astype(BF)
+            return unused
+
+        lax.fori_loop(0, h_ref.shape[0] // height, norm, 0)
+
     sides = []
     for which, pieces in enumerate(given):
         if halves:
@@ -329,8 +343,8 @@
         dh_ref[...] = acc[...].astype(BF)
 
 
-def mlp(normed, grad, index, gates, ups, downs):
-    rows, model = normed.shape
+def mlp(tokens, branch, gain, grad, index, gates, ups, downs):
+    rows, model = tokens.shape
     hidden = downs[0].shape[0]
     tile = 512
     whole = pl.BlockSpec((rows, model), lambda j, s: (0, 0))
@@ -342,19 +356,22 @@
         grid_spec=pltpu.PrefetchScalarGridSpec(
             num_scalar_prefetch=1,
             grid=(hidden // tile,),
-            in_specs=[whole] * 2 + wide + [tall] * 4,
-            out_specs=[out] * 3 + [whole],
+            in_specs=[whole, whole, pl.BlockSpec((1, model), lambda j, s: (0, 0)), whole]
+            + wide
+            + [tall] * 4,
+            out_specs=[whole] + [out] * 3 + [whole],
             scratch_shapes=[
                 pltpu.VMEM((rows, model), F32),
                 pltpu.VMEM((2, 2, model // 4, tile), BF),
             ],
         ),
-        out_shape=[jax.ShapeDtypeStruct((rows, hidden), BF)] * 3
+        out_shape=[jax.ShapeDtypeStruct((rows, model), BF)]
+        + [jax.ShapeDtypeStruct((rows, hidden), BF)] * 3
         + [jax.ShapeDtypeStruct((rows, model), BF)],
-        compiler_params=pltpu.CompilerParams(vmem_limit_bytes=44 << 20),
+        compiler_params=pltpu.CompilerParams(vmem_limit_bytes=60 << 20),
         cost_estimate=LIGHT,
         name="mlp",
-    )(index, normed, grad, *[v[0] for v in gates + ups], *downs)
+    )(index, tokens, branch, gain[None], grad, *[v[0] for v in gates + ups], *downs)
 
 
 def entry_kernel(dq_ref, own_ref, got_ref, cos_ref, sin_ref, *refs):
@@ -381,7 +398,7 @@
             jax.ShapeDtypeStruct((rows, width_q + key_pieces[0].shape[1]), BF),
             jax.ShapeDtypeStruct((rows, 4 * block), BF),
         ),
-        compiler_params=pltpu.CompilerParams(vmem_limit_bytes=24 << 20),
+        compiler_params=pltpu.CompilerParams(vmem_limit_bytes=60 << 20),
         cost_estimate=LIGHT,
         name="entry_grad",
     )(dq_low, own, got, cos_table, sin_table, *query_pieces, *key_pieces)
@@ -503,6 +520,37 @@
     )(attended, branch, normed, low, *[array for array, unused in adds])
 
 
+def exit_kernel(index_ref, middle_ref, dh_ref, x_ref, gain_ref, out_ref):
+    x = x_ref[...].astype(F32)
+    scale = lax.rsqrt(jnp.mean(x * x, axis=1, keepdims=True) + EPSILON)
+    weighted = gain_ref[...] * dh_ref[...].astype(F32)
+    inner = jnp.mean(weighted * x, axis=1, keepdims=True)
+    total = middle_ref[...] + scale * weighted - x * (scale * scale * scale * inner)
+    block = x.shape[1] // 4
+    for k, owner in enumerate(OWNERS):
+        place = pl.multiple_of((index_ref[0] ^ owner) * block, block)
+        out_ref[:, pl.ds(place, block)] = total[:, k * block : (k + 1) * block].astype(BF)
+
+
+def exit_grad(index, grad_middle, grad, tokens, gain):
+    rows, model = tokens.shape
+    height = 128
+    part = pl.BlockSpec((height, model), lambda i, s: (i, 0))
+    return pl.pallas_call(
+        exit_kernel,
+        grid_spec=pltpu.PrefetchScalarGridSpec(
+            num_scalar_prefetch=1,
+            grid=(rows // height,),
+            in_specs=[part, part, part, pl.BlockSpec((1, model), lambda i, s: (0, 0))],
+            out_specs=part,
+        ),
+        out_shape=jax.ShapeDtypeStruct((rows, model), BF),
+        compiler_params=pltpu.CompilerParams(vmem_limit_bytes=60 << 20),
+        cost_estimate=LIGHT,
+        name="exit_grad",
+    )(index, grad_middle, grad, tokens, gain[None])
+
+
 def after(value, *others):
     if not others:
         return value
@@ -541,17 +589,29 @@
     return lax.psum(low, "ctx").astype(F32)
 
 
-def far_halves(one, two, wait):
+def far_halves(one, two):
     if not two_ctx():
-        return swap_x(after(jnp.concatenate([one, two]), wait))
+        return jnp.concatenate([one, two])
     half = one.shape[0] // 2
     at = lax.axis_index("ctx") * half
-    mine = [lax.dynamic_slice_in_dim(v, at, half) for v in (one, two)]
-    return swap_x(after(jnp.concatenate(mine), wait))
+    return jnp.concatenate([lax.dynamic_slice_in_dim(v, at, half) for v in (one, two)])
 
 
 def psum_tensor(value):
     return lax.psum(value, "tensor")
+
+
+def sum_everywhere(gains):
+    gains = gains + swap_ctx(gains) if two_ctx() else lax.psum(gains, "ctx")
+    near, far, other, both = split4(gains, 1)
+    total = near + swap_x(far)
+    total = total + swap_core(after(other, total))
+    total = total + swap_both(after(both, total))
+    if lax.axis_size("tensor") != 4:
+        return lax.psum(total, "tensor")
+    for bit in (1, 2):
+        total = total + lax.ppermute(total, "tensor", [(i, i ^ bit) for i in range(4)])
+    return total
 
 
 def swap_bits(index):
@@ -565,9 +625,12 @@
     )
 
 
+OWNERS = (0, 2, 1, 3)
+
+
 def relative(value):
     mine = lax.axis_index("dp")
-    return take_blocks(value, [mine ^ k for k in (0, 2, 1, 3)])
+    return take_blocks(value, [mine ^ k for k in OWNERS])
 
 
 def absolute(value):
@@ -689,7 +752,8 @@
     kv_near = swap_core(kv_shard)
     out_far = swap_x(after(output_weight, kv_near))
     out_near = swap_core(after(output_weight, kv_near))
-    wide_got = far_halves(gate_weight, up_weight, out_far)
+    wide_sent = after(far_halves(*(after(v, query_near) for v in (gate_weight, up_weight))), query_near)
+    wide_got = swap_x(after(wide_sent, kv_far))
 
     tokens, block_order = (after(v, query_near) for v in (tokens, block_order))
     all_ids = jnp.arange(group_rows, dtype=jnp.int32)
@@ -727,15 +791,19 @@
         jnp.concatenate([p[i : i + gain_at - block_d].reshape(-1) for p in kv_pieces]).astype(F32)
         for i in (block_d, gain_at)
     )
-    normed, key_value = project_kv(tokens, scale_one, cos_table, sin_table, kv_pieces)
+    normed, key_value = project_kv(
+        tokens, after(scale_one, wide_sent), cos_table, sin_table, kv_pieces
+    )
     if two_ctx():
-        key_values = (key_value, swap_ctx(key_value))
+        other_kv = swap_ctx(key_value)
     else:
-        key_values = (lax.all_gather(key_value, "ctx", axis=0, tiled=True),)
+        other_kv = lax.all_gather(key_value, "ctx", axis=0, tiled=True)
     query_pieces = [query_weight, query_far, query_near, swap_core(query_far)]
     queries = project_q(normed, cos_table, sin_table, query_pieces)
+    other_kv = after(other_kv, queries)
+    key_values = (key_value, other_kv) if two_ctx() else (other_kv,)
     attended, log_total = attend_forward(queries, key_values, key_code, query_codes)
-    out_far = after(out_far, queries)
+    out_far = after(out_far, queries, key_values[-1])
     out_pieces = [output_weight, out_far, out_near, swap_core(out_far)]
     branch = out_project(attended, out_pieces)
     grad_out = relative(after(cotangent, log_total)).astype(F32)
@@ -765,14 +833,13 @@
     )
     wait = down_last
     branch = after(branch, wait)
-    middle = inputs + RESIDUAL * branch.astype(F32)
-
+    normed_two, hidden, grad_gate, grad_up, grad_two = mlp(
+        tokens, branch, gain_two, grad_mlp, lax.axis_index("ctx")[None], gates, ups, downs
+    )
+    two_part = grad_two
+    grad_two = psum_tensor(grad_two)
+    middle = inputs + RESIDUAL * after(branch, hidden).astype(F32)
     scale_two = norm_scale(middle)
-    normed_two = (middle * scale_two * gain_two).astype(BF)
-    hidden, grad_gate, grad_up, grad_two = mlp(
-        normed_two, grad_mlp, lax.axis_index("ctx")[None], gates, ups, downs
-    )
-    grad_two = psum_tensor(grad_two)
 
     def begin(hidden, normed_two, grad_mlp, grad_gate, grad_up, *downs):
         down_sum = outer_sum(hidden, grad_mlp, False, "down_outer")
@@ -794,7 +861,6 @@
     up_sum.cross(up_begun, grad_two)
     grad_two = grad_two.astype(F32)
 
-    gain_two_part = jnp.sum(grad_two * middle * scale_two, axis=0)
     grad_middle = grad_out + norm_back(middle, scale_two, gain_two, grad_two)
     grad_branch = (RESIDUAL * grad_middle).astype(BF)
     query_low, key_value_parts = attend_backward(
@@ -831,19 +897,31 @@
     begun = sealed(lambda *v: entry_term(*v).begin(), *entry_inputs)
     entry_sum = entry_term(*entry_inputs).cross(begun, gate_sum.low)
     mlp_sum = after(mlp_sum, qkv_low, down_sum.peer, gate_sum.low, up_sum.fold(qkv_low).low, entry_sum.sent)
+    gains = jnp.stack(
+        [
+            jnp.sum(grad_one.astype(F32) * inputs * scale_one, axis=0),
+            jnp.sum(two_part.astype(F32) * middle * scale_two, axis=0),
+        ]
+    )
     grad_one = psum_tensor(after(grad_one, mlp_sum))
 
 
     up_sum.swap()
 
-    def finish(middle, mlp_sum, *values):
+    def finish(gains, middle, mlp_sum, *values):
+        gains = sum_everywhere(gains)
         entry_sum = entry_term(*values[:4]).joined(*values[4:6]).fold().swap()
         layer_out = absolute((middle + RESIDUAL * mlp_sum.astype(F32)).astype(BF))
         totals = (combine(*values[i : i + 2]) for i in (6, 8, 10))
-        return layer_out, *totals, entry_sum.result()
-
-    layer_out, down_grad, gate_grad, up_grad, entry_total = sealed(
+        parts = (
+            combine(entry_sum.low[:, at], entry_sum.peer[:, at])
+            for at in (slice(0, block_d), slice(block_d, None))
+        )
+        return gains, layer_out, *totals, *parts
+
+    gain_grad, layer_out, down_grad, gate_grad, up_grad, output_grad, qkv_grad = sealed(
         finish,
+        gains,
         middle,
         mlp_sum,
         *entry_inputs,
@@ -856,19 +934,12 @@
         up_sum.low,
         up_sum.peer,
     )
-    grad_one = after(grad_one, down_grad)
-    output_grad, qkv_grad = entry_total[:, :block_d], entry_total[:, block_d:]
-    grad_one = grad_one.astype(F32)
-    gain_one_part = jnp.sum(grad_one * inputs * scale_one, axis=0)
-    tokens_grad = absolute(
-        (grad_middle + norm_back(inputs, scale_one, gain_one, grad_one)).astype(BF)
-    )
-    gain_blocks = split4(jnp.stack([gain_one_part, gain_two_part]), 1)
-    gain_grad = sum_ctx(
-        gain_blocks[0]
-        + swap_x(gain_blocks[1])
-        + swap_core(gain_blocks[2])
-        + swap_both(gain_blocks[3])
+    tokens_grad = exit_grad(
+        lax.axis_index("dp")[None],
+        grad_middle,
+        after(grad_one, down_grad),
+        tokens,
+        gain_one,
     )
     return (
         layer_out,

time: 485 us -> 470 us (0.969)
  waiting for transfers between devices: 227 us -> 213 us
  Pallas kernels: 128 us -> 139 us
  other arithmetic: 52.4 us -> 43.1 us
    ppermute x10, waiting for transfers between devices: 107 us -> 97.3 us  [swap_x(): return lax.ppermute(value, 'dp', [(i, i ^ 2) for i in range(4)])]
    ppermute x0 -> x2, waiting for transfers between devices: none -> 7.1 us  [sum_everywhere(): lax.ppermute(total, 'tensor', [(i, i ^ bit) for i in range(4)])]
    pallas_call x0 -> x1, Pallas kernels: none -> 5.83 us  [exit_grad(): pl.pallas_call(exit_kernel, grid_spec=pltpu.PrefetchScalarGridSpec(num_sc...]
    ppermute x8, waiting for transfers between devices: 68.8 us -> 63.8 us  [swap_ctx(): return lax.ppermute(value, 'ctx', [(0, 1), (1, 0)])]
    psum x4, waiting for transfers between devices: 34 us -> 29.1 us  [psum_tensor(): return lax.psum(value, 'tensor')]
    add x3 -> x4, other arithmetic: 16.9 us -> 17.9 us  [combine(): return low.astype(F32) + peer.astype(F32)]
  transfers between devices with their start and end apart: 40 -> 42, of which waited for: 23 -> 24; matrix products, arithmetic and copies ran while one was open for 12% -> 12% of each run, Pallas kernels for 20% -> 21%
where the time goes in v4:
time: 470 us; the launch traced here: 462 us
  waiting for transfers between devices  213 us (45%)
  Pallas kernels  139 us (30%)
  other arithmetic  43.1 us (9%)
  starting transfers between devices  32 us (7%)
  local copies, waits for them, and re-layouts  19.1 us (4%)
  between operations  15.4 us (3%)
    ppermute x10, waiting for transfers between devices, swap_x(): return lax.ppermute(value, 'dp', [(i, i ^ 2) for i in range(4)])  97.3 us
    ppermute x8, waiting for transfers between devices, swap_ctx(): return lax.ppermute(value, 'ctx', [(0, 1), (1, 0)])  63.8 us
    pallas_call x1, Pallas kernels, mlp(): pl.pallas_call(functools.partial(mlp_kernel, len(gates) > 4), grid_spec=p...  36.7 us
    pallas_call x9, Pallas kernels, outer(): pl.pallas_call(functools.partial(outer_kernel, len(adds)), grid=(count_m,...  35.2 us
    psum x4, waiting for transfers between devices, psum_tensor(): return lax.psum(value, 'tensor')  29.1 us
    add x4, other arithmetic, combine(): return low.astype(F32) + peer.astype(F32)  17.9 us
    pallas_call x1, Pallas kernels, attend_backward(): pl.pallas_call(functools.partial(backward_kernel, chunk, len(key_values))...  16.9 us
    ppermute x17, waiting for transfers between devices, swap_core(): return lax.ppermute(value, 'dp', [(i, i ^ 1) for i in range(4)])  16 us
  transfers between devices with their start and end apart: 42, of which 24 were waited for; matrix products, arithmetic and copies ran while one was open for 12% of the time, Pallas kernels for 21%

profile of v4, /device:TPU:0, one launch (start us, length us, event | category | flops | bytes accessed | tf_op | source)
XLA Modules:
  0.0 462.0 jit_solution(5410412218750017478)
XLA Ops:
  45.9 8.6 %attend_forward.1 = (bf16[512,512]{1,0:T(8,128)(2,1)S(1)}, f32[8,512]{1,0:T(8,128)S(1)}) custom-call(bf16[512,512]{1,0:T(8,128)(2,1)S(1)} %project_q.1.q_ref, s32[1024,1]{1,0:T(8,128)S(1)} %get-tuple-element.288.code_ref, s32[8,512]{1,0:T(8,128)S(1)} %stack.41.codes_ref, bf16[512,256]{1,0:T(8,128)(2,1)S(1)} %copy-done.17, ...), custom_call_target="tpu_custom_call" | custom-call | flops 1 | bytes 1 | tf_op jit(solution)/shard_map/attend_forward/pallas_call | solution.py:98
  55.9 4.1 out_project.1
  65.7 26.2 %collective-permute-done.29.refs_1_.refs_7_ = bf16[512,2048]{1,0:T(8,128)(2,1)} collective-permute-done((bf16[512,2048]{1,0:T(8,128)(2,1)}, bf16[512,2048]{1,0:T(8,128)(2,1)}, u32[]{:S(2)}, u32[]{:S(2)}) %collective-permute-start.29) | collective-permute-done | bytes 2097184 | tf_op jit(solution)/shard_map/ppermute | solution.py:570
  92.0 48.5 %conditional.5 = (bf16[512,2048]{1,0:T(8,128)(2,1)}, bf16[512,2048]{1,0:T(8,128)(2,1)}, bf16[512,2048]{1,0:T(8,128)(2,1)}, bf16[512,2048]{1,0:T(8,128)(2,1)}, bf16[2048,512]{1,0:T(8,128)(2,1)}) conditional(s32[]{:T(128)} %convert_element_type.96, () %tuple.96, (bf16[512,2048]{1,0:T(8,128)(2,1)}, bf16[512,2048]{1,0:T(8,128)(2,1)S(1)}, ...), branch_computations={%region_3.4_spmd, %region_4.5_spmd} | conditional | bytes 41943280 | solution.py:562
  96.8 43.6 %collective-permute-done = bf16[512,2048]{1,0:T(8,128)(2,1)} collective-permute-done((bf16[512,2048]{1,0:T(8,128)(2,1)}, bf16[512,2048]{1,0:T(8,128)(2,1)}, u32[]{:S(2)}, u32[]{:S(2)}) %collective-permute-start) | collective-permute-done | bytes 2097184 | tf_op jit(solution)/shard_map/cond/branch_1_fun/ppermute | solution.py:578
  140.4 7.6 %conditional.6 = (bf16[512,2048]{1,0:T(8,128)(2,1)}, bf16[2048,512]{1,0:T(8,128)(2,1)}) conditional(s32[]{:T(128)} %convert_element_type.96, () %tuple.95, (bf16[512,2048]{1,0:T(8,128)(2,1)}, bf16[2048,512]{1,0:T(8,128)(2,1)}) %tuple.101), branch_computations={%region_5.6_spmd, %region_6.7_spmd} | conditional | bytes 16777312 | solution.py:562
  141.0 4.0 collective-permute-done.5
  148.1 36.7 %mlp.1 = (bf16[512,2048]{1,0:T(8,128)(2,1)S(1)}, bf16[512,2048]{1,0:T(8,128)(2,1)}, bf16[512,2048]{1,0:T(8,128)(2,1)}, bf16[512,2048]{1,0:T(8,128)(2,1)}, bf16[512,2048]{1,0:T(8,128)(2,1)}) custom-call(s32[1]{0:T(128)} %bitcast.9.index_ref, bf16[512,2048]{1,0:T(8,128)(2,1)} %copy-done, bf16[512,2048]{1,0:T(8,128)(2,1)} %all-reduce.6.cloned.1.call-done.branch_ref, ...), custom_call_target="tpu_custom_call" | custom-call | flops 1 | bytes 1 | tf_op jit(solution)/shard_map/mlp/pallas_call | solution.py:354
  186.3 65.6 %conditional.7 = (bf16[2048,512]{1,0:T(8,128)(2,1)}, bf16[1024,2048]{1,0:T(8,128)(2,1)}, bf16[512,2048]{1,0:T(8,128)(2,1)}, bf16[1024,2048]{1,0:T(8,128)(2,1)}, ...) conditional(s32[]{:T(128)} %convert_element_type.96, () %tuple.104, (bf16[512,2048]{1,0:T(8,128)(2,1)}, ...), branch_computations={%region_9.10_spmd, %region_10.11_spmd} | conditional | flops 8 | bytes 100663640 | solution.py:562
  186.3 4.9 %down_outer.3 = bf16[2048,1024]{1,0:T(8,128)(2,1)S(1)} custom-call(bf16[512,2048]{1,0:T(8,128)(2,1)} %get-tuple-element.83.a_ref.hidden_ref, bf16[512,2048]{1,0:T(8,128)(2,1)} %get-tuple-element.84.b_ref), custom_call_target="tpu_custom_call" | custom-call | flops 1 | bytes 1 | tf_op jit(solution)/shard_map/cond/branch_1_fun/down_outer/pallas_call | solution.py:432
  202.4 11.4 %lift.1 = bf16[512,2048]{1,0:T(8,128)(2,1)} custom-call(bf16[512,2048]{1,0:T(8,128)(2,1)S(1)} %copy-done.30, bf16[2048,512]{1,0:T(8,128)(2,1)S(1)} %copy-done.41, bf16[2048,512]{1,0:T(8,128)(2,1)} %get-tuple-element.89.d1, bf16[2048,512]{1,0:T(8,128)(2,1)} %get-tuple-element.90.d2, bf16[2048,512]{1,0:T(8,128)(2,1)} %get-tuple-element.91.d3), custom_call_target="tpu_custom_call" | custom-call | flops 1 | bytes 1 | tf_op jit(solution)/shard_map/cond/branch_1_fun/lift/pallas_call | solution.py:468
  213.8 4.2 gate_outer.4
  218.0 4.2 up_outer.4
  222.2 26.2 %collective-permute-done.8.refs_1_ = bf16[2048,512]{1,0:T(8,128)(2,1)S(1)} collective-permute-done((bf16[2048,512]{1,0:T(8,128)(2,1)S(1)}, bf16[2048,512]{1,0:T(8,128)(2,1)S(1)}, u32[]{:S(2)}, u32[]{:S(2)}) %collective-permute-start.8) | collective-permute-done | bytes 2097184 | tf_op jit(solution)/shard_map/cond/branch_1_fun/ppermute | solution.py:570
  255.0 18.0 %all-reduce.8.cloned.1.call-done = bf16[512,2048]{1,0:T(8,128)(2,1)} async-done(((bf16[512,2048]{1,0:T(8,128)(2,1)}), bf16[512,2048]{1,0:T(8,128)(2,1)}) %all-reduce.8.cloned.1.call-update) | async-done | bytes 2097168 | tf_op jit(solution)/shard_map/psum | solution.py:601
  278.5 4.8 %multiply_convert_fusion = (bf16[512,2048]{1,0:T(8,128)(2,1)S(1)}, f32[512,2048]{1,0:T(8,128)}, f32[512,2048]{1,0:T(8,128)}) fusion(f32[512]{0:T(512)S(1)} %broadcast_multiply_fusion.1, f32[512]{0:T(512)S(1)} %get-tuple-element.307, bf16[512,2048]{1,0:T(8,128)(2,1)S(1)} %copy-done.29, bf16[512,2048]{1,0:T(8,128)(2,1)S(1)} %copy-done.1, ...), kind=kLoop, calls=%fused_computation.22 | loop fusion | flops 22020096 | bytes 18888704 | tf_op jit(solution)/shard_map/convert_element_type | solution.py:865
  283.3 16.9 %attend_backward.1 = (bf16[512,512]{1,0:T(8,128)(2,1)S(1)}, f32[1024,256]{1,0:T(8,128)S(1)}) custom-call(bf16[512,512]{1,0:T(8,128)(2,1)S(1)} %project_q.1.q_ref, s32[1024,1]{1,0:T(8,128)S(1)} %get-tuple-element.288.code_ref, s32[8,512]{1,0:T(8,128)S(1)} %stack.41.codes_ref, bf16[512,512]{1,0:T(8,128)(2,1)S(1)} %copy-done.38, ...), custom_call_target="tpu_custom_call" | custom-call | flops 1 | bytes 1 | tf_op jit(solution)/shard_map/attend_backward/pallas_call | solution.py:186
  301.9 5.0 %gate_outer.5 = bf16[512,2048]{1,0:T(8,128)(2,1)} custom-call(bf16[512,2048]{1,0:T(8,128)(2,1)S(1)} %copy-done.24, bf16[512,2048]{1,0:T(8,128)(2,1)S(1)} %copy-done.34, bf16[1024,2048]{1,0:T(8,128)(2,1)} %get-tuple-element.229.refs_0_, bf16[512,2048]{1,0:T(8,128)(2,1)} %collective-permute-done.33.refs_1_), custom_call_target="tpu_custom_call" | custom-call | flops 1 | bytes 1 | tf_op jit(solution)/shard_map/gate_outer/pallas_call | solution.py:432
  308.9 5.7 %entry_grad.1 = (bf16[512,768]{1,0:T(8,128)(2,1)S(1)}, bf16[512,2048]{1,0:T(8,128)(2,1)}) custom-call(bf16[512,512]{1,0:T(8,128)(2,1)} %copy-done.22, f32[512,256]{1,0:T(8,128)} %slice.103.own_ref, bf16[512,256]{1,0:T(8,128)(2,1)} %copy-done.57, f32[512,128]{1,0:T(8,128)} %copy-done.2, f32[512,128]{1,0:T(8,128)} %copy-done.3, bf16[512,512]{1,0:T(8,128)(2,1)} %refs_0_.3, ...), custom_call_target="tpu_custom_call" | custom-call | flops 1 | bytes 1 | tf_op jit(solution)/shard_map/entry_grad/pallas_call | solution.py:395
  316.0 11.7 %conditional.8 = (bf16[1024,1280]{1,0:T(8,128)(2,1)}, bf16[512,1280]{1,0:T(8,128)(2,1)}) conditional(s32[]{:T(128)} %convert_element_type.96, () %tuple.111, (bf16[512,512]{1,0:T(8,128)(2,1)S(1)}, bf16[512,2048]{1,0:T(8,128)(2,1)}, bf16[512,2048]{1,0:T(8,128)(2,1)}, bf16[512,768]{1,0:T(8,128)(2,1)S(1)}) %tuple.180), branch_computations={%region_14.15_spmd, %region_15.16_spmd} | conditional | flops 2 | bytes 27263088 | solution.py:562
  319.3 5.0 %collective-permute-done.11.refs_0_ = bf16[1024,1280]{1,0:T(8,128)(2,1)} collective-permute-done((bf16[1024,1280]{1,0:T(8,128)(2,1)S(1)}, bf16[1024,1280]{1,0:T(8,128)(2,1)}, u32[]{:S(2)}, u32[]{:S(2)}) %collective-permute-start.11) | collective-permute-done | bytes 2621472 | tf_op jit(solution)/shard_map/cond/branch_1_fun/ppermute | solution.py:566
  327.7 4.0 fusion.3
  332.0 12.1 %collective-permute-done.34.refs_1_ = bf16[512,2048]{1,0:T(8,128)(2,1)} collective-permute-done((bf16[512,2048]{1,0:T(8,128)(2,1)}, bf16[512,2048]{1,0:T(8,128)(2,1)}, u32[]{:S(2)}, u32[]{:S(2)}) %collective-permute-start.34) | collective-permute-done | bytes 2097184 | tf_op jit(solution)/shard_map/ppermute | solution.py:570
  344.1 5.8 %up_outer.5 = bf16[512,2048]{1,0:T(8,128)(2,1)} custom-call(bf16[512,2048]{1,0:T(8,128)(2,1)} %copy-done.23, bf16[512,2048]{1,0:T(8,128)(2,1)} %get-tuple-element.220.b_ref, bf16[1024,2048]{1,0:T(8,128)(2,1)} %get-tuple-element.232.refs_0_, bf16[512,2048]{1,0:T(8,128)(2,1)} %collective-permute-done.34.refs_1_), custom_call_target="tpu_custom_call" | custom-call | flops 1 | bytes 1 | tf_op jit(solution)/shard_map/up_outer/pallas_call | solution.py:432
  351.5 9.3 %all-reduce.10.cloned.1.call-done = bf16[512,2048]{1,0:T(8,128)(2,1)} async-done(((bf16[512,2048]{1,0:T(8,128)(2,1)}), bf16[512,2048]{1,0:T(8,128)(2,1)}) %all-reduce.10.cloned.1.call-update) | async-done | bytes 2097168 | tf_op jit(solution)/shard_map/psum | solution.py:601
  363.0 28.6 %collective-permute-done.37 = bf16[512,1280]{1,0:T(8,128)(2,1)S(1)} collective-permute-done((bf16[512,1280]{1,0:T(8,128)(2,1)}, bf16[512,1280]{1,0:T(8,128)(2,1)S(1)}, u32[]{:S(2)}, u32[]{:S(2)}) %collective-permute-start.37) | collective-permute-done | bytes 1310752 | tf_op jit(solution)/shard_map/ppermute | solution.py:570
  391.6 14.5 %collective-permute-done.36 = bf16[512,2048]{1,0:T(8,128)(2,1)} collective-permute-done((bf16[512,2048]{1,0:T(8,128)(2,1)}, bf16[512,2048]{1,0:T(8,128)(2,1)}, u32[]{:S(2)}, u32[]{:S(2)}) %collective-permute-start.36) | collective-permute-done | bytes 2097184 | tf_op jit(solution)/shard_map/ppermute | solution.py:578
  406.2 41.6 %conditional.9 = (f32[2,512]{1,0:T(2,128)}, bf16[512,2048]{1,0:T(8,128)(2,1)}, f32[2048,512]{1,0:T(8,128)}, f32[512,2048]{1,0:T(8,128)}, f32[512,2048]{1,0:T(8,1...) conditional(s32[]{:T(128)} %convert_element_type.96, () %tuple.83, ...), branch_computations={%region_17.18_spmd, %region_18.19_spmd} | conditional | flops 23995432 | bytes 92607496 | solution.py:562
  412.2 8.4 %convert_add_fusion = (f32[512,2048]{1,0:T(8,128)}, f32[512,2048]{1,0:T(8,128)}) fusion(bf16[512,2048]{1,0:T(8,128)(2,1)} %get-tuple-element.107, bf16[512,2048]{1,0:T(8,128)(2,1)} %get-tuple-element.106, bf16[512,2048]{1,0:T(8,128)(2,1)} %get-tuple-element.105, bf16[512,2048]{1,0:T(8,128)(2,1)S(1)} %copy-done.42), kind=kLoop, calls=%fused_computation | loop fusion | flops 6291456 | bytes 16777216 | tf_op jit(solution)/shard_map/cond/branch_1_fun/add | solution.py:674
  423.2 4.9 %convert_add_fusion.2 = f32[2048,512]{1,0:T(8,128)} fusion(bf16[2048,512]{1,0:T(8,128)(2,1)} %get-tuple-element.103, bf16[2048,512]{1,0:T(8,128)(2,1)} %get-tuple-element.102), kind=kLoop, calls=%fused_computation.2 | loop fusion | flops 3145728 | bytes 8388608 | tf_op jit(solution)/shard_map/cond/branch_1_fun/add | solution.py:674
  428.4 4.4 collective-permute-done.16
  449.4 5.8 %exit_grad.1 = bf16[512,2048]{1,0:T(8,128)(2,1)} custom-call(s32[1]{0:T(128)} %bitcast.12.index_ref, f32[512,2048]{1,0:T(8,128)} %get-tuple-element.258.middle_ref, bf16[512,2048]{1,0:T(8,128)(2,1)} %all-reduce.12.cloned.1.call-done.dh_ref, bf16[512,2048]{1,0:T(8,128)(2,1)} %copy-done, f32[1,2048]{1,0:T(1,128)} %maximum_convert_fusion.1.gain_ref), custom_call_target="tpu_custom_call" | custom-call | flops 1 | bytes 1 | tf_op jit(solution)/shard_map/exit_grad/pallas_call | solution.py:539
  (281 shorter events, 119.0 us)
Async XLA Ops:
  7.2 141.0 %all-reduce.6.cloned.1.call-start = ((), (), s32[]{:S(2)}) async-start(), calls=%async_computation | async-start | bytes 4194304 | tf_op jit(solution)/shard_map/psum | solution.py:601
  7.7 15.7 %collective-permute-start.23 = (bf16[512,512]{1,0:T(8,128)(2,1)}, bf16[512,512]{1,0:T(8,128)(2,1)}, u32[]{:S(2)}, u32[]{:S(2)}) collective-permute-start(bf16[512,512]{1,0:T(8,128)(2,1)} %refs_0_.3), channel_id=1, source_target_pairs={{0,16},{8,24},{16,0},{24,8},{1,17},{9,25},{17,1},{25,9},{2,18},{10... | collective-permute-start | bytes 1572872 | tf_op jit(solution)/shard_map/ppermute | solution.py:570
  13.6 15.7 %collective-permute-start.20 = (bf16[544,256]{1,0:T(8,128)(2,1)S(1)}, bf16[544,256]{1,0:T(8,128)(2,1)}, u32[]{:S(2)}, u32[]{:S(2)}) collective-permute-start(bf16[544,256]{1,0:T(8,128)(2,1)S(1)} %fusion.13.p0.refs_4_), channel_id=1, source_target_pairs={{0,16},{8,24},{16,0},{24,8},{1,17},{9,25},{17,1},{25,9},{2,18},{10... | collective-permute-start | bytes 835592 | tf_op jit(solution)/shard_map/ppermute | solution.py:570
  13.7 9.8 %collective-permute-start.21 = (bf16[544,256]{1,0:T(8,128)(2,1)S(1)}, bf16[544,256]{1,0:T(8,128)(2,1)S(1)}, u32[]{:S(2)}, u32[]{:S(2)}) collective-permute-start(bf16[544,256]{1,0:T(8,128)(2,1)S(1)} %fusion.13.p0.refs_4_), channel_id=1, source_target_pairs={{0,8},{8,0},{16,24},{24,16},{1,9},{9,1},{17,25},{25,17},{2,10},{10... | collective-permute-start | bytes 835592 | tf_op jit(solution)/shard_map/ppermute | solution.py:566
  23.4 12.9 %collective-permute-start.24 = (bf16[512,512]{1,0:T(8,128)(2,1)}, bf16[512,512]{1,0:T(8,128)(2,1)S(1)}, u32[]{:S(2)}, u32[]{:S(2)}) collective-permute-start(bf16[512,512]{1,0:T(8,128)(2,1)} %collective-permute-done.23.p1.refs_1_), channel_id=1, source_target_pairs={{0,8},{8,0},{16,24},{24,16},{1,9},{9,1},{17,25},{25,17},{2,10},{10... | collective-permute-start | bytes 1572872 | tf_op jit(solution)/shard_map/ppermute | solution.py:566
  23.5 19.6 %collective-permute-start.26 = (bf16[512,512]{1,0:T(8,128)(2,1)}, bf16[512,512]{1,0:T(8,128)(2,1)}, u32[]{:S(2)}, u32[]{:S(2)}) collective-permute-start(bf16[512,512]{1,0:T(8,128)(2,1)} %o0.3), channel_id=1, source_target_pairs={{0,16},{8,24},{16,0},{24,8},{1,17},{9,25},{17,1},{25,9},{2,18},{10... | collective-permute-start | bytes 1572872 | tf_op jit(solution)/shard_map/ppermute | solution.py:570
  34.3 8.8 %collective-permute-start.25 = (bf16[512,256]{1,0:T(8,128)(2,1)S(1)}, bf16[512,256]{1,0:T(8,128)(2,1)S(1)}, u32[]{:S(2)}, u32[]{:S(2)}) collective-permute-start(bf16[512,256]{1,0:T(8,128)(2,1)S(1)} %get-tuple-element.197.refs_0_), channel_id=1, source_target_pairs={{0,4},{4,0},{1,5},{5,1},{2,6},{6,2},{3,7},{7,3},{8,12},{12,8},{9,1... | collective-permute-start | bytes 786440 | tf_op jit(solution)/shard_map/ppermute | solution.py:578
  36.3 18.6 %collective-permute-start.27 = (bf16[512,512]{1,0:T(8,128)(2,1)}, bf16[512,512]{1,0:T(8,128)(2,1)S(1)}, u32[]{:S(2)}, u32[]{:S(2)}) collective-permute-start(bf16[512,512]{1,0:T(8,128)(2,1)} %o0.3), channel_id=1, source_target_pairs={{0,8},{8,0},{16,24},{24,16},{1,9},{9,1},{17,25},{25,17},{2,10},{10... | collective-permute-start | bytes 1572872 | tf_op jit(solution)/shard_map/ppermute | solution.py:566
  43.1 11.8 %collective-permute-start.28 = (bf16[512,512]{1,0:T(8,128)(2,1)}, bf16[512,512]{1,0:T(8,128)(2,1)S(1)}, u32[]{:S(2)}, u32[]{:S(2)}) collective-permute-start(bf16[512,512]{1,0:T(8,128)(2,1)} %collective-permute-done.26.o1), channel_id=1, source_target_pairs={{0,8},{8,0},{16,24},{24,16},{1,9},{9,1},{17,25},{25,17},{2,10},{10... | collective-permute-start | bytes 1572872 | tf_op jit(solution)/shard_map/ppermute | solution.py:566
  43.2 48.8 %collective-permute-start.29 = (bf16[512,2048]{1,0:T(8,128)(2,1)}, bf16[512,2048]{1,0:T(8,128)(2,1)}, u32[]{:S(2)}, u32[]{:S(2)}) collective-permute-start(bf16[512,2048]{1,0:T(8,128)(2,1)} %pad_maximum_fusion.2), channel_id=1, source_target_pairs={{0,16},{8,24},{16,0},{24,8},{1,17},{9,25},{17,1},{25,9},{2,18},{10... | collective-permute-start | bytes 6291464 | tf_op jit(solution)/shard_map/ppermute | solution.py:570
  54.5 85.9 %collective-permute-start.30 = (bf16[2048,512]{1,0:T(8,128)(2,1)}, bf16[2048,512]{1,0:T(8,128)(2,1)}, u32[]{:S(2)}, u32[]{:S(2)}) collective-permute-start(bf16[2048,512]{1,0:T(8,128)(2,1)} %refs_12_.1), channel_id=1, source_target_pairs={{0,16},{8,24},{16,0},{24,8},{1,17},{9,25},{17,1},{25,9},{2,18},{10... | collective-permute-start | bytes 6291464 | tf_op jit(solution)/shard_map/ppermute | solution.py:570
  60.0 212.9 %all-reduce.8.cloned.1.call-start = ((), (), s32[]{:S(2)}) async-start(), calls=%async_computation.1 | async-start | bytes 4194304 | tf_op jit(solution)/shard_map/psum | solution.py:601
  92.1 48.4 %collective-permute-start = (bf16[512,2048]{1,0:T(8,128)(2,1)}, bf16[512,2048]{1,0:T(8,128)(2,1)}, u32[]{:S(2)}, u32[]{:S(2)}) collective-permute-start(bf16[512,2048]{1,0:T(8,128)(2,1)} %get-tuple-element.78), channel_id=1, source_target_pairs={{0,4},{4,0},{1,5},{5,1},{2,6},{6,2},{3,7},{7,3},{8,12},{12,8},{9,1... | collective-permute-start | bytes 6291464 | tf_op jit(solution)/shard_map/cond/branch_1_fun/ppermute | solution.py:578
  93.9 46.6 %collective-permute-start.2 = (bf16[512,2048]{1,0:T(8,128)(2,1)S(1)}, bf16[512,2048]{1,0:T(8,128)(2,1)}, u32[]{:S(2)}, u32[]{:S(2)}) collective-permute-start(bf16[512,2048]{1,0:T(8,128)(2,1)S(1)} %get-tuple-element.77), channel_id=1, source_target_pairs={{0,8},{8,0},{16,24},{24,16},{1,9},{9,1},{17,25},{25,17},{2,10},{10... | collective-permute-start | bytes 6291464 | tf_op jit(solution)/shard_map/cond/branch_1_fun/ppermute | solution.py:566
  96.3 44.1 %collective-permute-start.3 = (bf16[512,2048]{1,0:T(8,128)(2,1)}, bf16[512,2048]{1,0:T(8,128)(2,1)}, u32[]{:S(2)}, u32[]{:S(2)}) collective-permute-start(bf16[512,2048]{1,0:T(8,128)(2,1)} %get-tuple-element.78), channel_id=1, source_target_pairs={{0,8},{8,0},{16,24},{24,16},{1,9},{9,1},{17,25},{25,17},{2,10},{10... | collective-permute-start | bytes 6291464 | tf_op jit(solution)/shard_map/cond/branch_1_fun/ppermute | solution.py:566
  96.5 44.0 %collective-permute-start.4 = (bf16[2048,512]{1,0:T(8,128)(2,1)S(1)}, bf16[2048,512]{1,0:T(8,128)(2,1)}, u32[]{:S(2)}, u32[]{:S(2)}) collective-permute-start(bf16[2048,512]{1,0:T(8,128)(2,1)S(1)} %get-tuple-element.80), channel_id=1, source_target_pairs={{0,8},{8,0},{16,24},{24,16},{1,9},{9,1},{17,25},{25,17},{2,10},{10... | collective-permute-start | bytes 6291464 | tf_op jit(solution)/shard_map/cond/branch_1_fun/ppermute | solution.py:566
  140.5 7.5 %collective-permute-start.6 = (bf16[2048,512]{1,0:T(8,128)(2,1)}, bf16[2048,512]{1,0:T(8,128)(2,1)}, u32[]{:S(2)}, u32[]{:S(2)}) collective-permute-start(bf16[2048,512]{1,0:T(8,128)(2,1)} %get-tuple-element.82), channel_id=1, source_target_pairs={{0,8},{8,0},{16,24},{24,16},{1,9},{9,1},{17,25},{25,17},{2,10},{10... | collective-permute-start | bytes 6291464 | tf_op jit(solution)/shard_map/cond/branch_1_fun/ppermute | solution.py:566
  184.9 175.9 %all-reduce.10.cloned.1.call-start = ((), (), s32[]{:S(2)}) async-start(), calls=%async_computation.2 | async-start | bytes 4194304 | tf_op jit(solution)/shard_map/psum | solution.py:601
  191.2 7.2 %collective-permute-start.7 = (bf16[2048,1024]{1,0:T(8,128)(2,1)S(1)}, bf16[2048,1024]{1,0:T(8,128)(2,1)S(1)}, u32[]{:S(2)}, u32[]{:S(2)}) collective-permute-start(bf16[2048,1024]{1,0:T(8,128)(2,1)S(1)} %down_outer.3), channel_id=1, source_target_pairs={{0,8},{8,0},{16,24},{24,16},{1,9},{9,1},{17,25},{25,17},{2,10},{10... | collective-permute-start | bytes 12582920 | tf_op jit(solution)/shard_map/cond/branch_1_fun/ppermute | solution.py:566
  194.0 19.8 %collective-permute-start.9 = (bf16[1024,2048]{1,0:T(8,128)(2,1)S(1)}, bf16[1024,2048]{1,0:T(8,128)(2,1)}, u32[]{:S(2)}, u32[]{:S(2)}) collective-permute-start(bf16[1024,2048]{1,0:T(8,128)(2,1)S(1)} %gate_outer.3), channel_id=1, source_target_pairs={{0,8},{8,0},{16,24},{24,16},{1,9},{9,1},{17,25},{25,17},{2,10},{10... | collective-permute-start | bytes 12582920 | tf_op jit(solution)/shard_map/cond/branch_1_fun/ppermute | solution.py:566
  197.2 20.8 %collective-permute-start.10 = (bf16[1024,2048]{1,0:T(8,128)(2,1)S(1)}, bf16[1024,2048]{1,0:T(8,128)(2,1)}, u32[]{:S(2)}, u32[]{:S(2)}) collective-permute-start(bf16[1024,2048]{1,0:T(8,128)(2,1)S(1)} %up_outer.3), channel_id=1, source_target_pairs={{0,8},{8,0},{16,24},{24,16},{1,9},{9,1},{17,25},{25,17},{2,10},{10... | collective-permute-start | bytes 12582920 | tf_op jit(solution)/shard_map/cond/branch_1_fun/ppermute | solution.py:566
  200.7 47.7 %collective-permute-start.8 = (bf16[2048,512]{1,0:T(8,128)(2,1)S(1)}, bf16[2048,512]{1,0:T(8,128)(2,1)S(1)}, u32[]{:S(2)}, u32[]{:S(2)}) collective-permute-start(bf16[2048,512]{1,0:T(8,128)(2,1)S(1)} %down_outer.4), channel_id=1, source_target_pairs={{0,16},{8,24},{16,0},{24,8},{1,17},{9,25},{17,1},{25,9},{2,18},{10... | collective-permute-start | bytes 6291464 | tf_op jit(solution)/shard_map/cond/branch_1_fun/ppermute | solution.py:570
  251.9 50.0 %collective-permute-start.33 = (bf16[512,2048]{1,0:T(8,128)(2,1)}, bf16[512,2048]{1,0:T(8,128)(2,1)}, u32[]{:S(2)}, u32[]{:S(2)}) collective-permute-start(bf16[512,2048]{1,0:T(8,128)(2,1)} %get-tuple-element.230), channel_id=1, source_target_pairs={{0,16},{8,24},{16,0},{24,8},{1,17},{9,25},{17,1},{25,9},{2,18},{10... | collective-permute-start | bytes 6291464 | tf_op jit(solution)/shard_map/ppermute | solution.py:570
  253.4 98.0 %collective-permute-start.32 = (bf16[2048,512]{1,0:T(8,128)(2,1)}, bf16[2048,512]{1,0:T(8,128)(2,1)}, u32[]{:S(2)}, u32[]{:S(2)}) collective-permute-start(bf16[2048,512]{1,0:T(8,128)(2,1)} %get-tuple-element.221), channel_id=1, source_target_pairs={{0,4},{4,0},{1,5},{5,1},{2,6},{6,2},{3,7},{7,3},{8,12},{12,8},{9,1... | collective-permute-start | bytes 6291464 | tf_op jit(solution)/shard_map/ppermute | solution.py:578
  272.9 71.1 %collective-permute-start.34 = (bf16[512,2048]{1,0:T(8,128)(2,1)}, bf16[512,2048]{1,0:T(8,128)(2,1)}, u32[]{:S(2)}, u32[]{:S(2)}) collective-permute-start(bf16[512,2048]{1,0:T(8,128)(2,1)} %get-tuple-element.234), channel_id=1, source_target_pairs={{0,16},{8,24},{16,0},{24,8},{1,17},{9,25},{17,1},{25,9},{2,18},{10... | collective-permute-start | bytes 6291464 | tf_op jit(solution)/shard_map/ppermute | solution.py:570
  300.3 7.8 %collective-permute-start.31 = (bf16[512,256]{1,0:T(8,128)(2,1)S(1)}, bf16[512,256]{1,0:T(8,128)(2,1)S(1)}, u32[]{:S(2)}, u32[]{:S(2)}) collective-permute-start(bf16[512,256]{1,0:T(8,128)(2,1)S(1)} %slice.151), channel_id=1, source_target_pairs={{0,4},{4,0},{1,5},{5,1},{2,6},{6,2},{3,7},{7,3},{8,12},{12,8},{9,1... | collective-permute-start | bytes 786440 | tf_op jit(solution)/shard_map/ppermute | solution.py:578
  314.5 77.1 %collective-permute-start.35 = (bf16[512,2048]{1,0:T(8,128)(2,1)}, bf16[512,2048]{1,0:T(8,128)(2,1)}, u32[]{:S(2)}, u32[]{:S(2)}) collective-permute-start(bf16[512,2048]{1,0:T(8,128)(2,1)} %gate_outer.5), channel_id=1, source_target_pairs={{0,4},{4,0},{1,5},{5,1},{2,6},{6,2},{3,7},{7,3},{8,12},{12,8},{9,1... | collective-permute-start | bytes 6291464 | tf_op jit(solution)/shard_map/ppermute | solution.py:578
  331.7 117.7 %all-reduce.12.cloned.1.call-start = ((), (), s32[]{:S(2)}) async-start(), calls=%async_computation.3 | async-start | bytes 4194304 | tf_op jit(solution)/shard_map/psum | solution.py:601
  349.9 56.3 %collective-permute-start.36 = (bf16[512,2048]{1,0:T(8,128)(2,1)}, bf16[512,2048]{1,0:T(8,128)(2,1)}, u32[]{:S(2)}, u32[]{:S(2)}) collective-permute-start(bf16[512,2048]{1,0:T(8,128)(2,1)} %up_outer.5), channel_id=1, source_target_pairs={{0,4},{4,0},{1,5},{5,1},{2,6},{6,2},{3,7},{7,3},{8,12},{12,8},{9,1... | collective-permute-start | bytes 6291464 | tf_op jit(solution)/shard_map/ppermute | solution.py:578
  360.8 30.8 %collective-permute-start.37 = (bf16[512,1280]{1,0:T(8,128)(2,1)}, bf16[512,1280]{1,0:T(8,128)(2,1)S(1)}, u32[]{:S(2)}, u32[]{:S(2)}) collective-permute-start(bf16[512,1280]{1,0:T(8,128)(2,1)} %get-tuple-element.240), channel_id=1, source_target_pairs={{0,16},{8,24},{16,0},{24,8},{1,17},{9,25},{17,1},{25,9},{2,18},{10... | collective-permute-start | bytes 3932168 | tf_op jit(solution)/shard_map/ppermute | solution.py:570
  410.6 28.4 %collective-permute-start.18 = (bf16[512,1280]{1,0:T(8,128)(2,1)S(1)}, bf16[512,1280]{1,0:T(8,128)(2,1)}, u32[]{:S(2)}, u32[]{:S(2)}) collective-permute-start(bf16[512,1280]{1,0:T(8,128)(2,1)S(1)} %entry_outer.5), channel_id=1, source_target_pairs={{0,4},{4,0},{1,5},{5,1},{2,6},{6,2},{3,7},{7,3},{8,12},{12,8},{9,1... | collective-permute-start | bytes 3932168 | tf_op jit(solution)/shard_map/cond/branch_1_fun/ppermute | solution.py:578
  411.6 9.0 %collective-permute-start.13 = (f32[2,512]{1,0:T(2,128)S(1)}, f32[2,512]{1,0:T(2,128)S(1)}, u32[]{:S(2)}, u32[]{:S(2)}) collective-permute-start(f32[2,512]{1,0:T(2,128)S(1)} %get-tuple-element.273), channel_id=1, source_target_pairs={{0,16},{8,24},{16,0},{24,8},{1,17},{9,25},{17,1},{25,9},{2,18},{10... | collective-permute-start | bytes 12296 | tf_op jit(solution)/shard_map/cond/branch_1_fun/ppermute | solution.py:570
  (75 other events, 542.7 us)
Sparse Core Ops, SparseCore 0:
  60.1 87.9 all-reduce.5
  185.1 87.8 all-reduce.7
  275.3 85.4 all-reduce.9
  363.7 85.6 all-reduce.11

commit v5 on v4

--- a/solution.py
+++ b/solution.py
@@ -277,7 +277,29 @@
     )(normed, cos_table, sin_table, *pieces)
 
 
-def mlp_kernel(halves, index_ref, x_ref, branch_ref, gain_ref, g_ref, *refs):
+def early_kernel(g_ref, d0, d2, out_ref):
+    block = d0.shape[1]
+    out_ref[...] = dot_nt(g_ref[:, :block], d0[...]) + dot_nt(g_ref[:, 2 * block : 3 * block], d2[...])
+
+
+def early_hidden(grad, own, near):
+    rows, model = grad.shape
+    hidden, block = own.shape
+    tile = 512
+    return pl.pallas_call(
+        early_kernel,
+        grid=(hidden // tile,),
+        in_specs=[pl.BlockSpec((rows, model), lambda j: (0, 0))]
+        + [pl.BlockSpec((tile, block), lambda j: (j, 0))] * 2,
+        out_specs=pl.BlockSpec((rows, tile), lambda j: (0, j)),
+        out_shape=jax.ShapeDtypeStruct((rows, hidden), F32),
+        compiler_params=pltpu.CompilerParams(vmem_limit_bytes=60 << 20),
+        cost_estimate=LIGHT,
+        name="early_hidden",
+    )(grad, own, near)
+
+
+def mlp_kernel(halves, index_ref, x_ref, branch_ref, gain_ref, g_ref, early_ref, *refs):
     count = 6 if halves else 4
     given, downs = (refs[:count], refs[count : 2 * count]), refs[2 * count : 2 * count + 4]
     h_ref, hidden_ref, dgate_ref, dup_ref, dh_ref, acc, joined = refs[2 * count + 4 :]
@@ -295,7 +317,7 @@
             h_ref[at, :] = (middle * lax.rsqrt(square + EPSILON) * gain_ref[...]).astype(BF)
             return unused
 
-        lax.fori_loop(0, h_ref.shape[0] // height, norm, 0)
+        lax.fori_loop(0, h_ref.shape[0] // height, norm, 0, unroll=True)
 
     sides = []
     for which, pieces in enumerate(given):
@@ -313,12 +335,12 @@
     for r in range(4):
         lanes = slice(r * block, (r + 1) * block)
         h = h_ref[:, lanes]
-        terms = (
-            dot_nn(h, gates[r][...]),
-            dot_nn(h, ups[r][...]),
-            dot_nt(g_ref[:, lanes], downs[r][...]),
-        )
-        gate, up, dhid = terms if r == 0 else (gate + terms[0], up + terms[1], dhid + terms[2])
+        terms = dot_nn(h, gates[r][...]), dot_nn(h, ups[r][...])
+        gate, up = terms if r == 0 else (gate + terms[0], up + terms[1])
+        if r == 0:
+            dhid = early_ref[...]
+        elif r != 2:
+            dhid += dot_nt(g_ref[:, lanes], downs[r][...])
     sigma = jax.nn.sigmoid(gate)
     active = gate * sigma
     hidden_ref[...] = (active * up).astype(BF)
@@ -343,7 +365,7 @@
         dh_ref[...] = acc[...].astype(BF)
 
 
-def mlp(tokens, branch, gain, grad, index, gates, ups, downs):
+def mlp(tokens, branch, gain, grad, early, index, gates, ups, downs):
     rows, model = tokens.shape
     hidden = downs[0].shape[0]
     tile = 512
@@ -356,7 +378,7 @@
         grid_spec=pltpu.PrefetchScalarGridSpec(
             num_scalar_prefetch=1,
             grid=(hidden // tile,),
-            in_specs=[whole, whole, pl.BlockSpec((1, model), lambda j, s: (0, 0)), whole]
+            in_specs=[whole, whole, pl.BlockSpec((1, model), lambda j, s: (0, 0)), whole, out]
             + wide
             + [tall] * 4,
             out_specs=[whole] + [out] * 3 + [whole],
@@ -371,7 +393,7 @@
         compiler_params=pltpu.CompilerParams(vmem_limit_bytes=60 << 20),
         cost_estimate=LIGHT,
         name="mlp",
-    )(index, tokens, branch, gain[None], grad, *[v[0] for v in gates + ups], *downs)
+    )(index, tokens, branch, gain[None], grad, early, *[v[0] for v in gates + ups], *downs)
 
 
 def entry_kernel(dq_ref, own_ref, got_ref, cos_ref, sin_ref, *refs):
@@ -534,7 +556,7 @@
 
 def exit_grad(index, grad_middle, grad, tokens, gain):
     rows, model = tokens.shape
-    height = 128
+    height = 256
     part = pl.BlockSpec((height, model), lambda i, s: (i, 0))
     return pl.pallas_call(
         exit_kernel,
@@ -810,17 +832,19 @@
     grad_mlp = (RESIDUAL * grad_out).astype(BF)
     branch = psum_tensor(branch)
 
-    def spread_wide(got, gate, up, down):
+    def spread_wide(got, gate, up, down, grad_mlp):
         gate_near = swap_core(gate)
-        near = gate_near, swap_core(up), swap_core(after(got, gate_near)), swap_core(after(down, gate_near))
-        return swap_ctx(got) if two_ctx() else got, *near
+        down_near = swap_core(after(down, gate_near))
+        near = gate_near, swap_core(up), swap_core(after(got, gate_near)), down_near
+        early = early_hidden(grad_mlp, down, down_near)
+        return swap_ctx(got) if two_ctx() else got, *near, early
 
     def spread_last(*values):
         return tuple(swap_core(v) for v in values)
 
     down_far = swap_x(after(down_weight, log_total))
-    wide_other, gate_near, up_near, last_got, down_near = sealed(
-        spread_wide, after(wide_got, log_total), gate_weight, up_weight, down_weight
+    wide_other, gate_near, up_near, last_got, down_near, early = sealed(
+        spread_wide, after(wide_got, log_total), gate_weight, up_weight, down_weight, grad_mlp
     )
     last_other, down_last = sealed(spread_last, wide_other, down_far)
     downs = [down_weight, down_far, down_near, down_last]
@@ -834,7 +858,7 @@
     wait = down_last
     branch = after(branch, wait)
     normed_two, hidden, grad_gate, grad_up, grad_two = mlp(
-        tokens, branch, gain_two, grad_mlp, lax.axis_index("ctx")[None], gates, ups, downs
+        tokens, branch, gain_two, grad_mlp, early, lax.axis_index("ctx")[None], gates, ups, downs
     )
     two_part = grad_two
     grad_two = psum_tensor(grad_two)

time: 470 us -> 468 us (level)
  waiting for transfers between devices: 213 us -> 208 us
    ppermute x8, waiting for transfers between devices: 63.8 us -> 52.8 us  [swap_ctx(): return lax.ppermute(value, 'ctx', [(0, 1), (1, 0)])]
    pallas_call x0 -> x1, Pallas kernels: none -> 6.07 us  [early_hidden(): pl.pallas_call(early_kernel, grid=(hidden // tile,), in_specs=[pl.BlockSp...]
    ppermute x17, waiting for transfers between devices: 16 us -> 21.4 us  [swap_core(): return lax.ppermute(value, 'dp', [(i, i ^ 1) for i in range(4)])]
  transfers between devices with their start and end apart: 42 -> 42, of which waited for: 24 -> 25; matrix products, arithmetic and copies ran while one was open for 12% -> 12% of each run, Pallas kernels for 21% -> 22%
where the time goes in v5:
time: 468 us; the launch traced here: 460 us
  waiting for transfers between devices  208 us (44%)
  Pallas kernels  143 us (31%)
  other arithmetic  41.8 us (9%)
  starting transfers between devices  32.4 us (7%)
  local copies, waits for them, and re-layouts  19.2 us (4%)
  between operations  15.6 us (3%)
    ppermute x10, waiting for transfers between devices, swap_x(): return lax.ppermute(value, 'dp', [(i, i ^ 2) for i in range(4)])  96.8 us
    ppermute x8, waiting for transfers between devices, swap_ctx(): return lax.ppermute(value, 'ctx', [(0, 1), (1, 0)])  52.8 us
    pallas_call x1, Pallas kernels, mlp(): pl.pallas_call(functools.partial(mlp_kernel, len(gates) > 4), grid_spec=p...  35.2 us
    pallas_call x9, Pallas kernels, outer(): pl.pallas_call(functools.partial(outer_kernel, len(adds)), grid=(count_m,...  35 us
    psum x4, waiting for transfers between devices, psum_tensor(): return lax.psum(value, 'tensor')  30.5 us
    ppermute x17, waiting for transfers between devices, swap_core(): return lax.ppermute(value, 'dp', [(i, i ^ 1) for i in range(4)])  21.4 us
    add x4, other arithmetic, combine(): return low.astype(F32) + peer.astype(F32)  17.8 us
    pallas_call x1, Pallas kernels, attend_backward(): pl.pallas_call(functools.partial(backward_kernel, chunk, len(key_values))...  16.9 us
  transfers between devices with their start and end apart: 42, of which 25 were waited for; matrix products, arithmetic and copies ran while one was open for 12% of the time, Pallas kernels for 22%

profile of v5, /device:TPU:0, one launch (start us, length us, event | category | flops | bytes accessed | tf_op | source)
XLA Modules:
  0.0 459.5 jit_solution(6451018717609116231)
XLA Ops:
  45.9 8.6 %attend_forward.1 = (bf16[512,512]{1,0:T(8,128)(2,1)S(1)}, f32[8,512]{1,0:T(8,128)S(1)}) custom-call(bf16[512,512]{1,0:T(8,128)(2,1)S(1)} %project_q.1.q_ref, s32[1024,1]{1,0:T(8,128)S(1)} %get-tuple-element.293.code_ref, s32[8,512]{1,0:T(8,128)S(1)} %stack.41.codes_ref, bf16[512,256]{1,0:T(8,128)(2,1)S(1)} %copy-done.17, ...), custom_call_target="tpu_custom_call" | custom-call | flops 1 | bytes 1 | tf_op jit(solution)/shard_map/attend_forward/pallas_call | solution.py:98
  55.9 4.1 out_project.1
  65.0 27.0 %collective-permute-done.29.refs_1_.refs_7_ = bf16[512,2048]{1,0:T(8,128)(2,1)} collective-permute-done((bf16[512,2048]{1,0:T(8,128)(2,1)}, bf16[512,2048]{1,0:T(8,128)(2,1)}, u32[]{:S(2)}, u32[]{:S(2)}) %collective-permute-start.29) | collective-permute-done | bytes 2097184 | tf_op jit(solution)/shard_map/ppermute | solution.py:592
  92.0 48.5 %conditional.5 = (bf16[512,2048]{1,0:T(8,128)(2,1)}, bf16[512,2048]{1,0:T(8,128)(2,1)}, bf16[512,2048]{1,0:T(8,128)(2,1)}, bf16[512,2048]{1,0:T(8,128)(2,1)}, bf...) conditional(s32[]{:T(128)} %convert_element_type.96, () %tuple.96, (bf16[512,2048]{1,0:T(8,128)(2,1)}, ...), branch_computations={%region_3.4_spmd, %region_4.5_spmd} | conditional | flops 1 | bytes 50331924 | solution.py:584
  97.0 5.3 %collective-permute-done.4.d2 = bf16[2048,512]{1,0:T(8,128)(2,1)} collective-permute-done((bf16[2048,512]{1,0:T(8,128)(2,1)S(1)}, bf16[2048,512]{1,0:T(8,128)(2,1)}, u32[]{:S(2)}, u32[]{:S(2)}) %collective-permute-start.4) | collective-permute-done | bytes 2097184 | tf_op jit(solution)/shard_map/cond/branch_1_fun/ppermute | solution.py:588
  102.2 6.1 %early_hidden.1 = f32[512,2048]{1,0:T(8,128)} custom-call(bf16[512,2048]{1,0:T(8,128)(2,1)S(1)} %get-tuple-element.83.g_ref, bf16[2048,512]{1,0:T(8,128)(2,1)} %copy-done.33, bf16[2048,512]{1,0:T(8,128)(2,1)} %collective-permute-done.4.d2), custom_call_target="tpu_custom_call" | custom-call | flops 1 | bytes 1 | tf_op jit(solution)/shard_map/cond/branch_1_fun/early_hidden/pallas_call | solution.py:289
  108.3 32.1 %collective-permute-done = bf16[512,2048]{1,0:T(8,128)(2,1)} collective-permute-done((bf16[512,2048]{1,0:T(8,128)(2,1)}, bf16[512,2048]{1,0:T(8,128)(2,1)}, u32[]{:S(2)}, u32[]{:S(2)}) %collective-permute-start) | collective-permute-done | bytes 2097184 | tf_op jit(solution)/shard_map/cond/branch_1_fun/ppermute | solution.py:600
  140.4 7.6 %conditional.6 = (bf16[512,2048]{1,0:T(8,128)(2,1)}, bf16[2048,512]{1,0:T(8,128)(2,1)}) conditional(s32[]{:T(128)} %convert_element_type.96, () %tuple.95, (bf16[512,2048]{1,0:T(8,128)(2,1)}, bf16[2048,512]{1,0:T(8,128)(2,1)}) %tuple.101), branch_computations={%region_5.6_spmd, %region_6.7_spmd} | conditional | bytes 16777312 | solution.py:584
  141.0 4.0 collective-permute-done.5
  148.1 35.2 %mlp.1 = (bf16[512,2048]{1,0:T(8,128)(2,1)}, bf16[512,2048]{1,0:T(8,128)(2,1)}, bf16[512,2048]{1,0:T(8,128)(2,1)}, bf16[512,2048]{1,0:T(8,128)(2,1)}, bf16[512,2048]{1,0:T(8,128)(2,1)}) custom-call(s32[1]{0:T(128)} %bitcast.9.index_ref, bf16[512,2048]{1,0:T(8,128)(2,1)} %copy-done, bf16[512,2048]{1,0:T(8,128)(2,1)} %all-reduce.6.cloned.1.call-done.branch_ref, ...), custom_call_target="tpu_custom_call" | custom-call | flops 1 | bytes 1 | tf_op jit(solution)/shard_map/mlp/pallas_call | solution.py:376
  184.0 65.3 %conditional.7 = (bf16[2048,512]{1,0:T(8,128)(2,1)}, bf16[1024,2048]{1,0:T(8,128)(2,1)}, bf16[512,2048]{1,0:T(8,128)(2,1)}, bf16[1024,2048]{1,0:T(8,128)(2,1)}, ...) conditional(s32[]{:T(128)} %convert_element_type.96, () %tuple.104, (bf16[512,2048]{1,0:T(8,128)(2,1)}, ...), branch_computations={%region_9.10_spmd, %region_10.11_spmd} | conditional | flops 8 | bytes 100663640 | solution.py:584
  184.0 4.6 down_outer.3
  199.8 11.4 %lift.1 = bf16[512,2048]{1,0:T(8,128)(2,1)} custom-call(bf16[512,2048]{1,0:T(8,128)(2,1)S(1)} %copy-done.29, bf16[2048,512]{1,0:T(8,128)(2,1)S(1)} %copy-done.34, bf16[2048,512]{1,0:T(8,128)(2,1)} %get-tuple-element.92.d1, bf16[2048,512]{1,0:T(8,128)(2,1)} %get-tuple-element.93.d2, bf16[2048,512]{1,0:T(8,128)(2,1)} %get-tuple-element.94.d3), custom_call_target="tpu_custom_call" | custom-call | flops 1 | bytes 1 | tf_op jit(solution)/shard_map/cond/branch_1_fun/lift/pallas_call | solution.py:490
  211.2 4.3 gate_outer.4
  215.4 4.3 up_outer.4
  219.7 26.1 %collective-permute-done.8.refs_1_ = bf16[2048,512]{1,0:T(8,128)(2,1)S(1)} collective-permute-done((bf16[2048,512]{1,0:T(8,128)(2,1)S(1)}, bf16[2048,512]{1,0:T(8,128)(2,1)S(1)}, u32[]{:S(2)}, u32[]{:S(2)}) %collective-permute-start.8) | collective-permute-done | bytes 2097184 | tf_op jit(solution)/shard_map/cond/branch_1_fun/ppermute | solution.py:592
  252.4 19.0 %all-reduce.8.cloned.1.call-done = bf16[512,2048]{1,0:T(8,128)(2,1)} async-done(((bf16[512,2048]{1,0:T(8,128)(2,1)}), bf16[512,2048]{1,0:T(8,128)(2,1)}) %all-reduce.8.cloned.1.call-update) | async-done | bytes 2097168 | tf_op jit(solution)/shard_map/psum | solution.py:623
  276.9 4.8 %multiply_convert_fusion = (bf16[512,2048]{1,0:T(8,128)(2,1)S(1)}, f32[512,2048]{1,0:T(8,128)}, f32[512,2048]{1,0:T(8,128)}) fusion(f32[512]{0:T(512)S(1)} %broadcast_multiply_fusion.1, f32[512]{0:T(512)S(1)} %get-tuple-element.312, bf16[512,2048]{1,0:T(8,128)(2,1)S(1)} %copy-done.28, bf16[512,2048]{1,0:T(8,128)(2,1)S(1)} %copy-done.1, ...), kind=kLoop, calls=%fused_computation.22 | loop fusion | flops 22020096 | bytes 18888704 | tf_op jit(solution)/shard_map/convert_element_type | solution.py:889
  281.8 16.9 %attend_backward.1 = (bf16[512,512]{1,0:T(8,128)(2,1)S(1)}, f32[1024,256]{1,0:T(8,128)S(1)}) custom-call(bf16[512,512]{1,0:T(8,128)(2,1)S(1)} %project_q.1.q_ref, s32[1024,1]{1,0:T(8,128)S(1)} %get-tuple-element.293.code_ref, s32[8,512]{1,0:T(8,128)S(1)} %stack.41.codes_ref, bf16[512,512]{1,0:T(8,128)(2,1)S(1)} %copy-done.40, ...), custom_call_target="tpu_custom_call" | custom-call | flops 1 | bytes 1 | tf_op jit(solution)/shard_map/attend_backward/pallas_call | solution.py:186
  300.4 5.0 %gate_outer.5 = bf16[512,2048]{1,0:T(8,128)(2,1)} custom-call(bf16[512,2048]{1,0:T(8,128)(2,1)S(1)} %copy-done.23, bf16[512,2048]{1,0:T(8,128)(2,1)S(1)} %copy-done.36, bf16[1024,2048]{1,0:T(8,128)(2,1)} %get-tuple-element.234.refs_0_, bf16[512,2048]{1,0:T(8,128)(2,1)} %collective-permute-done.33.refs_1_), custom_call_target="tpu_custom_call" | custom-call | flops 1 | bytes 1 | tf_op jit(solution)/shard_map/gate_outer/pallas_call | solution.py:454
  307.4 5.6 %entry_grad.1 = (bf16[512,768]{1,0:T(8,128)(2,1)S(1)}, bf16[512,2048]{1,0:T(8,128)(2,1)}) custom-call(bf16[512,512]{1,0:T(8,128)(2,1)} %copy-done.22, f32[512,256]{1,0:T(8,128)} %slice.103.own_ref, bf16[512,256]{1,0:T(8,128)(2,1)} %copy-done.56, f32[512,128]{1,0:T(8,128)} %copy-done.2, f32[512,128]{1,0:T(8,128)} %copy-done.3, bf16[512,512]{1,0:T(8,128)(2,1)} %refs_0_.3, ...), custom_call_target="tpu_custom_call" | custom-call | flops 1 | bytes 1 | tf_op jit(solution)/shard_map/entry_grad/pallas_call | solution.py:417
  314.5 11.7 %conditional.8 = (bf16[1024,1280]{1,0:T(8,128)(2,1)}, bf16[512,1280]{1,0:T(8,128)(2,1)}) conditional(s32[]{:T(128)} %convert_element_type.96, () %tuple.111, (bf16[512,512]{1,0:T(8,128)(2,1)S(1)}, bf16[512,2048]{1,0:T(8,128)(2,1)}, bf16[512,2048]{1,0:T(8,128)(2,1)}, bf16[512,768]{1,0:T(8,128)(2,1)S(1)}) %tuple.181), branch_computations={%region_14.15_spmd, %region_15.16_spmd} | conditional | flops 2 | bytes 27263088 | solution.py:584
  317.8 5.0 %collective-permute-done.11.refs_0_ = bf16[1024,1280]{1,0:T(8,128)(2,1)} collective-permute-done((bf16[1024,1280]{1,0:T(8,128)(2,1)S(1)}, bf16[1024,1280]{1,0:T(8,128)(2,1)}, u32[]{:S(2)}, u32[]{:S(2)}) %collective-permute-start.11) | collective-permute-done | bytes 2621472 | tf_op jit(solution)/shard_map/cond/branch_1_fun/ppermute | solution.py:588
  330.5 11.0 %collective-permute-done.34.refs_1_ = bf16[512,2048]{1,0:T(8,128)(2,1)} collective-permute-done((bf16[512,2048]{1,0:T(8,128)(2,1)}, bf16[512,2048]{1,0:T(8,128)(2,1)}, u32[]{:S(2)}, u32[]{:S(2)}) %collective-permute-start.34) | collective-permute-done | bytes 2097184 | tf_op jit(solution)/shard_map/ppermute | solution.py:592
  341.5 5.8 %up_outer.5 = bf16[512,2048]{1,0:T(8,128)(2,1)} custom-call(bf16[512,2048]{1,0:T(8,128)(2,1)} %get-tuple-element.223.a_ref, bf16[512,2048]{1,0:T(8,128)(2,1)} %get-tuple-element.225.b_ref, bf16[1024,2048]{1,0:T(8,128)(2,1)} %get-tuple-element.237.refs_0_, bf16[512,2048]{1,0:T(8,128)(2,1)} %collective-permute-done.34.refs_1_), custom_call_target="tpu_custom_call" | custom-call | flops 1 | bytes 1 | tf_op jit(solution)/shard_map/up_outer/pallas_call | solution.py:454
  348.9 10.4 %all-reduce.10.cloned.1.call-done = bf16[512,2048]{1,0:T(8,128)(2,1)} async-done(((bf16[512,2048]{1,0:T(8,128)(2,1)}), bf16[512,2048]{1,0:T(8,128)(2,1)}) %all-reduce.10.cloned.1.call-update) | async-done | bytes 2097168 | tf_op jit(solution)/shard_map/psum | solution.py:623
  361.5 28.6 %collective-permute-done.37 = bf16[512,1280]{1,0:T(8,128)(2,1)S(1)} collective-permute-done((bf16[512,1280]{1,0:T(8,128)(2,1)}, bf16[512,1280]{1,0:T(8,128)(2,1)S(1)}, u32[]{:S(2)}, u32[]{:S(2)}) %collective-permute-start.37) | collective-permute-done | bytes 1310752 | tf_op jit(solution)/shard_map/ppermute | solution.py:592
  390.1 14.5 %collective-permute-done.36 = bf16[512,2048]{1,0:T(8,128)(2,1)} collective-permute-done((bf16[512,2048]{1,0:T(8,128)(2,1)}, bf16[512,2048]{1,0:T(8,128)(2,1)}, u32[]{:S(2)}, u32[]{:S(2)}) %collective-permute-start.36) | collective-permute-done | bytes 2097184 | tf_op jit(solution)/shard_map/ppermute | solution.py:600
  404.6 41.6 %conditional.9 = (f32[2,512]{1,0:T(2,128)}, bf16[512,2048]{1,0:T(8,128)(2,1)}, f32[2048,512]{1,0:T(8,128)}, f32[512,2048]{1,0:T(8,128)}, f32[512,2048]{1,0:T(8,1...) conditional(s32[]{:T(128)} %convert_element_type.96, () %tuple.83, ...), branch_computations={%region_17.18_spmd, %region_18.19_spmd} | conditional | flops 23995432 | bytes 92607496 | solution.py:584
  410.7 8.3 %convert_add_fusion = (f32[512,2048]{1,0:T(8,128)}, f32[512,2048]{1,0:T(8,128)}) fusion(bf16[512,2048]{1,0:T(8,128)(2,1)} %get-tuple-element.110, bf16[512,2048]{1,0:T(8,128)(2,1)} %get-tuple-element.109, bf16[512,2048]{1,0:T(8,128)(2,1)} %get-tuple-element.108, bf16[512,2048]{1,0:T(8,128)(2,1)S(1)} %copy-done.42), kind=kLoop, calls=%fused_computation | loop fusion | flops 6291456 | bytes 16777216 | tf_op jit(solution)/shard_map/cond/branch_1_fun/add | solution.py:696
  421.6 4.9 %convert_add_fusion.2 = f32[2048,512]{1,0:T(8,128)} fusion(bf16[2048,512]{1,0:T(8,128)(2,1)} %get-tuple-element.106, bf16[2048,512]{1,0:T(8,128)(2,1)} %get-tuple-element.105), kind=kLoop, calls=%fused_computation.2 | loop fusion | flops 3145728 | bytes 8388608 | tf_op jit(solution)/shard_map/cond/branch_1_fun/add | solution.py:696
  447.3 5.3 %exit_grad.1 = bf16[512,2048]{1,0:T(8,128)(2,1)} custom-call(s32[1]{0:T(128)} %bitcast.12.index_ref, f32[512,2048]{1,0:T(8,128)} %get-tuple-element.263.middle_ref, bf16[512,2048]{1,0:T(8,128)(2,1)} %all-reduce.12.cloned.1.call-done.dh_ref, bf16[512,2048]{1,0:T(8,128)(2,1)} %copy-done, f32[1,2048]{1,0:T(1,128)} %maximum_convert_fusion.1.gain_ref), custom_call_target="tpu_custom_call" | custom-call | flops 1 | bytes 1 | tf_op jit(solution)/shard_map/exit_grad/pallas_call | solution.py:561
  (280 shorter events, 125.6 us)
Async XLA Ops:
  7.2 140.9 %all-reduce.6.cloned.1.call-start = ((), (), s32[]{:S(2)}) async-start(), calls=%async_computation | async-start | bytes 4194304 | tf_op jit(solution)/shard_map/psum | solution.py:623
  7.7 15.7 %collective-permute-start.23 = (bf16[512,512]{1,0:T(8,128)(2,1)}, bf16[512,512]{1,0:T(8,128)(2,1)}, u32[]{:S(2)}, u32[]{:S(2)}) collective-permute-start(bf16[512,512]{1,0:T(8,128)(2,1)} %refs_0_.3), channel_id=1, source_target_pairs={{0,16},{8,24},{16,0},{24,8},{1,17},{9,25},{17,1},{25,9},{2,18},{10... | collective-permute-start | bytes 1572872 | tf_op jit(solution)/shard_map/ppermute | solution.py:592
  13.6 15.7 %collective-permute-start.20 = (bf16[544,256]{1,0:T(8,128)(2,1)S(1)}, bf16[544,256]{1,0:T(8,128)(2,1)}, u32[]{:S(2)}, u32[]{:S(2)}) collective-permute-start(bf16[544,256]{1,0:T(8,128)(2,1)S(1)} %fusion.13.p0.refs_4_), channel_id=1, source_target_pairs={{0,16},{8,24},{16,0},{24,8},{1,17},{9,25},{17,1},{25,9},{2,18},{10... | collective-permute-start | bytes 835592 | tf_op jit(solution)/shard_map/ppermute | solution.py:592
  13.7 9.8 %collective-permute-start.21 = (bf16[544,256]{1,0:T(8,128)(2,1)S(1)}, bf16[544,256]{1,0:T(8,128)(2,1)S(1)}, u32[]{:S(2)}, u32[]{:S(2)}) collective-permute-start(bf16[544,256]{1,0:T(8,128)(2,1)S(1)} %fusion.13.p0.refs_4_), channel_id=1, source_target_pairs={{0,8},{8,0},{16,24},{24,16},{1,9},{9,1},{17,25},{25,17},{2,10},{10... | collective-permute-start | bytes 835592 | tf_op jit(solution)/shard_map/ppermute | solution.py:588
  23.4 12.9 %collective-permute-start.24 = (bf16[512,512]{1,0:T(8,128)(2,1)}, bf16[512,512]{1,0:T(8,128)(2,1)S(1)}, u32[]{:S(2)}, u32[]{:S(2)}) collective-permute-start(bf16[512,512]{1,0:T(8,128)(2,1)} %collective-permute-done.23.p1.refs_1_), channel_id=1, source_target_pairs={{0,8},{8,0},{16,24},{24,16},{1,9},{9,1},{17,25},{25,17},{2,10},{10... | collective-permute-start | bytes 1572872 | tf_op jit(solution)/shard_map/ppermute | solution.py:588
  23.5 19.6 %collective-permute-start.26 = (bf16[512,512]{1,0:T(8,128)(2,1)}, bf16[512,512]{1,0:T(8,128)(2,1)}, u32[]{:S(2)}, u32[]{:S(2)}) collective-permute-start(bf16[512,512]{1,0:T(8,128)(2,1)} %o0.3), channel_id=1, source_target_pairs={{0,16},{8,24},{16,0},{24,8},{1,17},{9,25},{17,1},{25,9},{2,18},{10... | collective-permute-start | bytes 1572872 | tf_op jit(solution)/shard_map/ppermute | solution.py:592
  34.3 8.8 %collective-permute-start.25 = (bf16[512,256]{1,0:T(8,128)(2,1)S(1)}, bf16[512,256]{1,0:T(8,128)(2,1)S(1)}, u32[]{:S(2)}, u32[]{:S(2)}) collective-permute-start(bf16[512,256]{1,0:T(8,128)(2,1)S(1)} %get-tuple-element.201.refs_0_), channel_id=1, source_target_pairs={{0,4},{4,0},{1,5},{5,1},{2,6},{6,2},{3,7},{7,3},{8,12},{12,8},{9,1... | collective-permute-start | bytes 786440 | tf_op jit(solution)/shard_map/ppermute | solution.py:600
  36.3 18.6 %collective-permute-start.27 = (bf16[512,512]{1,0:T(8,128)(2,1)}, bf16[512,512]{1,0:T(8,128)(2,1)S(1)}, u32[]{:S(2)}, u32[]{:S(2)}) collective-permute-start(bf16[512,512]{1,0:T(8,128)(2,1)} %o0.3), channel_id=1, source_target_pairs={{0,8},{8,0},{16,24},{24,16},{1,9},{9,1},{17,25},{25,17},{2,10},{10... | collective-permute-start | bytes 1572872 | tf_op jit(solution)/shard_map/ppermute | solution.py:588
  43.1 11.8 %collective-permute-start.28 = (bf16[512,512]{1,0:T(8,128)(2,1)}, bf16[512,512]{1,0:T(8,128)(2,1)S(1)}, u32[]{:S(2)}, u32[]{:S(2)}) collective-permute-start(bf16[512,512]{1,0:T(8,128)(2,1)} %collective-permute-done.26.o1), channel_id=1, source_target_pairs={{0,8},{8,0},{16,24},{24,16},{1,9},{9,1},{17,25},{25,17},{2,10},{10... | collective-permute-start | bytes 1572872 | tf_op jit(solution)/shard_map/ppermute | solution.py:588
  43.2 48.8 %collective-permute-start.29 = (bf16[512,2048]{1,0:T(8,128)(2,1)}, bf16[512,2048]{1,0:T(8,128)(2,1)}, u32[]{:S(2)}, u32[]{:S(2)}) collective-permute-start(bf16[512,2048]{1,0:T(8,128)(2,1)} %pad_maximum_fusion.2), channel_id=1, source_target_pairs={{0,16},{8,24},{16,0},{24,8},{1,17},{9,25},{17,1},{25,9},{2,18},{10... | collective-permute-start | bytes 6291464 | tf_op jit(solution)/shard_map/ppermute | solution.py:592
  54.5 85.9 %collective-permute-start.30 = (bf16[2048,512]{1,0:T(8,128)(2,1)}, bf16[2048,512]{1,0:T(8,128)(2,1)}, u32[]{:S(2)}, u32[]{:S(2)}) collective-permute-start(bf16[2048,512]{1,0:T(8,128)(2,1)} %refs_12_.1), channel_id=1, source_target_pairs={{0,16},{8,24},{16,0},{24,8},{1,17},{9,25},{17,1},{25,9},{2,18},{10... | collective-permute-start | bytes 6291464 | tf_op jit(solution)/shard_map/ppermute | solution.py:592
  60.0 211.4 %all-reduce.8.cloned.1.call-start = ((), (), s32[]{:S(2)}) async-start(), calls=%async_computation.1 | async-start | bytes 4194304 | tf_op jit(solution)/shard_map/psum | solution.py:623
  92.0 48.4 %collective-permute-start = (bf16[512,2048]{1,0:T(8,128)(2,1)}, bf16[512,2048]{1,0:T(8,128)(2,1)}, u32[]{:S(2)}, u32[]{:S(2)}) collective-permute-start(bf16[512,2048]{1,0:T(8,128)(2,1)} %get-tuple-element.80), channel_id=1, source_target_pairs={{0,4},{4,0},{1,5},{5,1},{2,6},{6,2},{3,7},{7,3},{8,12},{12,8},{9,1... | collective-permute-start | bytes 6291464 | tf_op jit(solution)/shard_map/cond/branch_1_fun/ppermute | solution.py:600
  96.5 43.9 %collective-permute-start.2 = (bf16[512,2048]{1,0:T(8,128)(2,1)}, bf16[512,2048]{1,0:T(8,128)(2,1)}, u32[]{:S(2)}, u32[]{:S(2)}) collective-permute-start(bf16[512,2048]{1,0:T(8,128)(2,1)} %get-tuple-element.79), channel_id=1, source_target_pairs={{0,8},{8,0},{16,24},{24,16},{1,9},{9,1},{17,25},{25,17},{2,10},{10... | collective-permute-start | bytes 6291464 | tf_op jit(solution)/shard_map/cond/branch_1_fun/ppermute | solution.py:588
  96.8 43.6 %collective-permute-start.3 = (bf16[512,2048]{1,0:T(8,128)(2,1)}, bf16[512,2048]{1,0:T(8,128)(2,1)}, u32[]{:S(2)}, u32[]{:S(2)}) collective-permute-start(bf16[512,2048]{1,0:T(8,128)(2,1)} %get-tuple-element.80), channel_id=1, source_target_pairs={{0,8},{8,0},{16,24},{24,16},{1,9},{9,1},{17,25},{25,17},{2,10},{10... | collective-permute-start | bytes 6291464 | tf_op jit(solution)/shard_map/cond/branch_1_fun/ppermute | solution.py:588
  140.5 7.5 %collective-permute-start.6 = (bf16[2048,512]{1,0:T(8,128)(2,1)}, bf16[2048,512]{1,0:T(8,128)(2,1)}, u32[]{:S(2)}, u32[]{:S(2)}) collective-permute-start(bf16[2048,512]{1,0:T(8,128)(2,1)} %get-tuple-element.85), channel_id=1, source_target_pairs={{0,8},{8,0},{16,24},{24,16},{1,9},{9,1},{17,25},{25,17},{2,10},{10... | collective-permute-start | bytes 6291464 | tf_op jit(solution)/shard_map/cond/branch_1_fun/ppermute | solution.py:588
  183.3 175.9 %all-reduce.10.cloned.1.call-start = ((), (), s32[]{:S(2)}) async-start(), calls=%async_computation.2 | async-start | bytes 4194304 | tf_op jit(solution)/shard_map/psum | solution.py:623
  188.6 7.2 %collective-permute-start.7 = (bf16[2048,1024]{1,0:T(8,128)(2,1)S(1)}, bf16[2048,1024]{1,0:T(8,128)(2,1)S(1)}, u32[]{:S(2)}, u32[]{:S(2)}) collective-permute-start(bf16[2048,1024]{1,0:T(8,128)(2,1)S(1)} %down_outer.3), channel_id=1, source_target_pairs={{0,8},{8,0},{16,24},{24,16},{1,9},{9,1},{17,25},{25,17},{2,10},{10... | collective-permute-start | bytes 12582920 | tf_op jit(solution)/shard_map/cond/branch_1_fun/ppermute | solution.py:588
  191.4 19.8 %collective-permute-start.9 = (bf16[1024,2048]{1,0:T(8,128)(2,1)S(1)}, bf16[1024,2048]{1,0:T(8,128)(2,1)}, u32[]{:S(2)}, u32[]{:S(2)}) collective-permute-start(bf16[1024,2048]{1,0:T(8,128)(2,1)S(1)} %gate_outer.3), channel_id=1, source_target_pairs={{0,8},{8,0},{16,24},{24,16},{1,9},{9,1},{17,25},{25,17},{2,10},{10... | collective-permute-start | bytes 12582920 | tf_op jit(solution)/shard_map/cond/branch_1_fun/ppermute | solution.py:588
  194.6 20.8 %collective-permute-start.10 = (bf16[1024,2048]{1,0:T(8,128)(2,1)S(1)}, bf16[1024,2048]{1,0:T(8,128)(2,1)}, u32[]{:S(2)}, u32[]{:S(2)}) collective-permute-start(bf16[1024,2048]{1,0:T(8,128)(2,1)S(1)} %up_outer.3), channel_id=1, source_target_pairs={{0,8},{8,0},{16,24},{24,16},{1,9},{9,1},{17,25},{25,17},{2,10},{10... | collective-permute-start | bytes 12582920 | tf_op jit(solution)/shard_map/cond/branch_1_fun/ppermute | solution.py:588
  198.1 47.7 %collective-permute-start.8 = (bf16[2048,512]{1,0:T(8,128)(2,1)S(1)}, bf16[2048,512]{1,0:T(8,128)(2,1)S(1)}, u32[]{:S(2)}, u32[]{:S(2)}) collective-permute-start(bf16[2048,512]{1,0:T(8,128)(2,1)S(1)} %down_outer.4), channel_id=1, source_target_pairs={{0,16},{8,24},{16,0},{24,8},{1,17},{9,25},{17,1},{25,9},{2,18},{10... | collective-permute-start | bytes 6291464 | tf_op jit(solution)/shard_map/cond/branch_1_fun/ppermute | solution.py:592
  249.3 51.1 %collective-permute-start.33 = (bf16[512,2048]{1,0:T(8,128)(2,1)}, bf16[512,2048]{1,0:T(8,128)(2,1)}, u32[]{:S(2)}, u32[]{:S(2)}) collective-permute-start(bf16[512,2048]{1,0:T(8,128)(2,1)} %get-tuple-element.235), channel_id=1, source_target_pairs={{0,16},{8,24},{16,0},{24,8},{1,17},{9,25},{17,1},{25,9},{2,18},{10... | collective-permute-start | bytes 6291464 | tf_op jit(solution)/shard_map/ppermute | solution.py:592
  250.9 98.0 %collective-permute-start.32 = (bf16[2048,512]{1,0:T(8,128)(2,1)}, bf16[2048,512]{1,0:T(8,128)(2,1)}, u32[]{:S(2)}, u32[]{:S(2)}) collective-permute-start(bf16[2048,512]{1,0:T(8,128)(2,1)} %get-tuple-element.226), channel_id=1, source_target_pairs={{0,4},{4,0},{1,5},{5,1},{2,6},{6,2},{3,7},{7,3},{8,12},{12,8},{9,1... | collective-permute-start | bytes 6291464 | tf_op jit(solution)/shard_map/ppermute | solution.py:600
  271.4 70.1 %collective-permute-start.34 = (bf16[512,2048]{1,0:T(8,128)(2,1)}, bf16[512,2048]{1,0:T(8,128)(2,1)}, u32[]{:S(2)}, u32[]{:S(2)}) collective-permute-start(bf16[512,2048]{1,0:T(8,128)(2,1)} %get-tuple-element.239), channel_id=1, source_target_pairs={{0,16},{8,24},{16,0},{24,8},{1,17},{9,25},{17,1},{25,9},{2,18},{10... | collective-permute-start | bytes 6291464 | tf_op jit(solution)/shard_map/ppermute | solution.py:592
  298.8 7.8 %collective-permute-start.31 = (bf16[512,256]{1,0:T(8,128)(2,1)S(1)}, bf16[512,256]{1,0:T(8,128)(2,1)S(1)}, u32[]{:S(2)}, u32[]{:S(2)}) collective-permute-start(bf16[512,256]{1,0:T(8,128)(2,1)S(1)} %slice.151), channel_id=1, source_target_pairs={{0,4},{4,0},{1,5},{5,1},{2,6},{6,2},{3,7},{7,3},{8,12},{12,8},{9,1... | collective-permute-start | bytes 786440 | tf_op jit(solution)/shard_map/ppermute | solution.py:600
  313.0 77.1 %collective-permute-start.35 = (bf16[512,2048]{1,0:T(8,128)(2,1)}, bf16[512,2048]{1,0:T(8,128)(2,1)}, u32[]{:S(2)}, u32[]{:S(2)}) collective-permute-start(bf16[512,2048]{1,0:T(8,128)(2,1)} %gate_outer.5), channel_id=1, source_target_pairs={{0,4},{4,0},{1,5},{5,1},{2,6},{6,2},{3,7},{7,3},{8,12},{12,8},{9,1... | collective-permute-start | bytes 6291464 | tf_op jit(solution)/shard_map/ppermute | solution.py:600
  330.2 117.1 %all-reduce.12.cloned.1.call-start = ((), (), s32[]{:S(2)}) async-start(), calls=%async_computation.3 | async-start | bytes 4194304 | tf_op jit(solution)/shard_map/psum | solution.py:623
  347.3 57.3 %collective-permute-start.36 = (bf16[512,2048]{1,0:T(8,128)(2,1)}, bf16[512,2048]{1,0:T(8,128)(2,1)}, u32[]{:S(2)}, u32[]{:S(2)}) collective-permute-start(bf16[512,2048]{1,0:T(8,128)(2,1)} %up_outer.5), channel_id=1, source_target_pairs={{0,4},{4,0},{1,5},{5,1},{2,6},{6,2},{3,7},{7,3},{8,12},{12,8},{9,1... | collective-permute-start | bytes 6291464 | tf_op jit(solution)/shard_map/ppermute | solution.py:600
  359.3 30.8 %collective-permute-start.37 = (bf16[512,1280]{1,0:T(8,128)(2,1)}, bf16[512,1280]{1,0:T(8,128)(2,1)S(1)}, u32[]{:S(2)}, u32[]{:S(2)}) collective-permute-start(bf16[512,1280]{1,0:T(8,128)(2,1)} %get-tuple-element.245), channel_id=1, source_target_pairs={{0,16},{8,24},{16,0},{24,8},{1,17},{9,25},{17,1},{25,9},{2,18},{10... | collective-permute-start | bytes 3932168 | tf_op jit(solution)/shard_map/ppermute | solution.py:592
  409.1 28.4 %collective-permute-start.18 = (bf16[512,1280]{1,0:T(8,128)(2,1)S(1)}, bf16[512,1280]{1,0:T(8,128)(2,1)}, u32[]{:S(2)}, u32[]{:S(2)}) collective-permute-start(bf16[512,1280]{1,0:T(8,128)(2,1)S(1)} %entry_outer.5), channel_id=1, source_target_pairs={{0,4},{4,0},{1,5},{5,1},{2,6},{6,2},{3,7},{7,3},{8,12},{12,8},{9,1... | collective-permute-start | bytes 3932168 | tf_op jit(solution)/shard_map/cond/branch_1_fun/ppermute | solution.py:600
  410.1 8.9 %collective-permute-start.13 = (f32[2,512]{1,0:T(2,128)S(1)}, f32[2,512]{1,0:T(2,128)S(1)}, u32[]{:S(2)}, u32[]{:S(2)}) collective-permute-start(f32[2,512]{1,0:T(2,128)S(1)} %get-tuple-element.278), channel_id=1, source_target_pairs={{0,16},{8,24},{16,0},{24,8},{1,17},{9,25},{17,1},{25,9},{2,18},{10... | collective-permute-start | bytes 12296 | tf_op jit(solution)/shard_map/cond/branch_1_fun/ppermute | solution.py:592
  420.3 6.2 %collective-permute-start.15 = (f32[2,512]{1,0:T(2,128)S(1)}, f32[2,512]{1,0:T(2,128)S(1)}, u32[]{:S(2)}, u32[]{:S(2)}) collective-permute-start(f32[2,512]{1,0:T(2,128)S(1)} %get-tuple-element.102), channel_id=1, source_target_pairs={{0,24},{8,16},{16,8},{24,0},{1,25},{9,17},{17,9},{25,1},{2,26},{10... | collective-permute-start | bytes 12296 | tf_op jit(solution)/shard_map/cond/branch_1_fun/ppermute | solution.py:596
  (74 other events, 514.4 us)
Sparse Core Ops, SparseCore 0:
  60.1 87.9 all-reduce.5
  183.5 87.8 all-reduce.7
  273.8 85.4 all-reduce.9
  361.6 85.6 all-reduce.11

commit v6 on v5

--- a/solution.py
+++ b/solution.py
@@ -299,12 +299,42 @@
     )(grad, own, near)
 
 
-def mlp_kernel(halves, index_ref, x_ref, branch_ref, gain_ref, g_ref, early_ref, *refs):
-    count = 6 if halves else 4
-    given, downs = (refs[:count], refs[count : 2 * count]), refs[2 * count : 2 * count + 4]
-    h_ref, hidden_ref, dgate_ref, dup_ref, dh_ref, acc, joined = refs[2 * count + 4 :]
-    step = pl.program_id(0)
+def mlp_kernel(side_places, index_ref, x_ref, branch_ref, gain_ref, g_ref, early_ref, *refs):
+    count = len(side_places[0])
+    sides, downs = (refs[:count], refs[count : 2 * count]), refs[2 * count : 2 * count + 2]
+    h_ref, hidden_ref, dgate_ref, dup_ref, dh_ref = refs[2 * count + 2 : 2 * count + 7]
+    grad, dgates, dups, wide, tall, sems, grad_sem = refs[2 * count + 7 :]
+    step, steps = pl.program_id(0), pl.num_programs(0)
     block = h_ref.shape[1] // 4
+    tile = tall.shape[2]
+    index = index_ref[0]
+
+    def copies(at_step):
+        columns = rows_at(at_step, tile)
+        made = []
+        for which, pieces in enumerate(sides):
+            for piece, (first, size, base, sign) in zip(pieces, side_places[which], strict=True):
+                if sign:
+                    base = pl.multiple_of(base + (index if sign > 0 else 1 - index) * size, size)
+                made.append((piece.at[pl.ds(first, size), columns], wide.at[which, pl.ds(base, size), columns]))
+        for k, piece in enumerate(downs):
+            made.append((piece.at[columns], tall.at[at_step, k]))
+        return [pltpu.make_async_copy(*ends, sems.at[at_step, n]) for n, ends in enumerate(made)]
+
+    grad_copy = pltpu.make_async_copy(g_ref, grad, grad_sem)
+
+    @pl.when(step == 0)
+    def _():
+        for copy in copies(0):
+            copy.start()
+        grad_copy.start()
+
+        def begin(j, unused):
+            for copy in copies(j):
+                copy.start()
+            return unused
+
+        lax.fori_loop(1, steps, begin, 0)
 
     @pl.when(step == 0)
     def _():
@@ -318,29 +348,17 @@
             return unused
 
         lax.fori_loop(0, h_ref.shape[0] // height, norm, 0, unroll=True)
-
-    sides = []
-    for which, pieces in enumerate(given):
-        if halves:
-            half = block // 2
-            first = pl.multiple_of(index_ref[0] * half, half)
-            second = pl.multiple_of((1 - index_ref[0]) * half, half)
-            for far in range(2):
-                joined[which, far, pl.ds(first, half), :] = pieces[3 * far + 1][...]
-                joined[which, far, pl.ds(second, half), :] = pieces[3 * far + 2][...]
-            pieces = (pieces[0], joined.at[which, 0], pieces[3], joined.at[which, 1])
-        sides.append(pieces)
-    gates, ups = sides
-    gate = up = dhid = None
-    for r in range(4):
-        lanes = slice(r * block, (r + 1) * block)
-        h = h_ref[:, lanes]
-        terms = dot_nn(h, gates[r][...]), dot_nn(h, ups[r][...])
-        gate, up = terms if r == 0 else (gate + terms[0], up + terms[1])
-        if r == 0:
-            dhid = early_ref[...]
-        elif r != 2:
-            dhid += dot_nt(g_ref[:, lanes], downs[r][...])
+        grad_copy.wait()
+
+    for copy in copies(step):
+        copy.wait()
+    columns = rows_at(step, tile)
+    gate = dot_nn(h_ref[...], wide[0, :, columns])
+    up = dot_nn(h_ref[...], wide[1, :, columns])
+    dhid = early_ref[...]
+    for k in range(2):
+        at = (2 * k + 1) * block
+        dhid += dot_nt(grad[:, at : at + block], tall[step, k])
     sigma = jax.nn.sigmoid(gate)
     active = gate * sigma
     hidden_ref[...] = (active * up).astype(BF)
@@ -348,43 +366,52 @@
     dup = (dhid * active).astype(BF)
     dgate_ref[...] = dgate
     dup_ref[...] = dup
-    for r in range(4):
-        lanes = slice(r * block, (r + 1) * block)
-        term = dot_nt(dgate, gates[r][...]) + dot_nt(dup, ups[r][...])
-
-        @pl.when(step == 0)
-        def _():
-            acc[:, lanes] = term
-
-        @pl.when(step != 0)
-        def _():
-            acc[:, lanes] += term
-
-    @pl.when(step == pl.num_programs(0) - 1)
+    dgates[:, columns] = dgate
+    dups[:, columns] = dup
+
+    @pl.when(step == steps - 1)
     def _():
-        dh_ref[...] = acc[...].astype(BF)
+        def block_of(r, unused):
+            at = rows_at(r, block)
+            term = dot_nt(dgates[...], wide[0, at, :]) + dot_nt(dups[...], wide[1, at, :])
+            dh_ref[:, at] = term.astype(BF)
+            return unused
+
+        lax.fori_loop(0, 4, block_of, 0)
 
 
 def mlp(tokens, branch, gain, grad, early, index, gates, ups, downs):
     rows, model = tokens.shape
     hidden = downs[0].shape[0]
     tile = 512
+    block = model // 4
+    bases = ((0, 0), (block, 0), (2 * block, 0), (3 * block, 0))
+    if len(gates) > 4:
+        bases = ((0, 0), (block, 1), (block, -1), (2 * block, 0), (3 * block, 1), (3 * block, -1))
+    calls = []
+    for side in (gates, ups):
+        calls.append(tuple((at * size, size, *base) for (unused, size, at), base in zip(side, bases, strict=True)))
     whole = pl.BlockSpec((rows, model), lambda j, s: (0, 0))
-    wide = [pl.BlockSpec((size, tile), lambda j, s, at=at: (at, j)) for unused, size, at in gates + ups]
-    tall = pl.BlockSpec((tile, downs[0].shape[1]), lambda j, s: (j, 0))
     out = pl.BlockSpec((rows, tile), lambda j, s: (0, j))
-    return pl.pallas_call(
-        functools.partial(mlp_kernel, len(gates) > 4),
+    far = [downs[1], downs[3]]
+    count = 2 * len(gates) + 2
+    return pl.pallas_call(
+        functools.partial(mlp_kernel, tuple(calls)),
         grid_spec=pltpu.PrefetchScalarGridSpec(
             num_scalar_prefetch=1,
             grid=(hidden // tile,),
-            in_specs=[whole, whole, pl.BlockSpec((1, model), lambda j, s: (0, 0)), whole, out]
-            + wide
-            + [tall] * 4,
+            in_specs=[whole, whole, pl.BlockSpec((1, model), lambda j, s: (0, 0))]
+            + [pl.BlockSpec(memory_space=pl.ANY), out]
+            + [pl.BlockSpec(memory_space=pl.ANY)] * count,
             out_specs=[whole] + [out] * 3 + [whole],
             scratch_shapes=[
-                pltpu.VMEM((rows, model), F32),
-                pltpu.VMEM((2, 2, model // 4, tile), BF),
+                pltpu.VMEM((rows, model), BF),
+                pltpu.VMEM((rows, hidden), BF),
+                pltpu.VMEM((rows, hidden), BF),
+                pltpu.VMEM((2, model, hidden), BF),
+                pltpu.VMEM((hidden // tile, 2, tile, block), BF),
+                pltpu.SemaphoreType.DMA((hidden // tile, count)),
+                pltpu.SemaphoreType.DMA,
             ],
         ),
         out_shape=[jax.ShapeDtypeStruct((rows, model), BF)]
@@ -393,7 +420,7 @@
         compiler_params=pltpu.CompilerParams(vmem_limit_bytes=60 << 20),
         cost_estimate=LIGHT,
         name="mlp",
-    )(index, tokens, branch, gain[None], grad, early, *[v[0] for v in gates + ups], *downs)
+    )(index, tokens, branch, gain[None], grad, early, *[v[0] for v in gates + ups], *far)
 
 
 def entry_kernel(dq_ref, own_ref, got_ref, cos_ref, sin_ref, *refs):

time: 468 us -> 463 us (0.989)
  Pallas kernels: 143 us -> 138 us
where the time goes in v6:
time: 463 us; the launch traced here: 455 us
  waiting for transfers between devices  208 us (45%)
  Pallas kernels  138 us (30%)
  other arithmetic  41.8 us (9%)
  starting transfers between devices  32.5 us (7%)
  local copies, waits for them, and re-layouts  19.2 us (4%)
  between operations  15.6 us (3%)
    ppermute x10, waiting for transfers between devices, swap_x(): return lax.ppermute(value, 'dp', [(i, i ^ 2) for i in range(4)])  96.7 us
    ppermute x8, waiting for transfers between devices, swap_ctx(): return lax.ppermute(value, 'ctx', [(0, 1), (1, 0)])  52.9 us
    pallas_call x9, Pallas kernels, outer(): pl.pallas_call(functools.partial(outer_kernel, len(adds)), grid=(count_m,...  35 us
    pallas_call x1, Pallas kernels, mlp(): pl.pallas_call(functools.partial(mlp_kernel, tuple(calls)), grid_spec=plt...  30.7 us
    psum x4, waiting for transfers between devices, psum_tensor(): return lax.psum(value, 'tensor')  30.5 us
    ppermute x17, waiting for transfers between devices, swap_core(): return lax.ppermute(value, 'dp', [(i, i ^ 1) for i in range(4)])  21.4 us
    add x4, other arithmetic, combine(): return low.astype(F32) + peer.astype(F32)  17.8 us
    pallas_call x1, Pallas kernels, attend_backward(): pl.pallas_call(functools.partial(backward_kernel, chunk, len(key_values))...  16.9 us
  transfers between devices with their start and end apart: 42, of which 25 were waited for; matrix products, arithmetic and copies ran while one was open for 12% of the time, Pallas kernels for 22%

profile of v6, /device:TPU:0, one launch (start us, length us, event | category | flops | bytes accessed | tf_op | source)
XLA Modules:
  0.0 455.0 jit_solution(15554237811875529437)
XLA Ops:
  45.9 8.6 %attend_forward.1 = (bf16[512,512]{1,0:T(8,128)(2,1)S(1)}, f32[8,512]{1,0:T(8,128)S(1)}) custom-call(bf16[512,512]{1,0:T(8,128)(2,1)S(1)} %project_q.1.q_ref, s32[1024,1]{1,0:T(8,128)S(1)} %get-tuple-element.293.code_ref, s32[8,512]{1,0:T(8,128)S(1)} %stack.41.codes_ref, bf16[512,256]{1,0:T(8,128)(2,1)S(1)} %copy-done.17, ...), custom_call_target="tpu_custom_call" | custom-call | flops 1 | bytes 1 | tf_op jit(solution)/shard_map/attend_forward/pallas_call | solution.py:98
  55.9 4.1 out_project.1
  65.0 27.0 %collective-permute-done.29.refs_1_.refs_7_ = bf16[512,2048]{1,0:T(8,128)(2,1)} collective-permute-done((bf16[512,2048]{1,0:T(8,128)(2,1)}, bf16[512,2048]{1,0:T(8,128)(2,1)}, u32[]{:S(2)}, u32[]{:S(2)}) %collective-permute-start.29) | collective-permute-done | bytes 2097184 | tf_op jit(solution)/shard_map/ppermute | solution.py:619
  92.0 48.5 %conditional.5 = (bf16[512,2048]{1,0:T(8,128)(2,1)}, bf16[512,2048]{1,0:T(8,128)(2,1)}, bf16[512,2048]{1,0:T(8,128)(2,1)}, bf16[512,2048]{1,0:T(8,128)(2,1)}, bf...) conditional(s32[]{:T(128)} %convert_element_type.96, () %tuple.96, (bf16[512,2048]{1,0:T(8,128)(2,1)}, ...), branch_computations={%region_3.4_spmd, %region_4.5_spmd} | conditional | flops 1 | bytes 50331924 | solution.py:611
  97.0 5.3 %collective-permute-done.4.d2 = bf16[2048,512]{1,0:T(8,128)(2,1)} collective-permute-done((bf16[2048,512]{1,0:T(8,128)(2,1)S(1)}, bf16[2048,512]{1,0:T(8,128)(2,1)}, u32[]{:S(2)}, u32[]{:S(2)}) %collective-permute-start.4) | collective-permute-done | bytes 2097184 | tf_op jit(solution)/shard_map/cond/branch_1_fun/ppermute | solution.py:615
  102.2 6.1 %early_hidden.1 = f32[512,2048]{1,0:T(8,128)} custom-call(bf16[512,2048]{1,0:T(8,128)(2,1)S(1)} %get-tuple-element.83.g_ref, bf16[2048,512]{1,0:T(8,128)(2,1)} %copy-done.40, bf16[2048,512]{1,0:T(8,128)(2,1)} %collective-permute-done.4.d2), custom_call_target="tpu_custom_call" | custom-call | flops 1 | bytes 1 | tf_op jit(solution)/shard_map/cond/branch_1_fun/early_hidden/pallas_call | solution.py:289
  108.3 32.1 %collective-permute-done = bf16[512,2048]{1,0:T(8,128)(2,1)} collective-permute-done((bf16[512,2048]{1,0:T(8,128)(2,1)}, bf16[512,2048]{1,0:T(8,128)(2,1)}, u32[]{:S(2)}, u32[]{:S(2)}) %collective-permute-start) | collective-permute-done | bytes 2097184 | tf_op jit(solution)/shard_map/cond/branch_1_fun/ppermute | solution.py:627
  140.4 7.6 %conditional.6 = (bf16[512,2048]{1,0:T(8,128)(2,1)}, bf16[2048,512]{1,0:T(8,128)(2,1)}) conditional(s32[]{:T(128)} %convert_element_type.96, () %tuple.95, (bf16[512,2048]{1,0:T(8,128)(2,1)}, bf16[2048,512]{1,0:T(8,128)(2,1)}) %tuple.101), branch_computations={%region_5.6_spmd, %region_6.7_spmd} | conditional | bytes 16777312 | solution.py:611
  141.0 4.0 collective-permute-done.5
  148.1 30.7 %mlp.1 = (bf16[512,2048]{1,0:T(8,128)(2,1)}, bf16[512,2048]{1,0:T(8,128)(2,1)}, bf16[512,2048]{1,0:T(8,128)(2,1)}, bf16[512,2048]{1,0:T(8,128)(2,1)}, bf16[512,2048]{1,0:T(8,128)(2,1)}) custom-call(s32[1]{0:T(128)} %bitcast.9.index_ref, bf16[512,2048]{1,0:T(8,128)(2,1)} %copy-done, bf16[512,2048]{1,0:T(8,128)(2,1)} %all-reduce.6.cloned.1.call-done.branch_ref, ...), custom_call_target="tpu_custom_call" | custom-call | flops 1 | bytes 1 | tf_op jit(solution)/shard_map/mlp/pallas_call | solution.py:398
  179.5 65.3 %conditional.7 = (bf16[2048,512]{1,0:T(8,128)(2,1)}, bf16[1024,2048]{1,0:T(8,128)(2,1)}, bf16[512,2048]{1,0:T(8,128)(2,1)}, bf16[1024,2048]{1,0:T(8,128)(2,1)}, ...) conditional(s32[]{:T(128)} %convert_element_type.96, () %tuple.104, (bf16[512,2048]{1,0:T(8,128)(2,1)}, ...), branch_computations={%region_9.10_spmd, %region_10.11_spmd} | conditional | flops 8 | bytes 100663640 | solution.py:611
  179.5 4.5 down_outer.3
  195.3 11.4 %lift.1 = bf16[512,2048]{1,0:T(8,128)(2,1)} custom-call(bf16[512,2048]{1,0:T(8,128)(2,1)S(1)} %copy-done.29, bf16[2048,512]{1,0:T(8,128)(2,1)S(1)} %copy-done.41, bf16[2048,512]{1,0:T(8,128)(2,1)} %get-tuple-element.92.d1, bf16[2048,512]{1,0:T(8,128)(2,1)} %get-tuple-element.93.d2, bf16[2048,512]{1,0:T(8,128)(2,1)} %get-tuple-element.94.d3), custom_call_target="tpu_custom_call" | custom-call | flops 1 | bytes 1 | tf_op jit(solution)/shard_map/cond/branch_1_fun/lift/pallas_call | solution.py:517
  206.7 4.3 gate_outer.4
  211.0 4.3 up_outer.4
  215.2 26.1 %collective-permute-done.8.refs_1_ = bf16[2048,512]{1,0:T(8,128)(2,1)S(1)} collective-permute-done((bf16[2048,512]{1,0:T(8,128)(2,1)S(1)}, bf16[2048,512]{1,0:T(8,128)(2,1)S(1)}, u32[]{:S(2)}, u32[]{:S(2)}) %collective-permute-start.8) | collective-permute-done | bytes 2097184 | tf_op jit(solution)/shard_map/cond/branch_1_fun/ppermute | solution.py:619
  247.9 19.0 %all-reduce.8.cloned.1.call-done = bf16[512,2048]{1,0:T(8,128)(2,1)} async-done(((bf16[512,2048]{1,0:T(8,128)(2,1)}), bf16[512,2048]{1,0:T(8,128)(2,1)}) %all-reduce.8.cloned.1.call-update) | async-done | bytes 2097168 | tf_op jit(solution)/shard_map/psum | solution.py:650
  272.5 4.8 %multiply_convert_fusion = (bf16[512,2048]{1,0:T(8,128)(2,1)S(1)}, f32[512,2048]{1,0:T(8,128)}, f32[512,2048]{1,0:T(8,128)}) fusion(f32[512]{0:T(512)S(1)} %broadcast_multiply_fusion.1, f32[512]{0:T(512)S(1)} %get-tuple-element.312, bf16[512,2048]{1,0:T(8,128)(2,1)S(1)} %copy-done.28, bf16[512,2048]{1,0:T(8,128)(2,1)S(1)} %copy-done.1, ...), kind=kLoop, calls=%fused_computation.22 | loop fusion | flops 22020096 | bytes 18888704 | tf_op jit(solution)/shard_map/convert_element_type | solution.py:916
  277.4 16.9 %attend_backward.1 = (bf16[512,512]{1,0:T(8,128)(2,1)S(1)}, f32[1024,256]{1,0:T(8,128)S(1)}) custom-call(bf16[512,512]{1,0:T(8,128)(2,1)S(1)} %project_q.1.q_ref, s32[1024,1]{1,0:T(8,128)S(1)} %get-tuple-element.293.code_ref, s32[8,512]{1,0:T(8,128)S(1)} %stack.41.codes_ref, bf16[512,512]{1,0:T(8,128)(2,1)S(1)} %copy-done.37, ...), custom_call_target="tpu_custom_call" | custom-call | flops 1 | bytes 1 | tf_op jit(solution)/shard_map/attend_backward/pallas_call | solution.py:186
  295.9 5.0 %gate_outer.5 = bf16[512,2048]{1,0:T(8,128)(2,1)} custom-call(bf16[512,2048]{1,0:T(8,128)(2,1)S(1)} %copy-done.23, bf16[512,2048]{1,0:T(8,128)(2,1)S(1)} %copy-done.33, bf16[1024,2048]{1,0:T(8,128)(2,1)} %get-tuple-element.234.refs_0_, bf16[512,2048]{1,0:T(8,128)(2,1)} %collective-permute-done.33.refs_1_), custom_call_target="tpu_custom_call" | custom-call | flops 1 | bytes 1 | tf_op jit(solution)/shard_map/gate_outer/pallas_call | solution.py:481
  302.9 5.6 %entry_grad.1 = (bf16[512,768]{1,0:T(8,128)(2,1)S(1)}, bf16[512,2048]{1,0:T(8,128)(2,1)}) custom-call(bf16[512,512]{1,0:T(8,128)(2,1)} %copy-done.22, f32[512,256]{1,0:T(8,128)} %slice.103.own_ref, bf16[512,256]{1,0:T(8,128)(2,1)} %copy-done.56, f32[512,128]{1,0:T(8,128)} %copy-done.2, f32[512,128]{1,0:T(8,128)} %copy-done.3, bf16[512,512]{1,0:T(8,128)(2,1)} %refs_0_.3, ...), custom_call_target="tpu_custom_call" | custom-call | flops 1 | bytes 1 | tf_op jit(solution)/shard_map/entry_grad/pallas_call | solution.py:444
  310.0 11.7 %conditional.8 = (bf16[1024,1280]{1,0:T(8,128)(2,1)}, bf16[512,1280]{1,0:T(8,128)(2,1)}) conditional(s32[]{:T(128)} %convert_element_type.96, () %tuple.111, (bf16[512,512]{1,0:T(8,128)(2,1)S(1)}, bf16[512,2048]{1,0:T(8,128)(2,1)}, bf16[512,2048]{1,0:T(8,128)(2,1)}, bf16[512,768]{1,0:T(8,128)(2,1)S(1)}) %tuple.180), branch_computations={%region_14.15_spmd, %region_15.16_spmd} | conditional | flops 2 | bytes 27263088 | solution.py:611
  313.3 5.0 %collective-permute-done.11.refs_0_ = bf16[1024,1280]{1,0:T(8,128)(2,1)} collective-permute-done((bf16[1024,1280]{1,0:T(8,128)(2,1)S(1)}, bf16[1024,1280]{1,0:T(8,128)(2,1)}, u32[]{:S(2)}, u32[]{:S(2)}) %collective-permute-start.11) | collective-permute-done | bytes 2621472 | tf_op jit(solution)/shard_map/cond/branch_1_fun/ppermute | solution.py:615
  326.0 10.9 %collective-permute-done.34.refs_1_ = bf16[512,2048]{1,0:T(8,128)(2,1)} collective-permute-done((bf16[512,2048]{1,0:T(8,128)(2,1)}, bf16[512,2048]{1,0:T(8,128)(2,1)}, u32[]{:S(2)}, u32[]{:S(2)}) %collective-permute-start.34) | collective-permute-done | bytes 2097184 | tf_op jit(solution)/shard_map/ppermute | solution.py:619
  337.0 5.8 %up_outer.5 = bf16[512,2048]{1,0:T(8,128)(2,1)} custom-call(bf16[512,2048]{1,0:T(8,128)(2,1)} %get-tuple-element.222.a_ref, bf16[512,2048]{1,0:T(8,128)(2,1)} %get-tuple-element.224.b_ref, bf16[1024,2048]{1,0:T(8,128)(2,1)} %get-tuple-element.237.refs_0_, bf16[512,2048]{1,0:T(8,128)(2,1)} %collective-permute-done.34.refs_1_), custom_call_target="tpu_custom_call" | custom-call | flops 1 | bytes 1 | tf_op jit(solution)/shard_map/up_outer/pallas_call | solution.py:481
  344.4 10.3 %all-reduce.10.cloned.1.call-done = bf16[512,2048]{1,0:T(8,128)(2,1)} async-done(((bf16[512,2048]{1,0:T(8,128)(2,1)}), bf16[512,2048]{1,0:T(8,128)(2,1)}) %all-reduce.10.cloned.1.call-update) | async-done | bytes 2097168 | tf_op jit(solution)/shard_map/psum | solution.py:650
  357.0 28.6 %collective-permute-done.37 = bf16[512,1280]{1,0:T(8,128)(2,1)S(1)} collective-permute-done((bf16[512,1280]{1,0:T(8,128)(2,1)}, bf16[512,1280]{1,0:T(8,128)(2,1)S(1)}, u32[]{:S(2)}, u32[]{:S(2)}) %collective-permute-start.37) | collective-permute-done | bytes 1310752 | tf_op jit(solution)/shard_map/ppermute | solution.py:619
  385.6 14.6 %collective-permute-done.36 = bf16[512,2048]{1,0:T(8,128)(2,1)} collective-permute-done((bf16[512,2048]{1,0:T(8,128)(2,1)}, bf16[512,2048]{1,0:T(8,128)(2,1)}, u32[]{:S(2)}, u32[]{:S(2)}) %collective-permute-start.36) | collective-permute-done | bytes 2097184 | tf_op jit(solution)/shard_map/ppermute | solution.py:627
  400.2 41.6 %conditional.9 = (f32[2,512]{1,0:T(2,128)}, bf16[512,2048]{1,0:T(8,128)(2,1)}, f32[2048,512]{1,0:T(8,128)}, f32[512,2048]{1,0:T(8,128)}, f32[512,2048]{1,0:T(8,1...) conditional(s32[]{:T(128)} %convert_element_type.96, () %tuple.83, ...), branch_computations={%region_17.18_spmd, %region_18.19_spmd} | conditional | flops 23995432 | bytes 92607496 | solution.py:611
  406.2 8.3 %convert_add_fusion = (f32[512,2048]{1,0:T(8,128)}, f32[512,2048]{1,0:T(8,128)}) fusion(bf16[512,2048]{1,0:T(8,128)(2,1)} %get-tuple-element.110, bf16[512,2048]{1,0:T(8,128)(2,1)} %get-tuple-element.109, bf16[512,2048]{1,0:T(8,128)(2,1)} %get-tuple-element.108, bf16[512,2048]{1,0:T(8,128)(2,1)S(1)} %copy-done.42), kind=kLoop, calls=%fused_computation | loop fusion | flops 6291456 | bytes 16777216 | tf_op jit(solution)/shard_map/cond/branch_1_fun/add | solution.py:723
  417.1 4.9 %convert_add_fusion.2 = f32[2048,512]{1,0:T(8,128)} fusion(bf16[2048,512]{1,0:T(8,128)(2,1)} %get-tuple-element.106, bf16[2048,512]{1,0:T(8,128)(2,1)} %get-tuple-element.105), kind=kLoop, calls=%fused_computation.2 | loop fusion | flops 3145728 | bytes 8388608 | tf_op jit(solution)/shard_map/cond/branch_1_fun/add | solution.py:723
  442.8 5.3 %exit_grad.1 = bf16[512,2048]{1,0:T(8,128)(2,1)} custom-call(s32[1]{0:T(128)} %bitcast.12.index_ref, f32[512,2048]{1,0:T(8,128)} %get-tuple-element.263.middle_ref, bf16[512,2048]{1,0:T(8,128)(2,1)} %all-reduce.12.cloned.1.call-done.dh_ref, bf16[512,2048]{1,0:T(8,128)(2,1)} %copy-done, f32[1,2048]{1,0:T(1,128)} %maximum_convert_fusion.1.gain_ref), custom_call_target="tpu_custom_call" | custom-call | flops 1 | bytes 1 | tf_op jit(solution)/shard_map/exit_grad/pallas_call | solution.py:588
  (280 shorter events, 125.7 us)
Async XLA Ops:
  7.2 140.9 %all-reduce.6.cloned.1.call-start = ((), (), s32[]{:S(2)}) async-start(), calls=%async_computation | async-start | bytes 4194304 | tf_op jit(solution)/shard_map/psum | solution.py:650
  7.7 15.7 %collective-permute-start.23 = (bf16[512,512]{1,0:T(8,128)(2,1)}, bf16[512,512]{1,0:T(8,128)(2,1)}, u32[]{:S(2)}, u32[]{:S(2)}) collective-permute-start(bf16[512,512]{1,0:T(8,128)(2,1)} %refs_0_.3), channel_id=1, source_target_pairs={{0,16},{8,24},{16,0},{24,8},{1,17},{9,25},{17,1},{25,9},{2,18},{10... | collective-permute-start | bytes 1572872 | tf_op jit(solution)/shard_map/ppermute | solution.py:619
  13.6 15.7 %collective-permute-start.20 = (bf16[544,256]{1,0:T(8,128)(2,1)S(1)}, bf16[544,256]{1,0:T(8,128)(2,1)}, u32[]{:S(2)}, u32[]{:S(2)}) collective-permute-start(bf16[544,256]{1,0:T(8,128)(2,1)S(1)} %fusion.13.p0.refs_4_), channel_id=1, source_target_pairs={{0,16},{8,24},{16,0},{24,8},{1,17},{9,25},{17,1},{25,9},{2,18},{10... | collective-permute-start | bytes 835592 | tf_op jit(solution)/shard_map/ppermute | solution.py:619
  13.7 9.8 %collective-permute-start.21 = (bf16[544,256]{1,0:T(8,128)(2,1)S(1)}, bf16[544,256]{1,0:T(8,128)(2,1)S(1)}, u32[]{:S(2)}, u32[]{:S(2)}) collective-permute-start(bf16[544,256]{1,0:T(8,128)(2,1)S(1)} %fusion.13.p0.refs_4_), channel_id=1, source_target_pairs={{0,8},{8,0},{16,24},{24,16},{1,9},{9,1},{17,25},{25,17},{2,10},{10... | collective-permute-start | bytes 835592 | tf_op jit(solution)/shard_map/ppermute | solution.py:615
  23.4 12.9 %collective-permute-start.24 = (bf16[512,512]{1,0:T(8,128)(2,1)}, bf16[512,512]{1,0:T(8,128)(2,1)S(1)}, u32[]{:S(2)}, u32[]{:S(2)}) collective-permute-start(bf16[512,512]{1,0:T(8,128)(2,1)} %collective-permute-done.23.p1.refs_1_), channel_id=1, source_target_pairs={{0,8},{8,0},{16,24},{24,16},{1,9},{9,1},{17,25},{25,17},{2,10},{10... | collective-permute-start | bytes 1572872 | tf_op jit(solution)/shard_map/ppermute | solution.py:615
  23.5 19.6 %collective-permute-start.26 = (bf16[512,512]{1,0:T(8,128)(2,1)}, bf16[512,512]{1,0:T(8,128)(2,1)}, u32[]{:S(2)}, u32[]{:S(2)}) collective-permute-start(bf16[512,512]{1,0:T(8,128)(2,1)} %o0.3), channel_id=1, source_target_pairs={{0,16},{8,24},{16,0},{24,8},{1,17},{9,25},{17,1},{25,9},{2,18},{10... | collective-permute-start | bytes 1572872 | tf_op jit(solution)/shard_map/ppermute | solution.py:619
  34.3 8.8 %collective-permute-start.25 = (bf16[512,256]{1,0:T(8,128)(2,1)S(1)}, bf16[512,256]{1,0:T(8,128)(2,1)S(1)}, u32[]{:S(2)}, u32[]{:S(2)}) collective-permute-start(bf16[512,256]{1,0:T(8,128)(2,1)S(1)} %get-tuple-element.201.refs_0_), channel_id=1, source_target_pairs={{0,4},{4,0},{1,5},{5,1},{2,6},{6,2},{3,7},{7,3},{8,12},{12,8},{9,1... | collective-permute-start | bytes 786440 | tf_op jit(solution)/shard_map/ppermute | solution.py:627
  36.3 18.6 %collective-permute-start.27 = (bf16[512,512]{1,0:T(8,128)(2,1)}, bf16[512,512]{1,0:T(8,128)(2,1)S(1)}, u32[]{:S(2)}, u32[]{:S(2)}) collective-permute-start(bf16[512,512]{1,0:T(8,128)(2,1)} %o0.3), channel_id=1, source_target_pairs={{0,8},{8,0},{16,24},{24,16},{1,9},{9,1},{17,25},{25,17},{2,10},{10... | collective-permute-start | bytes 1572872 | tf_op jit(solution)/shard_map/ppermute | solution.py:615
  43.1 11.8 %collective-permute-start.28 = (bf16[512,512]{1,0:T(8,128)(2,1)}, bf16[512,512]{1,0:T(8,128)(2,1)S(1)}, u32[]{:S(2)}, u32[]{:S(2)}) collective-permute-start(bf16[512,512]{1,0:T(8,128)(2,1)} %collective-permute-done.26.o1), channel_id=1, source_target_pairs={{0,8},{8,0},{16,24},{24,16},{1,9},{9,1},{17,25},{25,17},{2,10},{10... | collective-permute-start | bytes 1572872 | tf_op jit(solution)/shard_map/ppermute | solution.py:615
  43.2 48.8 %collective-permute-start.29 = (bf16[512,2048]{1,0:T(8,128)(2,1)}, bf16[512,2048]{1,0:T(8,128)(2,1)}, u32[]{:S(2)}, u32[]{:S(2)}) collective-permute-start(bf16[512,2048]{1,0:T(8,128)(2,1)} %pad_maximum_fusion.2), channel_id=1, source_target_pairs={{0,16},{8,24},{16,0},{24,8},{1,17},{9,25},{17,1},{25,9},{2,18},{10... | collective-permute-start | bytes 6291464 | tf_op jit(solution)/shard_map/ppermute | solution.py:619
  54.5 85.9 %collective-permute-start.30 = (bf16[2048,512]{1,0:T(8,128)(2,1)}, bf16[2048,512]{1,0:T(8,128)(2,1)}, u32[]{:S(2)}, u32[]{:S(2)}) collective-permute-start(bf16[2048,512]{1,0:T(8,128)(2,1)} %param.33), channel_id=1, source_target_pairs={{0,16},{8,24},{16,0},{24,8},{1,17},{9,25},{17,1},{25,9},{2,18},{10... | collective-permute-start | bytes 6291464 | tf_op jit(solution)/shard_map/ppermute | solution.py:619
  60.0 206.9 %all-reduce.8.cloned.1.call-start = ((), (), s32[]{:S(2)}) async-start(), calls=%async_computation.1 | async-start | bytes 4194304 | tf_op jit(solution)/shard_map/psum | solution.py:650
  92.0 48.4 %collective-permute-start = (bf16[512,2048]{1,0:T(8,128)(2,1)}, bf16[512,2048]{1,0:T(8,128)(2,1)}, u32[]{:S(2)}, u32[]{:S(2)}) collective-permute-start(bf16[512,2048]{1,0:T(8,128)(2,1)} %get-tuple-element.80), channel_id=1, source_target_pairs={{0,4},{4,0},{1,5},{5,1},{2,6},{6,2},{3,7},{7,3},{8,12},{12,8},{9,1... | collective-permute-start | bytes 6291464 | tf_op jit(solution)/shard_map/cond/branch_1_fun/ppermute | solution.py:627
  96.5 43.9 %collective-permute-start.2 = (bf16[512,2048]{1,0:T(8,128)(2,1)}, bf16[512,2048]{1,0:T(8,128)(2,1)}, u32[]{:S(2)}, u32[]{:S(2)}) collective-permute-start(bf16[512,2048]{1,0:T(8,128)(2,1)} %get-tuple-element.79), channel_id=1, source_target_pairs={{0,8},{8,0},{16,24},{24,16},{1,9},{9,1},{17,25},{25,17},{2,10},{10... | collective-permute-start | bytes 6291464 | tf_op jit(solution)/shard_map/cond/branch_1_fun/ppermute | solution.py:615
  96.8 43.6 %collective-permute-start.3 = (bf16[512,2048]{1,0:T(8,128)(2,1)}, bf16[512,2048]{1,0:T(8,128)(2,1)}, u32[]{:S(2)}, u32[]{:S(2)}) collective-permute-start(bf16[512,2048]{1,0:T(8,128)(2,1)} %get-tuple-element.80), channel_id=1, source_target_pairs={{0,8},{8,0},{16,24},{24,16},{1,9},{9,1},{17,25},{25,17},{2,10},{10... | collective-permute-start | bytes 6291464 | tf_op jit(solution)/shard_map/cond/branch_1_fun/ppermute | solution.py:615
  140.5 7.5 %collective-permute-start.6 = (bf16[2048,512]{1,0:T(8,128)(2,1)}, bf16[2048,512]{1,0:T(8,128)(2,1)}, u32[]{:S(2)}, u32[]{:S(2)}) collective-permute-start(bf16[2048,512]{1,0:T(8,128)(2,1)} %get-tuple-element.85), channel_id=1, source_target_pairs={{0,8},{8,0},{16,24},{24,16},{1,9},{9,1},{17,25},{25,17},{2,10},{10... | collective-permute-start | bytes 6291464 | tf_op jit(solution)/shard_map/cond/branch_1_fun/ppermute | solution.py:615
  178.8 176.0 %all-reduce.10.cloned.1.call-start = ((), (), s32[]{:S(2)}) async-start(), calls=%async_computation.2 | async-start | bytes 4194304 | tf_op jit(solution)/shard_map/psum | solution.py:650
  184.1 7.2 %collective-permute-start.7 = (bf16[2048,1024]{1,0:T(8,128)(2,1)S(1)}, bf16[2048,1024]{1,0:T(8,128)(2,1)S(1)}, u32[]{:S(2)}, u32[]{:S(2)}) collective-permute-start(bf16[2048,1024]{1,0:T(8,128)(2,1)S(1)} %down_outer.3), channel_id=1, source_target_pairs={{0,8},{8,0},{16,24},{24,16},{1,9},{9,1},{17,25},{25,17},{2,10},{10... | collective-permute-start | bytes 12582920 | tf_op jit(solution)/shard_map/cond/branch_1_fun/ppermute | solution.py:615
  186.9 19.8 %collective-permute-start.9 = (bf16[1024,2048]{1,0:T(8,128)(2,1)S(1)}, bf16[1024,2048]{1,0:T(8,128)(2,1)}, u32[]{:S(2)}, u32[]{:S(2)}) collective-permute-start(bf16[1024,2048]{1,0:T(8,128)(2,1)S(1)} %gate_outer.3), channel_id=1, source_target_pairs={{0,8},{8,0},{16,24},{24,16},{1,9},{9,1},{17,25},{25,17},{2,10},{10... | collective-permute-start | bytes 12582920 | tf_op jit(solution)/shard_map/cond/branch_1_fun/ppermute | solution.py:615
  190.1 20.8 %collective-permute-start.10 = (bf16[1024,2048]{1,0:T(8,128)(2,1)S(1)}, bf16[1024,2048]{1,0:T(8,128)(2,1)}, u32[]{:S(2)}, u32[]{:S(2)}) collective-permute-start(bf16[1024,2048]{1,0:T(8,128)(2,1)S(1)} %up_outer.3), channel_id=1, source_target_pairs={{0,8},{8,0},{16,24},{24,16},{1,9},{9,1},{17,25},{25,17},{2,10},{10... | collective-permute-start | bytes 12582920 | tf_op jit(solution)/shard_map/cond/branch_1_fun/ppermute | solution.py:615
  193.6 47.7 %collective-permute-start.8 = (bf16[2048,512]{1,0:T(8,128)(2,1)S(1)}, bf16[2048,512]{1,0:T(8,128)(2,1)S(1)}, u32[]{:S(2)}, u32[]{:S(2)}) collective-permute-start(bf16[2048,512]{1,0:T(8,128)(2,1)S(1)} %down_outer.4), channel_id=1, source_target_pairs={{0,16},{8,24},{16,0},{24,8},{1,17},{9,25},{17,1},{25,9},{2,18},{10... | collective-permute-start | bytes 6291464 | tf_op jit(solution)/shard_map/cond/branch_1_fun/ppermute | solution.py:619
  244.8 51.1 %collective-permute-start.33 = (bf16[512,2048]{1,0:T(8,128)(2,1)}, bf16[512,2048]{1,0:T(8,128)(2,1)}, u32[]{:S(2)}, u32[]{:S(2)}) collective-permute-start(bf16[512,2048]{1,0:T(8,128)(2,1)} %get-tuple-element.235), channel_id=1, source_target_pairs={{0,16},{8,24},{16,0},{24,8},{1,17},{9,25},{17,1},{25,9},{2,18},{10... | collective-permute-start | bytes 6291464 | tf_op jit(solution)/shard_map/ppermute | solution.py:619
  246.4 98.1 %collective-permute-start.32 = (bf16[2048,512]{1,0:T(8,128)(2,1)}, bf16[2048,512]{1,0:T(8,128)(2,1)}, u32[]{:S(2)}, u32[]{:S(2)}) collective-permute-start(bf16[2048,512]{1,0:T(8,128)(2,1)} %get-tuple-element.226), channel_id=1, source_target_pairs={{0,4},{4,0},{1,5},{5,1},{2,6},{6,2},{3,7},{7,3},{8,12},{12,8},{9,1... | collective-permute-start | bytes 6291464 | tf_op jit(solution)/shard_map/ppermute | solution.py:627
  266.9 70.0 %collective-permute-start.34 = (bf16[512,2048]{1,0:T(8,128)(2,1)}, bf16[512,2048]{1,0:T(8,128)(2,1)}, u32[]{:S(2)}, u32[]{:S(2)}) collective-permute-start(bf16[512,2048]{1,0:T(8,128)(2,1)} %get-tuple-element.239), channel_id=1, source_target_pairs={{0,16},{8,24},{16,0},{24,8},{1,17},{9,25},{17,1},{25,9},{2,18},{10... | collective-permute-start | bytes 6291464 | tf_op jit(solution)/shard_map/ppermute | solution.py:619
  294.4 7.8 %collective-permute-start.31 = (bf16[512,256]{1,0:T(8,128)(2,1)S(1)}, bf16[512,256]{1,0:T(8,128)(2,1)S(1)}, u32[]{:S(2)}, u32[]{:S(2)}) collective-permute-start(bf16[512,256]{1,0:T(8,128)(2,1)S(1)} %slice.151), channel_id=1, source_target_pairs={{0,4},{4,0},{1,5},{5,1},{2,6},{6,2},{3,7},{7,3},{8,12},{12,8},{9,1... | collective-permute-start | bytes 786440 | tf_op jit(solution)/shard_map/ppermute | solution.py:627
  308.5 77.1 %collective-permute-start.35 = (bf16[512,2048]{1,0:T(8,128)(2,1)}, bf16[512,2048]{1,0:T(8,128)(2,1)}, u32[]{:S(2)}, u32[]{:S(2)}) collective-permute-start(bf16[512,2048]{1,0:T(8,128)(2,1)} %gate_outer.5), channel_id=1, source_target_pairs={{0,4},{4,0},{1,5},{5,1},{2,6},{6,2},{3,7},{7,3},{8,12},{12,8},{9,1... | collective-permute-start | bytes 6291464 | tf_op jit(solution)/shard_map/ppermute | solution.py:627
  325.7 117.1 %all-reduce.12.cloned.1.call-start = ((), (), s32[]{:S(2)}) async-start(), calls=%async_computation.3 | async-start | bytes 4194304 | tf_op jit(solution)/shard_map/psum | solution.py:650
  342.8 57.4 %collective-permute-start.36 = (bf16[512,2048]{1,0:T(8,128)(2,1)}, bf16[512,2048]{1,0:T(8,128)(2,1)}, u32[]{:S(2)}, u32[]{:S(2)}) collective-permute-start(bf16[512,2048]{1,0:T(8,128)(2,1)} %up_outer.5), channel_id=1, source_target_pairs={{0,4},{4,0},{1,5},{5,1},{2,6},{6,2},{3,7},{7,3},{8,12},{12,8},{9,1... | collective-permute-start | bytes 6291464 | tf_op jit(solution)/shard_map/ppermute | solution.py:627
  354.8 30.8 %collective-permute-start.37 = (bf16[512,1280]{1,0:T(8,128)(2,1)}, bf16[512,1280]{1,0:T(8,128)(2,1)S(1)}, u32[]{:S(2)}, u32[]{:S(2)}) collective-permute-start(bf16[512,1280]{1,0:T(8,128)(2,1)} %get-tuple-element.245), channel_id=1, source_target_pairs={{0,16},{8,24},{16,0},{24,8},{1,17},{9,25},{17,1},{25,9},{2,18},{10... | collective-permute-start | bytes 3932168 | tf_op jit(solution)/shard_map/ppermute | solution.py:619
  404.6 28.4 %collective-permute-start.18 = (bf16[512,1280]{1,0:T(8,128)(2,1)S(1)}, bf16[512,1280]{1,0:T(8,128)(2,1)}, u32[]{:S(2)}, u32[]{:S(2)}) collective-permute-start(bf16[512,1280]{1,0:T(8,128)(2,1)S(1)} %entry_outer.5), channel_id=1, source_target_pairs={{0,4},{4,0},{1,5},{5,1},{2,6},{6,2},{3,7},{7,3},{8,12},{12,8},{9,1... | collective-permute-start | bytes 3932168 | tf_op jit(solution)/shard_map/cond/branch_1_fun/ppermute | solution.py:627
  405.6 8.9 %collective-permute-start.13 = (f32[2,512]{1,0:T(2,128)S(1)}, f32[2,512]{1,0:T(2,128)S(1)}, u32[]{:S(2)}, u32[]{:S(2)}) collective-permute-start(f32[2,512]{1,0:T(2,128)S(1)} %get-tuple-element.278), channel_id=1, source_target_pairs={{0,16},{8,24},{16,0},{24,8},{1,17},{9,25},{17,1},{25,9},{2,18},{10... | collective-permute-start | bytes 12296 | tf_op jit(solution)/shard_map/cond/branch_1_fun/ppermute | solution.py:619
  415.8 6.2 %collective-permute-start.15 = (f32[2,512]{1,0:T(2,128)S(1)}, f32[2,512]{1,0:T(2,128)S(1)}, u32[]{:S(2)}, u32[]{:S(2)}) collective-permute-start(f32[2,512]{1,0:T(2,128)S(1)} %get-tuple-element.102), channel_id=1, source_target_pairs={{0,24},{8,16},{16,8},{24,0},{1,25},{9,17},{17,9},{25,1},{2,26},{10... | collective-permute-start | bytes 12296 | tf_op jit(solution)/shard_map/cond/branch_1_fun/ppermute | solution.py:623
  (74 other events, 514.5 us)
Sparse Core Ops, SparseCore 0:
  60.1 87.9 all-reduce.5
  179.0 87.9 all-reduce.7
  269.3 85.4 all-reduce.9
  357.1 85.6 all-reduce.11

commit v7 on v6

--- a/solution.py
+++ b/solution.py
@@ -202,17 +202,29 @@
     )(queries, key_code, query_codes, attended, grad_branch, lse, turn, *out_pieces, *key_values)
 
 
-def out_kernel(attended_ref, o0, o1, o2, o3, branch_ref):
+def out_kernel(attended_ref, o0, o1, o2, o3, branch_ref, built, sems):
     block = o0.shape[1]
-    for r, piece in enumerate((o0, o1, o2, o3)):
-        branch_ref[:, r * block : (r + 1) * block] = dot_nn(attended_ref[...], piece[...]).astype(BF)
+    count = sems.shape[0]
+    height = built.shape[0] // count
+    copies = []
+    for i in range(count):
+        at = slice(i * height, (i + 1) * height)
+        for r, piece in enumerate((o0, o1, o2, o3)):
+            built[at, r * block : (r + 1) * block] = dot_nn(attended_ref[at, :], piece[...]).astype(BF)
+        copies.append(pltpu.make_async_copy(built.at[at], branch_ref.at[at], sems.at[i]))
+        copies[-1].start()
+    for copy in copies:
+        copy.wait()
 
 
 def out_project(attended, out_pieces):
+    out = jax.ShapeDtypeStruct((attended.shape[0], 4 * out_pieces[0].shape[1]), BF)
     return pl.pallas_call(
         out_kernel,
-        out_shape=jax.ShapeDtypeStruct((attended.shape[0], 4 * out_pieces[0].shape[1]), BF),
-        compiler_params=pltpu.CompilerParams(vmem_limit_bytes=60 << 20),
+        out_shape=out,
+        out_specs=pl.BlockSpec(memory_space=pltpu.HBM),
+        scratch_shapes=[pltpu.VMEM(out.shape, BF), pltpu.SemaphoreType.DMA((2,))],
+        compiler_params=pltpu.CompilerParams(vmem_limit_bytes=16 << 20),
         cost_estimate=LIGHT,
         name="out_project",
     )(attended, *out_pieces)
@@ -299,11 +311,13 @@
     )(grad, own, near)
 
 
-def mlp_kernel(side_places, index_ref, x_ref, branch_ref, gain_ref, g_ref, early_ref, *refs):
+def mlp_kernel(side_places, index_ref, x_hbm, branch_hbm, gain_ref, g_ref, early_ref, *refs):
     count = len(side_places[0])
     sides, downs = (refs[:count], refs[count : 2 * count]), refs[2 * count : 2 * count + 2]
     h_ref, hidden_ref, dgate_ref, dup_ref, dh_ref = refs[2 * count + 2 : 2 * count + 7]
-    grad, dgates, dups, wide, tall, sems, grad_sem = refs[2 * count + 7 :]
+    grad, dgates, dups, built, wide, tall, sems, grad_sem, out_sems, x_ref, branch_ref, in_sems = refs[
+        2 * count + 7 :
+    ]
     step, steps = pl.program_id(0), pl.num_programs(0)
     block = h_ref.shape[1] // 4
     tile = tall.shape[2]
@@ -323,8 +337,24 @@
 
     grad_copy = pltpu.make_async_copy(g_ref, grad, grad_sem)
 
+    def out_copy(r):
+        at = rows_at(r, block)
+        return pltpu.make_async_copy(built.at[:, at], dh_ref.at[:, at], out_sems.at[r])
+
+    height = 128
+
+    def in_copies(i):
+        at = rows_at(i, height)
+        return [
+            pltpu.make_async_copy(there.at[at], here.at[at], in_sems.at[k, i])
+            for k, (there, here) in enumerate(((x_hbm, x_ref), (branch_hbm, branch_ref)))
+        ]
+
     @pl.when(step == 0)
     def _():
+        for i in range(in_sems.shape[1]):
+            for copy in in_copies(i):
+                copy.start()
         for copy in copies(0):
             copy.start()
         grad_copy.start()
@@ -338,10 +368,10 @@
 
     @pl.when(step == 0)
     def _():
-        height = 128
-
         def norm(i, unused):
             at = rows_at(i, height)
+            for copy in in_copies(i):
+                copy.wait()
             middle = x_ref[at, :].astype(F32) + RESIDUAL * branch_ref[at, :].astype(F32)
             square = jnp.mean(middle * middle, axis=1, keepdims=True)
             h_ref[at, :] = (middle * lax.rsqrt(square + EPSILON) * gain_ref[...]).astype(BF)
@@ -374,10 +404,16 @@
         def block_of(r, unused):
             at = rows_at(r, block)
             term = dot_nt(dgates[...], wide[0, at, :]) + dot_nt(dups[...], wide[1, at, :])
-            dh_ref[:, at] = term.astype(BF)
+            built[:, at] = term.astype(BF)
+            out_copy(r).start()
             return unused
 
+        def end(r, unused):
+            out_copy(r).wait()
+            return unused
+
         lax.fori_loop(0, 4, block_of, 0)
+        lax.fori_loop(0, 4, end, 0)
 
 
 def mlp(tokens, branch, gain, grad, early, index, gates, ups, downs):
@@ -400,18 +436,24 @@
         grid_spec=pltpu.PrefetchScalarGridSpec(
             num_scalar_prefetch=1,
             grid=(hidden // tile,),
-            in_specs=[whole, whole, pl.BlockSpec((1, model), lambda j, s: (0, 0))]
+            in_specs=[pl.BlockSpec(memory_space=pl.ANY)] * 2
+            + [pl.BlockSpec((1, model), lambda j, s: (0, 0))]
             + [pl.BlockSpec(memory_space=pl.ANY), out]
             + [pl.BlockSpec(memory_space=pl.ANY)] * count,
-            out_specs=[whole] + [out] * 3 + [whole],
+            out_specs=[whole] + [out] * 3 + [pl.BlockSpec(memory_space=pltpu.HBM)],
             scratch_shapes=[
                 pltpu.VMEM((rows, model), BF),
                 pltpu.VMEM((rows, hidden), BF),
                 pltpu.VMEM((rows, hidden), BF),
+                pltpu.VMEM((rows, model), BF),
                 pltpu.VMEM((2, model, hidden), BF),
                 pltpu.VMEM((hidden // tile, 2, tile, block), BF),
                 pltpu.SemaphoreType.DMA((hidden // tile, count)),
                 pltpu.SemaphoreType.DMA,
+                pltpu.SemaphoreType.DMA((4,)),
+                pltpu.VMEM((rows, model), BF),
+                pltpu.VMEM((rows, model), BF),
+                pltpu.SemaphoreType.DMA((2, rows // 128)),
             ],
         ),
         out_shape=[jax.ShapeDtypeStruct((rows, model), BF)]

time: 463 us -> 463 us (level)
  transfers between devices with their start and end apart: 42 -> 42, of which waited for: 25 -> 24; matrix products, arithmetic and copies ran while one was open for 12% -> 12% of each run, Pallas kernels for 22% -> 22%
where the time goes in v7:
time: 463 us; the launch traced here: 455 us
  waiting for transfers between devices  208 us (45%)
  Pallas kernels  138 us (30%)
  other arithmetic  41.8 us (9%)
  starting transfers between devices  32.8 us (7%)
  local copies, waits for them, and re-layouts  18.7 us (4%)
  between operations  15.6 us (3%)
    ppermute x10, waiting for transfers between devices, swap_x(): return lax.ppermute(value, 'dp', [(i, i ^ 2) for i in range(4)])  97.8 us
    ppermute x8, waiting for transfers between devices, swap_ctx(): return lax.ppermute(value, 'ctx', [(0, 1), (1, 0)])  52.8 us
    pallas_call x9, Pallas kernels, outer(): pl.pallas_call(functools.partial(outer_kernel, len(adds)), grid=(count_m,...  35 us
    pallas_call x1, Pallas kernels, mlp(): pl.pallas_call(functools.partial(mlp_kernel, tuple(calls)), grid_spec=plt...  30.8 us
    psum x4, waiting for transfers between devices, psum_tensor(): return lax.psum(value, 'tensor')  30.3 us
    ppermute x17, waiting for transfers between devices, swap_core(): return lax.ppermute(value, 'dp', [(i, i ^ 1) for i in range(4)])  21.4 us
    add x4, other arithmetic, combine(): return low.astype(F32) + peer.astype(F32)  17.8 us
    pallas_call x1, Pallas kernels, attend_backward(): pl.pallas_call(functools.partial(backward_kernel, chunk, len(key_values))...  16.9 us
  transfers between devices with their start and end apart: 42, of which 24 were waited for; matrix products, arithmetic and copies ran while one was open for 12% of the time, Pallas kernels for 22%

profile of v7, /device:TPU:0, one launch (start us, length us, event | category | flops | bytes accessed | tf_op | source)
XLA Modules:
  0.0 455.1 jit_solution(4831929739726464545)
XLA Ops:
  45.9 8.6 %attend_forward.1 = (bf16[512,512]{1,0:T(8,128)(2,1)S(1)}, f32[8,512]{1,0:T(8,128)S(1)}) custom-call(bf16[512,512]{1,0:T(8,128)(2,1)S(1)} %project_q.1.q_ref, s32[1024,1]{1,0:T(8,128)S(1)} %get-tuple-element.293.code_ref, s32[8,512]{1,0:T(8,128)S(1)} %stack.41.codes_ref, bf16[512,256]{1,0:T(8,128)(2,1)S(1)} %copy-done.17, ...), custom_call_target="tpu_custom_call" | custom-call | flops 1 | bytes 1 | tf_op jit(solution)/shard_map/attend_forward/pallas_call | solution.py:98
  63.8 28.1 %collective-permute-done.29.refs_1_.refs_7_ = bf16[512,2048]{1,0:T(8,128)(2,1)} collective-permute-done((bf16[512,2048]{1,0:T(8,128)(2,1)}, bf16[512,2048]{1,0:T(8,128)(2,1)}, u32[]{:S(2)}, u32[]{:S(2)}) %collective-permute-start.29) | collective-permute-done | bytes 2097184 | tf_op jit(solution)/shard_map/ppermute | solution.py:661
  92.0 48.5 %conditional.5 = (bf16[512,2048]{1,0:T(8,128)(2,1)}, bf16[512,2048]{1,0:T(8,128)(2,1)}, bf16[512,2048]{1,0:T(8,128)(2,1)}, bf16[512,2048]{1,0:T(8,128)(2,1)}, bf...) conditional(s32[]{:T(128)} %convert_element_type.96, () %tuple.96, (bf16[512,2048]{1,0:T(8,128)(2,1)}, ...), branch_computations={%region_3.4_spmd, %region_4.5_spmd} | conditional | flops 1 | bytes 50331924 | solution.py:653
  97.0 5.3 %collective-permute-done.4.d2 = bf16[2048,512]{1,0:T(8,128)(2,1)} collective-permute-done((bf16[2048,512]{1,0:T(8,128)(2,1)S(1)}, bf16[2048,512]{1,0:T(8,128)(2,1)}, u32[]{:S(2)}, u32[]{:S(2)}) %collective-permute-start.4) | collective-permute-done | bytes 2097184 | tf_op jit(solution)/shard_map/cond/branch_1_fun/ppermute | solution.py:657
  102.2 6.1 %early_hidden.1 = f32[512,2048]{1,0:T(8,128)} custom-call(bf16[512,2048]{1,0:T(8,128)(2,1)S(1)} %get-tuple-element.83.g_ref, bf16[2048,512]{1,0:T(8,128)(2,1)} %copy-done.40, bf16[2048,512]{1,0:T(8,128)(2,1)} %collective-permute-done.4.d2), custom_call_target="tpu_custom_call" | custom-call | flops 1 | bytes 1 | tf_op jit(solution)/shard_map/cond/branch_1_fun/early_hidden/pallas_call | solution.py:301
  108.3 32.1 %collective-permute-done = bf16[512,2048]{1,0:T(8,128)(2,1)} collective-permute-done((bf16[512,2048]{1,0:T(8,128)(2,1)}, bf16[512,2048]{1,0:T(8,128)(2,1)}, u32[]{:S(2)}, u32[]{:S(2)}) %collective-permute-start) | collective-permute-done | bytes 2097184 | tf_op jit(solution)/shard_map/cond/branch_1_fun/ppermute | solution.py:669
  140.4 7.6 %conditional.6 = (bf16[512,2048]{1,0:T(8,128)(2,1)}, bf16[2048,512]{1,0:T(8,128)(2,1)}) conditional(s32[]{:T(128)} %convert_element_type.96, () %tuple.95, (bf16[512,2048]{1,0:T(8,128)(2,1)}, bf16[2048,512]{1,0:T(8,128)(2,1)}) %tuple.101), branch_computations={%region_5.6_spmd, %region_6.7_spmd} | conditional | bytes 16777312 | solution.py:653
  141.0 4.0 collective-permute-done.5
  148.0 30.8 %mlp.1 = (bf16[512,2048]{1,0:T(8,128)(2,1)}, bf16[512,2048]{1,0:T(8,128)(2,1)}, bf16[512,2048]{1,0:T(8,128)(2,1)}, bf16[512,2048]{1,0:T(8,128)(2,1)}, bf16[512,2048]{1,0:T(8,128)(2,1)}) custom-call(s32[1]{0:T(128)} %bitcast.9.index_ref, bf16[512,2048]{1,0:T(8,128)(2,1)} %copy-done, bf16[512,2048]{1,0:T(8,128)(2,1)} %all-reduce.6.cloned.1.call-done.branch_hbm, ...), custom_call_target="tpu_custom_call" | custom-call | flops 1 | bytes 1 | tf_op jit(solution)/shard_map/mlp/pallas_call | solution.py:434
  179.5 65.3 %conditional.7 = (bf16[2048,512]{1,0:T(8,128)(2,1)}, bf16[1024,2048]{1,0:T(8,128)(2,1)}, bf16[512,2048]{1,0:T(8,128)(2,1)}, bf16[1024,2048]{1,0:T(8,128)(2,1)}, ...) conditional(s32[]{:T(128)} %convert_element_type.96, () %tuple.104, (bf16[512,2048]{1,0:T(8,128)(2,1)}, ...), branch_computations={%region_9.10_spmd, %region_10.11_spmd} | conditional | flops 8 | bytes 100663640 | solution.py:653
  179.5 4.6 %down_outer.3 = bf16[2048,1024]{1,0:T(8,128)(2,1)S(1)} custom-call(bf16[512,2048]{1,0:T(8,128)(2,1)} %get-tuple-element.86.a_ref.hidden_ref, bf16[512,2048]{1,0:T(8,128)(2,1)S(1)} %get-tuple-element.87.b_ref), custom_call_target="tpu_custom_call" | custom-call | flops 1 | bytes 1 | tf_op jit(solution)/shard_map/cond/branch_1_fun/down_outer/pallas_call | solution.py:523
  195.4 11.4 %lift.1 = bf16[512,2048]{1,0:T(8,128)(2,1)} custom-call(bf16[512,2048]{1,0:T(8,128)(2,1)S(1)} %copy-done.29, bf16[2048,512]{1,0:T(8,128)(2,1)S(1)} %copy-done.41, bf16[2048,512]{1,0:T(8,128)(2,1)} %get-tuple-element.92.d1, bf16[2048,512]{1,0:T(8,128)(2,1)} %get-tuple-element.93.d2, bf16[2048,512]{1,0:T(8,128)(2,1)} %get-tuple-element.94.d3), custom_call_target="tpu_custom_call" | custom-call | flops 1 | bytes 1 | tf_op jit(solution)/shard_map/cond/branch_1_fun/lift/pallas_call | solution.py:559
  206.8 4.3 gate_outer.4
  211.1 4.3 up_outer.4
  215.3 26.0 %collective-permute-done.8.refs_1_ = bf16[2048,512]{1,0:T(8,128)(2,1)S(1)} collective-permute-done((bf16[2048,512]{1,0:T(8,128)(2,1)S(1)}, bf16[2048,512]{1,0:T(8,128)(2,1)S(1)}, u32[]{:S(2)}, u32[]{:S(2)}) %collective-permute-start.8) | collective-permute-done | bytes 2097184 | tf_op jit(solution)/shard_map/cond/branch_1_fun/ppermute | solution.py:661
  248.0 19.0 %all-reduce.8.cloned.1.call-done = bf16[512,2048]{1,0:T(8,128)(2,1)} async-done(((bf16[512,2048]{1,0:T(8,128)(2,1)}), bf16[512,2048]{1,0:T(8,128)(2,1)}) %all-reduce.8.cloned.1.call-update) | async-done | bytes 2097168 | tf_op jit(solution)/shard_map/psum | solution.py:692
  272.5 4.8 %multiply_convert_fusion = (bf16[512,2048]{1,0:T(8,128)(2,1)S(1)}, f32[512,2048]{1,0:T(8,128)}, f32[512,2048]{1,0:T(8,128)}) fusion(f32[512]{0:T(512)S(1)} %broadcast_multiply_fusion.1, f32[512]{0:T(512)S(1)} %get-tuple-element.312, bf16[512,2048]{1,0:T(8,128)(2,1)S(1)} %copy-done.28, bf16[512,2048]{1,0:T(8,128)(2,1)S(1)} %copy-done.1, ...), kind=kLoop, calls=%fused_computation.22 | loop fusion | flops 22020096 | bytes 18888704 | tf_op jit(solution)/shard_map/convert_element_type | solution.py:958
  277.4 16.9 %attend_backward.1 = (bf16[512,512]{1,0:T(8,128)(2,1)S(1)}, f32[1024,256]{1,0:T(8,128)S(1)}) custom-call(bf16[512,512]{1,0:T(8,128)(2,1)S(1)} %project_q.1.q_ref, s32[1024,1]{1,0:T(8,128)S(1)} %get-tuple-element.293.code_ref, s32[8,512]{1,0:T(8,128)S(1)} %stack.41.codes_ref, bf16[512,512]{1,0:T(8,128)(2,1)S(1)} %copy-done.37, ...), custom_call_target="tpu_custom_call" | custom-call | flops 1 | bytes 1 | tf_op jit(solution)/shard_map/attend_backward/pallas_call | solution.py:186
  296.0 5.0 %gate_outer.5 = bf16[512,2048]{1,0:T(8,128)(2,1)} custom-call(bf16[512,2048]{1,0:T(8,128)(2,1)S(1)} %copy-done.23, bf16[512,2048]{1,0:T(8,128)(2,1)S(1)} %copy-done.33, bf16[1024,2048]{1,0:T(8,128)(2,1)} %get-tuple-element.234.refs_0_, bf16[512,2048]{1,0:T(8,128)(2,1)} %collective-permute-done.33.refs_1_), custom_call_target="tpu_custom_call" | custom-call | flops 1 | bytes 1 | tf_op jit(solution)/shard_map/gate_outer/pallas_call | solution.py:523
  303.0 5.6 %entry_grad.1 = (bf16[512,768]{1,0:T(8,128)(2,1)S(1)}, bf16[512,2048]{1,0:T(8,128)(2,1)}) custom-call(bf16[512,512]{1,0:T(8,128)(2,1)} %copy-done.22, f32[512,256]{1,0:T(8,128)} %slice.103.own_ref, bf16[512,256]{1,0:T(8,128)(2,1)} %copy-done.56, f32[512,128]{1,0:T(8,128)} %copy-done.2, f32[512,128]{1,0:T(8,128)} %copy-done.3, bf16[512,512]{1,0:T(8,128)(2,1)} %refs_0_.3, ...), custom_call_target="tpu_custom_call" | custom-call | flops 1 | bytes 1 | tf_op jit(solution)/shard_map/entry_grad/pallas_call | solution.py:486
  310.1 11.7 %conditional.8 = (bf16[1024,1280]{1,0:T(8,128)(2,1)}, bf16[512,1280]{1,0:T(8,128)(2,1)}) conditional(s32[]{:T(128)} %convert_element_type.96, () %tuple.111, (bf16[512,512]{1,0:T(8,128)(2,1)S(1)}, bf16[512,2048]{1,0:T(8,128)(2,1)}, bf16[512,2048]{1,0:T(8,128)(2,1)}, bf16[512,768]{1,0:T(8,128)(2,1)S(1)}) %tuple.180), branch_computations={%region_14.15_spmd, %region_15.16_spmd} | conditional | flops 2 | bytes 27263088 | solution.py:653
  313.3 5.0 %collective-permute-done.11.refs_0_ = bf16[1024,1280]{1,0:T(8,128)(2,1)} collective-permute-done((bf16[1024,1280]{1,0:T(8,128)(2,1)S(1)}, bf16[1024,1280]{1,0:T(8,128)(2,1)}, u32[]{:S(2)}, u32[]{:S(2)}) %collective-permute-start.11) | collective-permute-done | bytes 2621472 | tf_op jit(solution)/shard_map/cond/branch_1_fun/ppermute | solution.py:657
  321.8 4.0 fusion.3
  326.1 10.9 %collective-permute-done.34.refs_1_ = bf16[512,2048]{1,0:T(8,128)(2,1)} collective-permute-done((bf16[512,2048]{1,0:T(8,128)(2,1)}, bf16[512,2048]{1,0:T(8,128)(2,1)}, u32[]{:S(2)}, u32[]{:S(2)}) %collective-permute-start.34) | collective-permute-done | bytes 2097184 | tf_op jit(solution)/shard_map/ppermute | solution.py:661
  337.0 5.8 %up_outer.5 = bf16[512,2048]{1,0:T(8,128)(2,1)} custom-call(bf16[512,2048]{1,0:T(8,128)(2,1)} %get-tuple-element.222.a_ref, bf16[512,2048]{1,0:T(8,128)(2,1)} %get-tuple-element.224.b_ref, bf16[1024,2048]{1,0:T(8,128)(2,1)} %get-tuple-element.237.refs_0_, bf16[512,2048]{1,0:T(8,128)(2,1)} %collective-permute-done.34.refs_1_), custom_call_target="tpu_custom_call" | custom-call | flops 1 | bytes 1 | tf_op jit(solution)/shard_map/up_outer/pallas_call | solution.py:523
  344.5 10.3 %all-reduce.10.cloned.1.call-done = bf16[512,2048]{1,0:T(8,128)(2,1)} async-done(((bf16[512,2048]{1,0:T(8,128)(2,1)}), bf16[512,2048]{1,0:T(8,128)(2,1)}) %all-reduce.10.cloned.1.call-update) | async-done | bytes 2097168 | tf_op jit(solution)/shard_map/psum | solution.py:692
  357.0 28.6 %collective-permute-done.37 = bf16[512,1280]{1,0:T(8,128)(2,1)S(1)} collective-permute-done((bf16[512,1280]{1,0:T(8,128)(2,1)}, bf16[512,1280]{1,0:T(8,128)(2,1)S(1)}, u32[]{:S(2)}, u32[]{:S(2)}) %collective-permute-start.37) | collective-permute-done | bytes 1310752 | tf_op jit(solution)/shard_map/ppermute | solution.py:661
  385.7 14.6 %collective-permute-done.36 = bf16[512,2048]{1,0:T(8,128)(2,1)} collective-permute-done((bf16[512,2048]{1,0:T(8,128)(2,1)}, bf16[512,2048]{1,0:T(8,128)(2,1)}, u32[]{:S(2)}, u32[]{:S(2)}) %collective-permute-start.36) | collective-permute-done | bytes 2097184 | tf_op jit(solution)/shard_map/ppermute | solution.py:669
  400.2 41.6 %conditional.9 = (f32[2,512]{1,0:T(2,128)}, bf16[512,2048]{1,0:T(8,128)(2,1)}, f32[2048,512]{1,0:T(8,128)}, f32[512,2048]{1,0:T(8,128)}, f32[512,2048]{1,0:T(8,1...) conditional(s32[]{:T(128)} %convert_element_type.96, () %tuple.83, ...), branch_computations={%region_17.18_spmd, %region_18.19_spmd} | conditional | flops 23995432 | bytes 92607496 | solution.py:653
  406.2 8.3 %convert_add_fusion = (f32[512,2048]{1,0:T(8,128)}, f32[512,2048]{1,0:T(8,128)}) fusion(bf16[512,2048]{1,0:T(8,128)(2,1)} %get-tuple-element.110, bf16[512,2048]{1,0:T(8,128)(2,1)} %get-tuple-element.109, bf16[512,2048]{1,0:T(8,128)(2,1)} %get-tuple-element.108, bf16[512,2048]{1,0:T(8,128)(2,1)S(1)} %copy-done.42), kind=kLoop, calls=%fused_computation | loop fusion | flops 6291456 | bytes 16777216 | tf_op jit(solution)/shard_map/cond/branch_1_fun/add | solution.py:765
  417.2 4.9 %convert_add_fusion.2 = f32[2048,512]{1,0:T(8,128)} fusion(bf16[2048,512]{1,0:T(8,128)(2,1)} %get-tuple-element.106, bf16[2048,512]{1,0:T(8,128)(2,1)} %get-tuple-element.105), kind=kLoop, calls=%fused_computation.2 | loop fusion | flops 3145728 | bytes 8388608 | tf_op jit(solution)/shard_map/cond/branch_1_fun/add | solution.py:765
  442.9 5.3 %exit_grad.1 = bf16[512,2048]{1,0:T(8,128)(2,1)} custom-call(s32[1]{0:T(128)} %bitcast.12.index_ref, f32[512,2048]{1,0:T(8,128)} %get-tuple-element.263.middle_ref, bf16[512,2048]{1,0:T(8,128)(2,1)} %all-reduce.12.cloned.1.call-done.dh_ref, bf16[512,2048]{1,0:T(8,128)(2,1)} %copy-done, f32[1,2048]{1,0:T(1,128)} %maximum_convert_fusion.1.gain_ref), custom_call_target="tpu_custom_call" | custom-call | flops 1 | bytes 1 | tf_op jit(solution)/shard_map/exit_grad/pallas_call | solution.py:630
  (280 shorter events, 124.7 us)
Async XLA Ops:
  7.2 140.8 %all-reduce.6.cloned.1.call-start = ((), (), s32[]{:S(2)}) async-start(), calls=%async_computation | async-start | bytes 4194304 | tf_op jit(solution)/shard_map/psum | solution.py:692
  7.7 15.7 %collective-permute-start.23 = (bf16[512,512]{1,0:T(8,128)(2,1)}, bf16[512,512]{1,0:T(8,128)(2,1)}, u32[]{:S(2)}, u32[]{:S(2)}) collective-permute-start(bf16[512,512]{1,0:T(8,128)(2,1)} %refs_0_.3), channel_id=1, source_target_pairs={{0,16},{8,24},{16,0},{24,8},{1,17},{9,25},{17,1},{25,9},{2,18},{10... | collective-permute-start | bytes 1572872 | tf_op jit(solution)/shard_map/ppermute | solution.py:661
  13.6 15.7 %collective-permute-start.20 = (bf16[544,256]{1,0:T(8,128)(2,1)S(1)}, bf16[544,256]{1,0:T(8,128)(2,1)}, u32[]{:S(2)}, u32[]{:S(2)}) collective-permute-start(bf16[544,256]{1,0:T(8,128)(2,1)S(1)} %fusion.13.p0.refs_4_), channel_id=1, source_target_pairs={{0,16},{8,24},{16,0},{24,8},{1,17},{9,25},{17,1},{25,9},{2,18},{10... | collective-permute-start | bytes 835592 | tf_op jit(solution)/shard_map/ppermute | solution.py:661
  13.7 9.8 %collective-permute-start.21 = (bf16[544,256]{1,0:T(8,128)(2,1)S(1)}, bf16[544,256]{1,0:T(8,128)(2,1)S(1)}, u32[]{:S(2)}, u32[]{:S(2)}) collective-permute-start(bf16[544,256]{1,0:T(8,128)(2,1)S(1)} %fusion.13.p0.refs_4_), channel_id=1, source_target_pairs={{0,8},{8,0},{16,24},{24,16},{1,9},{9,1},{17,25},{25,17},{2,10},{10... | collective-permute-start | bytes 835592 | tf_op jit(solution)/shard_map/ppermute | solution.py:657
  23.4 12.9 %collective-permute-start.24 = (bf16[512,512]{1,0:T(8,128)(2,1)}, bf16[512,512]{1,0:T(8,128)(2,1)S(1)}, u32[]{:S(2)}, u32[]{:S(2)}) collective-permute-start(bf16[512,512]{1,0:T(8,128)(2,1)} %collective-permute-done.23.p1.refs_1_), channel_id=1, source_target_pairs={{0,8},{8,0},{16,24},{24,16},{1,9},{9,1},{17,25},{25,17},{2,10},{10... | collective-permute-start | bytes 1572872 | tf_op jit(solution)/shard_map/ppermute | solution.py:657
  23.5 19.6 %collective-permute-start.26 = (bf16[512,512]{1,0:T(8,128)(2,1)}, bf16[512,512]{1,0:T(8,128)(2,1)}, u32[]{:S(2)}, u32[]{:S(2)}) collective-permute-start(bf16[512,512]{1,0:T(8,128)(2,1)} %o0.3), channel_id=1, source_target_pairs={{0,16},{8,24},{16,0},{24,8},{1,17},{9,25},{17,1},{25,9},{2,18},{10... | collective-permute-start | bytes 1572872 | tf_op jit(solution)/shard_map/ppermute | solution.py:661
  34.3 8.8 %collective-permute-start.25 = (bf16[512,256]{1,0:T(8,128)(2,1)S(1)}, bf16[512,256]{1,0:T(8,128)(2,1)S(1)}, u32[]{:S(2)}, u32[]{:S(2)}) collective-permute-start(bf16[512,256]{1,0:T(8,128)(2,1)S(1)} %get-tuple-element.201.refs_0_), channel_id=1, source_target_pairs={{0,4},{4,0},{1,5},{5,1},{2,6},{6,2},{3,7},{7,3},{8,12},{12,8},{9,1... | collective-permute-start | bytes 786440 | tf_op jit(solution)/shard_map/ppermute | solution.py:669
  36.3 18.6 %collective-permute-start.27 = (bf16[512,512]{1,0:T(8,128)(2,1)}, bf16[512,512]{1,0:T(8,128)(2,1)S(1)}, u32[]{:S(2)}, u32[]{:S(2)}) collective-permute-start(bf16[512,512]{1,0:T(8,128)(2,1)} %o0.3), channel_id=1, source_target_pairs={{0,8},{8,0},{16,24},{24,16},{1,9},{9,1},{17,25},{25,17},{2,10},{10... | collective-permute-start | bytes 1572872 | tf_op jit(solution)/shard_map/ppermute | solution.py:657
  43.1 11.8 %collective-permute-start.28 = (bf16[512,512]{1,0:T(8,128)(2,1)}, bf16[512,512]{1,0:T(8,128)(2,1)S(1)}, u32[]{:S(2)}, u32[]{:S(2)}) collective-permute-start(bf16[512,512]{1,0:T(8,128)(2,1)} %collective-permute-done.26.o1), channel_id=1, source_target_pairs={{0,8},{8,0},{16,24},{24,16},{1,9},{9,1},{17,25},{25,17},{2,10},{10... | collective-permute-start | bytes 1572872 | tf_op jit(solution)/shard_map/ppermute | solution.py:657
  43.2 48.8 %collective-permute-start.29 = (bf16[512,2048]{1,0:T(8,128)(2,1)}, bf16[512,2048]{1,0:T(8,128)(2,1)}, u32[]{:S(2)}, u32[]{:S(2)}) collective-permute-start(bf16[512,2048]{1,0:T(8,128)(2,1)} %pad_maximum_fusion.2), channel_id=1, source_target_pairs={{0,16},{8,24},{16,0},{24,8},{1,17},{9,25},{17,1},{25,9},{2,18},{10... | collective-permute-start | bytes 6291464 | tf_op jit(solution)/shard_map/ppermute | solution.py:661
  54.5 85.9 %collective-permute-start.30 = (bf16[2048,512]{1,0:T(8,128)(2,1)}, bf16[2048,512]{1,0:T(8,128)(2,1)}, u32[]{:S(2)}, u32[]{:S(2)}) collective-permute-start(bf16[2048,512]{1,0:T(8,128)(2,1)} %param.33), channel_id=1, source_target_pairs={{0,16},{8,24},{16,0},{24,8},{1,17},{9,25},{17,1},{25,9},{2,18},{10... | collective-permute-start | bytes 6291464 | tf_op jit(solution)/shard_map/ppermute | solution.py:661
  58.8 208.1 %all-reduce.8.cloned.1.call-start = ((), (), s32[]{:S(2)}) async-start(), calls=%async_computation.1 | async-start | bytes 4194304 | tf_op jit(solution)/shard_map/psum | solution.py:692
  92.0 48.4 %collective-permute-start = (bf16[512,2048]{1,0:T(8,128)(2,1)}, bf16[512,2048]{1,0:T(8,128)(2,1)}, u32[]{:S(2)}, u32[]{:S(2)}) collective-permute-start(bf16[512,2048]{1,0:T(8,128)(2,1)} %get-tuple-element.80), channel_id=1, source_target_pairs={{0,4},{4,0},{1,5},{5,1},{2,6},{6,2},{3,7},{7,3},{8,12},{12,8},{9,1... | collective-permute-start | bytes 6291464 | tf_op jit(solution)/shard_map/cond/branch_1_fun/ppermute | solution.py:669
  96.5 43.9 %collective-permute-start.2 = (bf16[512,2048]{1,0:T(8,128)(2,1)}, bf16[512,2048]{1,0:T(8,128)(2,1)}, u32[]{:S(2)}, u32[]{:S(2)}) collective-permute-start(bf16[512,2048]{1,0:T(8,128)(2,1)} %get-tuple-element.79), channel_id=1, source_target_pairs={{0,8},{8,0},{16,24},{24,16},{1,9},{9,1},{17,25},{25,17},{2,10},{10... | collective-permute-start | bytes 6291464 | tf_op jit(solution)/shard_map/cond/branch_1_fun/ppermute | solution.py:657
  96.8 43.6 %collective-permute-start.3 = (bf16[512,2048]{1,0:T(8,128)(2,1)}, bf16[512,2048]{1,0:T(8,128)(2,1)}, u32[]{:S(2)}, u32[]{:S(2)}) collective-permute-start(bf16[512,2048]{1,0:T(8,128)(2,1)} %get-tuple-element.80), channel_id=1, source_target_pairs={{0,8},{8,0},{16,24},{24,16},{1,9},{9,1},{17,25},{25,17},{2,10},{10... | collective-permute-start | bytes 6291464 | tf_op jit(solution)/shard_map/cond/branch_1_fun/ppermute | solution.py:657
  140.5 7.5 %collective-permute-start.6 = (bf16[2048,512]{1,0:T(8,128)(2,1)}, bf16[2048,512]{1,0:T(8,128)(2,1)}, u32[]{:S(2)}, u32[]{:S(2)}) collective-permute-start(bf16[2048,512]{1,0:T(8,128)(2,1)} %get-tuple-element.85), channel_id=1, source_target_pairs={{0,8},{8,0},{16,24},{24,16},{1,9},{9,1},{17,25},{25,17},{2,10},{10... | collective-permute-start | bytes 6291464 | tf_op jit(solution)/shard_map/cond/branch_1_fun/ppermute | solution.py:657
  178.8 176.0 %all-reduce.10.cloned.1.call-start = ((), (), s32[]{:S(2)}) async-start(), calls=%async_computation.2 | async-start | bytes 4194304 | tf_op jit(solution)/shard_map/psum | solution.py:692
  184.1 7.2 %collective-permute-start.7 = (bf16[2048,1024]{1,0:T(8,128)(2,1)S(1)}, bf16[2048,1024]{1,0:T(8,128)(2,1)S(1)}, u32[]{:S(2)}, u32[]{:S(2)}) collective-permute-start(bf16[2048,1024]{1,0:T(8,128)(2,1)S(1)} %down_outer.3), channel_id=1, source_target_pairs={{0,8},{8,0},{16,24},{24,16},{1,9},{9,1},{17,25},{25,17},{2,10},{10... | collective-permute-start | bytes 12582920 | tf_op jit(solution)/shard_map/cond/branch_1_fun/ppermute | solution.py:657
  187.0 19.8 %collective-permute-start.9 = (bf16[1024,2048]{1,0:T(8,128)(2,1)S(1)}, bf16[1024,2048]{1,0:T(8,128)(2,1)}, u32[]{:S(2)}, u32[]{:S(2)}) collective-permute-start(bf16[1024,2048]{1,0:T(8,128)(2,1)S(1)} %gate_outer.3), channel_id=1, source_target_pairs={{0,8},{8,0},{16,24},{24,16},{1,9},{9,1},{17,25},{25,17},{2,10},{10... | collective-permute-start | bytes 12582920 | tf_op jit(solution)/shard_map/cond/branch_1_fun/ppermute | solution.py:657
  190.1 20.9 %collective-permute-start.10 = (bf16[1024,2048]{1,0:T(8,128)(2,1)S(1)}, bf16[1024,2048]{1,0:T(8,128)(2,1)}, u32[]{:S(2)}, u32[]{:S(2)}) collective-permute-start(bf16[1024,2048]{1,0:T(8,128)(2,1)S(1)} %up_outer.3), channel_id=1, source_target_pairs={{0,8},{8,0},{16,24},{24,16},{1,9},{9,1},{17,25},{25,17},{2,10},{10... | collective-permute-start | bytes 12582920 | tf_op jit(solution)/shard_map/cond/branch_1_fun/ppermute | solution.py:657
  193.6 47.7 %collective-permute-start.8 = (bf16[2048,512]{1,0:T(8,128)(2,1)S(1)}, bf16[2048,512]{1,0:T(8,128)(2,1)S(1)}, u32[]{:S(2)}, u32[]{:S(2)}) collective-permute-start(bf16[2048,512]{1,0:T(8,128)(2,1)S(1)} %down_outer.4), channel_id=1, source_target_pairs={{0,16},{8,24},{16,0},{24,8},{1,17},{9,25},{17,1},{25,9},{2,18},{10... | collective-permute-start | bytes 6291464 | tf_op jit(solution)/shard_map/cond/branch_1_fun/ppermute | solution.py:661
  244.8 51.2 %collective-permute-start.33 = (bf16[512,2048]{1,0:T(8,128)(2,1)}, bf16[512,2048]{1,0:T(8,128)(2,1)}, u32[]{:S(2)}, u32[]{:S(2)}) collective-permute-start(bf16[512,2048]{1,0:T(8,128)(2,1)} %get-tuple-element.235), channel_id=1, source_target_pairs={{0,16},{8,24},{16,0},{24,8},{1,17},{9,25},{17,1},{25,9},{2,18},{10... | collective-permute-start | bytes 6291464 | tf_op jit(solution)/shard_map/ppermute | solution.py:661
  246.5 98.0 %collective-permute-start.32 = (bf16[2048,512]{1,0:T(8,128)(2,1)}, bf16[2048,512]{1,0:T(8,128)(2,1)}, u32[]{:S(2)}, u32[]{:S(2)}) collective-permute-start(bf16[2048,512]{1,0:T(8,128)(2,1)} %get-tuple-element.226), channel_id=1, source_target_pairs={{0,4},{4,0},{1,5},{5,1},{2,6},{6,2},{3,7},{7,3},{8,12},{12,8},{9,1... | collective-permute-start | bytes 6291464 | tf_op jit(solution)/shard_map/ppermute | solution.py:669
  267.0 70.0 %collective-permute-start.34 = (bf16[512,2048]{1,0:T(8,128)(2,1)}, bf16[512,2048]{1,0:T(8,128)(2,1)}, u32[]{:S(2)}, u32[]{:S(2)}) collective-permute-start(bf16[512,2048]{1,0:T(8,128)(2,1)} %get-tuple-element.239), channel_id=1, source_target_pairs={{0,16},{8,24},{16,0},{24,8},{1,17},{9,25},{17,1},{25,9},{2,18},{10... | collective-permute-start | bytes 6291464 | tf_op jit(solution)/shard_map/ppermute | solution.py:661
  294.4 7.8 %collective-permute-start.31 = (bf16[512,256]{1,0:T(8,128)(2,1)S(1)}, bf16[512,256]{1,0:T(8,128)(2,1)S(1)}, u32[]{:S(2)}, u32[]{:S(2)}) collective-permute-start(bf16[512,256]{1,0:T(8,128)(2,1)S(1)} %slice.151), channel_id=1, source_target_pairs={{0,4},{4,0},{1,5},{5,1},{2,6},{6,2},{3,7},{7,3},{8,12},{12,8},{9,1... | collective-permute-start | bytes 786440 | tf_op jit(solution)/shard_map/ppermute | solution.py:669
  308.6 77.1 %collective-permute-start.35 = (bf16[512,2048]{1,0:T(8,128)(2,1)}, bf16[512,2048]{1,0:T(8,128)(2,1)}, u32[]{:S(2)}, u32[]{:S(2)}) collective-permute-start(bf16[512,2048]{1,0:T(8,128)(2,1)} %gate_outer.5), channel_id=1, source_target_pairs={{0,4},{4,0},{1,5},{5,1},{2,6},{6,2},{3,7},{7,3},{8,12},{12,8},{9,1... | collective-permute-start | bytes 6291464 | tf_op jit(solution)/shard_map/ppermute | solution.py:669
  325.8 117.1 %all-reduce.12.cloned.1.call-start = ((), (), s32[]{:S(2)}) async-start(), calls=%async_computation.3 | async-start | bytes 4194304 | tf_op jit(solution)/shard_map/psum | solution.py:692
  342.8 57.4 %collective-permute-start.36 = (bf16[512,2048]{1,0:T(8,128)(2,1)}, bf16[512,2048]{1,0:T(8,128)(2,1)}, u32[]{:S(2)}, u32[]{:S(2)}) collective-permute-start(bf16[512,2048]{1,0:T(8,128)(2,1)} %up_outer.5), channel_id=1, source_target_pairs={{0,4},{4,0},{1,5},{5,1},{2,6},{6,2},{3,7},{7,3},{8,12},{12,8},{9,1... | collective-permute-start | bytes 6291464 | tf_op jit(solution)/shard_map/ppermute | solution.py:669
  354.9 30.8 %collective-permute-start.37 = (bf16[512,1280]{1,0:T(8,128)(2,1)}, bf16[512,1280]{1,0:T(8,128)(2,1)S(1)}, u32[]{:S(2)}, u32[]{:S(2)}) collective-permute-start(bf16[512,1280]{1,0:T(8,128)(2,1)} %get-tuple-element.245), channel_id=1, source_target_pairs={{0,16},{8,24},{16,0},{24,8},{1,17},{9,25},{17,1},{25,9},{2,18},{10... | collective-permute-start | bytes 3932168 | tf_op jit(solution)/shard_map/ppermute | solution.py:661
  404.7 28.4 %collective-permute-start.18 = (bf16[512,1280]{1,0:T(8,128)(2,1)S(1)}, bf16[512,1280]{1,0:T(8,128)(2,1)}, u32[]{:S(2)}, u32[]{:S(2)}) collective-permute-start(bf16[512,1280]{1,0:T(8,128)(2,1)S(1)} %entry_outer.5), channel_id=1, source_target_pairs={{0,4},{4,0},{1,5},{5,1},{2,6},{6,2},{3,7},{7,3},{8,12},{12,8},{9,1... | collective-permute-start | bytes 3932168 | tf_op jit(solution)/shard_map/cond/branch_1_fun/ppermute | solution.py:669
  405.7 8.9 %collective-permute-start.13 = (f32[2,512]{1,0:T(2,128)S(1)}, f32[2,512]{1,0:T(2,128)S(1)}, u32[]{:S(2)}, u32[]{:S(2)}) collective-permute-start(f32[2,512]{1,0:T(2,128)S(1)} %get-tuple-element.278), channel_id=1, source_target_pairs={{0,16},{8,24},{16,0},{24,8},{1,17},{9,25},{17,1},{25,9},{2,18},{10... | collective-permute-start | bytes 12296 | tf_op jit(solution)/shard_map/cond/branch_1_fun/ppermute | solution.py:661
  415.8 6.2 %collective-permute-start.15 = (f32[2,512]{1,0:T(2,128)S(1)}, f32[2,512]{1,0:T(2,128)S(1)}, u32[]{:S(2)}, u32[]{:S(2)}) collective-permute-start(f32[2,512]{1,0:T(2,128)S(1)} %get-tuple-element.102), channel_id=1, source_target_pairs={{0,24},{8,16},{16,8},{24,0},{1,25},{9,17},{17,9},{25,1},{2,26},{10... | collective-permute-start | bytes 12296 | tf_op jit(solution)/shard_map/cond/branch_1_fun/ppermute | solution.py:665
  (74 other events, 521.9 us)
Sparse Core Ops, SparseCore 0:
  59.0 87.9 all-reduce.5
  179.0 87.9 all-reduce.7
  269.3 85.4 all-reduce.9
  357.2 85.6 all-reduce.11
